TPU v7x, 32 devices: a whole 2x2x4 slice. The times are simulated.
32 devices in a mesh: ens: 2 (over y), seq: 4 (over z), mp: 2 (over x), sub: 2 (over core).
Axes of the slice: x: 2, y: 2, z: 4, core: 2. Of those that a mesh axis runs over, the one named last changes fastest.
Arguments:
- grid_latent: bfloat16 [16384, 1024], P(('ens', 'seq'), ('mp', 'sub')), parts along dimension 0, may hold values from -6 to 6
- grid_count: int32 [8], P(('ens', 'seq')), parts along dimension 0, may hold values from 1024 to 2048, as said below
- hidden_embed: bfloat16 [8192, 1024], P(('ens', 'seq'), ('mp', 'sub')), parts along dimension 0, may hold values from -6 to 6
- enc_src_rows: int32 [8, 32, 128], P(('ens', 'seq')), parts along dimension 0, may hold values from 0 to 2047, as said below
- enc_dst_rows: int32 [8, 32, 128], P(('ens', 'seq')), parts along dimension 0, may hold values from 0 to 1023
- enc_weight: float32 [8, 32, 128], P(('ens', 'seq')), parts along dimension 0, may hold values from 0.25 to 1
- dec_src_rows: int32 [8, 48, 128], P(('ens', 'seq')), parts along dimension 0, may hold values from 0 to 1023
- dec_dst_rows: int32 [8, 48, 128], P(('ens', 'seq')), parts along dimension 0, may hold values from 0 to 2047, as said below
- dec_weight: float32 [8, 48, 128], P(('ens', 'seq')), parts along dimension 0, may hold values from 0.25 to 1
- norm_gain: float32 [1024], replicated, may hold values from 0.1 to 1.9
- w_qkv: bfloat16 [1024, 3072], P(None, ('mp', 'sub'))
- w_out: bfloat16 [1024, 1024], P(('mp', 'sub')), may hold values from -0.1875 to 0.1875
- w_up: bfloat16 [1024, 4096], P(None, ('mp', 'sub')), may hold values from -0.1875 to 0.1875
- up_exp: int32 [4096], P(('mp', 'sub')), may hold values from -1 to 1
- w_down: bfloat16 [4096, 1024], P(('mp', 'sub')), may hold values from -0.09375 to 0.09375
- down_exp: int32 [1024], replicated, may hold values from -1 to 1
Outputs:
- hidden_out: bfloat16 [8192, 1024], P(('ens', 'seq'), ('mp', 'sub')), parts along dimension 0
- grid_out: bfloat16 [16384, 1024], P(('ens', 'seq'), ('mp', 'sub')), parts along dimension 0
There are 2 independent parts, one for each index of `ens`. A program takes and returns all parts, laid end to end along the dimension named above; an argument that names none is the same for every part. Nothing has to cross between parts.
Inputs may be any that keep to these rules, and one draw needn't show every extreme that they name: `grid_count`: each block holds between 1024 and 2048 live grid nodes; some block holds exactly 2048. `enc_src_rows`: each source row is below grid_count of its sending block s. `dec_dst_rows`: each destination row is below grid_count of its receiving block d.
All inputs are finite; a program needn't handle non-finite values.
Results may differ from a plain program's by a relative error of at most 0.013.
Values may be sent and summed in bfloat16 or wider, within the bound.
No kernel may reach another device: no remote copies, remote signals or barrier semaphores. Data moves between devices by JAX's collectives and lax.ppermute only.
A program may use at most 128 MiB of HBM per device.

v0:
```python
import jax
import jax.numpy as jnp
from jax import lax
from jax.sharding import PartitionSpec as P

HD = 64
WIN = 512
TILE = 128
ESIDE = 4
DSIDE = 4


def padded(cells, sides, width):
    for axis, dim in sides:
        count = lax.axis_size(axis)
        ends = count - 1
        head = lax.slice_in_dim(cells, 0, width, axis=dim)
        tail = lax.slice_in_dim(cells, cells.shape[dim] - width, cells.shape[dim], axis=dim)
        cells = jnp.concatenate(
            [
                lax.ppermute(tail, axis, [(i, (i + 1) % count) for i in range(ends)]),
                cells,
                lax.ppermute(head, axis, [((i + 1) % count, i) for i in range(ends)]),
            ],
            axis=dim,
        )
    return cells


def normed_rows(rows, norm_gain):
    values = rows.astype(jnp.float32)
    row_mean = jnp.mean(values, axis=-1, keepdims=True)
    centered = values - row_mean
    row_var = jnp.mean(centered * centered, axis=-1, keepdims=True)
    return (centered * lax.rsqrt(row_var + 1e-05) * norm_gain[None, :]).astype(jnp.bfloat16)


def split_heads(normed, w_qkv):
    heads_here = w_qkv.shape[1] // (3 * HD)
    qkv = jnp.dot(normed, w_qkv, preferred_element_type=jnp.float32).reshape(
        normed.shape[0], heads_here, 3, HD
    )
    return qkv.astype(jnp.bfloat16)


def edge_messages(source, src_rows, weights):
    picked = (
        jnp.take(source, src_rows.reshape(-1), axis=0).astype(jnp.float32)
        * weights.reshape(-1)[:, None]
    )
    return picked.astype(jnp.bfloat16)


def arrange_arrivals(messages, extended, width):
    return jnp.concatenate([extended[:width], extended[3 * width :], messages[2 * width :]], axis=0)


def shards(
    grid_latent,
    grid_count,
    hidden_embed,
    enc_src_rows,
    enc_dst_rows,
    enc_weight,
    dec_src_rows,
    dec_dst_rows,
    dec_weight,
    norm_gain,
    w_qkv,
    w_out,
    w_up,
    up_exp,
    w_down,
    down_exp,
):
    blocks = lax.axis_size("seq")
    seq_index = lax.axis_index("seq")
    hid_rows = hidden_embed.shape[0]
    enc_width = ESIDE * TILE
    enc_messages = edge_messages(grid_latent, enc_src_rows, enc_weight)
    enc_extended = padded(enc_messages[: 2 * enc_width], (("seq", 0),), enc_width)
    arrived = arrange_arrivals(enc_messages, enc_extended, enc_width)
    encoded = jax.ops.segment_sum(
        arrived.astype(jnp.float32), enc_dst_rows.reshape(-1), num_segments=hid_rows
    )
    latent = (hidden_embed.astype(jnp.float32) + encoded).astype(jnp.bfloat16)
    heads_here = w_qkv.shape[1] // (3 * HD)
    full_rows = lax.all_gather(latent, ("mp", "sub"), axis=1, tiled=True)
    normed = normed_rows(full_rows, norm_gain)
    qkv = split_heads(normed, w_qkv)
    queries = qkv[:, :, 0, :]
    stacked = qkv[:, :, 1:, :].transpose(0, 2, 1, 3).reshape(hid_rows, 2, heads_here * HD)
    stacked_ext = padded(stacked, (("seq", 0),), WIN)
    stacked_ext = stacked_ext.reshape(hid_rows + 2 * WIN, 2, heads_here, HD)
    keys_ext = stacked_ext[:, 0]
    values_ext = stacked_ext[:, 1]
    query_rows = min(512, hid_rows)
    span = query_rows + 2 * WIN
    hidden_total = hid_rows * blocks
    scale = HD ** (-0.5)
    attended_blocks = []
    for block in range(hid_rows // query_rows):
        first = block * query_rows
        query_block = queries[first : first + query_rows]
        key_block = keys_ext[first : first + span]
        value_block = values_ext[first : first + span]
        scores = (
            jnp.einsum("qhd,khd->hqk", query_block, key_block, preferred_element_type=jnp.float32)
            * scale
        )
        query_pos = seq_index * hid_rows + first + jnp.arange(query_rows, dtype=jnp.int32)
        key_pos = seq_index * hid_rows + first - WIN + jnp.arange(span, dtype=jnp.int32)
        allowed = (
            (jnp.abs(query_pos[:, None] - key_pos[None, :]) <= WIN)
            & (key_pos[None, :] >= 0)
            & (key_pos[None, :] < hidden_total)
        )
        scores = jnp.where(allowed[None, :, :], scores, -1e30)
        peak = jnp.max(scores, axis=-1, keepdims=True)
        expo = jnp.exp(scores - peak)
        attn_weights = (expo / jnp.sum(expo, axis=-1, keepdims=True)).astype(jnp.bfloat16)
        mixed = jnp.einsum(
            "hqk,khd->qhd", attn_weights, value_block, preferred_element_type=jnp.float32
        )
        attended_blocks.append(mixed.astype(jnp.bfloat16).reshape(query_rows, heads_here * HD))
    attended = jnp.concatenate(attended_blocks, axis=0)
    up_proj = (
        jnp.dot(normed, w_up, preferred_element_type=jnp.float32)
        * jnp.exp2(up_exp.astype(jnp.float32))[None, :]
    )
    activated = jax.nn.gelu(up_proj, approximate=False).astype(jnp.bfloat16)
    attn_part = jnp.dot(attended, w_out, preferred_element_type=jnp.float32)
    mlp_part = (
        jnp.dot(activated, w_down, preferred_element_type=jnp.float32)
        * jnp.exp2(down_exp.astype(jnp.float32))[None, :]
    )
    summed = lax.psum_scatter(
        (attn_part + mlp_part).astype(jnp.bfloat16), ("mp", "sub"), scatter_dimension=1, tiled=True
    ).astype(jnp.float32)
    hidden_out = (latent.astype(jnp.float32) + summed).astype(jnp.bfloat16)
    dec_width = DSIDE * TILE
    dec_messages = edge_messages(hidden_out, dec_src_rows, dec_weight)
    dec_extended = padded(dec_messages[: 2 * dec_width], (("seq", 0),), dec_width)
    arrived_dec = arrange_arrivals(dec_messages, dec_extended, dec_width)
    grid_rows = grid_latent.shape[0]
    decoded = jax.ops.segment_sum(
        arrived_dec.astype(jnp.float32), dec_dst_rows.reshape(-1), num_segments=grid_rows
    )
    live_rows = jnp.arange(grid_rows, dtype=jnp.int32) < grid_count[0]
    grid_out = jnp.where(live_rows[:, None], grid_latent.astype(jnp.float32) + decoded, 0.0).astype(
        jnp.bfloat16
    )
    return (hidden_out, grid_out)


def solution(mesh):
    placed = (
        P(("ens", "seq"), ("mp", "sub")),
        P(("ens", "seq")),
        P(("ens", "seq"), ("mp", "sub")),
        P(("ens", "seq"), None, None),
        P(("ens", "seq"), None, None),
        P(("ens", "seq"), None, None),
        P(("ens", "seq"), None, None),
        P(("ens", "seq"), None, None),
        P(("ens", "seq"), None, None),
        P(),
        P(None, ("mp", "sub")),
        P(("mp", "sub"), None),
        P(None, ("mp", "sub")),
        P(("mp", "sub")),
        P(("mp", "sub"), None),
        P(),
    )
    return jax.shard_map(
        shards,
        mesh=mesh,
        in_specs=placed,
        out_specs=(P(("ens", "seq"), ("mp", "sub")), P(("ens", "seq"), ("mp", "sub"))),
        check_vma=False,
    )
```

profile of v0, /device:TPU:0, one launch (start us, length us, event | category | flops | bytes accessed | tf_op | source)
XLA Modules:
  0.0 322.7 jit_solution(15461693998175101110)
XLA Ops:
  7.2 0.0 copy-start
  7.2 0.0 all-gather.2.cloned.1.call-start
  7.2 0.9 compare_and_fusion.1
  8.1 0.7 compare_select_fusion.1
  8.8 0.0 copy-start.11
  8.9 17.2 %gather_fusion = bf16[4096,256]{1,0:T(8,128)(2,1)} fusion(bf16[2048,256]{1,0:T(8,128)(2,1)} %param.16, s32[4096]{0:T(1024)S(1)} %broadcast_clamp_fusion.1), kind=kCustom, calls=%fused_computation | custom fusion | bytes 4210688 | tf_op jit(solution)/shard_map/jit(_take)/gather | solution.py:48
  26.1 0.0 copy-done.11
  26.1 3.2 %multiply_convert_fusion.1 = bf16[4096,256]{1,0:T(8,128)(2,1)S(1)} fusion(f32[4096]{0:T(1024)S(1)} %bitcast.73, bf16[4096,256]{1,0:T(8,128)(2,1)} %gather_fusion, pred[4096]{0:T(1024)(128)(4,1)S(1)} %compare_and_fusion.1), kind=kLoop, calls=%fused_computation.52 | loop fusion | flops 4194304 | bytes 4214784 | tf_op jit(solution)/shard_map/convert_element_type | solution.py:51
  29.4 5.0 %collective-permute-start = (bf16[512,256]{1,0:T(8,128)(2,1)S(1)}, bf16[512,256]{1,0:T(8,128)(2,1)S(1)}, u32[]{:S(2)}, u32[]{:S(2)}) collective-permute-start(bf16[512,256]{1,0:T(8,128)(2,1)S(1)} %get-tuple-element.4), channel_id=1, source_target_pairs={{0,4},{4,8},{8,12},{1,5},{5,9},{9,13},{2,6},{6,10},{10,14},{3,7},{... | collective-permute-start | bytes 786440 | tf_op jit(solution)/shard_map/ppermute | solution.py:21
  34.3 1.3 collective-permute-start.1
  35.6 1.2 slice.117
  36.9 0.0 copy-done.6
  36.9 0.1 convert_element_type.81
  37.0 2.9 collective-permute-done
  39.9 4.1 %collective-permute-done.1 = bf16[512,256]{1,0:T(8,128)(2,1)S(1)} collective-permute-done((bf16[512,256]{1,0:T(8,128)(2,1)S(1)}, bf16[512,256]{1,0:T(8,128)(2,1)S(1)}, u32[]{:S(2)}, u32[]{:S(2)}) %collective-permute-start.1) | collective-permute-done | bytes 262176 | tf_op jit(solution)/shard_map/ppermute | solution.py:23
  44.0 0.7 copy-done.8
  44.7 25.4 %scatter_custom_fusion = f32[1024,256]{1,0:T(8,128)S(1)} fusion(f32[1024,256]{1,0:T(8,128)S(1)} %convert_element_type.81, s32[4096]{0:T(1024)} %bitcast.75, bf16[3072,256]{1,0:T(8,128)(2,1)} %slice.117, bf16[]{:T(256)} %constant.130, bf16[512,256]{1,0:T(8,128)(2,1)} %copy-done.8, bf16[512,256]{1,0:T(8,128)(2,1)S(1)} %collective-permute-done), kind=kCustom, calls=%fused_computation.50 | custom fusion | flops 7340032 | bytes 3146240 | tf_op jit(solution)/shard_map/scatter-add | solution.py:83
  70.1 0.0 copy-start.3
  70.2 0.0 copy-start.15
  70.2 0.9 convert_element_type.85
  71.1 0.0 all-gather.2.cloned.1.call-update
  71.1 0.0 reduce-scatter.2.cloned.1.call-start
  71.3 0.0 copy-done.12
  71.3 0.0 copy-done.13
  71.3 2.1 fusion.37
  73.4 21.0 %all-gather.2.cloned.1.call-done = bf16[1024,1024]{1,0:T(8,128)(2,1)} async-done(((bf16[1024,256]{1,0:T(8,128)(2,1)}), bf16[1024,1024]{1,0:T(8,128)(2,1)}) %all-gather.2.cloned.1.call-update) | async-done | bytes 2097168 | tf_op jit(solution)/shard_map/all_gather | solution.py:88
  94.3 2.1 convert_reduce_fusion
  96.4 2.3 fusion.16
  98.7 0.0 copy-done.15
  98.7 0.0 copy-done.4
  98.7 0.0 copy-done.14
  98.7 2.2 convolution_convert_fusion
  101.0 0.1 copy_bitcast_fusion
  101.0 0.1 fusion.113
  101.1 3.4 %collective-permute-start.2 = (bf16[512,2,256]{0,2,1:T(8,128)(2,1)S(1)}, bf16[512,2,256]{0,2,1:T(8,128)(2,1)S(1)}, u32[]{:S(2)}, u32[]{:S(2)}) collective-permute-start(bf16[512,2,256]{0,2,1:T(8,128)(2,1)S(1)} %bitcast.65), channel_id=1, source_target_pairs={{0,4},{4,8},{8,12},{1,5},{5,9},{9,13},{2,6},{6,10},{10,14},{3,7},{... | collective-permute-start | bytes 1572872 | tf_op jit(solution)/shard_map/ppermute | solution.py:21
  104.6 1.1 fusion.39
  105.7 1.5 collective-permute-start.3
  107.2 8.9 %collective-permute-done.2 = bf16[512,2,256]{0,2,1:T(8,128)(2,1)S(1)} collective-permute-done((bf16[512,2,256]{0,2,1:T(8,128)(2,1)S(1)}, bf16[512,2,256]{0,2,1:T(8,128)(2,1)S(1)}, u32[]{:S(2)}, u32[]{:S(2)}) %collective-permute-start.2) | collective-permute-done | bytes 524320 | tf_op jit(solution)/shard_map/ppermute | solution.py:21
  116.1 6.3 %fusion.58 = f32[4,512,1536]{2,1,0:T(8,128)} fusion(bf16[1024,2,4,64]{0,3,2,1:T(8,128)(2,1)S(1)} %copy_bitcast_fusion, bf16[512,2,4,64]{0,3,2,1:T(8,128)(2,1)S(1)} %bitcast.60, bf16[1024,4,3,64]{0,3,2,1:T(8,128)(2,1)S(1)} %bitcast.58), kind=kOutput, calls=%fused_computation.91 | convolution fusion | flops 404226048 | bytes 14417920 | tf_op jit(solution)/shard_map/qhd,khd->hqk/dot_general | solution.py:108
  122.4 0.0 collective-permute-done.3
  122.4 6.4 %fusion.54 = f32[4,512,1536]{2,1,0:T(8,128)} fusion(bf16[512,2,4,64]{0,3,2,1:T(8,128)(2,1)S(1)} %bitcast.62, bf16[1024,2,4,64]{0,3,2,1:T(8,128)(2,1)S(1)} %copy_bitcast_fusion, bf16[1024,4,3,64]{0,3,2,1:T(8,128)(2,1)S(1)} %bitcast.59), kind=kOutput, calls=%fused_computation.87 | convolution fusion | flops 404226048 | bytes 14417920 | tf_op jit(solution)/shard_map/qhd,khd->hqk/dot_general | solution.py:108
  128.8 16.5 %fusion.115 = (f32[4,512]{1,0:T(4,128)S(1)}, f32[4,512,1536]{2,1,0:T(8,128)}) fusion(f32[4,512,1536]{2,1,0:T(8,128)} %fusion.58, pred[512,1536]{1,0:T(8,128)(4,1)S(1)} %copy-done.5), kind=kOutput, calls=%fused_computation.163 | output fusion | flops 18875904 | bytes 25960448 | tf_op jit(solution)/shard_map/sub | solution.py:120
  145.3 6.7 %fusion.46 = bf16[4,64,512]{2,1,0:T(8,128)(2,1)S(1)} fusion(f32[4,512,1536]{2,1,0:T(8,128)} %get-tuple-element.11, f32[4,512]{1,0:T(4,128)S(1)} %get-tuple-element.10, bf16[512,2,4,64]{0,3,2,1:T(8,128)(2,1)S(1)} %bitcast.61, bf16[1024,2,4,64]{0,3,2,1:T(8,128)(2,1)S(1)} %copy_bitcast_fusion), kind=kOutput, calls=%fused_computation.78 | convolution fusion | flops 410648576 | bytes 14426112 | tf_op jit(solution)/shard_map/hqk,khd->qhd/dot_general | solution.py:122
  151.9 16.1 %fusion.114 = (f32[4,512]{1,0:T(4,128)S(1)}, f32[4,512,1536]{2,1,0:T(8,128)}) fusion(f32[4,512,1536]{2,1,0:T(8,128)} %fusion.54, pred[512,1536]{1,0:T(8,128)(4,1)S(1)} %fusion.39), kind=kOutput, calls=%fused_computation.162 | output fusion | flops 18875904 | bytes 25960448 | tf_op jit(solution)/shard_map/sub | solution.py:120
  168.0 6.7 %fusion.45 = bf16[4,64,512]{2,1,0:T(8,128)(2,1)S(1)} fusion(f32[4,512,1536]{2,1,0:T(8,128)} %get-tuple-element.9, f32[4,512]{1,0:T(4,128)S(1)} %get-tuple-element.8, bf16[1024,2,4,64]{0,3,2,1:T(8,128)(2,1)S(1)} %copy_bitcast_fusion, bf16[512,2,4,64]{0,3,2,1:T(8,128)(2,1)S(1)} %bitcast.63), kind=kOutput, calls=%fused_computation.77 | convolution fusion | flops 410648576 | bytes 14426112 | tf_op jit(solution)/shard_map/hqk,khd->qhd/dot_general | solution.py:122
  174.8 2.7 fusion.61
  177.5 16.8 %add_convert_fusion = bf16[1024,1024]{1,0:T(8,128)(2,1)} fusion(f32[1024,1024]{1,0:T(8,128)} %fusion.61, bf16[1024,1024]{1,0:T(8,128)(2,1)S(1)} %copy-done, f32[1024]{0:T(1024)S(1)} %get-tuple-element.16, bf16[1024,1024]{1,0:T(8,128)(2,1)} %param.28, f32[1024]{0:T(1024)S(1)} %get-tuple-element.17, bf16[1024,1024]{1,0:T(8,128)(2,1)} %all-gather.2.cloned.1.call-done, ...), kind=kOutput, calls=%fused_computation.36 | convolution fusion | flops 4372561920 | bytes 12603392 | tf_op jit(solution)/shard_map/dot_general | solution.py:134
  194.3 0.0 reduce-scatter.2.cloned.1.call-update
  194.4 32.3 %reduce-scatter.2.cloned.1.call-done = bf16[1024,256]{1,0:T(8,128)(2,1)} async-done(((bf16[1024,1024]{1,0:T(8,128)(2,1)}), bf16[1024,256]{1,0:T(8,128)(2,1)}) %reduce-scatter.2.cloned.1.call-update) | async-done | bytes 524304 | tf_op jit(solution)/shard_map/reduce_scatter | solution.py:137
  226.7 1.5 add_convert_fusion.1
  228.2 0.0 copy-start.1
  228.2 0.0 copy-start.10
  228.2 25.0 %gather_fusion.1 = bf16[6144,256]{1,0:T(8,128)(2,1)} fusion(bf16[1024,256]{1,0:T(8,128)(2,1)S(1)} %add_convert_fusion.1, s32[6144]{0:T(1024)S(1)} %broadcast_clamp_fusion), kind=kCustom, calls=%fused_computation.1 | custom fusion | bytes 6316032 | tf_op jit(solution)/shard_map/jit(_take)/gather | solution.py:48
  253.2 0.0 copy-done.1
  253.2 0.0 copy-done.10
  253.2 4.7 %multiply_convert_fusion = bf16[6144,256]{1,0:T(8,128)(2,1)S(1)} fusion(f32[6144]{0:T(1024)S(1)} %bitcast.72, bf16[6144,256]{1,0:T(8,128)(2,1)} %gather_fusion.1, pred[6144]{0:T(1024)(128)(4,1)S(1)} %compare_and_fusion), kind=kLoop, calls=%fused_computation.16 | loop fusion | flops 6291456 | bytes 6322176 | tf_op jit(solution)/shard_map/convert_element_type | solution.py:51
  257.9 3.4 %collective-permute-start.4 = (bf16[512,256]{1,0:T(8,128)(2,1)S(1)}, bf16[512,256]{1,0:T(8,128)(2,1)S(1)}, u32[]{:S(2)}, u32[]{:S(2)}) collective-permute-start(bf16[512,256]{1,0:T(8,128)(2,1)S(1)} %get-tuple-element.2), channel_id=1, source_target_pairs={{0,4},{4,8},{8,12},{1,5},{5,9},{9,13},{2,6},{6,10},{10,14},{3,7},{... | collective-permute-start | bytes 786440 | tf_op jit(solution)/shard_map/ppermute | solution.py:21
  261.3 1.3 collective-permute-start.5
  262.6 1.5 convert_element_type.103
  264.8 1.7 slice.129
  266.5 0.2 collective-permute-done.4
  266.7 4.1 %collective-permute-done.5 = bf16[512,256]{1,0:T(8,128)(2,1)S(1)} collective-permute-done((bf16[512,256]{1,0:T(8,128)(2,1)S(1)}, bf16[512,256]{1,0:T(8,128)(2,1)S(1)}, u32[]{:S(2)}, u32[]{:S(2)}) %collective-permute-start.5) | collective-permute-done | bytes 262176 | tf_op jit(solution)/shard_map/ppermute | solution.py:23
  270.8 42.5 %scatter_custom_fusion.1 = f32[2048,256]{1,0:T(8,128)} fusion(f32[2048,256]{1,0:T(8,128)} %convert_element_type.103, s32[6144]{0:T(1024)} %bitcast.74, bf16[5120,256]{1,0:T(8,128)(2,1)} %slice.129, bf16[]{:T(256)} %constant.130, bf16[512,256]{1,0:T(8,128)(2,1)S(1)} %collective-permute-done.5, bf16[512,256]{1,0:T(8,128)(2,1)S(1)} %collective-permute-done.4), kind=kCustom, calls=%fused_computation.14 | custom fusion | flops 11010048 | bytes 5243392 | tf_op jit(solution)/shard_map/scatter-add | solution.py:146
  313.3 2.5 select_convert_fusion
  (32 shorter events, 0.2 us)
Async XLA Ops:
  7.2 170.3 %copy-start = (bf16[1024,1024]{1,0:T(8,128)(2,1)S(1)}, bf16[1024,1024]{1,0:T(8,128)(2,1)}, u32[]{:S(2)}) copy-start(bf16[1024,1024]{1,0:T(8,128)(2,1)} %param.30) | copy-start | bytes 6291460
  7.2 87.1 %all-gather.2.cloned.1.call-start = ((), (), s32[]{:S(2)}) async-start(), calls=%async_computation.1 | async-start | bytes 2621440 | tf_op jit(solution)/shard_map/all_gather | solution.py:88
  8.8 17.2 %copy-start.11 = (f32[1,32,128]{2,1,0:T(8,128)S(1)}, f32[1,32,128]{2,1,0:T(8,128)}, u32[]{:S(2)}) copy-start(f32[1,32,128]{2,1,0:T(8,128)} %param.21) | copy-start | bytes 49156
  26.1 10.8 %copy-start.6 = (bf16[1024,256]{1,0:T(8,128)(2,1)S(1)}, bf16[1024,256]{1,0:T(8,128)(2,1)}, u32[]{:S(2)}) copy-start(bf16[1024,256]{1,0:T(8,128)(2,1)} %param.18) | copy-start | bytes 1572868
  29.4 10.5 %collective-permute-start = (bf16[512,256]{1,0:T(8,128)(2,1)S(1)}, bf16[512,256]{1,0:T(8,128)(2,1)S(1)}, u32[]{:S(2)}, u32[]{:S(2)}) collective-permute-start(bf16[512,256]{1,0:T(8,128)(2,1)S(1)} %get-tuple-element.4), channel_id=1, source_target_pairs={{0,4},{4,8},{8,12},{1,5},{5,9},{9,13},{2,6},{6,10},{10,14},{3,7},{... | collective-permute-start | bytes 786440 | tf_op jit(solution)/shard_map/ppermute | solution.py:21
  34.3 9.7 %collective-permute-start.1 = (bf16[512,256]{1,0:T(8,128)(2,1)S(1)}, bf16[512,256]{1,0:T(8,128)(2,1)S(1)}, u32[]{:S(2)}, u32[]{:S(2)}) collective-permute-start(bf16[512,256]{1,0:T(8,128)(2,1)S(1)} %get-tuple-element.5), channel_id=1, source_target_pairs={{4,0},{8,4},{12,8},{5,1},{9,5},{13,9},{6,2},{10,6},{14,10},{7,3},{... | collective-permute-start | bytes 786440 | tf_op jit(solution)/shard_map/ppermute | solution.py:23
  36.9 34.4 %copy-start.12 = (s32[1024]{0:T(1024)S(1)}, s32[1024]{0:T(1024)}, u32[]{:S(2)}) copy-start(s32[1024]{0:T(1024)} %param.31) | copy-start | bytes 12292
  36.9 34.4 %copy-start.13 = (s32[1024]{0:T(1024)S(1)}, s32[1024]{0:T(1024)}, u32[]{:S(2)}) copy-start(s32[1024]{0:T(1024)} %param.29) | copy-start | bytes 12292
  44.0 0.7 copy-start.8
  70.1 30.8 %copy-start.3 = (f32[1024,256]{1,0:T(8,128)}, f32[1024,256]{1,0:T(8,128)S(1)}, u32[]{:S(2)}) copy-start(f32[1024,256]{1,0:T(8,128)S(1)} %scatter_custom_fusion) | copy-start | bytes 3145732
  70.2 28.6 %copy-start.15 = (f32[1024]{0:T(1024)S(1)}, f32[1024]{0:T(1024)}, u32[]{:S(2)}) copy-start(f32[1024]{0:T(1024)} %param.25) | copy-start | bytes 12292
  71.1 155.5 %reduce-scatter.2.cloned.1.call-start = ((), (), s32[]{:S(2)}) async-start(), calls=%async_computation.2 | async-start | bytes 2621440 | tf_op jit(solution)/shard_map/reduce_scatter | solution.py:137
  94.3 4.4 %copy-start.4 = (bf16[1024,1024]{1,0:T(8,128)(2,1)S(1)}, bf16[1024,1024]{1,0:T(8,128)(2,1)}, u32[]{:S(2)}) copy-start(bf16[1024,1024]{1,0:T(8,128)(2,1)} %all-gather.2.cloned.1.call-done) | copy-start | bytes 6291460
  94.3 4.4 %copy-start.14 = (bf16[1024,768]{1,0:T(8,128)(2,1)S(1)}, bf16[1024,768]{1,0:T(8,128)(2,1)}, u32[]{:S(2)}) copy-start(bf16[1024,768]{1,0:T(8,128)(2,1)} %param.26) | copy-start | bytes 4718596
  101.1 15.0 %collective-permute-start.2 = (bf16[512,2,256]{0,2,1:T(8,128)(2,1)S(1)}, bf16[512,2,256]{0,2,1:T(8,128)(2,1)S(1)}, u32[]{:S(2)}, u32[]{:S(2)}) collective-permute-start(bf16[512,2,256]{0,2,1:T(8,128)(2,1)S(1)} %bitcast.65), channel_id=1, source_target_pairs={{0,4},{4,8},{8,12},{1,5},{5,9},{9,13},{2,6},{6,10},{10,14},{3,7},{... | collective-permute-start | bytes 1572872 | tf_op jit(solution)/shard_map/ppermute | solution.py:21
  105.7 16.7 %collective-permute-start.3 = (bf16[512,2,256]{0,2,1:T(8,128)(2,1)S(1)}, bf16[512,2,256]{0,2,1:T(8,128)(2,1)S(1)}, u32[]{:S(2)}, u32[]{:S(2)}) collective-permute-start(bf16[512,2,256]{0,2,1:T(8,128)(2,1)S(1)} %bitcast.64), channel_id=1, source_target_pairs={{4,0},{8,4},{12,8},{5,1},{9,5},{13,9},{6,2},{10,6},{14,10},{7,3},{... | collective-permute-start | bytes 1572872 | tf_op jit(solution)/shard_map/ppermute | solution.py:23
  122.4 6.4 %copy-start.5 = (pred[512,1536]{1,0:T(8,128)(4,1)S(1)}, pred[512,1536]{1,0:T(8,128)(4,1)}, u32[]{:S(2)}) copy-start(pred[512,1536]{1,0:T(8,128)(4,1)} %fusion.37) | copy-start | bytes 2359300
  168.0 6.7 %copy-start.7 = (bf16[256,1024]{1,0:T(8,128)(2,1)S(1)}, bf16[256,1024]{1,0:T(8,128)(2,1)}, u32[]{:S(2)}) copy-start(bf16[256,1024]{1,0:T(8,128)(2,1)} %param.27) | copy-start | bytes 1572868
  177.5 16.9 %copy-start.9 = (s32[1,48,128]{2,1,0:T(8,128)S(1)}, s32[1,48,128]{2,1,0:T(8,128)}, u32[]{:S(2)}) copy-start(s32[1,48,128]{2,1,0:T(8,128)} %param.22) | copy-start | bytes 73732
  228.2 25.0 %copy-start.1 = (bf16[1024,256]{1,0:T(8,128)(2,1)}, bf16[1024,256]{1,0:T(8,128)(2,1)S(1)}, u32[]{:S(2)}) copy-start(bf16[1024,256]{1,0:T(8,128)(2,1)S(1)} %add_convert_fusion.1) | copy-start | bytes 1572868
  228.2 25.0 %copy-start.10 = (f32[1,48,128]{2,1,0:T(8,128)S(1)}, f32[1,48,128]{2,1,0:T(8,128)}, u32[]{:S(2)}) copy-start(f32[1,48,128]{2,1,0:T(8,128)} %param.24) | copy-start | bytes 73732
  253.2 9.4 %copy-start.2 = (bf16[2048,256]{1,0:T(8,128)(2,1)S(1)}, bf16[2048,256]{1,0:T(8,128)(2,1)}, u32[]{:S(2)}) copy-start(bf16[2048,256]{1,0:T(8,128)(2,1)} %param.16) | copy-start | bytes 3145732
  257.9 8.8 %collective-permute-start.4 = (bf16[512,256]{1,0:T(8,128)(2,1)S(1)}, bf16[512,256]{1,0:T(8,128)(2,1)S(1)}, u32[]{:S(2)}, u32[]{:S(2)}) collective-permute-start(bf16[512,256]{1,0:T(8,128)(2,1)S(1)} %get-tuple-element.2), channel_id=1, source_target_pairs={{0,4},{4,8},{8,12},{1,5},{5,9},{9,13},{2,6},{6,10},{10,14},{3,7},{... | collective-permute-start | bytes 786440 | tf_op jit(solution)/shard_map/ppermute | solution.py:21
  261.3 9.5 %collective-permute-start.5 = (bf16[512,256]{1,0:T(8,128)(2,1)S(1)}, bf16[512,256]{1,0:T(8,128)(2,1)S(1)}, u32[]{:S(2)}, u32[]{:S(2)}) collective-permute-start(bf16[512,256]{1,0:T(8,128)(2,1)S(1)} %get-tuple-element.3), channel_id=1, source_target_pairs={{4,0},{8,4},{12,8},{5,1},{9,5},{13,9},{6,2},{10,6},{14,10},{7,3},{... | collective-permute-start | bytes 786440 | tf_op jit(solution)/shard_map/ppermute | solution.py:23
Sparse Core Ops, SparseCore 0:
  71.3 23.0 all-gather.1
  194.5 32.1 reduce-scatter.1
where the time goes:
time: 323 us
  other arithmetic  124 us (38%)
  waiting for transfers between devices  73.6 us (23%)
  matrix products  47.8 us (15%)
  local copies, waits for them, and re-layouts  46.1 us (14%)
  starting transfers between devices  15.9 us (5%)
  between operations  15.1 us (5%)
    scatter-add x1, other arithmetic, shards(): jax.ops.segment_sum(arrived_dec.astype(jnp.float32), dec_dst_rows.reshape...  42.5 us
    gather x2, local copies, waits for them, and re-layouts, edge_messages(): jnp.take(source, src_rows.reshape(-1), axis=0).astype(jnp.float32)  42.2 us
    sub x2, other arithmetic, shards(): expo = jnp.exp(scores - peak)  32.6 us
    reduce_scatter x1, waiting for transfers between devices, shards(): lax.psum_scatter((attn_part + mlp_part).astype(jnp.bfloat16), ('mp', 'sub...  32.3 us
    scatter-add x1, other arithmetic, shards(): jax.ops.segment_sum(arrived.astype(jnp.float32), enc_dst_rows.reshape(-1)...  25.4 us
    all_gather x1, waiting for transfers between devices, shards(): full_rows = lax.all_gather(latent, ('mp', 'sub'), axis=1, tiled=True)  21 us
    dot_general x1, matrix products, shards(): jnp.dot(activated, w_down, preferred_element_type=jnp.float32)  16.8 us
    dot_general x2, matrix products, shards(): jnp.einsum('hqk,khd->qhd', attn_weights, value_block, preferred_element_t...  13.4 us
  transfers between devices with their start and end apart: 8, of which 7 were waited for; matrix products, arithmetic and copies ran while one was open for 4% of the time, Pallas kernels for 0%

commit v1 on v0

v1 whole, which is shorter than its diff:
```python
import functools

import jax
import jax.numpy as jnp
from jax import lax
from jax.experimental import pallas as pl
from jax.experimental.pallas import tpu as pltpu
from jax.sharding import PartitionSpec as P

HD = 64
WIN = 512
TILE = 128
ESIDE = 4
DSIDE = 4
STEP = 4
NEG = -1e30
BF = jnp.bfloat16
F32 = jnp.float32


def call(body, outs, args, flops, scratch=(), name=None):
    moved = sum(a.size * a.dtype.itemsize for a in args)
    moved += sum(o.size * o.dtype.itemsize for o in outs)
    return pl.pallas_call(
        body,
        out_shape=tuple(outs),
        in_specs=[pl.BlockSpec(memory_space=pltpu.VMEM)] * len(args),
        out_specs=tuple(pl.BlockSpec(memory_space=pltpu.VMEM) for _ in outs),
        scratch_shapes=list(scratch),
        cost_estimate=pl.CostEstimate(flops=flops, bytes_accessed=moved, transcendentals=0),
        compiler_params=pltpu.CompilerParams(vmem_limit_bytes=56 * 1024 * 1024),
        name=name,
    )(*args)


def column(row):
    return jnp.transpose(jnp.broadcast_to(row, (TILE, TILE)))


def picks(rows_ref, first, source_rows):
    cols = jnp.concatenate([column(rows_ref[pl.ds(first + i, 1), :]) for i in range(STEP)], axis=0)
    cols = cols.astype(jnp.int16)
    lane = lax.broadcasted_iota(jnp.int32, cols.shape, 1).astype(jnp.int16)
    tiles = []
    for j in range(source_rows // TILE):
        hit = cols == lane + jnp.int16(j * TILE)
        tiles.append(jnp.where(hit, jnp.ones_like(cols, BF), jnp.zeros_like(cols, BF)))
    return jnp.concatenate(tiles, axis=1)


def lands(rows_ref, first, target_rows):
    tiles = []
    spot = lax.broadcasted_iota(jnp.int32, (target_rows, TILE), 0).astype(jnp.int16)
    for i in range(STEP):
        row = jnp.broadcast_to(rows_ref[pl.ds(first + i, 1), :], (target_rows, TILE)).astype(jnp.int16)
        tiles.append(jnp.where(row == spot, jnp.ones_like(spot, BF), jnp.zeros_like(spot, BF)))
    return jnp.concatenate(tiles, axis=1)


def messages(src_ref, weight_ref, first, source_ref):
    picked = jnp.dot(
        picks(src_ref, first, source_ref.shape[0]), source_ref[...], preferred_element_type=F32
    )
    scale = jnp.concatenate([column(weight_ref[pl.ds(first + i, 1), :]) for i in range(STEP)], axis=0)
    scale = jnp.concatenate([scale] * (picked.shape[1] // TILE), axis=1)
    return (picked * scale).astype(BF)


def side_body(src_ref, weight_ref, source_ref, *outs):
    for side, out in enumerate(outs):
        for k in range(out.shape[0] // (STEP * TILE)):
            first = (side * out.shape[0]) // TILE + k * STEP
            out[k * STEP * TILE : (k + 1) * STEP * TILE, :] = messages(
                src_ref, weight_ref, first, source_ref
            )


def local_body(start, src_ref, dst_ref, weight_ref, source_ref, total_ref):
    total_ref[...] = jnp.zeros_like(total_ref)

    def step(k, carry):
        first = start + k * STEP
        moved = messages(src_ref, weight_ref, first, source_ref)
        total_ref[...] += jnp.dot(
            lands(dst_ref, first, total_ref.shape[0]), moved, preferred_element_type=F32
        )
        return carry

    lax.fori_loop(0, (src_ref.shape[0] - start) // STEP, step, 0)


def arrived(dst_ref, left_ref, right_ref, target_rows):
    total = jnp.dot(lands(dst_ref, 0, target_rows), left_ref[...], preferred_element_type=F32)
    return total + jnp.dot(
        lands(dst_ref, STEP, target_rows), right_ref[...], preferred_element_type=F32
    )


def latent_body(dst_ref, left_ref, right_ref, total_ref, embed_ref, out_ref):
    got = arrived(dst_ref, left_ref, right_ref, total_ref.shape[0]) + total_ref[...]
    out_ref[...] = (embed_ref[...].astype(F32) + got).astype(BF)


def grid_body(count_ref, dst_ref, left_ref, right_ref, total_ref, grid_ref, out_ref):
    got = arrived(dst_ref, left_ref, right_ref, total_ref.shape[0]) + total_ref[...]
    row = lax.broadcasted_iota(jnp.int32, got.shape, 0)
    value = grid_ref[...].astype(F32) + got
    out_ref[...] = jnp.where(row < count_ref[0, 0], value, 0.0).astype(BF)


def sent(edge_src, edge_weight, source, side):
    width = side * TILE
    out = jax.ShapeDtypeStruct((width, source.shape[1]), BF)
    flops = 4 * width * source.size
    to_left, to_right = call(side_body, (out, out), (edge_src, edge_weight, source), flops, name="side")
    count = lax.axis_size("seq")
    up = [(i, i + 1) for i in range(count - 1)]
    down = [(i + 1, i) for i in range(count - 1)]
    from_left = lax.ppermute(to_right, "seq", up)
    from_right = lax.ppermute(to_left, "seq", down)
    return from_left, from_right


def local(edge_src, edge_dst, edge_weight, source, target_rows, side):
    start = 2 * side
    edges = (edge_src.shape[0] - start) * TILE
    out = jax.ShapeDtypeStruct((target_rows, source.shape[1]), F32)
    flops = 2 * edges * source.shape[1] * (source.shape[0] + target_rows)
    (total,) = call(
        functools.partial(local_body, start),
        (out,),
        (edge_src, edge_dst, edge_weight, source),
        flops,
        name="local",
    )
    return total


def power(exponent):
    return jnp.where(exponent > 0, 2.0, jnp.where(exponent < 0, 0.5, 1.0)).astype(F32)


def place(step, parts):
    if parts == 1:
        return 0
    mp = lax.axis_index("mp")
    sub = lax.axis_index("sub")
    mp = mp if step < 2 else 1 - mp
    sub = sub if step % 2 == 0 else 1 - sub
    return 2 * mp + sub


def qkv_body(parts, *refs):
    pieces, (gain_ref, w_ref, normed_ref, q_ref, kv_ref) = refs[:parts], refs[parts:]
    rows, width = pieces[0].shape
    total = width * parts
    block = min(256, rows)
    lane = lax.broadcasted_iota(jnp.int32, (block, TILE), 1)

    def step(k, carry):
        at = pl.ds(pl.multiple_of(k * block, block), block)
        values = [p[at, :].astype(F32) for p in pieces]
        mean = sum(jnp.sum(v, axis=1, keepdims=True) for v in values) / total
        values = [v - mean for v in values]
        var = sum(jnp.sum(v * v, axis=1, keepdims=True) for v in values) / total
        scale = lax.rsqrt(var + 1e-05)
        for i, v in enumerate(values):
            cols = pl.ds(pl.multiple_of(place(i, parts) * width, width), width)
            normed_ref[at, cols] = (v * scale * gain_ref[:, cols]).astype(BF)
        out = jnp.dot(normed_ref[at, :], w_ref[...], preferred_element_type=F32)
        for pair in range(q_ref.shape[1] // TILE):
            a, b, c = [out[:, (3 * pair + i) * TILE : (3 * pair + i + 1) * TILE] for i in range(3)]
            q = pltpu.roll(jnp.where(lane < HD, a, b), HD, 1)
            q_ref[at, pair * TILE : (pair + 1) * TILE] = q.astype(BF)
            kv_ref[at, 2 * pair * TILE : (2 * pair + 1) * TILE] = jnp.where(lane < HD, b, a).astype(BF)
            kv_ref[at, (2 * pair + 1) * TILE : (2 * pair + 2) * TILE] = c.astype(BF)
        return carry

    lax.fori_loop(0, rows // block, step, 0)


def up_body(normed_ref, w_ref, exp_ref, out_ref):
    rows = normed_ref.shape[0]
    block = min(256, rows)
    cols = min(512, w_ref.shape[1])

    def step(k, carry):
        at = pl.ds(pl.multiple_of(k * block, block), block)
        for c in range(w_ref.shape[1] // cols):
            sl = slice(c * cols, (c + 1) * cols)
            up = jnp.dot(normed_ref[at, :], w_ref[:, sl], preferred_element_type=F32)
            up = up * power(exp_ref[:, sl])
            out_ref[at, sl] = (0.5 * up * (1.0 + lax.erf(up * 0.7071067811865476))).astype(BF)
        return carry

    lax.fori_loop(0, rows // block, step, 0)


def attend_body(where, q_ref, before_ref, here_ref, after_ref, out_ref):
    rows = q_ref.shape[0]
    block = 256
    lane = lax.broadcasted_iota(jnp.int32, (block, TILE), 1)
    i = lax.broadcasted_iota(jnp.int32, (block, block), 0)
    j = lax.broadcasted_iota(jnp.int32, (block, block), 1)
    seq = lax.axis_index("seq")
    before_ok = jnp.logical_or(where != 0, seq > 0)
    after_ok = jnp.logical_or(where != 1, seq < lax.axis_size("seq") - 1)
    before_bias = jnp.where(before_ok, 0.0, NEG).astype(F32)
    after_bias = jnp.where(after_ok, 0.0, NEG).astype(F32)
    low = jnp.where(j >= i, before_bias, NEG)
    high = jnp.where(j <= i, after_bias, NEG)
    contract = (((1,), (1,)), ((), ()))
    n = WIN // block
    for pair in range(q_ref.shape[1] // TILE):
        pair_cols = slice(pair * TILE, (pair + 1) * TILE)
        for b in range(rows // block):
            q2 = q_ref[b * block : (b + 1) * block, pair_cols]
            outs = []
            for half in range(2):
                cols = slice((2 * pair + half) * TILE, (2 * pair + half + 1) * TILE)
                keep = (lane >= HD) if half == 0 else (lane < HD)
                q = jnp.where(keep, q2 * BF(HD**-0.5), jnp.zeros_like(q2))
                keys = []
                for t in range(b, b + 2 * n + 1):
                    ref = (before_ref, here_ref, after_ref)[t // n]
                    keys.append((t, ref[(t % n) * block : (t % n + 1) * block, cols]))
                scores = []
                for t, key in keys:
                    s = lax.dot_general(q, key, contract, preferred_element_type=F32)
                    if t == b:
                        s = s + low
                    elif t == b + 2 * n:
                        s = s + high
                    elif t < n and where == 0:
                        s = s + before_bias
                    elif t >= 2 * n and where == 1:
                        s = s + after_bias
                    scores.append(s)
                peak = scores[0]
                for s in scores[1:]:
                    peak = jnp.maximum(peak, s)
                peak = jnp.max(peak, axis=1, keepdims=True)
                probs = [jnp.exp(s - peak) for s in scores]
                total = probs[0]
                for p in probs[1:]:
                    total = total + p
                total = jnp.sum(total, axis=1, keepdims=True)
                mixed = jnp.dot(
                    jnp.concatenate([p.astype(BF) for p in probs], axis=1),
                    jnp.concatenate([key for _, key in keys], axis=0),
                    preferred_element_type=F32,
                )
                outs.append(mixed / total)
            out_ref[b * block : (b + 1) * block, pair_cols] = jnp.where(
                lane < HD, outs[0], outs[1]
            ).astype(BF)


def down_body(parts, att_ref, act_ref, w_out_ref, w_down_ref, exp_ref, *outs):
    rows = att_ref.shape[0]
    width = w_out_ref.shape[1] // parts
    block = min(256, rows)

    def step(k, carry):
        at = pl.ds(pl.multiple_of(k * block, block), block)
        for i in range(parts):
            cols = pl.ds(pl.multiple_of(place(i, parts) * width, width), width)
            mlp = jnp.dot(act_ref[at, :], w_down_ref[:, cols], preferred_element_type=F32)
            att = jnp.dot(att_ref[at, :], w_out_ref[:, cols], preferred_element_type=F32)
            part = (att + mlp * power(exp_ref[:, cols])).astype(BF)
            outs[i][at, :] = part
        return carry

    lax.fori_loop(0, rows // block, step, 0)


SWAP = [(0, 1), (1, 0)]


def gather(rows, split):
    if not split:
        return [lax.all_gather(rows, ("mp", "sub"), axis=1, tiled=True)]
    far = lax.ppermute(rows, "mp", SWAP)
    near = lax.ppermute(rows, "sub", SWAP)
    both = lax.ppermute(far, "sub", SWAP)
    return [rows, near, far, both]


def reduce_parts(latent, parts, split):
    if not split:
        total = lax.psum_scatter(parts[0], ("mp", "sub"), scatter_dimension=1, tiled=True)
        return (latent.astype(F32) + total.astype(F32)).astype(BF)
    own, near, far, both = parts
    far_got = lax.ppermute(both, "sub", SWAP)
    near_got = lax.ppermute(near, "sub", SWAP)
    far_sum = (far.astype(F32) + far_got.astype(F32)).astype(BF)
    got = lax.ppermute(far_sum, "mp", SWAP)
    total = own.astype(F32) + near_got.astype(F32) + got.astype(F32)
    return (latent.astype(F32) + total).astype(BF)


def shards(
    grid_latent,
    grid_count,
    hidden_embed,
    enc_src_rows,
    enc_dst_rows,
    enc_weight,
    dec_src_rows,
    dec_dst_rows,
    dec_weight,
    norm_gain,
    w_qkv,
    w_out,
    w_up,
    up_exp,
    w_down,
    down_exp,
):
    split = lax.axis_size("mp") == 2 and lax.axis_size("sub") == 2
    parts = 4 if split else 1
    count = lax.axis_size("seq")
    up = [(i, i + 1) for i in range(count - 1)]
    down = [(i + 1, i) for i in range(count - 1)]
    hid_rows, features = hidden_embed.shape
    full = w_qkv.shape[0]
    heads = w_qkv.shape[1] // (3 * HD)
    units = w_up.shape[1]
    src, dst, wts = enc_src_rows[0], enc_dst_rows[0], enc_weight[0]
    from_left, from_right = sent(src, wts, grid_latent, ESIDE)
    total = local(src, dst, wts, grid_latent, hid_rows, ESIDE)
    (latent,) = call(
        latent_body,
        (jax.ShapeDtypeStruct(hidden_embed.shape, BF),),
        (dst, from_left, from_right, total, hidden_embed),
        4 * ESIDE * TILE * hid_rows * features,
        name="latent",
    )
    chunks = []
    rows = WIN
    for c in range(hid_rows // rows):
        part = latent[c * rows : (c + 1) * rows]
        pieces = gather(part, split)
        normed, q, kv = call(
            functools.partial(qkv_body, parts),
            (
                jax.ShapeDtypeStruct((rows, full), BF),
                jax.ShapeDtypeStruct((rows, heads * HD), BF),
                jax.ShapeDtypeStruct((rows, 2 * heads * HD), BF),
            ),
            (*pieces, norm_gain[None, :], w_qkv),
            2 * rows * w_qkv.size,
            name="qkv",
        )
        chunks.append((part, normed, q, kv))
    kvs = [chunk[3] for chunk in chunks]
    kvs = [
        lax.ppermute(kvs[-1], "seq", up),
        *kvs,
        lax.ppermute(kvs[0], "seq", down),
    ]
    hidden = []
    for c, (part, normed, q, _) in enumerate(chunks):
        (activated,) = call(
            up_body,
            (jax.ShapeDtypeStruct((rows, units), BF),),
            (normed, w_up, up_exp[None, :]),
            2 * rows * w_up.size,
            name="up",
        )
        where = 0 if c == 0 else (1 if c == len(chunks) - 1 else 2)
        (attended,) = call(
            functools.partial(attend_body, where),
            (jax.ShapeDtypeStruct((rows, heads * HD), BF),),
            (q, *kvs[c : c + 3]),
            4 * rows * 3 * WIN * heads * HD,
            name="attend",
        )
        outs = call(
            functools.partial(down_body, parts),
            [jax.ShapeDtypeStruct((rows, full // parts), BF)] * parts,
            (attended, activated, w_out, w_down, down_exp[None, :]),
            2 * rows * (w_out.size + w_down.size),
            name="down",
        )
        hidden.append(reduce_parts(part, outs, split))
    hidden_out = jnp.concatenate(hidden, axis=0)
    src, dst, wts = dec_src_rows[0], dec_dst_rows[0], dec_weight[0]
    from_left, from_right = sent(src, wts, hidden_out, DSIDE)
    total = local(src, dst, wts, hidden_out, grid_latent.shape[0], DSIDE)
    (grid_out,) = call(
        grid_body,
        (jax.ShapeDtypeStruct(grid_latent.shape, BF),),
        (grid_count[None, :], dst, from_left, from_right, total, grid_latent),
        4 * DSIDE * TILE * grid_latent.size,
        name="grid",
    )
    return (hidden_out, grid_out)


def solution(mesh):
    placed = (
        P(("ens", "seq"), ("mp", "sub")),
        P(("ens", "seq")),
        P(("ens", "seq"), ("mp", "sub")),
        P(("ens", "seq"), None, None),
        P(("ens", "seq"), None, None),
        P(("ens", "seq"), None, None),
        P(("ens", "seq"), None, None),
        P(("ens", "seq"), None, None),
        P(("ens", "seq"), None, None),
        P(),
        P(None, ("mp", "sub")),
        P(("mp", "sub"), None),
        P(None, ("mp", "sub")),
        P(("mp", "sub")),
        P(("mp", "sub"), None),
        P(),
    )
    return jax.shard_map(
        shards,
        mesh=mesh,
        in_specs=placed,
        out_specs=(P(("ens", "seq"), ("mp", "sub")), P(("ens", "seq"), ("mp", "sub"))),
        check_vma=False,
    )
```

time: 323 us -> 143 us (0.44)
  other arithmetic: 124 us -> 3.12 us
  Pallas kernels: 0 us -> 86.2 us
  waiting for transfers between devices: 73.6 us -> 20.8 us
  matrix products: 47.8 us -> 0 us
  local copies, waits for them, and re-layouts: 46.1 us -> 7.03 us
  between operations: 15.1 us -> 1.5 us
  starting transfers between devices: 15.9 us -> 23.7 us
    pallas_call x0 -> x14, Pallas kernels: none -> 86.2 us  [call(): pl.pallas_call(body, out_shape=tuple(outs), in_specs=[pl.BlockSpec(memory...]
    scatter-add x2 -> x0, other arithmetic: 67.9 us -> none  [the longest x1 42.5 us: shards(): jax.ops.segment_sum(arrived_dec.astype(jnp.float32), dec_dst_rows.reshape...]
    dot_general x7 -> x0, matrix products: 47.8 us -> none  [the longest x1 16.8 us: shards(): jnp.dot(activated, w_down, preferred_element_type=jnp.float32)]
    gather x2 -> x0, local copies, waits for them, and re-layouts: 42.2 us -> none  [edge_messages(): jnp.take(source, src_rows.reshape(-1), axis=0).astype(jnp.float32)]
    sub x2 -> x0, other arithmetic: 32.6 us -> none  [shards(): expo = jnp.exp(scores - peak)]
    reduce_scatter x1 -> x0, waiting for transfers between devices: 32.3 us -> none  [shards(): lax.psum_scatter((attn_part + mlp_part).astype(jnp.bfloat16), ('mp', 'sub...]
    all_gather x1 -> x0, waiting for transfers between devices: 21 us -> none  [shards(): full_rows = lax.all_gather(latent, ('mp', 'sub'), axis=1, tiled=True)]
    convert_element_type x7 -> x3, other arithmetic: 14.5 us -> 2.29 us  [the longest x1 1.21 us: reduce_parts(): return (latent.astype(F32) + total).astype(BF)]
  transfers between devices with their start and end apart: 8 -> 18, of which waited for: 7 -> 4; matrix products, arithmetic and copies ran while one was open for 4% -> 1% of each run, Pallas kernels for 0% -> 51%
where the time goes in v1:
time: 143 us; the launch traced here: 142 us
  Pallas kernels  86.2 us (60%)
  starting transfers between devices  23.7 us (17%)
  waiting for transfers between devices  20.8 us (15%)
  local copies, waits for them, and re-layouts  7.03 us (5%)
  other arithmetic  3.12 us (2%)
  between operations  1.5 us (1%)
    pallas_call x14, Pallas kernels, call(): pl.pallas_call(body, out_shape=tuple(outs), in_specs=[pl.BlockSpec(memory...  86.2 us
    ppermute x2, waiting for transfers between devices, gather(): far = lax.ppermute(rows, 'mp', SWAP)  10.8 us
    ppermute x2, waiting for transfers between devices, reduce_parts(): got = lax.ppermute(far_sum, 'mp', SWAP)  9.97 us
    ppermute x2, starting transfers between devices, sent(): from_left = lax.ppermute(to_right, 'seq', up)  8.73 us
    unnamed x36, local copies, waits for them, and re-layouts  5.97 us
    ppermute x1, starting transfers between devices, shards(): lax.ppermute(kvs[-1], 'seq', up)  5.1 us
  transfers between devices with their start and end apart: 18, of which 4 were waited for; matrix products, arithmetic and copies ran while one was open for 1% of the time, Pallas kernels for 51%

profile of v1, /device:TPU:0, one launch (start us, length us, event | category | flops | bytes accessed | tf_op | source)
XLA Modules:
  0.0 142.4 jit_solution(3882592318097655775)
XLA Ops:
  0.6 3.3 %side.2 = (bf16[512,256]{1,0:T(8,128)(2,1)}, bf16[512,256]{1,0:T(8,128)(2,1)}) custom-call(s32[32,128]{1,0:T(8,128)} %bitcast.21, f32[32,128]{1,0:T(8,128)} %bitcast.23, bf16[2048,256]{1,0:T(8,128)(2,1)} %grid_ref.1), custom_call_target="tpu_custom_call" | custom-call | flops 1073741824 | bytes 1605632 | tf_op jit(solution)/shard_map/side/pallas_call | solution.py:24
  4.0 5.0 %collective-permute-start = (bf16[512,256]{1,0:T(8,128)(2,1)}, bf16[512,256]{1,0:T(8,128)(2,1)S(1)}, u32[]{:S(2)}, u32[]{:S(2)}) collective-permute-start(bf16[512,256]{1,0:T(8,128)(2,1)} %get-tuple-element.20), channel_id=1, source_target_pairs={{0,4},{4,8},{8,12},{1,5},{5,9},{9,13},{2,6},{6,10},{10,14},{3,7},{... | collective-permute-start | bytes 786440 | tf_op jit(solution)/shard_map/ppermute | solution.py:119
  8.9 1.3 collective-permute-start.1
  10.2 12.0 %local.2.total_ref = f32[1024,256]{1,0:T(8,128)} custom-call(s32[32,128]{1,0:T(8,128)} %bitcast.22, s32[32,128]{1,0:T(8,128)} %bitcast.13, f32[32,128]{1,0:T(8,128)} %bitcast.24, bf16[2048,256]{1,0:T(8,128)(2,1)} %grid_ref.1), custom_call_target="tpu_custom_call" | custom-call | flops 4831838208 | bytes 2146304 | tf_op jit(solution)/shard_map/local/pallas_call | solution.py:24
  22.3 0.0 collective-permute-done.left_ref
  22.3 0.0 collective-permute-done.1.right_ref
  22.3 0.7 copy-done.4
  23.0 0.7 copy-done.6
  23.7 3.0 %latent.1 = bf16[1024,256]{1,0:T(8,128)(2,1)} custom-call(s32[32,128]{1,0:T(8,128)} %bitcast.14, bf16[512,256]{1,0:T(8,128)(2,1)} %copy-done.4, bf16[512,256]{1,0:T(8,128)(2,1)} %copy-done.6, f32[1024,256]{1,0:T(8,128)} %local.2.total_ref, bf16[1024,256]{1,0:T(8,128)(2,1)} %embed_ref.1), custom_call_target="tpu_custom_call" | custom-call | flops 536870912 | bytes 2637824 | tf_op jit(solution)/shard_map/latent/pallas_call | solution.py:24
  26.7 1.1 fusion
  27.8 1.6 %collective-permute-start.3 = (bf16[512,256]{1,0:T(8,128)(2,1)S(1)}, bf16[512,256]{1,0:T(8,128)(2,1)S(1)}, u32[]{:S(2)}, u32[]{:S(2)}) collective-permute-start(bf16[512,256]{1,0:T(8,128)(2,1)S(1)} %get-tuple-element.40.refs_0_), channel_id=1, source_target_pairs={{0,2},{2,0},{1,3},{3,1},{4,6},{6,4},{5,7},{7,5},{8,10},{10,8},{9,1... | collective-permute-start | bytes 786440 | tf_op jit(solution)/shard_map/ppermute | solution.py:283
  29.4 0.5 collective-permute-start.6
  29.9 0.0 collective-permute-start.2
  29.9 7.1 %collective-permute-done.3.refs_2_ = bf16[512,256]{1,0:T(8,128)(2,1)S(1)} collective-permute-done((bf16[512,256]{1,0:T(8,128)(2,1)S(1)}, bf16[512,256]{1,0:T(8,128)(2,1)S(1)}, u32[]{:S(2)}, u32[]{:S(2)}) %collective-permute-start.3) | collective-permute-done | bytes 262176 | tf_op jit(solution)/shard_map/ppermute | solution.py:283
  37.1 0.0 collective-permute-start.4
  37.1 0.5 collective-permute-start.5
  37.6 3.7 %collective-permute-done.6.refs_2_ = bf16[512,256]{1,0:T(8,128)(2,1)S(1)} collective-permute-done((bf16[512,256]{1,0:T(8,128)(2,1)S(1)}, bf16[512,256]{1,0:T(8,128)(2,1)S(1)}, u32[]{:S(2)}, u32[]{:S(2)}) %collective-permute-start.6) | collective-permute-done | bytes 262176 | tf_op jit(solution)/shard_map/ppermute | solution.py:283
  41.3 0.0 collective-permute-start.7
  41.3 0.0 collective-permute-done.2.refs_1_
  41.3 0.0 collective-permute-done.4.refs_3_
  41.3 0.7 copy-done.16
  42.0 0.1 copy-done.17
  42.1 5.0 %qkv.2 = (bf16[512,1024]{1,0:T(8,128)(2,1)}, bf16[512,256]{1,0:T(8,128)(2,1)}, bf16[512,512]{1,0:T(8,128)(2,1)}) custom-call(bf16[512,256]{1,0:T(8,128)(2,1)} %copy-done.8, bf16[512,256]{1,0:T(8,128)(2,1)} %copy-done.16, bf16[512,256]{1,0:T(8,128)(2,1)} %copy-done.13, bf16[512,256]{1,0:T(8,128)(2,1)} %copy-done.17, f32[1,1024]{1,0:T(1,128)} %bitcast.25, ...), custom_call_target="tpu_custom_call" | custom-call | flops 805306368 | bytes 4460544 | tf_op jit(solution)/shard_map/qkv/pallas_call | solution.py:24
  47.1 1.3 collective-permute-start.12
  48.4 0.0 collective-permute-done.5.refs_1_
  48.5 0.0 collective-permute-done.7.refs_3_
  48.5 0.7 copy-done.14
  49.2 0.7 copy-done.15
  49.8 5.1 %qkv.3 = (bf16[512,1024]{1,0:T(8,128)(2,1)}, bf16[512,256]{1,0:T(8,128)(2,1)}, bf16[512,512]{1,0:T(8,128)(2,1)}) custom-call(bf16[512,256]{1,0:T(8,128)(2,1)} %copy-done.7, bf16[512,256]{1,0:T(8,128)(2,1)} %copy-done.14, bf16[512,256]{1,0:T(8,128)(2,1)} %copy-done.12, bf16[512,256]{1,0:T(8,128)(2,1)} %copy-done.15, f32[1,1024]{1,0:T(1,128)} %bitcast.26, ...), custom_call_target="tpu_custom_call" | custom-call | flops 805306368 | bytes 4460544 | tf_op jit(solution)/shard_map/qkv/pallas_call | solution.py:24
  54.9 5.1 %collective-permute-start.8 = (bf16[512,512]{1,0:T(8,128)(2,1)}, bf16[512,512]{1,0:T(8,128)(2,1)S(1)}, u32[]{:S(2)}, u32[]{:S(2)}) collective-permute-start(bf16[512,512]{1,0:T(8,128)(2,1)} %get-tuple-element.23.after_ref.here_ref), channel_id=1, source_target_pairs={{0,4},{4,8},{8,12},{1,5},{5,9},{9,13},{2,6},{6,10},{10,14},{3,7},{... | collective-permute-start | bytes 1572872 | tf_op jit(solution)/shard_map/ppermute | solution.py:358
  60.0 4.5 %up.3.act_ref = bf16[512,1024]{1,0:T(8,128)(2,1)} custom-call(bf16[512,1024]{1,0:T(8,128)(2,1)} %get-tuple-element.31.normed_ref, bf16[1024,1024]{1,0:T(8,128)(2,1)} %w_ref.3, s32[1,1024]{1,0:T(1,128)} %bitcast.15), custom_call_target="tpu_custom_call" | custom-call | flops 1073741824 | bytes 4198400 | tf_op jit(solution)/shard_map/up/pallas_call | solution.py:24
  64.5 0.0 collective-permute-done.12.after_ref
  64.5 0.8 copy-done.10
  65.3 6.8 %attend.3.att_ref = bf16[512,256]{1,0:T(8,128)(2,1)} custom-call(bf16[512,256]{1,0:T(8,128)(2,1)} %get-tuple-element.30.q_ref, bf16[512,512]{1,0:T(8,128)(2,1)} %get-tuple-element.24.here_ref.before_ref, bf16[512,512]{1,0:T(8,128)(2,1)} %get-tuple-element.23.after_ref.here_ref, bf16[512,512]{1,0:T(8,128)(2,1)} %copy-done.10), custom_call_target="tpu_custom_call" | custom-call | flops 805306368 | bytes 2097152 | tf_op jit(solution)/shard_map/attend/pallas_call | solution.py:24
  72.2 4.6 %down.3 = (bf16[512,256]{1,0:T(8,128)(2,1)}, bf16[512,256]{1,0:T(8,128)(2,1)}, bf16[512,256]{1,0:T(8,128)(2,1)}, bf16[512,256]{1,0:T(8,128)(2,1)}) custom-call(bf16[512,256]{1,0:T(8,128)(2,1)} %attend.3.att_ref, bf16[512,1024]{1,0:T(8,128)(2,1)} %up.3.act_ref, bf16[256,1024]{1,0:T(8,128)(2,1)} %w_out_ref.3, bf16[1024,1024]{1,0:T(8,128)(2,1)} %w_down_ref.3, ...), custom_call_target="tpu_custom_call" | custom-call | flops 1342177280 | bytes 4984832 | tf_op jit(solution)/shard_map/down/pallas_call | solution.py:24
  76.7 0.2 collective-permute-start.14
  76.9 4.5 %up.2.act_ref = bf16[512,1024]{1,0:T(8,128)(2,1)} custom-call(bf16[512,1024]{1,0:T(8,128)(2,1)} %get-tuple-element.25.normed_ref, bf16[1024,1024]{1,0:T(8,128)(2,1)} %w_ref.3, s32[1,1024]{1,0:T(1,128)} %bitcast.16), custom_call_target="tpu_custom_call" | custom-call | flops 1073741824 | bytes 4198400 | tf_op jit(solution)/shard_map/up/pallas_call | solution.py:24
  81.4 0.0 collective-permute-done.8.before_ref
  81.4 0.8 copy-done.9
  82.2 6.8 %attend.2.att_ref = bf16[512,256]{1,0:T(8,128)(2,1)} custom-call(bf16[512,256]{1,0:T(8,128)(2,1)} %get-tuple-element.22.q_ref, bf16[512,512]{1,0:T(8,128)(2,1)} %copy-done.9, bf16[512,512]{1,0:T(8,128)(2,1)} %get-tuple-element.24.here_ref.before_ref, bf16[512,512]{1,0:T(8,128)(2,1)} %get-tuple-element.23.after_ref.here_ref), custom_call_target="tpu_custom_call" | custom-call | flops 805306368 | bytes 2097152 | tf_op jit(solution)/shard_map/attend/pallas_call | solution.py:24
  89.0 4.9 %down.2 = (bf16[512,256]{1,0:T(8,128)(2,1)}, bf16[512,256]{1,0:T(8,128)(2,1)}, bf16[512,256]{1,0:T(8,128)(2,1)}, bf16[512,256]{1,0:T(8,128)(2,1)}) custom-call(bf16[512,256]{1,0:T(8,128)(2,1)} %attend.2.att_ref, bf16[512,1024]{1,0:T(8,128)(2,1)} %up.2.act_ref, bf16[256,1024]{1,0:T(8,128)(2,1)} %w_out_ref.3, bf16[1024,1024]{1,0:T(8,128)(2,1)} %w_down_ref.3, ...), custom_call_target="tpu_custom_call" | custom-call | flops 1342177280 | bytes 4984832 | tf_op jit(solution)/shard_map/down/pallas_call | solution.py:24
  93.9 0.3 collective-permute-start.10
  94.3 0.2 collective-permute-start.13
  94.4 0.3 collective-permute-start.9
  94.8 0.0 collective-permute-done.14
  94.8 0.1 add_convert_fusion.1
  94.8 1.6 %collective-permute-start.15 = (bf16[512,256]{1,0:T(8,128)(2,1)S(1)}, bf16[512,256]{1,0:T(8,128)(2,1)S(1)}, u32[]{:S(2)}, u32[]{:S(2)}) collective-permute-start(bf16[512,256]{1,0:T(8,128)(2,1)S(1)} %add_convert_fusion.1), channel_id=1, source_target_pairs={{0,2},{2,0},{1,3},{3,1},{4,6},{6,4},{5,7},{7,5},{8,10},{10,8},{9,1... | collective-permute-start | bytes 786440 | tf_op jit(solution)/shard_map/ppermute | solution.py:297
  96.4 0.0 collective-permute-done.10
  96.4 1.0 add_convert_fusion.3
  97.4 0.9 collective-permute-start.11
  98.9 0.0 collective-permute-done.13
  98.9 5.1 %collective-permute-done.15 = bf16[512,256]{1,0:T(8,128)(2,1)S(1)} collective-permute-done((bf16[512,256]{1,0:T(8,128)(2,1)S(1)}, bf16[512,256]{1,0:T(8,128)(2,1)S(1)}, u32[]{:S(2)}, u32[]{:S(2)}) %collective-permute-start.15) | collective-permute-done | bytes 262176 | tf_op jit(solution)/shard_map/ppermute | solution.py:297
  104.1 4.8 %collective-permute-done.11 = bf16[512,256]{1,0:T(8,128)(2,1)S(1)} collective-permute-done((bf16[512,256]{1,0:T(8,128)(2,1)S(1)}, bf16[512,256]{1,0:T(8,128)(2,1)S(1)}, u32[]{:S(2)}, u32[]{:S(2)}) %collective-permute-start.11) | collective-permute-done | bytes 262176 | tf_op jit(solution)/shard_map/ppermute | solution.py:297
  108.9 1.2 add_convert_fusion.2
  110.1 0.8 pad_maximum_fusion.source_ref
  111.0 2.6 %side.3 = (bf16[512,256]{1,0:T(8,128)(2,1)}, bf16[512,256]{1,0:T(8,128)(2,1)}) custom-call(s32[48,128]{1,0:T(8,128)} %bitcast.17, f32[48,128]{1,0:T(8,128)} %bitcast.19, bf16[1024,256]{1,0:T(8,128)(2,1)} %pad_maximum_fusion.source_ref), custom_call_target="tpu_custom_call" | custom-call | flops 536870912 | bytes 1097728 | tf_op jit(solution)/shard_map/side/pallas_call | solution.py:24
  113.6 3.8 %collective-permute-start.16 = (bf16[512,256]{1,0:T(8,128)(2,1)}, bf16[512,256]{1,0:T(8,128)(2,1)S(1)}, u32[]{:S(2)}, u32[]{:S(2)}) collective-permute-start(bf16[512,256]{1,0:T(8,128)(2,1)} %get-tuple-element.36), channel_id=1, source_target_pairs={{0,4},{4,8},{8,12},{1,5},{5,9},{9,13},{2,6},{6,10},{10,14},{3,7},{... | collective-permute-start | bytes 786440 | tf_op jit(solution)/shard_map/ppermute | solution.py:119
  117.4 1.3 collective-permute-start.17
  118.7 18.6 %local.3.total_ref = f32[2048,256]{1,0:T(8,128)} custom-call(s32[48,128]{1,0:T(8,128)} %bitcast.18, s32[48,128]{1,0:T(8,128)} %bitcast.11, f32[48,128]{1,0:T(8,128)} %bitcast.20, bf16[1024,256]{1,0:T(8,128)(2,1)} %pad_maximum_fusion.source_ref), custom_call_target="tpu_custom_call" | custom-call | flops 8053063680 | bytes 2695168 | tf_op jit(solution)/shard_map/local/pallas_call | solution.py:24
  137.3 0.0 collective-permute-done.16.left_ref
  137.3 0.0 collective-permute-done.17.right_ref
  137.3 0.7 copy-done.3
  138.0 0.1 copy-done.5
  138.1 4.3 %grid.1 = bf16[2048,256]{1,0:T(8,128)(2,1)} custom-call(s32[1,1]{1,0:T(1,128)} %bitcast.10.count_ref, s32[48,128]{1,0:T(8,128)} %bitcast.12, bf16[512,256]{1,0:T(8,128)(2,1)} %copy-done.3, bf16[512,256]{1,0:T(8,128)(2,1)} %copy-done.5, f32[2048,256]{1,0:T(8,128)} %local.3.total_ref, bf16[2048,256]{1,0:T(8,128)(2,1)} %grid_ref.1), custom_call_target="tpu_custom_call" | custom-call | flops 1073741824 | bytes 4743172 | tf_op jit(solution)/shard_map/grid/pallas_call | solution.py:24
  (27 shorter events, 0.1 us)
Async XLA Ops:
  4.0 18.3 %collective-permute-start = (bf16[512,256]{1,0:T(8,128)(2,1)}, bf16[512,256]{1,0:T(8,128)(2,1)S(1)}, u32[]{:S(2)}, u32[]{:S(2)}) collective-permute-start(bf16[512,256]{1,0:T(8,128)(2,1)} %get-tuple-element.20), channel_id=1, source_target_pairs={{0,4},{4,8},{8,12},{1,5},{5,9},{9,13},{2,6},{6,10},{10,14},{3,7},{... | collective-permute-start | bytes 786440 | tf_op jit(solution)/shard_map/ppermute | solution.py:119
  8.9 13.3 %collective-permute-start.1 = (bf16[512,256]{1,0:T(8,128)(2,1)}, bf16[512,256]{1,0:T(8,128)(2,1)S(1)}, u32[]{:S(2)}, u32[]{:S(2)}) collective-permute-start(bf16[512,256]{1,0:T(8,128)(2,1)} %get-tuple-element.21), channel_id=1, source_target_pairs={{4,0},{8,4},{12,8},{5,1},{9,5},{13,9},{6,2},{10,6},{14,10},{7,3},{... | collective-permute-start | bytes 786440 | tf_op jit(solution)/shard_map/ppermute | solution.py:120
  22.3 0.7 copy-start.4
  23.0 0.7 copy-start.6
  27.8 13.5 %copy-start.8 = (bf16[512,256]{1,0:T(8,128)(2,1)}, bf16[512,256]{1,0:T(8,128)(2,1)S(1)}, u32[]{:S(2)}) copy-start(bf16[512,256]{1,0:T(8,128)(2,1)S(1)} %get-tuple-element.40.refs_0_) | copy-start | bytes 786436
  27.8 20.7 %copy-start.7 = (bf16[512,256]{1,0:T(8,128)(2,1)}, bf16[512,256]{1,0:T(8,128)(2,1)S(1)}, u32[]{:S(2)}) copy-start(bf16[512,256]{1,0:T(8,128)(2,1)S(1)} %get-tuple-element.41.refs_0_) | copy-start | bytes 786436
  27.8 9.2 %collective-permute-start.3 = (bf16[512,256]{1,0:T(8,128)(2,1)S(1)}, bf16[512,256]{1,0:T(8,128)(2,1)S(1)}, u32[]{:S(2)}, u32[]{:S(2)}) collective-permute-start(bf16[512,256]{1,0:T(8,128)(2,1)S(1)} %get-tuple-element.40.refs_0_), channel_id=1, source_target_pairs={{0,2},{2,0},{1,3},{3,1},{4,6},{6,4},{5,7},{7,5},{8,10},{10,8},{9,1... | collective-permute-start | bytes 786440 | tf_op jit(solution)/shard_map/ppermute | solution.py:283
  29.4 11.9 %collective-permute-start.6 = (bf16[512,256]{1,0:T(8,128)(2,1)S(1)}, bf16[512,256]{1,0:T(8,128)(2,1)S(1)}, u32[]{:S(2)}, u32[]{:S(2)}) collective-permute-start(bf16[512,256]{1,0:T(8,128)(2,1)S(1)} %get-tuple-element.41.refs_0_), channel_id=1, source_target_pairs={{0,2},{2,0},{1,3},{3,1},{4,6},{6,4},{5,7},{7,5},{8,10},{10,8},{9,1... | collective-permute-start | bytes 786440 | tf_op jit(solution)/shard_map/ppermute | solution.py:283
  29.9 11.4 %collective-permute-start.2 = (bf16[512,256]{1,0:T(8,128)(2,1)S(1)}, bf16[512,256]{1,0:T(8,128)(2,1)S(1)}, u32[]{:S(2)}, u32[]{:S(2)}) collective-permute-start(bf16[512,256]{1,0:T(8,128)(2,1)S(1)} %get-tuple-element.40.refs_0_), channel_id=1, source_target_pairs={{0,1},{1,0},{2,3},{3,2},{4,5},{5,4},{6,7},{7,6},{8,9},{9,8},{10,11... | collective-permute-start | bytes 786440 | tf_op jit(solution)/shard_map/ppermute | solution.py:284
  37.1 4.3 %copy-start.13 = (bf16[512,256]{1,0:T(8,128)(2,1)}, bf16[512,256]{1,0:T(8,128)(2,1)S(1)}, u32[]{:S(2)}) copy-start(bf16[512,256]{1,0:T(8,128)(2,1)S(1)} %collective-permute-done.3.refs_2_) | copy-start | bytes 786436
  37.1 4.2 %collective-permute-start.4 = (bf16[512,256]{1,0:T(8,128)(2,1)S(1)}, bf16[512,256]{1,0:T(8,128)(2,1)S(1)}, u32[]{:S(2)}, u32[]{:S(2)}) collective-permute-start(bf16[512,256]{1,0:T(8,128)(2,1)S(1)} %collective-permute-done.3.refs_2_), channel_id=1, source_target_pairs={{0,1},{1,0},{2,3},{3,2},{4,5},{5,4},{6,7},{7,6},{8,9},{9,8},{10,11... | collective-permute-start | bytes 786440 | tf_op jit(solution)/shard_map/ppermute | solution.py:285
  37.1 11.4 %collective-permute-start.5 = (bf16[512,256]{1,0:T(8,128)(2,1)S(1)}, bf16[512,256]{1,0:T(8,128)(2,1)S(1)}, u32[]{:S(2)}, u32[]{:S(2)}) collective-permute-start(bf16[512,256]{1,0:T(8,128)(2,1)S(1)} %get-tuple-element.41.refs_0_), channel_id=1, source_target_pairs={{0,1},{1,0},{2,3},{3,2},{4,5},{5,4},{6,7},{7,6},{8,9},{9,8},{10,11... | collective-permute-start | bytes 786440 | tf_op jit(solution)/shard_map/ppermute | solution.py:284
  41.3 7.2 %copy-start.12 = (bf16[512,256]{1,0:T(8,128)(2,1)}, bf16[512,256]{1,0:T(8,128)(2,1)S(1)}, u32[]{:S(2)}) copy-start(bf16[512,256]{1,0:T(8,128)(2,1)S(1)} %collective-permute-done.6.refs_2_) | copy-start | bytes 786436
  41.3 7.2 %collective-permute-start.7 = (bf16[512,256]{1,0:T(8,128)(2,1)S(1)}, bf16[512,256]{1,0:T(8,128)(2,1)S(1)}, u32[]{:S(2)}, u32[]{:S(2)}) collective-permute-start(bf16[512,256]{1,0:T(8,128)(2,1)S(1)} %collective-permute-done.6.refs_2_), channel_id=1, source_target_pairs={{0,1},{1,0},{2,3},{3,2},{4,5},{5,4},{6,7},{7,6},{8,9},{9,8},{10,11... | collective-permute-start | bytes 786440 | tf_op jit(solution)/shard_map/ppermute | solution.py:285
  41.3 0.8 copy-start.16
  41.3 0.8 copy-start.17
  47.1 17.4 %collective-permute-start.12 = (bf16[512,512]{1,0:T(8,128)(2,1)}, bf16[512,512]{1,0:T(8,128)(2,1)S(1)}, u32[]{:S(2)}, u32[]{:S(2)}) collective-permute-start(bf16[512,512]{1,0:T(8,128)(2,1)} %get-tuple-element.24.here_ref.before_ref), channel_id=1, source_target_pairs={{4,0},{8,4},{12,8},{5,1},{9,5},{13,9},{6,2},{10,6},{14,10},{7,3},{... | collective-permute-start | bytes 1572872 | tf_op jit(solution)/shard_map/ppermute | solution.py:360
  48.4 0.7 copy-start.14
  49.2 0.7 copy-start.15
  54.9 26.5 %collective-permute-start.8 = (bf16[512,512]{1,0:T(8,128)(2,1)}, bf16[512,512]{1,0:T(8,128)(2,1)S(1)}, u32[]{:S(2)}, u32[]{:S(2)}) collective-permute-start(bf16[512,512]{1,0:T(8,128)(2,1)} %get-tuple-element.23.after_ref.here_ref), channel_id=1, source_target_pairs={{0,4},{4,8},{8,12},{1,5},{5,9},{9,13},{2,6},{6,10},{10,14},{3,7},{... | collective-permute-start | bytes 1572872 | tf_op jit(solution)/shard_map/ppermute | solution.py:358
  64.5 0.8 copy-start.10
  76.7 18.0 %collective-permute-start.14 = (bf16[512,256]{1,0:T(8,128)(2,1)}, bf16[512,256]{1,0:T(8,128)(2,1)S(1)}, u32[]{:S(2)}, u32[]{:S(2)}) collective-permute-start(bf16[512,256]{1,0:T(8,128)(2,1)} %get-tuple-element.35), channel_id=1, source_target_pairs={{0,1},{1,0},{2,3},{3,2},{4,5},{5,4},{6,7},{7,6},{8,9},{9,8},{10,11... | collective-permute-start | bytes 786440 | tf_op jit(solution)/shard_map/ppermute | solution.py:294
  81.4 0.8 copy-start.9
  89.0 5.2 %copy-start.11 = (bf16[512,256]{1,0:T(8,128)(2,1)S(1)}, bf16[512,256]{1,0:T(8,128)(2,1)}, u32[]{:S(2)}) copy-start(bf16[512,256]{1,0:T(8,128)(2,1)} %get-tuple-element.33) | copy-start | bytes 786436
  89.0 5.7 %copy-start.2 = (bf16[512,256]{1,0:T(8,128)(2,1)S(1)}, bf16[512,256]{1,0:T(8,128)(2,1)}, u32[]{:S(2)}) copy-start(bf16[512,256]{1,0:T(8,128)(2,1)} %get-tuple-element.34) | copy-start | bytes 786436
  89.0 19.9 %copy-start = (bf16[1024,256]{1,0:T(8,128)(2,1)S(1)}, bf16[1024,256]{1,0:T(8,128)(2,1)}, u32[]{:S(2)}) copy-start(bf16[1024,256]{1,0:T(8,128)(2,1)} %latent.1) | copy-start | bytes 1572868
  89.0 19.9 %copy-start.1 = (bf16[512,256]{1,0:T(8,128)(2,1)S(1)}, bf16[512,256]{1,0:T(8,128)(2,1)}, u32[]{:S(2)}) copy-start(bf16[512,256]{1,0:T(8,128)(2,1)} %get-tuple-element.32) | copy-start | bytes 786436
  93.9 2.5 %collective-permute-start.10 = (bf16[512,256]{1,0:T(8,128)(2,1)}, bf16[512,256]{1,0:T(8,128)(2,1)S(1)}, u32[]{:S(2)}, u32[]{:S(2)}) collective-permute-start(bf16[512,256]{1,0:T(8,128)(2,1)} %get-tuple-element.29), channel_id=1, source_target_pairs={{0,1},{1,0},{2,3},{3,2},{4,5},{5,4},{6,7},{7,6},{8,9},{9,8},{10,11... | collective-permute-start | bytes 786440 | tf_op jit(solution)/shard_map/ppermute | solution.py:294
  94.3 4.7 %collective-permute-start.13 = (bf16[512,256]{1,0:T(8,128)(2,1)S(1)}, bf16[512,256]{1,0:T(8,128)(2,1)S(1)}, u32[]{:S(2)}, u32[]{:S(2)}) collective-permute-start(bf16[512,256]{1,0:T(8,128)(2,1)S(1)} %copy-done.11), channel_id=1, source_target_pairs={{0,1},{1,0},{2,3},{3,2},{4,5},{5,4},{6,7},{7,6},{8,9},{9,8},{10,11... | collective-permute-start | bytes 786440 | tf_op jit(solution)/shard_map/ppermute | solution.py:295
  94.4 4.5 %collective-permute-start.9 = (bf16[512,256]{1,0:T(8,128)(2,1)}, bf16[512,256]{1,0:T(8,128)(2,1)S(1)}, u32[]{:S(2)}, u32[]{:S(2)}) collective-permute-start(bf16[512,256]{1,0:T(8,128)(2,1)} %get-tuple-element.27), channel_id=1, source_target_pairs={{0,1},{1,0},{2,3},{3,2},{4,5},{5,4},{6,7},{7,6},{8,9},{9,8},{10,11... | collective-permute-start | bytes 786440 | tf_op jit(solution)/shard_map/ppermute | solution.py:295
  94.8 9.2 %collective-permute-start.15 = (bf16[512,256]{1,0:T(8,128)(2,1)S(1)}, bf16[512,256]{1,0:T(8,128)(2,1)S(1)}, u32[]{:S(2)}, u32[]{:S(2)}) collective-permute-start(bf16[512,256]{1,0:T(8,128)(2,1)S(1)} %add_convert_fusion.1), channel_id=1, source_target_pairs={{0,2},{2,0},{1,3},{3,1},{4,6},{6,4},{5,7},{7,5},{8,10},{10,8},{9,1... | collective-permute-start | bytes 786440 | tf_op jit(solution)/shard_map/ppermute | solution.py:297
  97.4 11.5 %collective-permute-start.11 = (bf16[512,256]{1,0:T(8,128)(2,1)S(1)}, bf16[512,256]{1,0:T(8,128)(2,1)S(1)}, u32[]{:S(2)}, u32[]{:S(2)}) collective-permute-start(bf16[512,256]{1,0:T(8,128)(2,1)S(1)} %add_convert_fusion.3), channel_id=1, source_target_pairs={{0,2},{2,0},{1,3},{3,1},{4,6},{6,4},{5,7},{7,5},{8,10},{10,8},{9,1... | collective-permute-start | bytes 786440 | tf_op jit(solution)/shard_map/ppermute | solution.py:297
  113.6 23.7 %collective-permute-start.16 = (bf16[512,256]{1,0:T(8,128)(2,1)}, bf16[512,256]{1,0:T(8,128)(2,1)S(1)}, u32[]{:S(2)}, u32[]{:S(2)}) collective-permute-start(bf16[512,256]{1,0:T(8,128)(2,1)} %get-tuple-element.36), channel_id=1, source_target_pairs={{0,4},{4,8},{8,12},{1,5},{5,9},{9,13},{2,6},{6,10},{10,14},{3,7},{... | collective-permute-start | bytes 786440 | tf_op jit(solution)/shard_map/ppermute | solution.py:119
  117.4 19.9 %collective-permute-start.17 = (bf16[512,256]{1,0:T(8,128)(2,1)}, bf16[512,256]{1,0:T(8,128)(2,1)S(1)}, u32[]{:S(2)}, u32[]{:S(2)}) collective-permute-start(bf16[512,256]{1,0:T(8,128)(2,1)} %get-tuple-element.37), channel_id=1, source_target_pairs={{4,0},{8,4},{12,8},{5,1},{9,5},{13,9},{6,2},{10,6},{14,10},{7,3},{... | collective-permute-start | bytes 786440 | tf_op jit(solution)/shard_map/ppermute | solution.py:120
  137.3 0.7 copy-start.3
  137.3 0.8 copy-start.5

commit v2 on v1

v2 whole, which is shorter than its diff:
```python
import functools

import jax
import jax.numpy as jnp
from jax import lax
from jax.experimental import pallas as pl
from jax.experimental.pallas import tpu as pltpu
from jax.sharding import PartitionSpec as P

HD = 64
WIN = 512
TILE = 128
ESIDE = 4
DSIDE = 4
STEP = 4
NEG = -1e30
BF = jnp.bfloat16
F32 = jnp.float32


def call(body, outs, args, flops, scratch=(), name=None, spare=8):
    moved = sum(a.size * a.dtype.itemsize for a in args)
    moved += sum(o.size * o.dtype.itemsize for o in outs)
    return pl.pallas_call(
        body,
        out_shape=tuple(outs),
        in_specs=[pl.BlockSpec(memory_space=pltpu.VMEM)] * len(args),
        out_specs=tuple(pl.BlockSpec(memory_space=pltpu.VMEM) for _ in outs),
        scratch_shapes=list(scratch),
        cost_estimate=pl.CostEstimate(flops=flops, bytes_accessed=moved, transcendentals=0),
        compiler_params=pltpu.CompilerParams(vmem_limit_bytes=moved + spare * 1024 * 1024),
        name=name,
    )(*args)


def column(row):
    return jnp.transpose(jnp.broadcast_to(row, (TILE, TILE)))


def picks(rows_ref, first, source_rows):
    cols = jnp.concatenate([column(rows_ref[pl.ds(first + i, 1), :]) for i in range(STEP)], axis=0)
    cols = cols.astype(jnp.int16)
    lane = lax.broadcasted_iota(jnp.int32, cols.shape, 1).astype(jnp.int16)
    tiles = []
    for j in range(source_rows // TILE):
        hit = cols == lane + jnp.int16(j * TILE)
        tiles.append(jnp.where(hit, jnp.ones_like(cols, BF), jnp.zeros_like(cols, BF)))
    return jnp.concatenate(tiles, axis=1)


def messages(src_ref, weight_ref, first, source_ref):
    picked = jnp.dot(
        picks(src_ref, first, source_ref.shape[0]), source_ref[...], preferred_element_type=F32
    )
    scale = jnp.concatenate([column(weight_ref[pl.ds(first + i, 1), :]) for i in range(STEP)], axis=0)
    scale = jnp.concatenate([scale] * (picked.shape[1] // TILE), axis=1)
    return (picked * scale).astype(BF)


def parity():
    return lax.rem(lax.axis_index("seq"), 2)


def outward(which, side):
    return jnp.where(parity() == which, side, 0)


def block_of(step, count):
    return step if count == 1 else jnp.where(parity() == 0, count - 1 - step, step)


def partners(count):
    first = [(i, i ^ 1) for i in range(count) if i ^ 1 < count]
    second = [(i, (i - 1 ^ 1) + 1) for i in range(1, count) if (i - 1 ^ 1) + 1 < count]
    return first, second


def put_messages(src_ref, weight_ref, first, source_ref, out, at):
    edges = STEP * TILE
    for k in range(out.shape[0] // edges):
        out[k * edges : (k + 1) * edges, :] = messages(
            src_ref, weight_ref, first + k * STEP, source_ref
        )


def side_body(side, src_ref, weight_ref, source_ref, first_ref, second_ref):
    for which, out in enumerate((first_ref, second_ref)):
        put_messages(src_ref, weight_ref, outward(which, side), source_ref, out, 0)


def gather_body(start, src_ref, weight_ref, source_ref, out_ref):
    edges = STEP * TILE
    pair = 2

    def step(k, carry):
        for i in range(pair):
            n = k * pair + i
            out_ref[pl.ds(pl.multiple_of(n * edges, edges), edges), :] = messages(
                src_ref, weight_ref, start + n * STEP, source_ref
            )
        return carry

    lax.fori_loop(0, out_ref.shape[0] // (pair * edges), step, 0)


def lands(rows_ref, tiles, base, target_rows):
    spot = lax.broadcasted_iota(jnp.int32, (target_rows, TILE), 0).astype(jnp.int16)
    out = []
    for tile in tiles:
        row = rows_ref[pl.ds(tile, 1), :] - base
        row = jnp.broadcast_to(row, (target_rows, TILE)).astype(jnp.int16)
        out.append(jnp.where(row == spot, jnp.ones_like(spot, BF), jnp.zeros_like(spot, BF)))
    return jnp.concatenate(out, axis=1)


def landed(side, dst_ref, first_ref, second_ref, local_ref, base, target_rows):
    first, second = outward(0, side), outward(1, side)
    n = local_ref.shape[0] // TILE
    total = jnp.dot(
        lands(dst_ref, [2 * side + i for i in range(n)], base, target_rows),
        local_ref[...],
        preferred_element_type=F32,
    )
    total = total + jnp.dot(
        lands(dst_ref, [first + i for i in range(side)], base, target_rows),
        first_ref[...],
        preferred_element_type=F32,
    )
    return total + jnp.dot(
        lands(dst_ref, [second + i for i in range(side)], base, target_rows),
        second_ref[...],
        preferred_element_type=F32,
    )


def latent_body(side, which, count, dst_ref, first_ref, second_ref, local_ref, embed_ref, out_ref):
    rows = out_ref.shape[0]
    base = block_of(which, count) * rows
    half = 256
    for h in range(rows // half):
        at = pl.multiple_of(base + h * half, half)
        got = landed(side, dst_ref, first_ref, second_ref, local_ref, at, half)
        out_ref[h * half : (h + 1) * half, :] = (
            embed_ref[pl.ds(at, half), :].astype(F32) + got
        ).astype(BF)


def grid_body(side, count_ref, dst_ref, first_ref, second_ref, local_ref, grid_ref, out_ref):
    half = 512

    def step(k, carry):
        for i in range(2):
            at = pl.multiple_of((2 * k + i) * half, half)
            got = landed(side, dst_ref, first_ref, second_ref, local_ref, at, half)
            row = at + lax.broadcasted_iota(jnp.int32, got.shape, 0)
            value = grid_ref[pl.ds(at, half), :].astype(F32) + got
            out_ref[pl.ds(at, half), :] = jnp.where(row < count_ref[0, 0], value, 0.0).astype(BF)
        return carry

    lax.fori_loop(0, out_ref.shape[0] // (2 * half), step, 0)


def swapped(first, second):
    one, two = partners(lax.axis_size("seq"))
    return lax.ppermute(first, "seq", one), lax.ppermute(second, "seq", two)


def gathered(edge_src, edge_weight, source, side):
    edges = edge_src.shape[0] * TILE - 2 * side * TILE
    out = jax.ShapeDtypeStruct((edges, source.shape[1]), BF)
    (local,) = call(
        functools.partial(gather_body, 2 * side),
        (out,),
        (edge_src, edge_weight, source),
        2 * edges * source.size,
        name="gather",
    )
    return local


def power(exponent):
    return jnp.where(exponent > 0, 2.0, jnp.where(exponent < 0, 0.5, 1.0)).astype(F32)


def place(step, parts):
    if parts == 1:
        return 0
    mp = lax.axis_index("mp")
    sub = lax.axis_index("sub")
    mp = mp if step < 2 else 1 - mp
    sub = sub if step % 2 == 0 else 1 - sub
    return 2 * mp + sub


def qkv_body(parts, *refs):
    pieces, (gain_ref, w_ref, normed_ref, q_ref, kv_ref) = refs[:parts], refs[parts:]
    rows, width = pieces[0].shape
    total = width * parts
    block = min(256, rows)
    lane = lax.broadcasted_iota(jnp.int32, (block, TILE), 1)

    def step(k, carry):
        at = pl.ds(pl.multiple_of(k * block, block), block)
        values = [p[at, :].astype(F32) for p in pieces]
        mean = sum(jnp.sum(v, axis=1, keepdims=True) for v in values) / total
        values = [v - mean for v in values]
        var = sum(jnp.sum(v * v, axis=1, keepdims=True) for v in values) / total
        scale = lax.rsqrt(var + 1e-05)
        for i, v in enumerate(values):
            cols = pl.ds(pl.multiple_of(place(i, parts) * width, width), width)
            normed_ref[at, cols] = (v * scale * gain_ref[:, cols]).astype(BF)
        out = jnp.dot(normed_ref[at, :], w_ref[...], preferred_element_type=F32)
        for pair in range(q_ref.shape[1] // TILE):
            a, b, c = [out[:, (3 * pair + i) * TILE : (3 * pair + i + 1) * TILE] for i in range(3)]
            q = pltpu.roll(jnp.where(lane < HD, a, b), HD, 1)
            q_ref[at, pair * TILE : (pair + 1) * TILE] = q.astype(BF)
            kv_ref[at, 2 * pair * TILE : (2 * pair + 1) * TILE] = jnp.where(lane < HD, b, a).astype(BF)
            kv_ref[at, (2 * pair + 1) * TILE : (2 * pair + 2) * TILE] = c.astype(BF)
        return carry

    lax.fori_loop(0, rows // block, step, 0)


def up_body(normed_ref, w_ref, exp_ref, out_ref):
    rows = normed_ref.shape[0]
    block = min(256, rows)
    cols = min(512, w_ref.shape[1])

    def step(k, carry):
        at = pl.ds(pl.multiple_of(k * block, block), block)
        for c in range(w_ref.shape[1] // cols):
            sl = slice(c * cols, (c + 1) * cols)
            up = jnp.dot(normed_ref[at, :], w_ref[:, sl], preferred_element_type=F32)
            up = up * power(exp_ref[:, sl])
            out_ref[at, sl] = (0.5 * up * (1.0 + lax.erf(up * 0.7071067811865476))).astype(BF)
        return carry

    lax.fori_loop(0, rows // block, step, 0)


def attend_body(which, q_ref, inner_ref, here_ref, outer_ref, out_ref):
    rows = q_ref.shape[0]
    block = 256
    n = WIN // block
    lane = lax.broadcasted_iota(jnp.int32, (block, TILE), 1)
    i = lax.broadcasted_iota(jnp.int32, (block, block), 0)
    j = lax.broadcasted_iota(jnp.int32, (block, block), 1)
    seq = lax.axis_index("seq")
    after = parity() == which
    outer_ok = jnp.where(after, seq < lax.axis_size("seq") - 1, seq > 0)
    outer_bias = jnp.where(outer_ok, 0.0, NEG).astype(F32)
    ahead = jnp.where(after, i - j, j - i)
    inner_mask = jnp.where(ahead <= 0, 0.0, NEG).astype(F32)
    outer_mask = jnp.where(ahead >= 0, outer_bias, NEG).astype(F32)
    contract = (((1,), (1,)), ((), ()))

    def at(b):
        return pl.ds(pl.multiple_of(jnp.where(after, b, n - 1 - b) * block, block), block)

    for pair in range(q_ref.shape[1] // TILE):
        pair_cols = slice(pair * TILE, (pair + 1) * TILE)
        for b in range(rows // block):
            q2 = q_ref[at(b), pair_cols]
            outs = []
            for half in range(2):
                cols = slice((2 * pair + half) * TILE, (2 * pair + half + 1) * TILE)
                keep = (lane >= HD) if half == 0 else (lane < HD)
                q = jnp.where(keep, q2 * BF(HD**-0.5), jnp.zeros_like(q2))
                keys = []
                for t in range(b, b + 2 * n + 1):
                    ref = (inner_ref, here_ref, outer_ref)[t // n]
                    keys.append((t, ref[at(t % n), cols]))
                scores = []
                for t, key in keys:
                    s = lax.dot_general(q, key, contract, preferred_element_type=F32)
                    if t == b:
                        s = s + inner_mask
                    elif t == b + 2 * n:
                        s = s + outer_mask
                    elif t >= 2 * n:
                        s = s + outer_bias
                    scores.append(s)
                peak = scores[0]
                for s in scores[1:]:
                    peak = jnp.maximum(peak, s)
                peak = jnp.max(peak, axis=1, keepdims=True)
                probs = [jnp.exp(s - peak) for s in scores]
                total = probs[0]
                for p in probs[1:]:
                    total = total + p
                total = jnp.sum(total, axis=1, keepdims=True)
                mixed = jnp.dot(
                    jnp.concatenate([p.astype(BF) for p in probs], axis=1),
                    jnp.concatenate([key for _, key in keys], axis=0),
                    preferred_element_type=F32,
                )
                outs.append(mixed / total)
            out_ref[at(b), pair_cols] = jnp.where(lane < HD, outs[0], outs[1]).astype(BF)


def down_body(parts, att_ref, act_ref, w_out_ref, w_down_ref, exp_ref, *outs):
    rows = att_ref.shape[0]
    width = w_out_ref.shape[1] // parts
    block = min(256, rows)

    def step(k, carry):
        at = pl.ds(pl.multiple_of(k * block, block), block)
        for i in range(parts):
            cols = pl.ds(pl.multiple_of(place(i, parts) * width, width), width)
            mlp = jnp.dot(act_ref[at, :], w_down_ref[:, cols], preferred_element_type=F32)
            att = jnp.dot(att_ref[at, :], w_out_ref[:, cols], preferred_element_type=F32)
            part = (att + mlp * power(exp_ref[:, cols])).astype(BF)
            outs[i][at, :] = part
        return carry

    lax.fori_loop(0, rows // block, step, 0)


SWAP = [(0, 1), (1, 0)]


def gather(rows, split):
    if not split:
        return [lax.all_gather(rows, ("mp", "sub"), axis=1, tiled=True)]
    far = lax.ppermute(rows, "mp", SWAP)
    near = lax.ppermute(rows, "sub", SWAP)
    both = lax.ppermute(far, "sub", SWAP)
    return [rows, near, far, both]


def reduce_parts(parts, split):
    if not split:
        return [lax.psum_scatter(parts[0], ("mp", "sub"), scatter_dimension=1, tiled=True)]
    own, near, far, both = parts
    far_got = lax.ppermute(both, "sub", SWAP)
    near_got = lax.ppermute(near, "sub", SWAP)
    far_sum = (far.astype(F32) + far_got.astype(F32)).astype(BF)
    return [own, near_got, lax.ppermute(far_sum, "mp", SWAP)]


def settle_body(side, count, terms, src_ref, weight_ref, *refs):
    adds, (hidden_ref, first_ref, second_ref) = refs[: count * terms], refs[count * terms :]
    rows = adds[0].shape[0]
    for c in range(count):
        at = pl.ds(pl.multiple_of(block_of(c, count) * rows, rows), rows)
        latent, *more = adds[c * terms : (c + 1) * terms]
        total = more[0][...].astype(F32)
        for term in more[1:]:
            total = total + term[...].astype(F32)
        hidden_ref[at, :] = (latent[...].astype(F32) + total).astype(BF)
    side_body(side, src_ref, weight_ref, hidden_ref, first_ref, second_ref)


def shards(
    grid_latent,
    grid_count,
    hidden_embed,
    enc_src_rows,
    enc_dst_rows,
    enc_weight,
    dec_src_rows,
    dec_dst_rows,
    dec_weight,
    norm_gain,
    w_qkv,
    w_out,
    w_up,
    up_exp,
    w_down,
    down_exp,
):
    split = lax.axis_size("mp") == 2 and lax.axis_size("sub") == 2
    parts = 4 if split else 1
    hid_rows, features = hidden_embed.shape
    full = w_qkv.shape[0]
    heads = w_qkv.shape[1] // (3 * HD)
    units = w_up.shape[1]
    rows = WIN
    count = hid_rows // rows
    assert count == 2
    src, dst, wts = enc_src_rows[0], enc_dst_rows[0], enc_weight[0]
    out = jax.ShapeDtypeStruct((ESIDE * TILE, features), BF)
    sides = call(
        functools.partial(side_body, ESIDE),
        (out, out),
        (src, wts, grid_latent),
        4 * ESIDE * TILE * grid_latent.size,
        name="side",
    )
    arrived = swapped(*sides)
    moved = gathered(src, wts, grid_latent, ESIDE)
    chunks = []
    for c in range(count):
        (part,) = call(
            functools.partial(latent_body, ESIDE, c, count),
            (jax.ShapeDtypeStruct((rows, features), BF),),
            (dst, *arrived, moved, hidden_embed),
            2 * dst.size * rows * features,
            name="latent",
        )
        chunks.append([part, gather(part, split)])
    for chunk in chunks:
        chunk.append(
            call(
                functools.partial(qkv_body, parts),
                (
                    jax.ShapeDtypeStruct((rows, full), BF),
                    jax.ShapeDtypeStruct((rows, heads * HD), BF),
                    jax.ShapeDtypeStruct((rows, 2 * heads * HD), BF),
                ),
                (*chunk[1], norm_gain[None, :], w_qkv),
                2 * rows * w_qkv.size,
                name="qkv",
            )
        )
    outer = swapped(chunks[0][2][2], chunks[1][2][2])
    for c, chunk in enumerate(chunks):
        part, _, (normed, q, kv) = chunk
        (activated,) = call(
            up_body,
            (jax.ShapeDtypeStruct((rows, units), BF),),
            (normed, w_up, up_exp[None, :]),
            2 * rows * w_up.size,
            name="up",
        )
        (attended,) = call(
            functools.partial(attend_body, c),
            (jax.ShapeDtypeStruct((rows, heads * HD), BF),),
            (q, chunks[1 - c][2][2], kv, outer[c]),
            4 * rows * 3 * WIN * heads * HD,
            name="attend",
            spare=12,
        )
        outs = call(
            functools.partial(down_body, parts),
            [jax.ShapeDtypeStruct((rows, full // parts), BF)] * parts,
            (attended, activated, w_out, w_down, down_exp[None, :]),
            2 * rows * (w_out.size + w_down.size),
            name="down",
        )
        chunk.append([part, *reduce_parts(outs, split)])
    adds = [term for chunk in chunks for term in chunk[3]]
    src, dst, wts = dec_src_rows[0], dec_dst_rows[0], dec_weight[0]
    out = jax.ShapeDtypeStruct((DSIDE * TILE, features), BF)
    hidden_out, *sides = call(
        functools.partial(settle_body, DSIDE, count, len(adds) // count),
        (jax.ShapeDtypeStruct(hidden_embed.shape, BF), out, out),
        (src, wts, *adds),
        4 * DSIDE * TILE * hidden_embed.size,
        name="settle",
    )
    arrived = swapped(*sides)
    moved = gathered(src, wts, hidden_out, DSIDE)
    (grid_out,) = call(
        functools.partial(grid_body, DSIDE),
        (jax.ShapeDtypeStruct(grid_latent.shape, BF),),
        (grid_count[None, :], dst, *arrived, moved, grid_latent),
        2 * dst.size * grid_latent.size,
        name="grid",
    )
    return (hidden_out, grid_out)


def solution(mesh):
    placed = (
        P(("ens", "seq"), ("mp", "sub")),
        P(("ens", "seq")),
        P(("ens", "seq"), ("mp", "sub")),
        P(("ens", "seq"), None, None),
        P(("ens", "seq"), None, None),
        P(("ens", "seq"), None, None),
        P(("ens", "seq"), None, None),
        P(("ens", "seq"), None, None),
        P(("ens", "seq"), None, None),
        P(),
        P(None, ("mp", "sub")),
        P(("mp", "sub"), None),
        P(None, ("mp", "sub")),
        P(("mp", "sub")),
        P(("mp", "sub"), None),
        P(),
    )
    return jax.shard_map(
        shards,
        mesh=mesh,
        in_specs=placed,
        out_specs=(P(("ens", "seq"), ("mp", "sub")), P(("ens", "seq"), ("mp", "sub"))),
        check_vma=False,
    )
```

time: 143 us -> 96 us (0.67)
  Pallas kernels: 86.2 us -> 42.2 us
  waiting for transfers between devices: 20.8 us -> 30.1 us
  starting transfers between devices: 23.7 us -> 17.8 us
  local copies, waits for them, and re-layouts: 7.03 us -> 3.77 us
  other arithmetic: 3.12 us -> 0.14 us
    pallas_call x14 -> x15, Pallas kernels: 86.2 us -> 42.2 us  [call(): pl.pallas_call(body, out_shape=tuple(outs), in_specs=[pl.BlockSpec(memory...]
    ppermute x8, waiting for transfers between devices: 9.99 us -> 20.8 us  [the longest x2 11.7 us: reduce_parts(): return [own, near_got, lax.ppermute(far_sum, 'mp', SWAP)]]
    ppermute x8, starting transfers between devices: 20.1 us -> 14 us  [the longest x6 11.9 us: swapped(): return (lax.ppermute(first, 'seq', one), lax.ppermute(second, 'seq', two))]
    unnamed x36 -> x38, local copies, waits for them, and re-layouts: 5.97 us -> 3.77 us
    ppermute x2, waiting for transfers between devices: 10.8 us -> 9.23 us  [gather(): far = lax.ppermute(rows, 'mp', SWAP)]
  transfers between devices with their start and end apart: 18 -> 18, of which waited for: 4 -> 6; matrix products, arithmetic and copies ran while one was open for 1% -> 0% of each run, Pallas kernels for 51% -> 32%
where the time goes in v2:
time: 96 us; the launch traced here: 95.7 us
  Pallas kernels  42.2 us (44%)
  waiting for transfers between devices  30.1 us (31%)
  starting transfers between devices  17.8 us (19%)
  local copies, waits for them, and re-layouts  3.77 us (4%)
  between operations  1.62 us (2%)
    pallas_call x15, Pallas kernels, call(): pl.pallas_call(body, out_shape=tuple(outs), in_specs=[pl.BlockSpec(memory...  42.2 us
    ppermute x6, starting transfers between devices, swapped(): return (lax.ppermute(first, 'seq', one), lax.ppermute(second, 'seq', two))  11.9 us
    ppermute x2, waiting for transfers between devices, reduce_parts(): return [own, near_got, lax.ppermute(far_sum, 'mp', SWAP)]  11.7 us
    ppermute x2, waiting for transfers between devices, gather(): far = lax.ppermute(rows, 'mp', SWAP)  9.23 us
    ppermute x6, waiting for transfers between devices, swapped(): return (lax.ppermute(first, 'seq', one), lax.ppermute(second, 'seq', two))  9.09 us
    unnamed x38, local copies, waits for them, and re-layouts  3.77 us
    ppermute x2, starting transfers between devices, reduce_parts(): return [own, near_got, lax.ppermute(far_sum, 'mp', SWAP)]  2.16 us
    ppermute x2, starting transfers between devices, gather(): far = lax.ppermute(rows, 'mp', SWAP)  2.16 us
  transfers between devices with their start and end apart: 18, of which 6 were waited for; matrix products, arithmetic and copies ran while one was open for 0% of the time, Pallas kernels for 32%

profile of v2, /device:TPU:0, one launch (start us, length us, event | category | flops | bytes accessed | tf_op | source)
XLA Modules:
  0.0 95.7 jit_solution(5069619735170943750)
XLA Ops:
  0.6 1.2 %copy-done.6 = bf16[2048,256]{1,0:T(8,128)(2,1)S(1)} copy-done((bf16[2048,256]{1,0:T(8,128)(2,1)S(1)}, bf16[2048,256]{1,0:T(8,128)(2,1)}, u32[]{:S(2)}) %copy-start.6) | copy-done | bytes 1048600
  1.9 0.7 copy-done.12
  2.6 0.7 copy-done.14
  3.3 1.3 %side.1 = (bf16[512,256]{1,0:T(8,128)(2,1)S(1)}, bf16[512,256]{1,0:T(8,128)(2,1)S(1)}) custom-call(s32[32,128]{1,0:T(8,128)S(1)} %bitcast.18, f32[32,128]{1,0:T(8,128)S(1)} %bitcast.20, bf16[2048,256]{1,0:T(8,128)(2,1)S(1)} %copy-done.6), custom_call_target="tpu_custom_call" | custom-call | flops 1073741824 | bytes 1605632 | tf_op jit(solution)/shard_map/side/pallas_call | solution.py:24
  4.6 3.1 %collective-permute-start = (bf16[512,256]{1,0:T(8,128)(2,1)S(1)}, bf16[512,256]{1,0:T(8,128)(2,1)S(1)}, u32[]{:S(2)}, u32[]{:S(2)}) collective-permute-start(bf16[512,256]{1,0:T(8,128)(2,1)S(1)} %get-tuple-element.21), channel_id=1, source_target_pairs={{0,4},{4,0},{8,12},{12,8},{1,5},{5,1},{9,13},{13,9},{2,6},{6,2},{1... | collective-permute-start | bytes 786440 | tf_op jit(solution)/shard_map/ppermute | solution.py:165
  7.7 0.8 collective-permute-start.1
  8.6 4.0 %gather.2.local_ref = bf16[3072,256]{1,0:T(8,128)(2,1)S(1)} custom-call(s32[32,128]{1,0:T(8,128)S(1)} %bitcast.19, f32[32,128]{1,0:T(8,128)S(1)} %bitcast.21, bf16[2048,256]{1,0:T(8,128)(2,1)S(1)} %copy-done.7), custom_call_target="tpu_custom_call" | custom-call | flops 3221225472 | bytes 2654208 | tf_op jit(solution)/shard_map/gather/pallas_call | solution.py:24
  12.5 1.5 %collective-permute-done.first_ref = bf16[512,256]{1,0:T(8,128)(2,1)S(1)} collective-permute-done((bf16[512,256]{1,0:T(8,128)(2,1)S(1)}, bf16[512,256]{1,0:T(8,128)(2,1)S(1)}, u32[]{:S(2)}, u32[]{:S(2)}) %collective-permute-start) | collective-permute-done | bytes 262176 | tf_op jit(solution)/shard_map/ppermute | solution.py:165
  14.0 0.0 collective-permute-done.1.second_ref
  14.0 1.2 %latent.2.refs_0_ = bf16[512,256]{1,0:T(8,128)(2,1)S(1)} custom-call(s32[32,128]{1,0:T(8,128)S(1)} %bitcast.22, bf16[512,256]{1,0:T(8,128)(2,1)S(1)} %collective-permute-done.first_ref, bf16[512,256]{1,0:T(8,128)(2,1)S(1)} %collective-permute-done.1.second_ref, bf16[3072,256]{1,0:T(8,128)(2,1)S(1)} %gather.2.local_ref, bf16[1024,256]{1,0:T(8,128)(2,1)S(1)} %copy-done.8), custom_call_target="tpu_custom_call" | custom-call | flops 1073741824 | bytes 2899968 | tf_op jit(solution)/shard_map/latent/pallas_call | solution.py:24
  15.3 0.0 copy-start.5
  15.3 0.0 copy-start.17
  15.3 1.7 %collective-permute-start.3 = (bf16[512,256]{1,0:T(8,128)(2,1)S(1)}, bf16[512,256]{1,0:T(8,128)(2,1)S(1)}, u32[]{:S(2)}, u32[]{:S(2)}) collective-permute-start(bf16[512,256]{1,0:T(8,128)(2,1)S(1)} %latent.2.refs_0_), channel_id=1, source_target_pairs={{0,2},{2,0},{1,3},{3,1},{4,6},{6,4},{5,7},{7,5},{8,10},{10,8},{9,1... | collective-permute-start | bytes 786440 | tf_op jit(solution)/shard_map/ppermute | solution.py:325
  17.0 1.2 %latent.3.refs_0_.refs_4_ = bf16[512,256]{1,0:T(8,128)(2,1)S(1)} custom-call(s32[32,128]{1,0:T(8,128)S(1)} %bitcast.23, bf16[512,256]{1,0:T(8,128)(2,1)S(1)} %collective-permute-done.first_ref, bf16[512,256]{1,0:T(8,128)(2,1)S(1)} %collective-permute-done.1.second_ref, bf16[3072,256]{1,0:T(8,128)(2,1)S(1)} %gather.2.local_ref, bf16[1024,256]{1,0:T(8,128)(2,1)S(1)} %copy-done.8), custom_call_target="tpu_custom_call" | custom-call | flops 1073741824 | bytes 2899968 | tf_op jit(solution)/shard_map/latent/pallas_call | solution.py:24
  18.3 0.4 collective-permute-start.6
  18.7 0.0 collective-permute-start.2
  18.7 5.8 %collective-permute-done.3.refs_2_ = bf16[512,256]{1,0:T(8,128)(2,1)S(1)} collective-permute-done((bf16[512,256]{1,0:T(8,128)(2,1)S(1)}, bf16[512,256]{1,0:T(8,128)(2,1)S(1)}, u32[]{:S(2)}, u32[]{:S(2)}) %collective-permute-start.3) | collective-permute-done | bytes 262176 | tf_op jit(solution)/shard_map/ppermute | solution.py:325
  24.6 0.0 collective-permute-start.4
  24.6 0.5 collective-permute-start.5
  25.1 3.4 %collective-permute-done.6.refs_2_ = bf16[512,256]{1,0:T(8,128)(2,1)S(1)} collective-permute-done((bf16[512,256]{1,0:T(8,128)(2,1)S(1)}, bf16[512,256]{1,0:T(8,128)(2,1)S(1)}, u32[]{:S(2)}, u32[]{:S(2)}) %collective-permute-start.6) | collective-permute-done | bytes 262176 | tf_op jit(solution)/shard_map/ppermute | solution.py:325
  28.5 0.0 collective-permute-start.7
  28.5 0.0 collective-permute-done.2.refs_1_
  28.5 0.0 collective-permute-done.4.refs_3_
  28.5 2.4 %qkv.2 = (bf16[512,1024]{1,0:T(8,128)(2,1)S(1)}, bf16[512,256]{1,0:T(8,128)(2,1)S(1)}, bf16[512,512]{1,0:T(8,128)(2,1)S(1)}) custom-call(bf16[512,256]{1,0:T(8,128)(2,1)S(1)} %latent.2.refs_0_, bf16[512,256]{1,0:T(8,128)(2,1)S(1)} %collective-permute-done.2.refs_1_, bf16[512,256]{1,0:T(8,128)(2,1)S(1)} %collective-permute-done.3.refs_2_, ...), custom_call_target="tpu_custom_call" | custom-call | flops 805306368 | bytes 4460544 | tf_op jit(solution)/shard_map/qkv/pallas_call | solution.py:24
  30.9 0.0 copy-start
  30.9 0.0 copy-start.3
  30.9 4.7 %collective-permute-start.8 = (bf16[512,512]{1,0:T(8,128)(2,1)S(1)}, bf16[512,512]{1,0:T(8,128)(2,1)S(1)}, u32[]{:S(2)}, u32[]{:S(2)}) collective-permute-start(bf16[512,512]{1,0:T(8,128)(2,1)S(1)} %get-tuple-element.25.here_ref.inner_ref), channel_id=1, source_target_pairs={{0,4},{4,0},{8,12},{12,8},{1,5},{5,1},{9,13},{13,9},{2,6},{6,2},{1... | collective-permute-start | bytes 1572872 | tf_op jit(solution)/shard_map/ppermute | solution.py:165
  35.6 0.0 collective-permute-done.5.refs_1_
  35.6 2.4 %qkv.3 = (bf16[512,1024]{1,0:T(8,128)(2,1)S(1)}, bf16[512,256]{1,0:T(8,128)(2,1)S(1)}, bf16[512,512]{1,0:T(8,128)(2,1)S(1)}) custom-call(bf16[512,256]{1,0:T(8,128)(2,1)S(1)} %latent.3.refs_0_.refs_4_, bf16[512,256]{1,0:T(8,128)(2,1)S(1)} %collective-permute-done.5.refs_1_, bf16[512,256]{1,0:T(8,128)(2,1)S(1)} %collective-permute-done.6.refs_2_, ...), custom_call_target="tpu_custom_call" | custom-call | flops 805306368 | bytes 4460544 | tf_op jit(solution)/shard_map/qkv/pallas_call | solution.py:24
  38.0 0.9 collective-permute-start.12
  38.9 1.7 %up.2.act_ref = bf16[512,1024]{1,0:T(8,128)(2,1)S(1)} custom-call(bf16[512,1024]{1,0:T(8,128)(2,1)S(1)} %get-tuple-element.26.normed_ref, bf16[1024,1024]{1,0:T(8,128)(2,1)S(1)} %copy-done, s32[1,1024]{1,0:T(1,128)S(1)} %bitcast.15), custom_call_target="tpu_custom_call" | custom-call | flops 1073741824 | bytes 4198400 | tf_op jit(solution)/shard_map/up/pallas_call | solution.py:24
  40.6 0.0 copy-start.4
  40.6 0.0 copy-start.9
  40.6 0.0 copy-start.18
  40.6 7.6 %collective-permute-done.8.outer_ref = bf16[512,512]{1,0:T(8,128)(2,1)S(1)} collective-permute-done((bf16[512,512]{1,0:T(8,128)(2,1)S(1)}, bf16[512,512]{1,0:T(8,128)(2,1)S(1)}, u32[]{:S(2)}, u32[]{:S(2)}) %collective-permute-start.8) | collective-permute-done | bytes 524320 | tf_op jit(solution)/shard_map/ppermute | solution.py:165
  48.2 4.8 %attend.2.att_ref = bf16[512,256]{1,0:T(8,128)(2,1)S(1)} custom-call(bf16[512,256]{1,0:T(8,128)(2,1)S(1)} %get-tuple-element.23.q_ref, bf16[512,512]{1,0:T(8,128)(2,1)S(1)} %get-tuple-element.24.inner_ref.here_ref, bf16[512,512]{1,0:T(8,128)(2,1)S(1)} %get-tuple-element.25.here_ref.inner_ref, bf16[512,512]{1,0:T(8,128)(2,1)S(1)} %collective-permute-done.8.outer_ref), custom_call_target="tpu_custom_call" | custom-call | flops 805306368 | bytes 2097152 | tf_op jit(solution)/shard_map/attend/pallas_call | solution.py:24
  53.0 1.8 %down.2 = (bf16[512,256]{1,0:T(8,128)(2,1)S(1)}, bf16[512,256]{1,0:T(8,128)(2,1)S(1)}, bf16[512,256]{1,0:T(8,128)(2,1)S(1)}, bf16[512,256]{1,0:T(8,128)(2,1)S(1)}) custom-call(bf16[512,256]{1,0:T(8,128)(2,1)S(1)} %attend.2.att_ref, bf16[512,1024]{1,0:T(8,128)(2,1)S(1)} %up.2.act_ref, bf16[256,1024]{1,0:T(8,128)(2,1)S(1)} %copy-done.9, ...), custom_call_target="tpu_custom_call" | custom-call | flops 1342177280 | bytes 4984832 | tf_op jit(solution)/shard_map/down/pallas_call | solution.py:24
  54.8 0.1 collective-permute-start.10
  54.9 1.7 %up.3.act_ref = bf16[512,1024]{1,0:T(8,128)(2,1)S(1)} custom-call(bf16[512,1024]{1,0:T(8,128)(2,1)S(1)} %get-tuple-element.32.normed_ref, bf16[1024,1024]{1,0:T(8,128)(2,1)S(1)} %copy-done, s32[1,1024]{1,0:T(1,128)S(1)} %bitcast.16), custom_call_target="tpu_custom_call" | custom-call | flops 1073741824 | bytes 4198400 | tf_op jit(solution)/shard_map/up/pallas_call | solution.py:24
  56.6 4.8 %attend.3.att_ref = bf16[512,256]{1,0:T(8,128)(2,1)S(1)} custom-call(bf16[512,256]{1,0:T(8,128)(2,1)S(1)} %get-tuple-element.31.q_ref, bf16[512,512]{1,0:T(8,128)(2,1)S(1)} %get-tuple-element.25.here_ref.inner_ref, bf16[512,512]{1,0:T(8,128)(2,1)S(1)} %get-tuple-element.24.inner_ref.here_ref, bf16[512,512]{1,0:T(8,128)(2,1)S(1)} %collective-permute-done.12.outer_ref), custom_call_target="tpu_custom_call" | custom-call | flops 805306368 | bytes 2097152 | tf_op jit(solution)/shard_map/attend/pallas_call | solution.py:24
  61.4 0.0 copy-start.1
  61.5 0.0 copy-start.2
  61.5 2.0 %down.3 = (bf16[512,256]{1,0:T(8,128)(2,1)S(1)}, bf16[512,256]{1,0:T(8,128)(2,1)S(1)}, bf16[512,256]{1,0:T(8,128)(2,1)S(1)}, bf16[512,256]{1,0:T(8,128)(2,1)S(1)}) custom-call(bf16[512,256]{1,0:T(8,128)(2,1)S(1)} %attend.3.att_ref, bf16[512,1024]{1,0:T(8,128)(2,1)S(1)} %up.3.act_ref, bf16[256,1024]{1,0:T(8,128)(2,1)S(1)} %copy-done.9, ...), custom_call_target="tpu_custom_call" | custom-call | flops 1342177280 | bytes 4984832 | tf_op jit(solution)/shard_map/down/pallas_call | solution.py:24
  63.5 0.6 collective-permute-start.14
  64.1 0.1 collective-permute-start.9
  64.1 0.4 collective-permute-start.13
  64.6 0.0 collective-permute-done.10
  64.6 0.1 add_convert_fusion.1
  64.6 1.6 %collective-permute-start.11 = (bf16[512,256]{1,0:T(8,128)(2,1)S(1)}, bf16[512,256]{1,0:T(8,128)(2,1)S(1)}, u32[]{:S(2)}, u32[]{:S(2)}) collective-permute-start(bf16[512,256]{1,0:T(8,128)(2,1)S(1)} %add_convert_fusion.1), channel_id=1, source_target_pairs={{0,2},{2,0},{1,3},{3,1},{4,6},{6,4},{5,7},{7,5},{8,10},{10,8},{9,1... | collective-permute-start | bytes 786440 | tf_op jit(solution)/shard_map/ppermute | solution.py:338
  66.2 0.1 add_convert_fusion
  66.3 0.6 collective-permute-start.15
  66.9 0.0 collective-permute-done.9.refs_2_
  66.9 0.0 collective-permute-done.13.refs_6_
  66.9 7.0 %collective-permute-done.11.refs_3_ = bf16[512,256]{1,0:T(8,128)(2,1)S(1)} collective-permute-done((bf16[512,256]{1,0:T(8,128)(2,1)S(1)}, bf16[512,256]{1,0:T(8,128)(2,1)S(1)}, u32[]{:S(2)}, u32[]{:S(2)}) %collective-permute-start.11) | collective-permute-done | bytes 262176 | tf_op jit(solution)/shard_map/ppermute | solution.py:338
  73.9 4.7 %collective-permute-done.15.refs_7_ = bf16[512,256]{1,0:T(8,128)(2,1)S(1)} collective-permute-done((bf16[512,256]{1,0:T(8,128)(2,1)S(1)}, bf16[512,256]{1,0:T(8,128)(2,1)S(1)}, u32[]{:S(2)}, u32[]{:S(2)}) %collective-permute-start.15) | collective-permute-done | bytes 262176 | tf_op jit(solution)/shard_map/ppermute | solution.py:338
  78.6 1.1 %settle.1 = (bf16[1024,256]{1,0:T(8,128)(2,1)}, bf16[512,256]{1,0:T(8,128)(2,1)S(1)}, bf16[512,256]{1,0:T(8,128)(2,1)S(1)}) custom-call(s32[48,128]{1,0:T(8,128)S(1)} %bitcast.11, f32[48,128]{1,0:T(8,128)S(1)} %bitcast.13, bf16[512,256]{1,0:T(8,128)(2,1)S(1)} %latent.2.refs_0_, bf16[512,256]{1,0:T(8,128)(2,1)S(1)} %get-tuple-element.27.refs_1_, ...), custom_call_target="tpu_custom_call" | custom-call | flops 536870912 | bytes 3194880 | tf_op jit(solution)/shard_map/settle/pallas_call | solution.py:24
  79.8 1.7 %collective-permute-start.16 = (bf16[512,256]{1,0:T(8,128)(2,1)S(1)}, bf16[512,256]{1,0:T(8,128)(2,1)S(1)}, u32[]{:S(2)}, u32[]{:S(2)}) collective-permute-start(bf16[512,256]{1,0:T(8,128)(2,1)S(1)} %get-tuple-element.38), channel_id=1, source_target_pairs={{0,4},{4,0},{8,12},{12,8},{1,5},{5,1},{9,13},{13,9},{2,6},{6,2},{1... | collective-permute-start | bytes 786440 | tf_op jit(solution)/shard_map/ppermute | solution.py:165
  81.5 0.7 collective-permute-start.17
  82.8 0.0 copy-start.10
  82.8 1.0 %copy-done.10 = bf16[1024,256]{1,0:T(8,128)(2,1)S(1)} copy-done((bf16[1024,256]{1,0:T(8,128)(2,1)S(1)}, bf16[1024,256]{1,0:T(8,128)(2,1)}, u32[]{:S(2)}) %copy-start.10) | copy-done | bytes 524312
  83.8 3.9 %gather.3.local_ref = bf16[5120,256]{1,0:T(8,128)(2,1)S(1)} custom-call(s32[48,128]{1,0:T(8,128)S(1)} %bitcast.12, f32[48,128]{1,0:T(8,128)S(1)} %bitcast.14, bf16[1024,256]{1,0:T(8,128)(2,1)S(1)} %copy-done.10), custom_call_target="tpu_custom_call" | custom-call | flops 2684354560 | bytes 3194880 | tf_op jit(solution)/shard_map/gather/pallas_call | solution.py:24
  87.8 0.0 collective-permute-done.16.first_ref
  87.8 0.0 collective-permute-done.17.second_ref
  87.8 7.9 %grid.1 = bf16[2048,256]{1,0:T(8,128)(2,1)} custom-call(s32[1,1]{1,0:T(1,128)} %bitcast.10.count_ref, s32[48,128]{1,0:T(8,128)S(1)} %bitcast.17, bf16[512,256]{1,0:T(8,128)(2,1)S(1)} %collective-permute-done.16.first_ref, bf16[512,256]{1,0:T(8,128)(2,1)S(1)} %collective-permute-done.17.second_ref, bf16[5120,256]{1,0:T(8,128)(2,1)S(1)} %gather.3.local_ref, ...), custom_call_target="tpu_custom_call" | custom-call | flops 6442450944 | bytes 5267460 | tf_op jit(solution)/shard_map/grid/pallas_call | solution.py:24
  (27 shorter events, 0.1 us)
Async XLA Ops:
  0.6 1.2 %copy-start.6 = (bf16[2048,256]{1,0:T(8,128)(2,1)S(1)}, bf16[2048,256]{1,0:T(8,128)(2,1)}, u32[]{:S(2)}) copy-start(bf16[2048,256]{1,0:T(8,128)(2,1)} %grid_ref.1) | copy-start | bytes 3145732
  1.9 0.7 copy-start.12
  2.6 0.7 copy-start.14
  3.3 5.2 %copy-start.7 = (bf16[2048,256]{1,0:T(8,128)(2,1)S(1)}, bf16[2048,256]{1,0:T(8,128)(2,1)}, u32[]{:S(2)}) copy-start(bf16[2048,256]{1,0:T(8,128)(2,1)} %grid_ref.1) | copy-start | bytes 3145732
  3.3 5.3 %copy-start.13 = (s32[1,32,128]{2,1,0:T(8,128)S(1)}, s32[1,32,128]{2,1,0:T(8,128)}, u32[]{:S(2)}) copy-start(s32[1,32,128]{2,1,0:T(8,128)} %param.19) | copy-start | bytes 49156
  3.3 5.3 %copy-start.15 = (f32[1,32,128]{2,1,0:T(8,128)S(1)}, f32[1,32,128]{2,1,0:T(8,128)}, u32[]{:S(2)}) copy-start(f32[1,32,128]{2,1,0:T(8,128)} %param.21) | copy-start | bytes 49156
  4.6 9.4 %collective-permute-start = (bf16[512,256]{1,0:T(8,128)(2,1)S(1)}, bf16[512,256]{1,0:T(8,128)(2,1)S(1)}, u32[]{:S(2)}, u32[]{:S(2)}) collective-permute-start(bf16[512,256]{1,0:T(8,128)(2,1)S(1)} %get-tuple-element.21), channel_id=1, source_target_pairs={{0,4},{4,0},{8,12},{12,8},{1,5},{5,1},{9,13},{13,9},{2,6},{6,2},{1... | collective-permute-start | bytes 786440 | tf_op jit(solution)/shard_map/ppermute | solution.py:165
  7.7 6.3 %copy-start.8 = (bf16[1024,256]{1,0:T(8,128)(2,1)S(1)}, bf16[1024,256]{1,0:T(8,128)(2,1)}, u32[]{:S(2)}) copy-start(bf16[1024,256]{1,0:T(8,128)(2,1)} %embed_ref.3) | copy-start | bytes 1572868
  7.7 6.3 %copy-start.16 = (s32[1,32,128]{2,1,0:T(8,128)S(1)}, s32[1,32,128]{2,1,0:T(8,128)}, u32[]{:S(2)}) copy-start(s32[1,32,128]{2,1,0:T(8,128)} %param.20) | copy-start | bytes 49156
  7.7 6.3 %collective-permute-start.1 = (bf16[512,256]{1,0:T(8,128)(2,1)S(1)}, bf16[512,256]{1,0:T(8,128)(2,1)S(1)}, u32[]{:S(2)}, u32[]{:S(2)}) collective-permute-start(bf16[512,256]{1,0:T(8,128)(2,1)S(1)} %get-tuple-element.22), channel_id=1, source_target_pairs={{4,8},{8,4},{5,9},{9,5},{6,10},{10,6},{7,11},{11,7},{20,24},{24,20... | collective-permute-start | bytes 786440 | tf_op jit(solution)/shard_map/ppermute | solution.py:165
  15.3 13.2 %copy-start.5 = (bf16[1024,768]{1,0:T(8,128)(2,1)S(1)}, bf16[1024,768]{1,0:T(8,128)(2,1)}, u32[]{:S(2)}) copy-start(bf16[1024,768]{1,0:T(8,128)(2,1)} %refs_5_.3) | copy-start | bytes 4718596
  15.3 13.2 %copy-start.17 = (f32[1024]{0:T(1024)S(1)}, f32[1024]{0:T(1024)}, u32[]{:S(2)}) copy-start(f32[1024]{0:T(1024)} %param.25) | copy-start | bytes 12292
  15.3 9.2 %collective-permute-start.3 = (bf16[512,256]{1,0:T(8,128)(2,1)S(1)}, bf16[512,256]{1,0:T(8,128)(2,1)S(1)}, u32[]{:S(2)}, u32[]{:S(2)}) collective-permute-start(bf16[512,256]{1,0:T(8,128)(2,1)S(1)} %latent.2.refs_0_), channel_id=1, source_target_pairs={{0,2},{2,0},{1,3},{3,1},{4,6},{6,4},{5,7},{7,5},{8,10},{10,8},{9,1... | collective-permute-start | bytes 786440 | tf_op jit(solution)/shard_map/ppermute | solution.py:325
  18.3 10.2 %collective-permute-start.6 = (bf16[512,256]{1,0:T(8,128)(2,1)S(1)}, bf16[512,256]{1,0:T(8,128)(2,1)S(1)}, u32[]{:S(2)}, u32[]{:S(2)}) collective-permute-start(bf16[512,256]{1,0:T(8,128)(2,1)S(1)} %latent.3.refs_0_.refs_4_), channel_id=1, source_target_pairs={{0,2},{2,0},{1,3},{3,1},{4,6},{6,4},{5,7},{7,5},{8,10},{10,8},{9,1... | collective-permute-start | bytes 786440 | tf_op jit(solution)/shard_map/ppermute | solution.py:325
  18.7 9.8 %collective-permute-start.2 = (bf16[512,256]{1,0:T(8,128)(2,1)S(1)}, bf16[512,256]{1,0:T(8,128)(2,1)S(1)}, u32[]{:S(2)}, u32[]{:S(2)}) collective-permute-start(bf16[512,256]{1,0:T(8,128)(2,1)S(1)} %latent.2.refs_0_), channel_id=1, source_target_pairs={{0,1},{1,0},{2,3},{3,2},{4,5},{5,4},{6,7},{7,6},{8,9},{9,8},{10,11... | collective-permute-start | bytes 786440 | tf_op jit(solution)/shard_map/ppermute | solution.py:326
  24.6 3.9 %collective-permute-start.4 = (bf16[512,256]{1,0:T(8,128)(2,1)S(1)}, bf16[512,256]{1,0:T(8,128)(2,1)S(1)}, u32[]{:S(2)}, u32[]{:S(2)}) collective-permute-start(bf16[512,256]{1,0:T(8,128)(2,1)S(1)} %collective-permute-done.3.refs_2_), channel_id=1, source_target_pairs={{0,1},{1,0},{2,3},{3,2},{4,5},{5,4},{6,7},{7,6},{8,9},{9,8},{10,11... | collective-permute-start | bytes 786440 | tf_op jit(solution)/shard_map/ppermute | solution.py:327
  24.6 11.0 %collective-permute-start.5 = (bf16[512,256]{1,0:T(8,128)(2,1)S(1)}, bf16[512,256]{1,0:T(8,128)(2,1)S(1)}, u32[]{:S(2)}, u32[]{:S(2)}) collective-permute-start(bf16[512,256]{1,0:T(8,128)(2,1)S(1)} %latent.3.refs_0_.refs_4_), channel_id=1, source_target_pairs={{0,1},{1,0},{2,3},{3,2},{4,5},{5,4},{6,7},{7,6},{8,9},{9,8},{10,11... | collective-permute-start | bytes 786440 | tf_op jit(solution)/shard_map/ppermute | solution.py:326
  28.5 7.1 %collective-permute-start.7 = (bf16[512,256]{1,0:T(8,128)(2,1)S(1)}, bf16[512,256]{1,0:T(8,128)(2,1)S(1)}, u32[]{:S(2)}, u32[]{:S(2)}) collective-permute-start(bf16[512,256]{1,0:T(8,128)(2,1)S(1)} %collective-permute-done.6.refs_2_), channel_id=1, source_target_pairs={{0,1},{1,0},{2,3},{3,2},{4,5},{5,4},{6,7},{7,6},{8,9},{9,8},{10,11... | collective-permute-start | bytes 786440 | tf_op jit(solution)/shard_map/ppermute | solution.py:327
  30.9 8.0 %copy-start = (bf16[1024,1024]{1,0:T(8,128)(2,1)S(1)}, bf16[1024,1024]{1,0:T(8,128)(2,1)}, u32[]{:S(2)}) copy-start(bf16[1024,1024]{1,0:T(8,128)(2,1)} %w_ref.3) | copy-start | bytes 6291460
  30.9 8.0 %copy-start.3 = (s32[1024]{0:T(1024)S(1)}, s32[1024]{0:T(1024)}, u32[]{:S(2)}) copy-start(s32[1024]{0:T(1024)} %param.29) | copy-start | bytes 12292
  30.9 17.3 %collective-permute-start.8 = (bf16[512,512]{1,0:T(8,128)(2,1)S(1)}, bf16[512,512]{1,0:T(8,128)(2,1)S(1)}, u32[]{:S(2)}, u32[]{:S(2)}) collective-permute-start(bf16[512,512]{1,0:T(8,128)(2,1)S(1)} %get-tuple-element.25.here_ref.inner_ref), channel_id=1, source_target_pairs={{0,4},{4,0},{8,12},{12,8},{1,5},{5,1},{9,13},{13,9},{2,6},{6,2},{1... | collective-permute-start | bytes 1572872 | tf_op jit(solution)/shard_map/ppermute | solution.py:165
  38.0 18.6 %collective-permute-start.12 = (bf16[512,512]{1,0:T(8,128)(2,1)S(1)}, bf16[512,512]{1,0:T(8,128)(2,1)S(1)}, u32[]{:S(2)}, u32[]{:S(2)}) collective-permute-start(bf16[512,512]{1,0:T(8,128)(2,1)S(1)} %get-tuple-element.24.inner_ref.here_ref), channel_id=1, source_target_pairs={{4,8},{8,4},{5,9},{9,5},{6,10},{10,6},{7,11},{11,7},{20,24},{24,20... | collective-permute-start | bytes 1572872 | tf_op jit(solution)/shard_map/ppermute | solution.py:165
  40.6 12.5 %copy-start.4 = (bf16[1024,1024]{1,0:T(8,128)(2,1)S(1)}, bf16[1024,1024]{1,0:T(8,128)(2,1)}, u32[]{:S(2)}) copy-start(bf16[1024,1024]{1,0:T(8,128)(2,1)} %w_down_ref.3) | copy-start | bytes 6291460
  40.6 12.5 %copy-start.9 = (bf16[256,1024]{1,0:T(8,128)(2,1)S(1)}, bf16[256,1024]{1,0:T(8,128)(2,1)}, u32[]{:S(2)}) copy-start(bf16[256,1024]{1,0:T(8,128)(2,1)} %w_out_ref.3) | copy-start | bytes 1572868
  40.6 12.4 %copy-start.18 = (s32[1024]{0:T(1024)S(1)}, s32[1024]{0:T(1024)}, u32[]{:S(2)}) copy-start(s32[1024]{0:T(1024)} %param.31) | copy-start | bytes 12292
  54.8 9.7 %collective-permute-start.10 = (bf16[512,256]{1,0:T(8,128)(2,1)S(1)}, bf16[512,256]{1,0:T(8,128)(2,1)S(1)}, u32[]{:S(2)}, u32[]{:S(2)}) collective-permute-start(bf16[512,256]{1,0:T(8,128)(2,1)S(1)} %get-tuple-element.30), channel_id=1, source_target_pairs={{0,1},{1,0},{2,3},{3,2},{4,5},{5,4},{6,7},{7,6},{8,9},{9,8},{10,11... | collective-permute-start | bytes 786440 | tf_op jit(solution)/shard_map/ppermute | solution.py:335
  61.4 17.2 %copy-start.1 = (s32[1,48,128]{2,1,0:T(8,128)S(1)}, s32[1,48,128]{2,1,0:T(8,128)}, u32[]{:S(2)}) copy-start(s32[1,48,128]{2,1,0:T(8,128)} %param.22) | copy-start | bytes 73732
  61.5 17.2 %copy-start.2 = (f32[1,48,128]{2,1,0:T(8,128)S(1)}, f32[1,48,128]{2,1,0:T(8,128)}, u32[]{:S(2)}) copy-start(f32[1,48,128]{2,1,0:T(8,128)} %param.24) | copy-start | bytes 73732
  63.5 2.7 %collective-permute-start.14 = (bf16[512,256]{1,0:T(8,128)(2,1)S(1)}, bf16[512,256]{1,0:T(8,128)(2,1)S(1)}, u32[]{:S(2)}, u32[]{:S(2)}) collective-permute-start(bf16[512,256]{1,0:T(8,128)(2,1)S(1)} %get-tuple-element.36), channel_id=1, source_target_pairs={{0,1},{1,0},{2,3},{3,2},{4,5},{5,4},{6,7},{7,6},{8,9},{9,8},{10,11... | collective-permute-start | bytes 786440 | tf_op jit(solution)/shard_map/ppermute | solution.py:335
  64.1 2.8 %collective-permute-start.9 = (bf16[512,256]{1,0:T(8,128)(2,1)S(1)}, bf16[512,256]{1,0:T(8,128)(2,1)S(1)}, u32[]{:S(2)}, u32[]{:S(2)}) collective-permute-start(bf16[512,256]{1,0:T(8,128)(2,1)S(1)} %get-tuple-element.28), channel_id=1, source_target_pairs={{0,1},{1,0},{2,3},{3,2},{4,5},{5,4},{6,7},{7,6},{8,9},{9,8},{10,11... | collective-permute-start | bytes 786440 | tf_op jit(solution)/shard_map/ppermute | solution.py:336
  64.1 2.7 %collective-permute-start.13 = (bf16[512,256]{1,0:T(8,128)(2,1)S(1)}, bf16[512,256]{1,0:T(8,128)(2,1)S(1)}, u32[]{:S(2)}, u32[]{:S(2)}) collective-permute-start(bf16[512,256]{1,0:T(8,128)(2,1)S(1)} %get-tuple-element.34), channel_id=1, source_target_pairs={{0,1},{1,0},{2,3},{3,2},{4,5},{5,4},{6,7},{7,6},{8,9},{9,8},{10,11... | collective-permute-start | bytes 786440 | tf_op jit(solution)/shard_map/ppermute | solution.py:336
  64.6 9.2 %collective-permute-start.11 = (bf16[512,256]{1,0:T(8,128)(2,1)S(1)}, bf16[512,256]{1,0:T(8,128)(2,1)S(1)}, u32[]{:S(2)}, u32[]{:S(2)}) collective-permute-start(bf16[512,256]{1,0:T(8,128)(2,1)S(1)} %add_convert_fusion.1), channel_id=1, source_target_pairs={{0,2},{2,0},{1,3},{3,1},{4,6},{6,4},{5,7},{7,5},{8,10},{10,8},{9,1... | collective-permute-start | bytes 786440 | tf_op jit(solution)/shard_map/ppermute | solution.py:338
  66.3 12.3 %collective-permute-start.15 = (bf16[512,256]{1,0:T(8,128)(2,1)S(1)}, bf16[512,256]{1,0:T(8,128)(2,1)S(1)}, u32[]{:S(2)}, u32[]{:S(2)}) collective-permute-start(bf16[512,256]{1,0:T(8,128)(2,1)S(1)} %add_convert_fusion), channel_id=1, source_target_pairs={{0,2},{2,0},{1,3},{3,1},{4,6},{6,4},{5,7},{7,5},{8,10},{10,8},{9,1... | collective-permute-start | bytes 786440 | tf_op jit(solution)/shard_map/ppermute | solution.py:338
  79.8 8.0 %collective-permute-start.16 = (bf16[512,256]{1,0:T(8,128)(2,1)S(1)}, bf16[512,256]{1,0:T(8,128)(2,1)S(1)}, u32[]{:S(2)}, u32[]{:S(2)}) collective-permute-start(bf16[512,256]{1,0:T(8,128)(2,1)S(1)} %get-tuple-element.38), channel_id=1, source_target_pairs={{0,4},{4,0},{8,12},{12,8},{1,5},{5,1},{9,13},{13,9},{2,6},{6,2},{1... | collective-permute-start | bytes 786440 | tf_op jit(solution)/shard_map/ppermute | solution.py:165
  81.5 6.3 %collective-permute-start.17 = (bf16[512,256]{1,0:T(8,128)(2,1)S(1)}, bf16[512,256]{1,0:T(8,128)(2,1)S(1)}, u32[]{:S(2)}, u32[]{:S(2)}) collective-permute-start(bf16[512,256]{1,0:T(8,128)(2,1)S(1)} %get-tuple-element.39), channel_id=1, source_target_pairs={{4,8},{8,4},{5,9},{9,5},{6,10},{10,6},{7,11},{11,7},{20,24},{24,20... | collective-permute-start | bytes 786440 | tf_op jit(solution)/shard_map/ppermute | solution.py:165
  82.8 1.0 %copy-start.10 = (bf16[1024,256]{1,0:T(8,128)(2,1)S(1)}, bf16[1024,256]{1,0:T(8,128)(2,1)}, u32[]{:S(2)}) copy-start(bf16[1024,256]{1,0:T(8,128)(2,1)} %get-tuple-element.19.source_ref) | copy-start | bytes 1572868
  83.8 3.9 %copy-start.11 = (s32[1,48,128]{2,1,0:T(8,128)S(1)}, s32[1,48,128]{2,1,0:T(8,128)}, u32[]{:S(2)}) copy-start(s32[1,48,128]{2,1,0:T(8,128)} %param.23) | copy-start | bytes 73732

commit v3 on v2

--- a/solution.py
+++ b/solution.py
@@ -13,23 +13,23 @@
 ESIDE = 4
 DSIDE = 4
 STEP = 4
+BLOCK = 256
 NEG = -1e30
 BF = jnp.bfloat16
 F32 = jnp.float32
 
 
-def call(body, outs, args, flops, scratch=(), name=None, spare=8):
+def call(body, outs, args, flops, scratch=(), spare=8, space=pltpu.VMEM, limit=None):
     moved = sum(a.size * a.dtype.itemsize for a in args)
     moved += sum(o.size * o.dtype.itemsize for o in outs)
     return pl.pallas_call(
         body,
         out_shape=tuple(outs),
-        in_specs=[pl.BlockSpec(memory_space=pltpu.VMEM)] * len(args),
+        in_specs=[pl.BlockSpec(memory_space=space)] * len(args),
         out_specs=tuple(pl.BlockSpec(memory_space=pltpu.VMEM) for _ in outs),
         scratch_shapes=list(scratch),
         cost_estimate=pl.CostEstimate(flops=flops, bytes_accessed=moved, transcendentals=0),
-        compiler_params=pltpu.CompilerParams(vmem_limit_bytes=moved + spare * 1024 * 1024),
-        name=name,
+        compiler_params=pltpu.CompilerParams(vmem_limit_bytes=limit or moved + spare * 1024 * 1024),
     )(*args)
 
 
@@ -75,7 +75,7 @@
     return first, second
 
 
-def put_messages(src_ref, weight_ref, first, source_ref, out, at):
+def put_messages(src_ref, weight_ref, first, source_ref, out):
     edges = STEP * TILE
     for k in range(out.shape[0] // edges):
         out[k * edges : (k + 1) * edges, :] = messages(
@@ -85,7 +85,17 @@
 
 def side_body(side, src_ref, weight_ref, source_ref, first_ref, second_ref):
     for which, out in enumerate((first_ref, second_ref)):
-        put_messages(src_ref, weight_ref, outward(which, side), source_ref, out, 0)
+        put_messages(src_ref, weight_ref, outward(which, side), source_ref, out)
+
+
+def fetch_side_body(side, *refs):
+    sources, outs, held, sems = refs[:3], refs[3:5], refs[5:8], refs[8]
+    copies = [pltpu.make_async_copy(a, b, sems.at[i]) for i, (a, b) in enumerate(zip(sources, held))]
+    for copy in copies:
+        copy.start()
+    for copy in copies:
+        copy.wait()
+    side_body(side, *held, *outs)
 
 
 def gather_body(start, src_ref, weight_ref, source_ref, out_ref):
@@ -113,51 +123,55 @@
     return jnp.concatenate(out, axis=1)
 
 
-def landed(side, dst_ref, first_ref, second_ref, local_ref, base, target_rows):
-    first, second = outward(0, side), outward(1, side)
-    n = local_ref.shape[0] // TILE
-    total = jnp.dot(
-        lands(dst_ref, [2 * side + i for i in range(n)], base, target_rows),
-        local_ref[...],
-        preferred_element_type=F32,
-    )
-    total = total + jnp.dot(
-        lands(dst_ref, [first + i for i in range(side)], base, target_rows),
-        first_ref[...],
-        preferred_element_type=F32,
-    )
-    return total + jnp.dot(
-        lands(dst_ref, [second + i for i in range(side)], base, target_rows),
-        second_ref[...],
-        preferred_element_type=F32,
-    )
-
-
-def latent_body(side, which, count, dst_ref, first_ref, second_ref, local_ref, embed_ref, out_ref):
+def landed(side, dst_ref, first_ref, second_ref, base, target_rows):
+    total = None
+    for which, got_ref in enumerate((first_ref, second_ref)):
+        first = outward(which, side)
+        got = jnp.dot(
+            lands(dst_ref, [first + i for i in range(side)], base, target_rows),
+            got_ref[...],
+            preferred_element_type=F32,
+        )
+        total = got if total is None else total + got
+    return total
+
+
+def spread_body(side, dst_ref, local_ref, out_ref):
+    block = 512
+
+    def step(k, carry):
+        for i in range(2):
+            at = pl.multiple_of((2 * k + i) * block, block)
+            tiles = [2 * side + t for t in range(local_ref.shape[0] // TILE)]
+            out_ref[pl.ds(at, block), :] = jnp.dot(
+                lands(dst_ref, tiles, at, block), local_ref[...], preferred_element_type=F32
+            )
+        return carry
+
+    lax.fori_loop(0, out_ref.shape[0] // (2 * block), step, 0)
+
+
+def latent_body(side, which, count, dst_ref, first_ref, second_ref, total_ref, embed_ref, out_ref):
     rows = out_ref.shape[0]
     base = block_of(which, count) * rows
-    half = 256
-    for h in range(rows // half):
-        at = pl.multiple_of(base + h * half, half)
-        got = landed(side, dst_ref, first_ref, second_ref, local_ref, at, half)
-        out_ref[h * half : (h + 1) * half, :] = (
-            embed_ref[pl.ds(at, half), :].astype(F32) + got
+    for h in range(rows // BLOCK):
+        at = pl.multiple_of(base + h * BLOCK, BLOCK)
+        got = landed(side, dst_ref, first_ref, second_ref, at, BLOCK)
+        got = got + total_ref[pl.ds(at, BLOCK), :]
+        out_ref[h * BLOCK : (h + 1) * BLOCK, :] = (
+            embed_ref[pl.ds(at, BLOCK), :].astype(F32) + got
         ).astype(BF)
 
 
-def grid_body(side, count_ref, dst_ref, first_ref, second_ref, local_ref, grid_ref, out_ref):
-    half = 512
-
-    def step(k, carry):
-        for i in range(2):
-            at = pl.multiple_of((2 * k + i) * half, half)
-            got = landed(side, dst_ref, first_ref, second_ref, local_ref, at, half)
-            row = at + lax.broadcasted_iota(jnp.int32, got.shape, 0)
-            value = grid_ref[pl.ds(at, half), :].astype(F32) + got
-            out_ref[pl.ds(at, half), :] = jnp.where(row < count_ref[0, 0], value, 0.0).astype(BF)
-        return carry
-
-    lax.fori_loop(0, out_ref.shape[0] // (2 * half), step, 0)
+def grid_body(side, count_ref, dst_ref, first_ref, second_ref, total_ref, grid_ref, out_ref):
+    rows = out_ref.shape[0]
+    for h in range(rows // BLOCK):
+        at = pl.program_id(0) * rows + h * BLOCK
+        here = slice(h * BLOCK, (h + 1) * BLOCK)
+        got = landed(side, dst_ref, first_ref, second_ref, at, BLOCK) + total_ref[here, :]
+        row = at + lax.broadcasted_iota(jnp.int32, got.shape, 0)
+        value = grid_ref[here, :].astype(F32) + got
+        out_ref[here, :] = jnp.where(row < count_ref[0, 0], value, 0.0).astype(BF)
 
 
 def swapped(first, second):
@@ -165,17 +179,43 @@
     return lax.ppermute(first, "seq", one), lax.ppermute(second, "seq", two)
 
 
-def gathered(edge_src, edge_weight, source, side):
+def gathered(edge_src, edge_dst, edge_weight, source, target_rows, side):
     edges = edge_src.shape[0] * TILE - 2 * side * TILE
-    out = jax.ShapeDtypeStruct((edges, source.shape[1]), BF)
+    features = source.shape[1]
     (local,) = call(
         functools.partial(gather_body, 2 * side),
-        (out,),
+        (jax.ShapeDtypeStruct((edges, features), BF),),
         (edge_src, edge_weight, source),
         2 * edges * source.size,
-        name="gather",
-    )
-    return local
+    )
+    (total,) = call(
+        functools.partial(spread_body, side),
+        (jax.ShapeDtypeStruct((target_rows, features), F32),),
+        (edge_dst, local),
+        2 * edges * target_rows * features,
+    )
+    return total
+
+
+def settled(side, grid_count, edge_dst, first, second, total, grid_latent):
+    rows, features = grid_latent.shape
+    block = 512
+    whole = pl.BlockSpec(memory_space=pltpu.VMEM)
+    piece = pl.BlockSpec((block, features), lambda i: (i, 0))
+    return pl.pallas_call(
+        functools.partial(grid_body, side),
+        grid=(rows // block,),
+        out_shape=jax.ShapeDtypeStruct(grid_latent.shape, BF),
+        in_specs=[whole, whole, whole, whole, piece, piece],
+        out_specs=piece,
+        cost_estimate=pl.CostEstimate(
+            flops=4 * side * TILE * grid_latent.size,
+            bytes_accessed=8 * grid_latent.size,
+            transcendentals=0,
+        ),
+        compiler_params=pltpu.CompilerParams(vmem_limit_bytes=16 * 1024 * 1024),
+        name="grid",
+    )(grid_count, edge_dst, first, second, total, grid_latent)
 
 
 def power(exponent):
@@ -238,9 +278,14 @@
     lax.fori_loop(0, rows // block, step, 0)
 
 
-def attend_body(which, q_ref, inner_ref, here_ref, outer_ref, out_ref):
-    rows = q_ref.shape[0]
-    block = 256
+def spot(which, b):
+    n = WIN // BLOCK
+    where = jnp.where(parity() == which, b, n - 1 - b)
+    return pl.ds(pl.multiple_of(where * BLOCK, BLOCK), BLOCK)
+
+
+def attend_body(which, blocks, q_ref, inner_ref, here_ref, outer_ref, out_ref):
+    block = BLOCK
     n = WIN // block
     lane = lax.broadcasted_iota(jnp.int32, (block, TILE), 1)
     i = lax.broadcasted_iota(jnp.int32, (block, block), 0)
@@ -254,13 +299,10 @@
     outer_mask = jnp.where(ahead >= 0, outer_bias, NEG).astype(F32)
     contract = (((1,), (1,)), ((), ()))
 
-    def at(b):
-        return pl.ds(pl.multiple_of(jnp.where(after, b, n - 1 - b) * block, block), block)
-
     for pair in range(q_ref.shape[1] // TILE):
         pair_cols = slice(pair * TILE, (pair + 1) * TILE)
-        for b in range(rows // block):
-            q2 = q_ref[at(b), pair_cols]
+        for k, b in enumerate(blocks):
+            q2 = q_ref[spot(which, b), pair_cols]
             outs = []
             for half in range(2):
                 cols = slice((2 * pair + half) * TILE, (2 * pair + half + 1) * TILE)
@@ -269,7 +311,7 @@
                 keys = []
                 for t in range(b, b + 2 * n + 1):
                     ref = (inner_ref, here_ref, outer_ref)[t // n]
-                    keys.append((t, ref[at(t % n), cols]))
+                    keys.append((t, ref[spot(which, t % n), cols]))
                 scores = []
                 for t, key in keys:
                     s = lax.dot_general(q, key, contract, preferred_element_type=F32)
@@ -295,28 +337,24 @@
                     preferred_element_type=F32,
                 )
                 outs.append(mixed / total)
-            out_ref[at(b), pair_cols] = jnp.where(lane < HD, outs[0], outs[1]).astype(BF)
-
-
-def down_body(parts, att_ref, act_ref, w_out_ref, w_down_ref, exp_ref, *outs):
-    rows = att_ref.shape[0]
+            out_ref[k * block : (k + 1) * block, pair_cols] = jnp.where(
+                lane < HD, outs[0], outs[1]
+            ).astype(BF)
+
+
+def down_body(parts, which, blocks, att_ref, act_ref, w_out_ref, w_down_ref, exp_ref, *outs):
     width = w_out_ref.shape[1] // parts
-    block = min(256, rows)
-
-    def step(k, carry):
-        at = pl.ds(pl.multiple_of(k * block, block), block)
+    for k, b in enumerate(blocks):
+        at = slice(k * BLOCK, (k + 1) * BLOCK)
         for i in range(parts):
             cols = pl.ds(pl.multiple_of(place(i, parts) * width, width), width)
-            mlp = jnp.dot(act_ref[at, :], w_down_ref[:, cols], preferred_element_type=F32)
+            mlp = jnp.dot(act_ref[spot(which, b), :], w_down_ref[:, cols], preferred_element_type=F32)
             att = jnp.dot(att_ref[at, :], w_out_ref[:, cols], preferred_element_type=F32)
-            part = (att + mlp * power(exp_ref[:, cols])).astype(BF)
-            outs[i][at, :] = part
-        return carry
-
-    lax.fori_loop(0, rows // block, step, 0)
+            outs[i][at, :] = (att + mlp * power(exp_ref[:, cols])).astype(BF)
 
 
 SWAP = [(0, 1), (1, 0)]
+UNITS = ((0, (0, 1)), (1, (0,)), (1, (1,)))
 
 
 def gather(rows, split):
@@ -338,17 +376,24 @@
     return [own, near_got, lax.ppermute(far_sum, "mp", SWAP)]
 
 
-def settle_body(side, count, terms, src_ref, weight_ref, *refs):
-    adds, (hidden_ref, first_ref, second_ref) = refs[: count * terms], refs[count * terms :]
-    rows = adds[0].shape[0]
-    for c in range(count):
-        at = pl.ds(pl.multiple_of(block_of(c, count) * rows, rows), rows)
-        latent, *more = adds[c * terms : (c + 1) * terms]
-        total = more[0][...].astype(F32)
-        for term in more[1:]:
-            total = total + term[...].astype(F32)
-        hidden_ref[at, :] = (latent[...].astype(F32) + total).astype(BF)
-    side_body(side, src_ref, weight_ref, hidden_ref, first_ref, second_ref)
+def settle_body(side, count, units, src_ref, weight_ref, *refs):
+    latents, refs = refs[:count], refs[count:]
+    terms = (len(refs) - 4) // len(units)
+    hidden_ref, copy_ref, first_ref, second_ref = refs[-4:]
+    for u, (c, blocks) in enumerate(units):
+        adds = refs[u * terms : (u + 1) * terms]
+        base = block_of(c, count) * WIN
+        for k, b in enumerate(blocks):
+            at = slice(k * BLOCK, (k + 1) * BLOCK)
+            total = adds[0][at, :].astype(F32)
+            for term in adds[1:]:
+                total = total + term[at, :].astype(F32)
+            spots = spot(c, b)
+            value = (latents[c][spots, :].astype(F32) + total).astype(BF)
+            rows = pl.ds(pl.multiple_of(base + spots.start, BLOCK), BLOCK)
+            hidden_ref[rows, :] = value
+            copy_ref[rows, :] = value
+    side_body(side, src_ref, weight_ref, copy_ref, first_ref, second_ref)
 
 
 def shards(
@@ -380,23 +425,28 @@
     assert count == 2
     src, dst, wts = enc_src_rows[0], enc_dst_rows[0], enc_weight[0]
     out = jax.ShapeDtypeStruct((ESIDE * TILE, features), BF)
+    args = (src, wts, grid_latent)
     sides = call(
-        functools.partial(side_body, ESIDE),
+        functools.partial(fetch_side_body, ESIDE),
         (out, out),
-        (src, wts, grid_latent),
+        args,
         4 * ESIDE * TILE * grid_latent.size,
-        name="side",
+        scratch=[
+            *(pltpu.VMEM(a.shape, a.dtype) for a in args),
+            pltpu.SemaphoreType.DMA((len(args),)),
+        ],
+        space=pltpu.HBM,
+        limit=60 * 1024 * 1024,
     )
     arrived = swapped(*sides)
-    moved = gathered(src, wts, grid_latent, ESIDE)
+    total = gathered(src, dst, wts, grid_latent, hid_rows, ESIDE)
     chunks = []
     for c in range(count):
         (part,) = call(
             functools.partial(latent_body, ESIDE, c, count),
             (jax.ShapeDtypeStruct((rows, features), BF),),
-            (dst, *arrived, moved, hidden_embed),
-            2 * dst.size * rows * features,
-            name="latent",
+            (dst, *arrived, total, hidden_embed),
+            4 * ESIDE * TILE * rows * features,
         )
         chunks.append([part, gather(part, split)])
     for chunk in chunks:
@@ -410,54 +460,47 @@
                 ),
                 (*chunk[1], norm_gain[None, :], w_qkv),
                 2 * rows * w_qkv.size,
-                name="qkv",
             )
         )
     outer = swapped(chunks[0][2][2], chunks[1][2][2])
-    for c, chunk in enumerate(chunks):
-        part, _, (normed, q, kv) = chunk
+    for chunk in chunks:
         (activated,) = call(
             up_body,
             (jax.ShapeDtypeStruct((rows, units), BF),),
-            (normed, w_up, up_exp[None, :]),
+            (chunk[2][0], w_up, up_exp[None, :]),
             2 * rows * w_up.size,
-            name="up",
-        )
+        )
+        chunk.append(activated)
+    sums = []
+    for c, blocks in UNITS:
+        part, _, (_, q, kv), activated = chunks[c]
+        size = len(blocks) * BLOCK
         (attended,) = call(
-            functools.partial(attend_body, c),
-            (jax.ShapeDtypeStruct((rows, heads * HD), BF),),
+            functools.partial(attend_body, c, blocks),
+            (jax.ShapeDtypeStruct((size, heads * HD), BF),),
             (q, chunks[1 - c][2][2], kv, outer[c]),
-            4 * rows * 3 * WIN * heads * HD,
-            name="attend",
+            4 * size * 3 * WIN * heads * HD,
             spare=12,
         )
         outs = call(
-            functools.partial(down_body, parts),
-            [jax.ShapeDtypeStruct((rows, full // parts), BF)] * parts,
+            functools.partial(down_body, parts, c, blocks),
+            [jax.ShapeDtypeStruct((size, full // parts), BF)] * parts,
             (attended, activated, w_out, w_down, down_exp[None, :]),
-            2 * rows * (w_out.size + w_down.size),
-            name="down",
-        )
-        chunk.append([part, *reduce_parts(outs, split)])
-    adds = [term for chunk in chunks for term in chunk[3]]
+            2 * size * (w_out.size + w_down.size),
+        )
+        sums += reduce_parts(outs, split)
     src, dst, wts = dec_src_rows[0], dec_dst_rows[0], dec_weight[0]
     out = jax.ShapeDtypeStruct((DSIDE * TILE, features), BF)
-    hidden_out, *sides = call(
-        functools.partial(settle_body, DSIDE, count, len(adds) // count),
-        (jax.ShapeDtypeStruct(hidden_embed.shape, BF), out, out),
-        (src, wts, *adds),
+    whole = jax.ShapeDtypeStruct(hidden_embed.shape, BF)
+    hidden_out, hidden, *sides = call(
+        functools.partial(settle_body, DSIDE, count, UNITS),
+        (whole, whole, out, out),
+        (src, wts, *(chunk[0] for chunk in chunks), *sums),
         4 * DSIDE * TILE * hidden_embed.size,
-        name="settle",
     )
     arrived = swapped(*sides)
-    moved = gathered(src, wts, hidden_out, DSIDE)
-    (grid_out,) = call(
-        functools.partial(grid_body, DSIDE),
-        (jax.ShapeDtypeStruct(grid_latent.shape, BF),),
-        (grid_count[None, :], dst, *arrived, moved, grid_latent),
-        2 * dst.size * grid_latent.size,
-        name="grid",
-    )
+    total = gathered(src, dst, wts, hidden, grid_latent.shape[0], DSIDE)
+    grid_out = settled(DSIDE, grid_count[None, :], dst, *arrived, total, grid_latent)
     return (hidden_out, grid_out)
 
 

time: 96 us -> 95 us (0.990)
  waiting for transfers between devices: 30.1 us -> 25.4 us
  starting transfers between devices: 17.8 us -> 21.7 us
  local copies, waits for them, and re-layouts: 3.77 us -> 0.09 us
  Pallas kernels: 42.2 us -> 45.7 us
    ppermute x6, waiting for transfers between devices: 9.09 us -> 5.23 us  [swapped(): return (lax.ppermute(first, 'seq', one), lax.ppermute(second, 'seq', two))]
    unnamed x38 -> x30, local copies, waits for them, and re-layouts: 3.77 us -> 0.09 us
    pallas_call x0 -> x1, Pallas kernels: none -> 2.87 us  [settled(): pl.pallas_call(functools.partial(grid_body, side), grid=(rows // block,),...]
    ppermute x6, starting transfers between devices: 11.9 us -> 14 us  [swapped(): return (lax.ppermute(first, 'seq', one), lax.ppermute(second, 'seq', two))]
    ppermute x2 -> x3, waiting for transfers between devices: 11.7 us -> 9.82 us  [reduce_parts(): return [own, near_got, lax.ppermute(far_sum, 'mp', SWAP)]]
    ppermute x2 -> x3, starting transfers between devices: 2.16 us -> 3.71 us  [reduce_parts(): return [own, near_got, lax.ppermute(far_sum, 'mp', SWAP)]]
    ppermute x2, waiting for transfers between devices: 9.23 us -> 10.3 us  [gather(): far = lax.ppermute(rows, 'mp', SWAP)]
    pallas_call x15 -> x18, Pallas kernels: 42.2 us -> 42.8 us  [call(): pl.pallas_call(body, out_shape=tuple(outs), in_specs=[pl.BlockSpec(memory...]
  transfers between devices with their start and end apart: 18 -> 21, of which waited for: 6 -> 5; matrix products, arithmetic and copies ran while one was open for 0% -> 0% of each run, Pallas kernels for 32% -> 40%
where the time goes in v3:
time: 95 us; the launch traced here: 94.8 us
  Pallas kernels  45.7 us (48%)
  waiting for transfers between devices  25.4 us (27%)
  starting transfers between devices  21.7 us (23%)
  between operations  1.75 us (2%)
    pallas_call x18, Pallas kernels, call(): pl.pallas_call(body, out_shape=tuple(outs), in_specs=[pl.BlockSpec(memory...  42.8 us
    ppermute x6, starting transfers between devices, swapped(): return (lax.ppermute(first, 'seq', one), lax.ppermute(second, 'seq', two))  14 us
    ppermute x2, waiting for transfers between devices, gather(): far = lax.ppermute(rows, 'mp', SWAP)  10.3 us
    ppermute x3, waiting for transfers between devices, reduce_parts(): return [own, near_got, lax.ppermute(far_sum, 'mp', SWAP)]  9.82 us
    ppermute x6, waiting for transfers between devices, swapped(): return (lax.ppermute(first, 'seq', one), lax.ppermute(second, 'seq', two))  5.23 us
    ppermute x3, starting transfers between devices, reduce_parts(): return [own, near_got, lax.ppermute(far_sum, 'mp', SWAP)]  3.71 us
    pallas_call x1, Pallas kernels, settled(): pl.pallas_call(functools.partial(grid_body, side), grid=(rows // block,),...  2.87 us
    ppermute x2, starting transfers between devices, gather(): far = lax.ppermute(rows, 'mp', SWAP)  2.16 us
  transfers between devices with their start and end apart: 21, of which 5 were waited for; matrix products, arithmetic and copies ran while one was open for 0% of the time, Pallas kernels for 40%

profile of v3, /device:TPU:0, one launch (start us, length us, event | category | flops | bytes accessed | tf_op | source)
XLA Modules:
  0.0 94.8 jit_solution(10940367543200600104)
XLA Ops:
  0.7 3.5 %shard_map.167 = (bf16[512,256]{1,0:T(8,128)(2,1)}, bf16[512,256]{1,0:T(8,128)(2,1)}) custom-call(s32[32,128]{1,0:T(8,128)} %bitcast.25, f32[32,128]{1,0:T(8,128)} %bitcast.27, bf16[2048,256]{1,0:T(8,128)(2,1)} %grid_ref.1), custom_call_target="tpu_custom_call" | custom-call | flops 1073741824 | bytes 1605632 | tf_op jit(solution)/shard_map/pallas_call | solution.py:25
  4.1 3.1 %collective-permute-start = (bf16[512,256]{1,0:T(8,128)(2,1)}, bf16[512,256]{1,0:T(8,128)(2,1)S(1)}, u32[]{:S(2)}, u32[]{:S(2)}) collective-permute-start(bf16[512,256]{1,0:T(8,128)(2,1)} %get-tuple-element.26), channel_id=1, source_target_pairs={{0,4},{4,0},{8,12},{12,8},{1,5},{5,1},{9,13},{13,9},{2,6},{6,2},{1... | collective-permute-start | bytes 786440 | tf_op jit(solution)/shard_map/ppermute | solution.py:179
  7.3 0.8 collective-permute-start.1
  8.1 4.0 %shard_map.168.local_ref = bf16[3072,256]{1,0:T(8,128)(2,1)S(1)} custom-call(s32[32,128]{1,0:T(8,128)S(1)} %bitcast.26, f32[32,128]{1,0:T(8,128)S(1)} %bitcast.28, bf16[2048,256]{1,0:T(8,128)(2,1)S(1)} %copy-done.4), custom_call_target="tpu_custom_call" | custom-call | flops 3221225472 | bytes 2654208 | tf_op jit(solution)/shard_map/pallas_call | solution.py:25
  12.1 0.0 copy-start.2
  12.1 1.8 %shard_map.169.total_ref = f32[1024,256]{1,0:T(8,128)S(1)} custom-call(s32[32,128]{1,0:T(8,128)S(1)} %bitcast.11, bf16[3072,256]{1,0:T(8,128)(2,1)S(1)} %shard_map.168.local_ref), custom_call_target="tpu_custom_call" | custom-call | flops 1610612736 | bytes 2637824 | tf_op jit(solution)/shard_map/pallas_call | solution.py:25
  13.9 0.0 copy-start.11
  13.9 0.0 copy-start.14
  13.9 0.0 collective-permute-done.1.second_ref
  13.9 0.4 shard_map.171.refs_0_.refs_1_
  14.4 1.6 %collective-permute-start.6 = (bf16[512,256]{1,0:T(8,128)(2,1)S(1)}, bf16[512,256]{1,0:T(8,128)(2,1)S(1)}, u32[]{:S(2)}, u32[]{:S(2)}) collective-permute-start(bf16[512,256]{1,0:T(8,128)(2,1)S(1)} %shard_map.171.refs_0_.refs_1_), channel_id=1, source_target_pairs={{0,2},{2,0},{1,3},{3,1},{4,6},{6,4},{5,7},{7,5},{8,10},{10,8},{9,1... | collective-permute-start | bytes 786440 | tf_op jit(solution)/shard_map/ppermute | solution.py:363
  15.9 0.4 shard_map.170.refs_0_
  16.4 0.6 collective-permute-start.3
  17.0 0.0 collective-permute-start.5
  17.0 6.6 %collective-permute-done.6.refs_2_ = bf16[512,256]{1,0:T(8,128)(2,1)S(1)} collective-permute-done((bf16[512,256]{1,0:T(8,128)(2,1)S(1)}, bf16[512,256]{1,0:T(8,128)(2,1)S(1)}, u32[]{:S(2)}, u32[]{:S(2)}) %collective-permute-start.6) | collective-permute-done | bytes 262176 | tf_op jit(solution)/shard_map/ppermute | solution.py:363
  23.6 0.5 collective-permute-start.2
  24.1 3.7 %collective-permute-done.3.refs_2_ = bf16[512,256]{1,0:T(8,128)(2,1)S(1)} collective-permute-done((bf16[512,256]{1,0:T(8,128)(2,1)S(1)}, bf16[512,256]{1,0:T(8,128)(2,1)S(1)}, u32[]{:S(2)}, u32[]{:S(2)}) %collective-permute-start.3) | collective-permute-done | bytes 262176 | tf_op jit(solution)/shard_map/ppermute | solution.py:363
  27.8 0.0 collective-permute-start.4
  27.8 0.0 collective-permute-done.5.refs_1_
  27.8 0.0 collective-permute-done.7.refs_3_
  27.8 2.4 %shard_map.173 = (bf16[512,1024]{1,0:T(8,128)(2,1)S(1)}, bf16[512,256]{1,0:T(8,128)(2,1)S(1)}, bf16[512,512]{1,0:T(8,128)(2,1)S(1)}) custom-call(bf16[512,256]{1,0:T(8,128)(2,1)S(1)} %shard_map.171.refs_0_.refs_1_, bf16[512,256]{1,0:T(8,128)(2,1)S(1)} %collective-permute-done.5.refs_1_, bf16[512,256]{1,0:T(8,128)(2,1)S(1)} %collective-permute-done.6.refs_2_, ...), custom_call_target="tpu_custom_call" | custom-call | flops 805306368 | bytes 4460544 | tf_op jit(solution)/shard_map/pallas_call | solution.py:25
  30.2 0.0 copy-start
  30.3 0.0 copy-start.9
  30.3 0.8 collective-permute-start.12
  31.1 0.0 collective-permute-done.2.refs_1_
  31.1 0.0 collective-permute-done.4.refs_3_
  31.1 2.4 %shard_map.172 = (bf16[512,1024]{1,0:T(8,128)(2,1)S(1)}, bf16[512,256]{1,0:T(8,128)(2,1)S(1)}, bf16[512,512]{1,0:T(8,128)(2,1)S(1)}) custom-call(bf16[512,256]{1,0:T(8,128)(2,1)S(1)} %shard_map.170.refs_0_, bf16[512,256]{1,0:T(8,128)(2,1)S(1)} %collective-permute-done.2.refs_1_, bf16[512,256]{1,0:T(8,128)(2,1)S(1)} %collective-permute-done.3.refs_2_, ...), custom_call_target="tpu_custom_call" | custom-call | flops 805306368 | bytes 4460544 | tf_op jit(solution)/shard_map/pallas_call | solution.py:25
  33.5 6.9 %collective-permute-start.8 = (bf16[512,512]{1,0:T(8,128)(2,1)S(1)}, bf16[512,512]{1,0:T(8,128)(2,1)S(1)}, u32[]{:S(2)}, u32[]{:S(2)}) collective-permute-start(bf16[512,512]{1,0:T(8,128)(2,1)S(1)} %get-tuple-element.30.here_ref.inner_ref), channel_id=1, source_target_pairs={{0,4},{4,0},{8,12},{12,8},{1,5},{5,1},{9,13},{13,9},{2,6},{6,2},{1... | collective-permute-start | bytes 1572872 | tf_op jit(solution)/shard_map/ppermute | solution.py:179
  40.4 1.7 %shard_map.178.act_ref = bf16[512,1024]{1,0:T(8,128)(2,1)S(1)} custom-call(bf16[512,1024]{1,0:T(8,128)(2,1)S(1)} %get-tuple-element.37.normed_ref, bf16[1024,1024]{1,0:T(8,128)(2,1)S(1)} %copy-done, s32[1,1024]{1,0:T(1,128)S(1)} %bitcast.20), custom_call_target="tpu_custom_call" | custom-call | flops 1073741824 | bytes 4198400 | tf_op jit(solution)/shard_map/pallas_call | solution.py:25
  42.1 0.0 copy-start.1
  42.1 0.0 copy-start.3
  42.1 0.0 copy-start.10
  42.1 1.8 %shard_map.175.act_ref = bf16[512,1024]{1,0:T(8,128)(2,1)S(1)} custom-call(bf16[512,1024]{1,0:T(8,128)(2,1)S(1)} %get-tuple-element.31.normed_ref, bf16[1024,1024]{1,0:T(8,128)(2,1)S(1)} %copy-done, s32[1,1024]{1,0:T(1,128)S(1)} %bitcast.21), custom_call_target="tpu_custom_call" | custom-call | flops 1073741824 | bytes 4198400 | tf_op jit(solution)/shard_map/pallas_call | solution.py:25
  44.0 0.0 collective-permute-done.12.outer_ref
  44.0 2.5 %shard_map.177.att_ref = bf16[256,256]{1,0:T(8,128)(2,1)S(1)} custom-call(bf16[512,256]{1,0:T(8,128)(2,1)S(1)} %get-tuple-element.36.q_ref, bf16[512,512]{1,0:T(8,128)(2,1)S(1)} %get-tuple-element.30.here_ref.inner_ref, bf16[512,512]{1,0:T(8,128)(2,1)S(1)} %get-tuple-element.29.inner_ref.here_ref, bf16[512,512]{1,0:T(8,128)(2,1)S(1)} %collective-permute-done.12.outer_ref), custom_call_target="tpu_custom_call" | custom-call | flops 402653184 | bytes 1966080 | tf_op jit(solution)/shard_map/pallas_call | solution.py:25
  46.5 0.9 shard_map.179
  47.4 0.1 collective-permute-start.14
  47.5 5.2 %collective-permute-done.8.outer_ref = bf16[512,512]{1,0:T(8,128)(2,1)S(1)} collective-permute-done((bf16[512,512]{1,0:T(8,128)(2,1)S(1)}, bf16[512,512]{1,0:T(8,128)(2,1)S(1)}, u32[]{:S(2)}, u32[]{:S(2)}) %collective-permute-start.8) | collective-permute-done | bytes 524320 | tf_op jit(solution)/shard_map/ppermute | solution.py:179
  52.7 4.7 %shard_map.174.att_ref = bf16[512,256]{1,0:T(8,128)(2,1)S(1)} custom-call(bf16[512,256]{1,0:T(8,128)(2,1)S(1)} %get-tuple-element.28.q_ref, bf16[512,512]{1,0:T(8,128)(2,1)S(1)} %get-tuple-element.29.inner_ref.here_ref, bf16[512,512]{1,0:T(8,128)(2,1)S(1)} %get-tuple-element.30.here_ref.inner_ref, bf16[512,512]{1,0:T(8,128)(2,1)S(1)} %collective-permute-done.8.outer_ref), custom_call_target="tpu_custom_call" | custom-call | flops 805306368 | bytes 2097152 | tf_op jit(solution)/shard_map/pallas_call | solution.py:25
  57.4 1.6 %shard_map.176 = (bf16[512,256]{1,0:T(8,128)(2,1)S(1)}, bf16[512,256]{1,0:T(8,128)(2,1)S(1)}, bf16[512,256]{1,0:T(8,128)(2,1)S(1)}, bf16[512,256]{1,0:T(8,128)(2,1)S(1)}) custom-call(bf16[512,256]{1,0:T(8,128)(2,1)S(1)} %shard_map.174.att_ref, bf16[512,1024]{1,0:T(8,128)(2,1)S(1)} %shard_map.175.act_ref, bf16[256,1024]{1,0:T(8,128)(2,1)S(1)} %copy-done.3, ...), custom_call_target="tpu_custom_call" | custom-call | flops 1342177280 | bytes 4984832 | tf_op jit(solution)/shard_map/pallas_call | solution.py:25
  59.1 0.1 collective-permute-start.10
  59.1 2.5 %shard_map.180.att_ref = bf16[256,256]{1,0:T(8,128)(2,1)S(1)} custom-call(bf16[512,256]{1,0:T(8,128)(2,1)S(1)} %get-tuple-element.36.q_ref, bf16[512,512]{1,0:T(8,128)(2,1)S(1)} %get-tuple-element.30.here_ref.inner_ref, bf16[512,512]{1,0:T(8,128)(2,1)S(1)} %get-tuple-element.29.inner_ref.here_ref, bf16[512,512]{1,0:T(8,128)(2,1)S(1)} %collective-permute-done.12.outer_ref), custom_call_target="tpu_custom_call" | custom-call | flops 402653184 | bytes 1966080 | tf_op jit(solution)/shard_map/pallas_call | solution.py:25
  61.7 0.0 copy-start.6
  61.7 0.0 copy-start.7
  61.7 1.1 %shard_map.181 = (bf16[256,256]{1,0:T(8,128)(2,1)S(1)}, bf16[256,256]{1,0:T(8,128)(2,1)S(1)}, bf16[256,256]{1,0:T(8,128)(2,1)S(1)}, bf16[256,256]{1,0:T(8,128)(2,1)S(1)}) custom-call(bf16[256,256]{1,0:T(8,128)(2,1)S(1)} %shard_map.180.att_ref, bf16[512,1024]{1,0:T(8,128)(2,1)S(1)} %shard_map.178.act_ref, bf16[256,1024]{1,0:T(8,128)(2,1)S(1)} %copy-done.3, ...), custom_call_target="tpu_custom_call" | custom-call | flops 671088640 | bytes 4329472 | tf_op jit(solution)/shard_map/pallas_call | solution.py:25
  62.8 0.5 collective-permute-start.13
  63.4 0.1 collective-permute-start.16
  63.4 0.4 collective-permute-start.17
  63.9 0.0 collective-permute-done.14
  63.9 0.1 collective-permute-start.9
  64.0 0.0 collective-permute-done.10
  64.0 1.6 %collective-permute-start.15 = (bf16[256,256]{1,0:T(8,128)(2,1)S(1)}, bf16[256,256]{1,0:T(8,128)(2,1)S(1)}, u32[]{:S(2)}, u32[]{:S(2)}) collective-permute-start(bf16[256,256]{1,0:T(8,128)(2,1)S(1)} %add_convert_fusion.2), channel_id=1, source_target_pairs={{0,2},{2,0},{1,3},{3,1},{4,6},{6,4},{5,7},{7,5},{8,10},{10,8},{9,1... | collective-permute-start | bytes 393224 | tf_op jit(solution)/shard_map/ppermute | solution.py:376
  65.6 0.1 add_convert_fusion
  65.6 0.8 collective-permute-start.11
  66.4 1.4 %collective-permute-start.18 = (bf16[256,256]{1,0:T(8,128)(2,1)S(1)}, bf16[256,256]{1,0:T(8,128)(2,1)S(1)}, u32[]{:S(2)}, u32[]{:S(2)}) collective-permute-start(bf16[256,256]{1,0:T(8,128)(2,1)S(1)} %add_convert_fusion.1), channel_id=1, source_target_pairs={{0,2},{2,0},{1,3},{3,1},{4,6},{6,4},{5,7},{7,5},{8,10},{10,8},{9,1... | collective-permute-start | bytes 393224 | tf_op jit(solution)/shard_map/ppermute | solution.py:376
  68.5 1.9 %collective-permute-done.15.refs_7_ = bf16[256,256]{1,0:T(8,128)(2,1)S(1)} collective-permute-done((bf16[256,256]{1,0:T(8,128)(2,1)S(1)}, bf16[256,256]{1,0:T(8,128)(2,1)S(1)}, u32[]{:S(2)}, u32[]{:S(2)}) %collective-permute-start.15) | collective-permute-done | bytes 131104 | tf_op jit(solution)/shard_map/ppermute | solution.py:376
  70.4 7.9 %collective-permute-done.18.refs_10_ = bf16[256,256]{1,0:T(8,128)(2,1)S(1)} collective-permute-done((bf16[256,256]{1,0:T(8,128)(2,1)S(1)}, bf16[256,256]{1,0:T(8,128)(2,1)S(1)}, u32[]{:S(2)}, u32[]{:S(2)}) %collective-permute-start.18) | collective-permute-done | bytes 131104 | tf_op jit(solution)/shard_map/ppermute | solution.py:376
  78.3 1.4 %shard_map.182 = (bf16[1024,256]{1,0:T(8,128)(2,1)}, bf16[1024,256]{1,0:T(8,128)(2,1)S(1)}, bf16[512,256]{1,0:T(8,128)(2,1)S(1)}, bf16[512,256]{1,0:T(8,128)(2,1)S(1)}) custom-call(s32[48,128]{1,0:T(8,128)S(1)} %bitcast.14, f32[48,128]{1,0:T(8,128)S(1)} %bitcast.16, bf16[512,256]{1,0:T(8,128)(2,1)S(1)} %shard_map.170.refs_0_, ...), custom_call_target="tpu_custom_call" | custom-call | flops 536870912 | bytes 3719168 | tf_op jit(solution)/shard_map/pallas_call | solution.py:25
  79.8 1.7 %collective-permute-start.19 = (bf16[512,256]{1,0:T(8,128)(2,1)S(1)}, bf16[512,256]{1,0:T(8,128)(2,1)S(1)}, u32[]{:S(2)}, u32[]{:S(2)}) collective-permute-start(bf16[512,256]{1,0:T(8,128)(2,1)S(1)} %get-tuple-element.47), channel_id=1, source_target_pairs={{0,4},{4,0},{8,12},{12,8},{1,5},{5,1},{9,13},{13,9},{2,6},{6,2},{1... | collective-permute-start | bytes 786440 | tf_op jit(solution)/shard_map/ppermute | solution.py:179
  81.5 0.7 collective-permute-start.20
  82.2 0.0 copy-start.8
  82.2 3.9 %shard_map.183.local_ref = bf16[5120,256]{1,0:T(8,128)(2,1)S(1)} custom-call(s32[48,128]{1,0:T(8,128)S(1)} %bitcast.15, f32[48,128]{1,0:T(8,128)S(1)} %bitcast.17, bf16[1024,256]{1,0:T(8,128)(2,1)S(1)} %get-tuple-element.49.source_ref), custom_call_target="tpu_custom_call" | custom-call | flops 2684354560 | bytes 3194880 | tf_op jit(solution)/shard_map/pallas_call | solution.py:25
  86.1 5.8 %shard_map.184.total_ref = f32[2048,256]{1,0:T(8,128)S(1)} custom-call(s32[48,128]{1,0:T(8,128)S(1)} %bitcast.18, bf16[5120,256]{1,0:T(8,128)(2,1)S(1)} %shard_map.183.local_ref), custom_call_target="tpu_custom_call" | custom-call | flops 5368709120 | bytes 4743168 | tf_op jit(solution)/shard_map/pallas_call | solution.py:25
  91.9 2.9 %grid.1 = bf16[2048,256]{1,0:T(8,128)(2,1)} custom-call(s32[1,1]{1,0:T(1,128)} %bitcast.10.count_ref, s32[48,128]{1,0:T(8,128)S(1)} %bitcast.19, bf16[512,256]{1,0:T(8,128)(2,1)S(1)} %collective-permute-done.19.first_ref, bf16[512,256]{1,0:T(8,128)(2,1)S(1)} %collective-permute-done.20.second_ref, f32[2048,256]{1,0:T(8,128)S(1)} %shard_map.184.total_ref, ...), custom_call_target="tpu_custom_call" | custom-call | flops 1073741824 | bytes 4194304 | tf_op jit(solution)/shard_map/grid/pallas_call | solution.py:205
  (30 shorter events, 0.1 us)
Async XLA Ops:
  0.6 7.4 %copy-start.4 = (bf16[2048,256]{1,0:T(8,128)(2,1)S(1)}, bf16[2048,256]{1,0:T(8,128)(2,1)}, u32[]{:S(2)}) copy-start(bf16[2048,256]{1,0:T(8,128)(2,1)} %grid_ref.1) | copy-start | bytes 3145732
  0.6 7.4 %copy-start.13 = (f32[1,32,128]{2,1,0:T(8,128)S(1)}, f32[1,32,128]{2,1,0:T(8,128)}, u32[]{:S(2)}) copy-start(f32[1,32,128]{2,1,0:T(8,128)} %param.21) | copy-start | bytes 49156
  0.6 7.4 %copy-start.12 = (s32[1,32,128]{2,1,0:T(8,128)S(1)}, s32[1,32,128]{2,1,0:T(8,128)}, u32[]{:S(2)}) copy-start(s32[1,32,128]{2,1,0:T(8,128)} %param.19) | copy-start | bytes 49156
  4.1 9.8 %collective-permute-start = (bf16[512,256]{1,0:T(8,128)(2,1)}, bf16[512,256]{1,0:T(8,128)(2,1)S(1)}, u32[]{:S(2)}, u32[]{:S(2)}) collective-permute-start(bf16[512,256]{1,0:T(8,128)(2,1)} %get-tuple-element.26), channel_id=1, source_target_pairs={{0,4},{4,0},{8,12},{12,8},{1,5},{5,1},{9,13},{13,9},{2,6},{6,2},{1... | collective-permute-start | bytes 786440 | tf_op jit(solution)/shard_map/ppermute | solution.py:179
  7.3 4.8 %copy-start.5 = (s32[1,32,128]{2,1,0:T(8,128)S(1)}, s32[1,32,128]{2,1,0:T(8,128)}, u32[]{:S(2)}) copy-start(s32[1,32,128]{2,1,0:T(8,128)} %param.20) | copy-start | bytes 49156
  7.3 6.6 %collective-permute-start.1 = (bf16[512,256]{1,0:T(8,128)(2,1)}, bf16[512,256]{1,0:T(8,128)(2,1)S(1)}, u32[]{:S(2)}, u32[]{:S(2)}) collective-permute-start(bf16[512,256]{1,0:T(8,128)(2,1)} %get-tuple-element.27), channel_id=1, source_target_pairs={{4,8},{8,4},{5,9},{9,5},{6,10},{10,6},{7,11},{11,7},{20,24},{24,20... | collective-permute-start | bytes 786440 | tf_op jit(solution)/shard_map/ppermute | solution.py:179
  12.1 1.8 %copy-start.2 = (bf16[1024,256]{1,0:T(8,128)(2,1)S(1)}, bf16[1024,256]{1,0:T(8,128)(2,1)}, u32[]{:S(2)}) copy-start(bf16[1024,256]{1,0:T(8,128)(2,1)} %embed_ref.3) | copy-start | bytes 1572868
  13.9 14.0 %copy-start.11 = (bf16[1024,768]{1,0:T(8,128)(2,1)S(1)}, bf16[1024,768]{1,0:T(8,128)(2,1)}, u32[]{:S(2)}) copy-start(bf16[1024,768]{1,0:T(8,128)(2,1)} %refs_5_.3) | copy-start | bytes 4718596
  13.9 14.0 %copy-start.14 = (f32[1024]{0:T(1024)S(1)}, f32[1024]{0:T(1024)}, u32[]{:S(2)}) copy-start(f32[1024]{0:T(1024)} %param.25) | copy-start | bytes 12292
  14.4 9.2 %collective-permute-start.6 = (bf16[512,256]{1,0:T(8,128)(2,1)S(1)}, bf16[512,256]{1,0:T(8,128)(2,1)S(1)}, u32[]{:S(2)}, u32[]{:S(2)}) collective-permute-start(bf16[512,256]{1,0:T(8,128)(2,1)S(1)} %shard_map.171.refs_0_.refs_1_), channel_id=1, source_target_pairs={{0,2},{2,0},{1,3},{3,1},{4,6},{6,4},{5,7},{7,5},{8,10},{10,8},{9,1... | collective-permute-start | bytes 786440 | tf_op jit(solution)/shard_map/ppermute | solution.py:363
  16.4 11.4 %collective-permute-start.3 = (bf16[512,256]{1,0:T(8,128)(2,1)S(1)}, bf16[512,256]{1,0:T(8,128)(2,1)S(1)}, u32[]{:S(2)}, u32[]{:S(2)}) collective-permute-start(bf16[512,256]{1,0:T(8,128)(2,1)S(1)} %shard_map.170.refs_0_), channel_id=1, source_target_pairs={{0,2},{2,0},{1,3},{3,1},{4,6},{6,4},{5,7},{7,5},{8,10},{10,8},{9,1... | collective-permute-start | bytes 786440 | tf_op jit(solution)/shard_map/ppermute | solution.py:363
  17.0 10.9 %collective-permute-start.5 = (bf16[512,256]{1,0:T(8,128)(2,1)S(1)}, bf16[512,256]{1,0:T(8,128)(2,1)S(1)}, u32[]{:S(2)}, u32[]{:S(2)}) collective-permute-start(bf16[512,256]{1,0:T(8,128)(2,1)S(1)} %shard_map.171.refs_0_.refs_1_), channel_id=1, source_target_pairs={{0,1},{1,0},{2,3},{3,2},{4,5},{5,4},{6,7},{7,6},{8,9},{9,8},{10,11... | collective-permute-start | bytes 786440 | tf_op jit(solution)/shard_map/ppermute | solution.py:364
  23.6 4.2 %collective-permute-start.7 = (bf16[512,256]{1,0:T(8,128)(2,1)S(1)}, bf16[512,256]{1,0:T(8,128)(2,1)S(1)}, u32[]{:S(2)}, u32[]{:S(2)}) collective-permute-start(bf16[512,256]{1,0:T(8,128)(2,1)S(1)} %collective-permute-done.6.refs_2_), channel_id=1, source_target_pairs={{0,1},{1,0},{2,3},{3,2},{4,5},{5,4},{6,7},{7,6},{8,9},{9,8},{10,11... | collective-permute-start | bytes 786440 | tf_op jit(solution)/shard_map/ppermute | solution.py:365
  23.6 7.5 %collective-permute-start.2 = (bf16[512,256]{1,0:T(8,128)(2,1)S(1)}, bf16[512,256]{1,0:T(8,128)(2,1)S(1)}, u32[]{:S(2)}, u32[]{:S(2)}) collective-permute-start(bf16[512,256]{1,0:T(8,128)(2,1)S(1)} %shard_map.170.refs_0_), channel_id=1, source_target_pairs={{0,1},{1,0},{2,3},{3,2},{4,5},{5,4},{6,7},{7,6},{8,9},{9,8},{10,11... | collective-permute-start | bytes 786440 | tf_op jit(solution)/shard_map/ppermute | solution.py:364
  27.8 3.3 %collective-permute-start.4 = (bf16[512,256]{1,0:T(8,128)(2,1)S(1)}, bf16[512,256]{1,0:T(8,128)(2,1)S(1)}, u32[]{:S(2)}, u32[]{:S(2)}) collective-permute-start(bf16[512,256]{1,0:T(8,128)(2,1)S(1)} %collective-permute-done.3.refs_2_), channel_id=1, source_target_pairs={{0,1},{1,0},{2,3},{3,2},{4,5},{5,4},{6,7},{7,6},{8,9},{9,8},{10,11... | collective-permute-start | bytes 786440 | tf_op jit(solution)/shard_map/ppermute | solution.py:365
  30.2 10.2 %copy-start = (bf16[1024,1024]{1,0:T(8,128)(2,1)S(1)}, bf16[1024,1024]{1,0:T(8,128)(2,1)}, u32[]{:S(2)}) copy-start(bf16[1024,1024]{1,0:T(8,128)(2,1)} %w_ref.3) | copy-start | bytes 6291460
  30.3 10.2 %copy-start.9 = (s32[1024]{0:T(1024)S(1)}, s32[1024]{0:T(1024)}, u32[]{:S(2)}) copy-start(s32[1024]{0:T(1024)} %param.29) | copy-start | bytes 12292
  30.3 13.7 %collective-permute-start.12 = (bf16[512,512]{1,0:T(8,128)(2,1)S(1)}, bf16[512,512]{1,0:T(8,128)(2,1)S(1)}, u32[]{:S(2)}, u32[]{:S(2)}) collective-permute-start(bf16[512,512]{1,0:T(8,128)(2,1)S(1)} %get-tuple-element.29.inner_ref.here_ref), channel_id=1, source_target_pairs={{4,8},{8,4},{5,9},{9,5},{6,10},{10,6},{7,11},{11,7},{20,24},{24,20... | collective-permute-start | bytes 1572872 | tf_op jit(solution)/shard_map/ppermute | solution.py:179
  33.5 19.2 %collective-permute-start.8 = (bf16[512,512]{1,0:T(8,128)(2,1)S(1)}, bf16[512,512]{1,0:T(8,128)(2,1)S(1)}, u32[]{:S(2)}, u32[]{:S(2)}) collective-permute-start(bf16[512,512]{1,0:T(8,128)(2,1)S(1)} %get-tuple-element.30.here_ref.inner_ref), channel_id=1, source_target_pairs={{0,4},{4,0},{8,12},{12,8},{1,5},{5,1},{9,13},{13,9},{2,6},{6,2},{1... | collective-permute-start | bytes 1572872 | tf_op jit(solution)/shard_map/ppermute | solution.py:179
  42.1 4.4 %copy-start.1 = (bf16[1024,1024]{1,0:T(8,128)(2,1)S(1)}, bf16[1024,1024]{1,0:T(8,128)(2,1)}, u32[]{:S(2)}) copy-start(bf16[1024,1024]{1,0:T(8,128)(2,1)} %w_down_ref.5) | copy-start | bytes 6291460
  42.1 4.4 %copy-start.3 = (bf16[256,1024]{1,0:T(8,128)(2,1)S(1)}, bf16[256,1024]{1,0:T(8,128)(2,1)}, u32[]{:S(2)}) copy-start(bf16[256,1024]{1,0:T(8,128)(2,1)} %w_out_ref.5) | copy-start | bytes 1572868
  42.1 4.4 %copy-start.10 = (s32[1024]{0:T(1024)S(1)}, s32[1024]{0:T(1024)}, u32[]{:S(2)}) copy-start(s32[1024]{0:T(1024)} %param.31) | copy-start | bytes 12292
  47.4 16.4 %collective-permute-start.14 = (bf16[256,256]{1,0:T(8,128)(2,1)S(1)}, bf16[256,256]{1,0:T(8,128)(2,1)S(1)}, u32[]{:S(2)}, u32[]{:S(2)}) collective-permute-start(bf16[256,256]{1,0:T(8,128)(2,1)S(1)} %get-tuple-element.41), channel_id=1, source_target_pairs={{0,1},{1,0},{2,3},{3,2},{4,5},{5,4},{6,7},{7,6},{8,9},{9,8},{10,11... | collective-permute-start | bytes 393224 | tf_op jit(solution)/shard_map/ppermute | solution.py:373
  59.1 4.9 %collective-permute-start.10 = (bf16[512,256]{1,0:T(8,128)(2,1)S(1)}, bf16[512,256]{1,0:T(8,128)(2,1)S(1)}, u32[]{:S(2)}, u32[]{:S(2)}) collective-permute-start(bf16[512,256]{1,0:T(8,128)(2,1)S(1)} %get-tuple-element.35), channel_id=1, source_target_pairs={{0,1},{1,0},{2,3},{3,2},{4,5},{5,4},{6,7},{7,6},{8,9},{9,8},{10,11... | collective-permute-start | bytes 786440 | tf_op jit(solution)/shard_map/ppermute | solution.py:373
  61.7 16.7 %copy-start.6 = (s32[1,48,128]{2,1,0:T(8,128)S(1)}, s32[1,48,128]{2,1,0:T(8,128)}, u32[]{:S(2)}) copy-start(s32[1,48,128]{2,1,0:T(8,128)} %param.22) | copy-start | bytes 73732
  61.7 16.7 %copy-start.7 = (f32[1,48,128]{2,1,0:T(8,128)S(1)}, f32[1,48,128]{2,1,0:T(8,128)}, u32[]{:S(2)}) copy-start(f32[1,48,128]{2,1,0:T(8,128)} %param.24) | copy-start | bytes 73732
  62.8 3.6 %collective-permute-start.13 = (bf16[256,256]{1,0:T(8,128)(2,1)S(1)}, bf16[256,256]{1,0:T(8,128)(2,1)S(1)}, u32[]{:S(2)}, u32[]{:S(2)}) collective-permute-start(bf16[256,256]{1,0:T(8,128)(2,1)S(1)} %get-tuple-element.39), channel_id=1, source_target_pairs={{0,1},{1,0},{2,3},{3,2},{4,5},{5,4},{6,7},{7,6},{8,9},{9,8},{10,11... | collective-permute-start | bytes 393224 | tf_op jit(solution)/shard_map/ppermute | solution.py:374
  63.4 5.1 %collective-permute-start.16 = (bf16[256,256]{1,0:T(8,128)(2,1)S(1)}, bf16[256,256]{1,0:T(8,128)(2,1)S(1)}, u32[]{:S(2)}, u32[]{:S(2)}) collective-permute-start(bf16[256,256]{1,0:T(8,128)(2,1)S(1)} %get-tuple-element.43), channel_id=1, source_target_pairs={{0,1},{1,0},{2,3},{3,2},{4,5},{5,4},{6,7},{7,6},{8,9},{9,8},{10,11... | collective-permute-start | bytes 393224 | tf_op jit(solution)/shard_map/ppermute | solution.py:374
  63.4 2.2 %collective-permute-start.17 = (bf16[256,256]{1,0:T(8,128)(2,1)S(1)}, bf16[256,256]{1,0:T(8,128)(2,1)S(1)}, u32[]{:S(2)}, u32[]{:S(2)}) collective-permute-start(bf16[256,256]{1,0:T(8,128)(2,1)S(1)} %get-tuple-element.45), channel_id=1, source_target_pairs={{0,1},{1,0},{2,3},{3,2},{4,5},{5,4},{6,7},{7,6},{8,9},{9,8},{10,11... | collective-permute-start | bytes 393224 | tf_op jit(solution)/shard_map/ppermute | solution.py:373
  63.9 14.5 %collective-permute-start.9 = (bf16[512,256]{1,0:T(8,128)(2,1)S(1)}, bf16[512,256]{1,0:T(8,128)(2,1)S(1)}, u32[]{:S(2)}, u32[]{:S(2)}) collective-permute-start(bf16[512,256]{1,0:T(8,128)(2,1)S(1)} %get-tuple-element.33), channel_id=1, source_target_pairs={{0,1},{1,0},{2,3},{3,2},{4,5},{5,4},{6,7},{7,6},{8,9},{9,8},{10,11... | collective-permute-start | bytes 786440 | tf_op jit(solution)/shard_map/ppermute | solution.py:374
  64.0 6.4 %collective-permute-start.15 = (bf16[256,256]{1,0:T(8,128)(2,1)S(1)}, bf16[256,256]{1,0:T(8,128)(2,1)S(1)}, u32[]{:S(2)}, u32[]{:S(2)}) collective-permute-start(bf16[256,256]{1,0:T(8,128)(2,1)S(1)} %add_convert_fusion.2), channel_id=1, source_target_pairs={{0,2},{2,0},{1,3},{3,1},{4,6},{6,4},{5,7},{7,5},{8,10},{10,8},{9,1... | collective-permute-start | bytes 393224 | tf_op jit(solution)/shard_map/ppermute | solution.py:376
  65.6 12.7 %collective-permute-start.11 = (bf16[512,256]{1,0:T(8,128)(2,1)S(1)}, bf16[512,256]{1,0:T(8,128)(2,1)S(1)}, u32[]{:S(2)}, u32[]{:S(2)}) collective-permute-start(bf16[512,256]{1,0:T(8,128)(2,1)S(1)} %add_convert_fusion), channel_id=1, source_target_pairs={{0,2},{2,0},{1,3},{3,1},{4,6},{6,4},{5,7},{7,5},{8,10},{10,8},{9,1... | collective-permute-start | bytes 786440 | tf_op jit(solution)/shard_map/ppermute | solution.py:376
  66.4 11.9 %collective-permute-start.18 = (bf16[256,256]{1,0:T(8,128)(2,1)S(1)}, bf16[256,256]{1,0:T(8,128)(2,1)S(1)}, u32[]{:S(2)}, u32[]{:S(2)}) collective-permute-start(bf16[256,256]{1,0:T(8,128)(2,1)S(1)} %add_convert_fusion.1), channel_id=1, source_target_pairs={{0,2},{2,0},{1,3},{3,1},{4,6},{6,4},{5,7},{7,5},{8,10},{10,8},{9,1... | collective-permute-start | bytes 393224 | tf_op jit(solution)/shard_map/ppermute | solution.py:376
  79.8 12.2 %collective-permute-start.19 = (bf16[512,256]{1,0:T(8,128)(2,1)S(1)}, bf16[512,256]{1,0:T(8,128)(2,1)S(1)}, u32[]{:S(2)}, u32[]{:S(2)}) collective-permute-start(bf16[512,256]{1,0:T(8,128)(2,1)S(1)} %get-tuple-element.47), channel_id=1, source_target_pairs={{0,4},{4,0},{8,12},{12,8},{1,5},{5,1},{9,13},{13,9},{2,6},{6,2},{1... | collective-permute-start | bytes 786440 | tf_op jit(solution)/shard_map/ppermute | solution.py:179
  81.5 10.4 %collective-permute-start.20 = (bf16[512,256]{1,0:T(8,128)(2,1)S(1)}, bf16[512,256]{1,0:T(8,128)(2,1)S(1)}, u32[]{:S(2)}, u32[]{:S(2)}) collective-permute-start(bf16[512,256]{1,0:T(8,128)(2,1)S(1)} %get-tuple-element.48), channel_id=1, source_target_pairs={{4,8},{8,4},{5,9},{9,5},{6,10},{10,6},{7,11},{11,7},{20,24},{24,20... | collective-permute-start | bytes 786440 | tf_op jit(solution)/shard_map/ppermute | solution.py:179
  82.2 3.9 %copy-start.8 = (s32[1,48,128]{2,1,0:T(8,128)S(1)}, s32[1,48,128]{2,1,0:T(8,128)}, u32[]{:S(2)}) copy-start(s32[1,48,128]{2,1,0:T(8,128)} %param.23) | copy-start | bytes 73732

commit v4 on v3

v4 whole, which is shorter than its diff:
```python
import functools

import jax
import jax.numpy as jnp
from jax import lax
from jax.experimental import pallas as pl
from jax.experimental.pallas import tpu as pltpu
from jax.sharding import PartitionSpec as P

HD = 64
WIN = 512
TILE = 128
ESIDE = 4
DSIDE = 4
STEP = 4
BLOCK = 256
NEG = -1e30
BF = jnp.bfloat16
F32 = jnp.float32


def call(body, outs, args, flops, scratch=(), spare=8, space=pltpu.VMEM, limit=None):
    moved = sum(a.size * a.dtype.itemsize for a in args)
    moved += sum(o.size * o.dtype.itemsize for o in outs)
    return pl.pallas_call(
        body,
        out_shape=tuple(outs),
        in_specs=[pl.BlockSpec(memory_space=space)] * len(args),
        out_specs=tuple(pl.BlockSpec(memory_space=pltpu.VMEM) for _ in outs),
        scratch_shapes=list(scratch),
        cost_estimate=pl.CostEstimate(flops=flops, bytes_accessed=moved, transcendentals=0),
        compiler_params=pltpu.CompilerParams(vmem_limit_bytes=limit or moved + spare * 1024 * 1024),
    )(*args)


def column(row):
    return jnp.transpose(jnp.broadcast_to(row, (TILE, TILE)))


def picks(rows_ref, first, base, source_rows):
    tiles = [column(rows_ref[pl.ds(first + i, 1), :] - base) for i in range(STEP)]
    cols = jnp.concatenate(tiles, axis=0)
    cols = cols.astype(jnp.int16)
    lane = lax.broadcasted_iota(jnp.int32, cols.shape, 1).astype(jnp.int16)
    tiles = []
    for j in range(source_rows // TILE):
        hit = cols == lane + jnp.int16(j * TILE)
        tiles.append(jnp.where(hit, jnp.ones_like(cols, BF), jnp.zeros_like(cols, BF)))
    return jnp.concatenate(tiles, axis=1)


def picked(src_ref, first, sources, bases):
    total = None
    for source_ref, base in zip(sources, bases):
        part = jnp.dot(
            picks(src_ref, first, base, source_ref.shape[0]),
            source_ref[...],
            preferred_element_type=F32,
        )
        total = part if total is None else total + part
    return total


def scaled(rows, weight_ref, first):
    scale = jnp.concatenate([column(weight_ref[pl.ds(first + i, 1), :]) for i in range(STEP)], axis=0)
    return (rows * jnp.concatenate([scale] * (rows.shape[1] // TILE), axis=1)).astype(BF)


def parity():
    return lax.rem(lax.axis_index("seq"), 2)


def outward(which, side):
    return jnp.where(parity() == which, side, 0)


def block_of(step, count):
    return step if count == 1 else jnp.where(parity() == 0, count - 1 - step, step)


def partners(count, groups):
    both = []
    for which in range(2):
        pairs = []
        for e in range(groups):
            for i in range(count):
                j = ((i - which) ^ 1) + which
                if 0 <= j < count:
                    pairs.append((e * count + i, e * count + j))
                elif e ^ 1 < groups:
                    pairs.append((e * count + i, (e ^ 1) * count + i))
        both.append(pairs)
    return both


def has_partner(which):
    seq = lax.axis_index("seq")
    return jnp.where(parity() == which, seq < lax.axis_size("seq") - 1, seq > 0)


def sides(side, src_ref, weight_ref, sources, bases, outs, before=None):
    edges = STEP * TILE
    for which, out in enumerate(outs):
        for k in range(out.shape[0] // edges):
            at = slice(k * edges, (k + 1) * edges)
            first = outward(which, side) + k * STEP
            rows = picked(src_ref, first, sources, bases)
            if before is not None:
                rows = rows + before[which][at, :].astype(F32)
            out[at, :] = rows.astype(BF) if weight_ref is None else scaled(rows, weight_ref, first)


def fetch_side_body(side, *refs):
    sources, outs, held, sems = refs[:3], refs[3:5], refs[5:8], refs[8]
    copies = [pltpu.make_async_copy(a, b, sems.at[i]) for i, (a, b) in enumerate(zip(sources, held))]
    for copy in copies:
        copy.start()
    for copy in copies:
        copy.wait()
    sides(side, held[0], held[1], held[2:], (0,), outs)


def locals_(start, src_ref, weight_ref, sources, bases, out_ref, before_ref=None):
    edges = STEP * TILE
    pair = 2

    def step(k, carry):
        for i in range(pair):
            n = k * pair + i
            at = pl.ds(pl.multiple_of(n * edges, edges), edges)
            first = start + n * STEP
            rows = picked(src_ref, first, sources, bases)
            if before_ref is not None:
                rows = rows + before_ref[at, :].astype(F32)
            out_ref[at, :] = rows.astype(BF) if weight_ref is None else scaled(rows, weight_ref, first)
        return carry

    lax.fori_loop(0, out_ref.shape[0] // (pair * edges), step, 0)


def gather_body(start, src_ref, weight_ref, source_ref, out_ref):
    locals_(start, src_ref, weight_ref, (source_ref,), (0,), out_ref)


def lands(rows_ref, tiles, base, target_rows, there=None):
    spot = lax.broadcasted_iota(jnp.int32, (target_rows, TILE), 0).astype(jnp.int16)
    out = []
    for tile in tiles:
        row = rows_ref[pl.ds(tile, 1), :] - base
        row = row if there is None else jnp.where(there, row, -1)
        row = jnp.broadcast_to(row, (target_rows, TILE)).astype(jnp.int16)
        out.append(jnp.where(row == spot, jnp.ones_like(spot, BF), jnp.zeros_like(spot, BF)))
    return jnp.concatenate(out, axis=1)


def landed(side, dst_ref, first_ref, second_ref, base, target_rows):
    total = None
    for which, got_ref in enumerate((first_ref, second_ref)):
        first = outward(which, side)
        got = jnp.dot(
            lands(dst_ref, [first + i for i in range(side)], base, target_rows, has_partner(which)),
            got_ref[...],
            preferred_element_type=F32,
        )
        total = got if total is None else total + got
    return total


def spread_body(side, dst_ref, local_ref, out_ref):
    block = 512

    def step(k, carry):
        for i in range(2):
            at = pl.multiple_of((2 * k + i) * block, block)
            tiles = [2 * side + t for t in range(local_ref.shape[0] // TILE)]
            out_ref[pl.ds(at, block), :] = jnp.dot(
                lands(dst_ref, tiles, at, block), local_ref[...], preferred_element_type=F32
            )
        return carry

    lax.fori_loop(0, out_ref.shape[0] // (2 * block), step, 0)


def start_of(c, b, count):
    return block_of(c, count) * WIN + spot(c, b)


def latent_body(side, c, b, count, dst_ref, first_ref, second_ref, total_ref, embed_ref, out_ref):
    at = pl.multiple_of(start_of(c, b, count), BLOCK)
    got = landed(side, dst_ref, first_ref, second_ref, at, BLOCK)
    got = got + total_ref[pl.ds(at, BLOCK), :]
    out_ref[...] = (embed_ref[pl.ds(at, BLOCK), :].astype(F32) + got).astype(BF)


def grid_body(side, count, count_ref, dst_ref, first_ref, second_ref, total_ref, grid_ref, *refs):
    *hiddens, hidden_ref, out_ref = refs
    rows = out_ref.shape[0]
    step = pl.program_id(0)
    for h in range(rows // BLOCK):
        at = pl.multiple_of(step * rows + h * BLOCK, BLOCK)
        here = slice(h * BLOCK, (h + 1) * BLOCK)
        from_ = pl.ds(at, BLOCK)
        got = landed(side, dst_ref, first_ref, second_ref, at, BLOCK) + total_ref[from_, :]
        row = at + lax.broadcasted_iota(jnp.int32, got.shape, 0)
        value = grid_ref[from_, :].astype(F32) + got
        out_ref[here, :] = jnp.where(row < count_ref[0, 0], value, 0.0).astype(BF)
    for unit, unit_ref in zip(UNITS, hiddens):
        for k, start in enumerate(unit_starts(unit, count)):

            @pl.when(start == step * BLOCK)
            def _():
                hidden_ref[...] = unit_ref[k * BLOCK : (k + 1) * BLOCK, :]


def swapped(first, second):
    one, two = partners(lax.axis_size("seq"), lax.axis_size("ens"))
    axes = ("ens", "seq")
    return lax.ppermute(first, axes, one), lax.ppermute(second, axes, two)


def gathered(edge_src, edge_weight, source, side):
    edges = edge_src.shape[0] * TILE - 2 * side * TILE
    (local,) = call(
        functools.partial(gather_body, 2 * side),
        (jax.ShapeDtypeStruct((edges, source.shape[1]), BF),),
        (edge_src, edge_weight, source),
        2 * edges * source.size,
    )
    return local


def spread(edge_dst, local, target_rows, side):
    (total,) = call(
        functools.partial(spread_body, side),
        (jax.ShapeDtypeStruct((target_rows, local.shape[1]), F32),),
        (edge_dst, local),
        2 * local.size * target_rows,
    )
    return total


def settled(side, count, grid_count, edge_dst, first, second, total, grid_latent, hiddens):
    rows, features = grid_latent.shape
    steps = sum(h.shape[0] for h in hiddens) // BLOCK
    block = rows // steps
    args = (grid_count, edge_dst, first, second, total, grid_latent, *hiddens)
    return pl.pallas_call(
        functools.partial(grid_body, side, count),
        grid=(steps,),
        out_shape=(
            jax.ShapeDtypeStruct((steps * BLOCK, features), BF),
            jax.ShapeDtypeStruct((rows, features), BF),
        ),
        in_specs=[pl.BlockSpec(memory_space=pltpu.VMEM)] * len(args),
        out_specs=(
            pl.BlockSpec((BLOCK, features), lambda i: (i, 0)),
            pl.BlockSpec((block, features), lambda i: (i, 0)),
        ),
        cost_estimate=pl.CostEstimate(
            flops=4 * side * TILE * grid_latent.size,
            bytes_accessed=8 * grid_latent.size,
            transcendentals=0,
        ),
        compiler_params=pltpu.CompilerParams(vmem_limit_bytes=16 * 1024 * 1024),
        name="grid",
    )(*args)


def power(exponent):
    return jnp.where(exponent > 0, 2.0, jnp.where(exponent < 0, 0.5, 1.0)).astype(F32)


def place(step, parts):
    if parts == 1:
        return 0
    mp = lax.axis_index("mp")
    sub = lax.axis_index("sub")
    mp = mp if step < 2 else 1 - mp
    sub = sub if step % 2 == 0 else 1 - sub
    return 2 * mp + sub


def qkv_body(parts, *refs):
    pieces, (gain_ref, w_ref, *refs) = refs[:parts], refs[parts:]
    normed_ref, q_ref, kv_ref = refs
    rows, width = pieces[0].shape
    total = width * parts
    block = min(256, rows)
    lane = lax.broadcasted_iota(jnp.int32, (block, TILE), 1)

    def step(k, carry):
        at = pl.ds(pl.multiple_of(k * block, block), block)
        values = [p[at, :].astype(F32) for p in pieces]
        mean = sum(jnp.sum(v, axis=1, keepdims=True) for v in values) / total
        values = [v - mean for v in values]
        var = sum(jnp.sum(v * v, axis=1, keepdims=True) for v in values) / total
        scale = lax.rsqrt(var + 1e-05)
        for i, v in enumerate(values):
            cols = pl.ds(pl.multiple_of(place(i, parts) * width, width), width)
            normed_ref[at, cols] = (v * scale * gain_ref[:, cols]).astype(BF)
        out = jnp.dot(normed_ref[at, :], w_ref[...], preferred_element_type=F32)
        for pair in range(q_ref.shape[1] // TILE):
            a, b, c = [out[:, (3 * pair + i) * TILE : (3 * pair + i + 1) * TILE] for i in range(3)]
            q = pltpu.roll(jnp.where(lane < HD, a, b), HD, 1)
            q_ref[at, pair * TILE : (pair + 1) * TILE] = q.astype(BF)
            kv_ref[at, 2 * pair * TILE : (2 * pair + 1) * TILE] = jnp.where(lane < HD, b, a).astype(BF)
            kv_ref[at, (2 * pair + 1) * TILE : (2 * pair + 2) * TILE] = c.astype(BF)
        return carry

    lax.fori_loop(0, rows // block, step, 0)


def up_body(normed_ref, w_ref, exp_ref, out_ref):
    rows = normed_ref.shape[0]
    block = min(256, rows)
    cols = min(512, w_ref.shape[1])

    def step(k, carry):
        at = pl.ds(pl.multiple_of(k * block, block), block)
        for c in range(w_ref.shape[1] // cols):
            sl = slice(c * cols, (c + 1) * cols)
            up = jnp.dot(normed_ref[at, :], w_ref[:, sl], preferred_element_type=F32)
            up = up * power(exp_ref[:, sl])
            out_ref[at, sl] = (0.5 * up * (1.0 + lax.erf(up * 0.7071067811865476))).astype(BF)
        return carry

    lax.fori_loop(0, rows // block, step, 0)


def spot(which, b):
    n = WIN // BLOCK
    return jnp.where(parity() == which, b, n - 1 - b) * BLOCK


def slanted(which):
    i = lax.broadcasted_iota(jnp.int32, (BLOCK, BLOCK), 0)
    j = lax.broadcasted_iota(jnp.int32, (BLOCK, BLOCK), 1)
    return jnp.where(parity() == which, i - j, j - i)


def lane_ids():
    return lax.broadcasted_iota(jnp.int32, (BLOCK, TILE), 1)


def query_of(q_ref, pair, half):
    q = q_ref[:, pair * TILE : (pair + 1) * TILE] * BF(HD**-0.5)
    keep = (lane_ids() >= HD) if half == 0 else (lane_ids() < HD)
    return jnp.where(keep, q, jnp.zeros_like(q))


def scored(q, key):
    return lax.dot_general(q, key, (((1,), (1,)), ((), ())), preferred_element_type=F32)


def peak_of(scores):
    peak = scores[0]
    for s in scores[1:]:
        peak = jnp.maximum(peak, s)
    return jnp.max(peak, axis=1, keepdims=True)


def weighed(scores, peak, keys):
    probs = [jnp.exp(s - peak) for s in scores]
    total = probs[0]
    for p in probs[1:]:
        total = total + p
    mixed = jnp.dot(
        jnp.concatenate([p.astype(BF) for p in probs], axis=1),
        jnp.concatenate(keys, axis=0),
        preferred_element_type=F32,
    )
    return jnp.sum(total, axis=1, keepdims=True), mixed


def attend_body(which, b, q_ref, *refs):
    *refs, out_ref = refs
    bias = jnp.where(has_partner(which), 0.0, NEG).astype(F32)
    ahead = slanted(which)
    inner_mask = jnp.where(ahead <= 0, 0.0, NEG).astype(F32)
    outer_mask = jnp.where(ahead >= 0, bias, NEG).astype(F32)
    left = lane_ids() < HD
    for pair in range(q_ref.shape[1] // TILE):
        outs = []
        for half in range(2):
            cols = slice((2 * pair + half) * TILE, (2 * pair + half + 1) * TILE)
            q = query_of(q_ref, pair, half)
            keys = [ref[:, cols] for ref in refs]
            scores = [scored(q, key) for key in keys]
            scores[0] = scores[0] + inner_mask
            scores[4] = scores[4] + outer_mask
            if b == 1:
                scores[3] = scores[3] + bias
            total, mixed = weighed(scores, peak_of(scores), keys)
            outs.append(mixed / total)
        out_ref[:, pair * TILE : (pair + 1) * TILE] = jnp.where(left, outs[0], outs[1]).astype(BF)


def down_body(parts, n, *refs):
    atts, acts, (w_out_ref, w_down_ref, exp_ref), outs = (
        refs[:n],
        refs[n : 2 * n],
        refs[2 * n : 2 * n + 3],
        refs[2 * n + 3 :],
    )
    width = w_out_ref.shape[1] // parts
    for k in range(n):
        at = slice(k * BLOCK, (k + 1) * BLOCK)
        for i in range(parts):
            cols = pl.ds(pl.multiple_of(place(i, parts) * width, width), width)
            mlp = jnp.dot(acts[k][...], w_down_ref[:, cols], preferred_element_type=F32)
            att = jnp.dot(atts[k][...], w_out_ref[:, cols], preferred_element_type=F32)
            outs[i][at, :] = (att + mlp * power(exp_ref[:, cols])).astype(BF)


SWAP = [(0, 1), (1, 0)]
PIECES = ((0, 1), (0, 0), (1, 1), (1, 0))
UNITS = ((1, 0), (3,), (2,))


def gather(rows, split):
    if not split:
        return [lax.all_gather(rows, ("mp", "sub"), axis=1, tiled=True)]
    far = lax.ppermute(rows, "mp", SWAP)
    near = lax.ppermute(rows, "sub", SWAP)
    both = lax.ppermute(far, "sub", SWAP)
    return [rows, near, far, both]


def reduce_parts(parts, split):
    if not split:
        return [lax.psum_scatter(parts[0], ("mp", "sub"), scatter_dimension=1, tiled=True)]
    own, near, far, both = parts
    far_got = lax.ppermute(both, "sub", SWAP)
    near_got = lax.ppermute(near, "sub", SWAP)
    far_sum = (far.astype(F32) + far_got.astype(F32)).astype(BF)
    return [own, near_got, lax.ppermute(far_sum, "mp", SWAP)]


def settle_body(n, *refs):
    latents, adds, out = refs[:n], refs[n:-1], refs[-1]
    for k in range(n):
        at = slice(k * BLOCK, (k + 1) * BLOCK)
        total = adds[0][at, :].astype(F32)
        for term in adds[1:]:
            total = total + term[at, :].astype(F32)
        out[at, :] = (latents[k][...].astype(F32) + total).astype(BF)


def unit_starts(unit, count):
    return [start_of(*PIECES[g], count) for g in unit]


def unit_sources(unit, hidden_ref):
    return [hidden_ref.at[k * BLOCK : (k + 1) * BLOCK, :] for k in range(len(unit))]


def collect_body(side, units, count, part, weighted, earlier, src_ref, *refs):
    weight_ref, refs = (refs[0], refs[1:]) if weighted else (None, refs)
    hiddens, refs = refs[: len(units)], refs[len(units) :]
    n = {"sides": 2, "local": 1, "all": 3}[part]
    before, outs = refs[: n * earlier], refs[n * earlier :]
    before = list(before) or [None] * n
    sources, bases = [], []
    for unit, hidden_ref in zip(units, hiddens):
        sources += unit_sources(unit, hidden_ref)
        bases += unit_starts(unit, count)
    if part != "local":
        sides(side, src_ref, weight_ref, sources, bases, outs[:2], before[:2] if earlier else None)
    if part != "sides":
        locals_(2 * side, src_ref, weight_ref, sources, bases, outs[-1], before[-1])


def collect(side, units, count, part, edges, hiddens, before):
    features = hiddens[0].shape[1]
    out = jax.ShapeDtypeStruct((side * TILE, features), BF)
    local = jax.ShapeDtypeStruct(((edges[0].shape[0] - 2 * side) * TILE, features), BF)
    outs = {"sides": [out, out], "local": [local], "all": [out, out, local]}[part]
    return call(
        functools.partial(
            collect_body, side, units, count, part, len(edges) > 1, 1 if before else 0
        ),
        outs,
        (*edges, *hiddens, *before),
        2 * sum(h.size for h in hiddens) * sum(o.shape[0] for o in outs),
    )


def shards(
    grid_latent,
    grid_count,
    hidden_embed,
    enc_src_rows,
    enc_dst_rows,
    enc_weight,
    dec_src_rows,
    dec_dst_rows,
    dec_weight,
    norm_gain,
    w_qkv,
    w_out,
    w_up,
    up_exp,
    w_down,
    down_exp,
):
    split = lax.axis_size("mp") == 2 and lax.axis_size("sub") == 2
    parts = 4 if split else 1
    hid_rows, features = hidden_embed.shape
    full = w_qkv.shape[0]
    heads = w_qkv.shape[1] // (3 * HD)
    units = w_up.shape[1]
    rows = WIN
    count = hid_rows // rows
    assert count == 2
    src, dst, wts = enc_src_rows[0], enc_dst_rows[0], enc_weight[0]
    out = jax.ShapeDtypeStruct((ESIDE * TILE, features), BF)
    args = (src, wts, grid_latent)
    leaving = call(
        functools.partial(fetch_side_body, ESIDE),
        (out, out),
        args,
        4 * ESIDE * TILE * grid_latent.size,
        scratch=[
            *(pltpu.VMEM(a.shape, a.dtype) for a in args),
            pltpu.SemaphoreType.DMA((len(args),)),
        ],
        space=pltpu.HBM,
        limit=60 * 1024 * 1024,
    )
    arrived = swapped(*leaving)
    moved = gathered(src, wts, grid_latent, ESIDE)
    total = spread(dst, moved, hid_rows, ESIDE)
    latents, gathers = [], []
    for c, b in PIECES:
        (latent,) = call(
            functools.partial(latent_body, ESIDE, c, b, count),
            (jax.ShapeDtypeStruct((BLOCK, features), BF),),
            (dst, *arrived, total, hidden_embed),
            4 * ESIDE * TILE * BLOCK * features,
        )
        latents.append(latent)
        gathers.append(gather(latent, split))
    links = partners(lax.axis_size("seq"), lax.axis_size("ens"))
    queries, kvs, outer, activated = [], [], [], []
    for g, (c, b) in enumerate(PIECES):
        normed, q, part = call(
            functools.partial(qkv_body, parts),
            (
                jax.ShapeDtypeStruct((BLOCK, full), BF),
                jax.ShapeDtypeStruct((BLOCK, heads * HD), BF),
                jax.ShapeDtypeStruct((BLOCK, 2 * heads * HD), BF),
            ),
            (*gathers[g], norm_gain[None, :], w_qkv),
            2 * BLOCK * w_qkv.size,
        )
        queries.append(q)
        kvs.append(part)
        outer.append(lax.ppermute(part, ("ens", "seq"), links[c]))
        (act,) = call(
            up_body,
            (jax.ShapeDtypeStruct((BLOCK, units), BF),),
            (normed, w_up, up_exp[None, :]),
            2 * BLOCK * w_up.size,
        )
        activated.append(act)
    attended = []
    for g, (c, b) in enumerate(PIECES):
        o, h = 2 * (1 - c), 2 * c
        keys = (kvs[o], kvs[o + 1], kvs[h + 1], kvs[h], outer[h], outer[h + 1])[b : b + 5]
        (att,) = call(
            functools.partial(attend_body, c, b),
            (jax.ShapeDtypeStruct((BLOCK, heads * HD), BF),),
            (queries[g], *keys),
            4 * BLOCK * 5 * BLOCK * heads * HD,
            spare=12,
        )
        attended.append(att)
    src, dst, wts = dec_src_rows[0], dec_dst_rows[0], dec_weight[0]
    hiddens = []
    for unit in UNITS:
        size = len(unit) * BLOCK
        outs = call(
            functools.partial(down_body, parts, len(unit)),
            [jax.ShapeDtypeStruct((size, full // parts), BF)] * parts,
            (
                *(attended[g] for g in unit),
                *(activated[g] for g in unit),
                w_out,
                w_down,
                down_exp[None, :],
            ),
            2 * size * (w_out.size + w_down.size),
        )
        sums = reduce_parts(outs, split)
        (hidden,) = call(
            functools.partial(settle_body, len(unit)),
            (jax.ShapeDtypeStruct((size, features), BF),),
            (*(latents[g] for g in unit), *sums),
            4 * size * features,
        )
        hiddens.append(hidden)
    before = collect(DSIDE, UNITS[:1], count, "all", (src,), hiddens[:1], ())
    args = (src, wts)
    leaving = collect(DSIDE, UNITS[1:], count, "sides", args, hiddens[1:], before[:2])
    arrived = swapped(*leaving)
    (moved,) = collect(DSIDE, UNITS[1:], count, "local", args, hiddens[1:], before[2:])
    total = spread(dst, moved, grid_latent.shape[0], DSIDE)
    return settled(DSIDE, count, grid_count[None, :], dst, *arrived, total, grid_latent, hiddens)


def solution(mesh):
    placed = (
        P(("ens", "seq"), ("mp", "sub")),
        P(("ens", "seq")),
        P(("ens", "seq"), ("mp", "sub")),
        P(("ens", "seq"), None, None),
        P(("ens", "seq"), None, None),
        P(("ens", "seq"), None, None),
        P(("ens", "seq"), None, None),
        P(("ens", "seq"), None, None),
        P(("ens", "seq"), None, None),
        P(),
        P(None, ("mp", "sub")),
        P(("mp", "sub"), None),
        P(None, ("mp", "sub")),
        P(("mp", "sub")),
        P(("mp", "sub"), None),
        P(),
    )
    return jax.shard_map(
        shards,
        mesh=mesh,
        in_specs=placed,
        out_specs=(P(("ens", "seq"), ("mp", "sub")), P(("ens", "seq"), ("mp", "sub"))),
        check_vma=False,
    )
```

time: 95 us -> 91.1 us (0.959)
  waiting for transfers between devices: 25.4 us -> 20.1 us
    ppermute x6 -> x8, waiting for transfers between devices: 5.23 us -> 1.22 us  [the longest x4 0.67 us: swapped(): return (lax.ppermute(first, axes, one), lax.ppermute(second, axes, two))]
    ppermute x2 -> x4, starting transfers between devices: 2.16 us -> 4.25 us  [gather(): far = lax.ppermute(rows, 'mp', SWAP)]
    ppermute x6 -> x8, starting transfers between devices: 14 us -> 12 us  [the longest x4 7.66 us: swapped(): return (lax.ppermute(first, axes, one), lax.ppermute(second, axes, two))]
    ppermute x2 -> x4, waiting for transfers between devices: 10.3 us -> 9.5 us  [gather(): far = lax.ppermute(rows, 'mp', SWAP)]
    pallas_call x18 -> x29, Pallas kernels: 42.8 us -> 43.5 us  [call(): pl.pallas_call(body, out_shape=tuple(outs), in_specs=[pl.BlockSpec(memory...]
  transfers between devices with their start and end apart: 21 -> 29, of which waited for: 5 -> 8; matrix products, arithmetic and copies ran while one was open for 0% -> 0% of each run, Pallas kernels for 40% -> 40%
where the time goes in v4:
time: 91.1 us; the launch traced here: 90.9 us
  Pallas kernels  46.5 us (51%)
  starting transfers between devices  22.3 us (24%)
  waiting for transfers between devices  20.1 us (22%)
  between operations  1.76 us (2%)
    pallas_call x29, Pallas kernels, call(): pl.pallas_call(body, out_shape=tuple(outs), in_specs=[pl.BlockSpec(memory...  43.5 us
    ppermute x4, waiting for transfers between devices, gather(): far = lax.ppermute(rows, 'mp', SWAP)  9.5 us
    ppermute x3, waiting for transfers between devices, reduce_parts(): return [own, near_got, lax.ppermute(far_sum, 'mp', SWAP)]  9.39 us
    ppermute x4, starting transfers between devices, swapped(): return (lax.ppermute(first, axes, one), lax.ppermute(second, axes, two))  7.66 us
    ppermute x4, starting transfers between devices, shards(): outer.append(lax.ppermute(part, ('ens', 'seq'), links[c]))  4.31 us
    ppermute x4, starting transfers between devices, gather(): far = lax.ppermute(rows, 'mp', SWAP)  4.25 us
    ppermute x3, starting transfers between devices, reduce_parts(): return [own, near_got, lax.ppermute(far_sum, 'mp', SWAP)]  3.72 us
    pallas_call x1, Pallas kernels, settled(): pl.pallas_call(functools.partial(grid_body, side, count), grid=(steps,),...  3.03 us
  transfers between devices with their start and end apart: 29, of which 8 were waited for; matrix products, arithmetic and copies ran while one was open for 0% of the time, Pallas kernels for 40%

profile of v4, /device:TPU:0, one launch (start us, length us, event | category | flops | bytes accessed | tf_op | source)
XLA Modules:
  0.0 90.9 jit_solution(995567760366604627)
XLA Ops:
  0.7 3.5 %shard_map.167 = (bf16[512,256]{1,0:T(8,128)(2,1)}, bf16[512,256]{1,0:T(8,128)(2,1)}) custom-call(s32[32,128]{1,0:T(8,128)} %bitcast.34, f32[32,128]{1,0:T(8,128)} %bitcast.36, bf16[2048,256]{1,0:T(8,128)(2,1)} %grid_ref.1), custom_call_target="tpu_custom_call" | custom-call | flops 1073741824 | bytes 1605632 | tf_op jit(solution)/shard_map/pallas_call | solution.py:25
  4.1 3.1 %collective-permute-start = (bf16[512,256]{1,0:T(8,128)(2,1)}, bf16[512,256]{1,0:T(8,128)(2,1)S(1)}, u32[]{:S(2)}, u32[]{:S(2)}) collective-permute-start(bf16[512,256]{1,0:T(8,128)(2,1)} %get-tuple-element.33), channel_id=1, source_target_pairs={{0,4},{4,0},{8,12},{12,8},{16,20},{20,16},{24,28},{28,24},{1,5},{5... | collective-permute-start | bytes 786440 | tf_op jit(solution)/shard_map/ppermute | solution.py:218
  7.3 1.5 %collective-permute-start.1 = (bf16[512,256]{1,0:T(8,128)(2,1)}, bf16[512,256]{1,0:T(8,128)(2,1)S(1)}, u32[]{:S(2)}, u32[]{:S(2)}) collective-permute-start(bf16[512,256]{1,0:T(8,128)(2,1)} %get-tuple-element.34), channel_id=1, source_target_pairs={{0,16},{4,8},{8,4},{12,28},{16,0},{20,24},{24,20},{28,12},{1,17},{... | collective-permute-start | bytes 786440 | tf_op jit(solution)/shard_map/ppermute | solution.py:218
  8.8 4.0 %shard_map.168.local_ref = bf16[3072,256]{1,0:T(8,128)(2,1)S(1)} custom-call(s32[32,128]{1,0:T(8,128)S(1)} %bitcast.35, f32[32,128]{1,0:T(8,128)S(1)} %bitcast.37, bf16[2048,256]{1,0:T(8,128)(2,1)S(1)} %copy-done.5), custom_call_target="tpu_custom_call" | custom-call | flops 3221225472 | bytes 2654208 | tf_op jit(solution)/shard_map/pallas_call | solution.py:25
  12.8 0.0 copy-start.2
  12.8 1.8 %shard_map.169.total_ref = f32[1024,256]{1,0:T(8,128)S(1)} custom-call(s32[32,128]{1,0:T(8,128)S(1)} %bitcast.11, bf16[3072,256]{1,0:T(8,128)(2,1)S(1)} %shard_map.168.local_ref), custom_call_target="tpu_custom_call" | custom-call | flops 1610612736 | bytes 2637824 | tf_op jit(solution)/shard_map/pallas_call | solution.py:25
  14.6 0.7 collective-permute-done.1.second_ref
  15.2 0.3 shard_map.170.refs_0_
  15.6 0.1 collective-permute-start.2
  15.6 0.3 shard_map.176.refs_0_
  16.0 1.6 %collective-permute-start.12 = (bf16[256,256]{1,0:T(8,128)(2,1)S(1)}, bf16[256,256]{1,0:T(8,128)(2,1)S(1)}, u32[]{:S(2)}, u32[]{:S(2)}) collective-permute-start(bf16[256,256]{1,0:T(8,128)(2,1)S(1)} %shard_map.176.refs_0_), channel_id=1, source_target_pairs={{0,2},{2,0},{1,3},{3,1},{4,6},{6,4},{5,7},{7,5},{8,10},{10,8},{9,1... | collective-permute-start | bytes 393224 | tf_op jit(solution)/shard_map/ppermute | solution.py:423
  17.5 0.5 collective-permute-start.3
  18.1 0.3 shard_map.172.refs_0_.refs_1_
  18.4 1.6 %collective-permute-start.6 = (bf16[256,256]{1,0:T(8,128)(2,1)S(1)}, bf16[256,256]{1,0:T(8,128)(2,1)S(1)}, u32[]{:S(2)}, u32[]{:S(2)}) collective-permute-start(bf16[256,256]{1,0:T(8,128)(2,1)S(1)} %shard_map.172.refs_0_.refs_1_), channel_id=1, source_target_pairs={{0,2},{2,0},{1,3},{3,1},{4,6},{6,4},{5,7},{7,5},{8,10},{10,8},{9,1... | collective-permute-start | bytes 393224 | tf_op jit(solution)/shard_map/ppermute | solution.py:423
  19.9 0.3 shard_map.174.refs_0_
  20.2 0.6 collective-permute-start.9
  20.8 1.6 %collective-permute-done.12.refs_2_ = bf16[256,256]{1,0:T(8,128)(2,1)S(1)} collective-permute-done((bf16[256,256]{1,0:T(8,128)(2,1)S(1)}, bf16[256,256]{1,0:T(8,128)(2,1)S(1)}, u32[]{:S(2)}, u32[]{:S(2)}) %collective-permute-start.12) | collective-permute-done | bytes 131104 | tf_op jit(solution)/shard_map/ppermute | solution.py:423
  22.4 2.8 %collective-permute-done.3.refs_2_ = bf16[256,256]{1,0:T(8,128)(2,1)S(1)} collective-permute-done((bf16[256,256]{1,0:T(8,128)(2,1)S(1)}, bf16[256,256]{1,0:T(8,128)(2,1)S(1)}, u32[]{:S(2)}, u32[]{:S(2)}) %collective-permute-start.3) | collective-permute-done | bytes 131104 | tf_op jit(solution)/shard_map/ppermute | solution.py:423
  25.2 2.8 %collective-permute-done.6.refs_2_ = bf16[256,256]{1,0:T(8,128)(2,1)S(1)} collective-permute-done((bf16[256,256]{1,0:T(8,128)(2,1)S(1)}, bf16[256,256]{1,0:T(8,128)(2,1)S(1)}, u32[]{:S(2)}, u32[]{:S(2)}) %collective-permute-start.6) | collective-permute-done | bytes 131104 | tf_op jit(solution)/shard_map/ppermute | solution.py:423
  28.0 2.3 %collective-permute-done.9.refs_2_ = bf16[256,256]{1,0:T(8,128)(2,1)S(1)} collective-permute-done((bf16[256,256]{1,0:T(8,128)(2,1)S(1)}, bf16[256,256]{1,0:T(8,128)(2,1)S(1)}, u32[]{:S(2)}, u32[]{:S(2)}) %collective-permute-start.9) | collective-permute-done | bytes 131104 | tf_op jit(solution)/shard_map/ppermute | solution.py:423
  30.4 0.5 collective-permute-start.8
  30.9 0.1 collective-permute-start.10
  31.0 1.0 %shard_map.177 = (bf16[256,1024]{1,0:T(8,128)(2,1)S(1)}, bf16[256,256]{1,0:T(8,128)(2,1)S(1)}, bf16[256,512]{1,0:T(8,128)(2,1)S(1)}) custom-call(bf16[256,256]{1,0:T(8,128)(2,1)S(1)} %shard_map.176.refs_0_, bf16[256,256]{1,0:T(8,128)(2,1)S(1)} %collective-permute-done.11.refs_1_, bf16[256,256]{1,0:T(8,128)(2,1)S(1)} %collective-permute-done.12.refs_2_, ...), custom_call_target="tpu_custom_call" | custom-call | flops 402653184 | bytes 3018752 | tf_op jit(solution)/shard_map/pallas_call | solution.py:25
  31.9 1.6 %collective-permute-start.14 = (bf16[256,512]{1,0:T(8,128)(2,1)S(1)}, bf16[256,512]{1,0:T(8,128)(2,1)S(1)}, u32[]{:S(2)}, u32[]{:S(2)}) collective-permute-start(bf16[256,512]{1,0:T(8,128)(2,1)S(1)} %get-tuple-element.39.refs_3_.refs_2_.refs_0_), channel_id=1, source_target_pairs={{0,16},{4,8},{8,4},{12,28},{16,0},{20,24},{24,20},{28,12},{1,17},{... | collective-permute-start | bytes 786440 | tf_op jit(solution)/shard_map/ppermute | solution.py:558
  33.5 1.0 %shard_map.171 = (bf16[256,1024]{1,0:T(8,128)(2,1)S(1)}, bf16[256,256]{1,0:T(8,128)(2,1)S(1)}, bf16[256,512]{1,0:T(8,128)(2,1)S(1)}) custom-call(bf16[256,256]{1,0:T(8,128)(2,1)S(1)} %shard_map.170.refs_0_, bf16[256,256]{1,0:T(8,128)(2,1)S(1)} %collective-permute-done.2.refs_1_, bf16[256,256]{1,0:T(8,128)(2,1)S(1)} %collective-permute-done.3.refs_2_, ...), custom_call_target="tpu_custom_call" | custom-call | flops 402653184 | bytes 3018752 | tf_op jit(solution)/shard_map/pallas_call | solution.py:25
  34.5 0.6 collective-permute-start.18
  35.1 1.0 %shard_map.173 = (bf16[256,1024]{1,0:T(8,128)(2,1)S(1)}, bf16[256,256]{1,0:T(8,128)(2,1)S(1)}, bf16[256,512]{1,0:T(8,128)(2,1)S(1)}) custom-call(bf16[256,256]{1,0:T(8,128)(2,1)S(1)} %shard_map.172.refs_0_.refs_1_, bf16[256,256]{1,0:T(8,128)(2,1)S(1)} %collective-permute-done.5.refs_1_, bf16[256,256]{1,0:T(8,128)(2,1)S(1)} %collective-permute-done.6.refs_2_, ...), custom_call_target="tpu_custom_call" | custom-call | flops 402653184 | bytes 3018752 | tf_op jit(solution)/shard_map/pallas_call | solution.py:25
  36.1 1.5 %collective-permute-start.22 = (bf16[256,512]{1,0:T(8,128)(2,1)S(1)}, bf16[256,512]{1,0:T(8,128)(2,1)S(1)}, u32[]{:S(2)}, u32[]{:S(2)}) collective-permute-start(bf16[256,512]{1,0:T(8,128)(2,1)S(1)} %get-tuple-element.36.refs_0_.refs_3_.refs_2_), channel_id=1, source_target_pairs={{0,4},{4,0},{8,12},{12,8},{16,20},{20,16},{24,28},{28,24},{1,5},{5... | collective-permute-start | bytes 786440 | tf_op jit(solution)/shard_map/ppermute | solution.py:558
  37.6 1.0 %shard_map.175 = (bf16[256,1024]{1,0:T(8,128)(2,1)S(1)}, bf16[256,256]{1,0:T(8,128)(2,1)S(1)}, bf16[256,512]{1,0:T(8,128)(2,1)S(1)}) custom-call(bf16[256,256]{1,0:T(8,128)(2,1)S(1)} %shard_map.174.refs_0_, bf16[256,256]{1,0:T(8,128)(2,1)S(1)} %collective-permute-done.8.refs_1_, bf16[256,256]{1,0:T(8,128)(2,1)S(1)} %collective-permute-done.9.refs_2_, ...), custom_call_target="tpu_custom_call" | custom-call | flops 402653184 | bytes 3018752 | tf_op jit(solution)/shard_map/pallas_call | solution.py:25
  38.5 0.7 collective-permute-start.23
  39.2 0.8 shard_map.179.refs_1_
  40.0 0.8 shard_map.183.refs_1_
  40.9 0.8 shard_map.188.refs_2_
  41.8 0.8 shard_map.189.refs_3_
  42.6 2.5 %shard_map.178.refs_0_ = bf16[256,256]{1,0:T(8,128)(2,1)S(1)} custom-call(bf16[256,256]{1,0:T(8,128)(2,1)S(1)} %get-tuple-element.35.q_ref, bf16[256,512]{1,0:T(8,128)(2,1)S(1)} %get-tuple-element.36.refs_0_.refs_3_.refs_2_, bf16[256,512]{1,0:T(8,128)(2,1)S(1)} %get-tuple-element.37.refs_1_.refs_0_.refs_2_, ...), custom_call_target="tpu_custom_call" | custom-call | flops 335544320 | bytes 1572864 | tf_op jit(solution)/shard_map/pallas_call | solution.py:25
  45.2 0.9 shard_map.180
  46.1 0.1 collective-permute-start.15
  46.1 0.5 collective-permute-start.16
  46.6 2.7 %shard_map.186.refs_0_ = bf16[256,256]{1,0:T(8,128)(2,1)S(1)} custom-call(bf16[256,256]{1,0:T(8,128)(2,1)S(1)} %get-tuple-element.51.q_ref, bf16[256,512]{1,0:T(8,128)(2,1)S(1)} %get-tuple-element.39.refs_3_.refs_2_.refs_0_, bf16[256,512]{1,0:T(8,128)(2,1)S(1)} %get-tuple-element.38.refs_2_.refs_1_.refs_0_, ...), custom_call_target="tpu_custom_call" | custom-call | flops 335544320 | bytes 1572864 | tf_op jit(solution)/shard_map/pallas_call | solution.py:25
  49.4 0.5 collective-permute-done.23.refs_4_
  49.9 2.5 %shard_map.187.refs_1_ = bf16[256,256]{1,0:T(8,128)(2,1)S(1)} custom-call(bf16[256,256]{1,0:T(8,128)(2,1)S(1)} %get-tuple-element.52.q_ref, bf16[256,512]{1,0:T(8,128)(2,1)S(1)} %get-tuple-element.38.refs_2_.refs_1_.refs_0_, bf16[256,512]{1,0:T(8,128)(2,1)S(1)} %get-tuple-element.37.refs_1_.refs_0_.refs_2_, ...), custom_call_target="tpu_custom_call" | custom-call | flops 335544320 | bytes 1572864 | tf_op jit(solution)/shard_map/pallas_call | solution.py:25
  52.4 1.6 %shard_map.190 = (bf16[512,256]{1,0:T(8,128)(2,1)S(1)}, bf16[512,256]{1,0:T(8,128)(2,1)S(1)}, bf16[512,256]{1,0:T(8,128)(2,1)S(1)}, bf16[512,256]{1,0:T(8,128)(2,1)S(1)}) custom-call(bf16[256,256]{1,0:T(8,128)(2,1)S(1)} %shard_map.186.refs_0_, bf16[256,256]{1,0:T(8,128)(2,1)S(1)} %shard_map.187.refs_1_, bf16[256,1024]{1,0:T(8,128)(2,1)S(1)} %shard_map.188.refs_2_, ...), custom_call_target="tpu_custom_call" | custom-call | flops 1342177280 | bytes 4984832 | tf_op jit(solution)/shard_map/pallas_call | solution.py:25
  54.0 0.1 collective-permute-start.25
  54.1 2.5 %shard_map.182.refs_0_ = bf16[256,256]{1,0:T(8,128)(2,1)S(1)} custom-call(bf16[256,256]{1,0:T(8,128)(2,1)S(1)} %get-tuple-element.45.q_ref, bf16[256,512]{1,0:T(8,128)(2,1)S(1)} %get-tuple-element.37.refs_1_.refs_0_.refs_2_, bf16[256,512]{1,0:T(8,128)(2,1)S(1)} %get-tuple-element.38.refs_2_.refs_1_.refs_0_, ...), custom_call_target="tpu_custom_call" | custom-call | flops 335544320 | bytes 1572864 | tf_op jit(solution)/shard_map/pallas_call | solution.py:25
  56.6 0.9 shard_map.184
  57.5 0.6 collective-permute-start.19
  58.0 0.1 collective-permute-start.20
  58.1 0.4 collective-permute-start.24
  58.6 1.6 %collective-permute-start.17 = (bf16[256,256]{1,0:T(8,128)(2,1)S(1)}, bf16[256,256]{1,0:T(8,128)(2,1)S(1)}, u32[]{:S(2)}, u32[]{:S(2)}) collective-permute-start(bf16[256,256]{1,0:T(8,128)(2,1)S(1)} %add_convert_fusion.2), channel_id=1, source_target_pairs={{0,2},{2,0},{1,3},{3,1},{4,6},{6,4},{5,7},{7,5},{8,10},{10,8},{9,1... | collective-permute-start | bytes 393224 | tf_op jit(solution)/shard_map/ppermute | solution.py:436
  60.1 0.1 add_convert_fusion
  60.2 0.6 collective-permute-start.26
  60.9 1.5 %collective-permute-start.21 = (bf16[256,256]{1,0:T(8,128)(2,1)S(1)}, bf16[256,256]{1,0:T(8,128)(2,1)S(1)}, u32[]{:S(2)}, u32[]{:S(2)}) collective-permute-start(bf16[256,256]{1,0:T(8,128)(2,1)S(1)} %add_convert_fusion.1), channel_id=1, source_target_pairs={{0,2},{2,0},{1,3},{3,1},{4,6},{6,4},{5,7},{7,5},{8,10},{10,8},{9,1... | collective-permute-start | bytes 393224 | tf_op jit(solution)/shard_map/ppermute | solution.py:436
  63.1 1.9 %collective-permute-done.17.refs_3_ = bf16[256,256]{1,0:T(8,128)(2,1)S(1)} collective-permute-done((bf16[256,256]{1,0:T(8,128)(2,1)S(1)}, bf16[256,256]{1,0:T(8,128)(2,1)S(1)}, u32[]{:S(2)}, u32[]{:S(2)}) %collective-permute-start.17) | collective-permute-done | bytes 131104 | tf_op jit(solution)/shard_map/ppermute | solution.py:436
  65.0 0.1 shard_map.181.refs_1_
  65.1 7.5 %collective-permute-done.21.refs_3_ = bf16[256,256]{1,0:T(8,128)(2,1)S(1)} collective-permute-done((bf16[256,256]{1,0:T(8,128)(2,1)S(1)}, bf16[256,256]{1,0:T(8,128)(2,1)S(1)}, u32[]{:S(2)}, u32[]{:S(2)}) %collective-permute-start.21) | collective-permute-done | bytes 131104 | tf_op jit(solution)/shard_map/ppermute | solution.py:436
  72.6 0.1 shard_map.185.refs_2_
  72.6 0.1 shard_map.191.refs_0_
  72.8 3.1 %shard_map.192 = (bf16[512,256]{1,0:T(8,128)(2,1)S(1)}, bf16[512,256]{1,0:T(8,128)(2,1)S(1)}, bf16[5120,256]{1,0:T(8,128)(2,1)S(1)}) custom-call(s32[48,128]{1,0:T(8,128)S(1)} %bitcast.24, bf16[512,256]{1,0:T(8,128)(2,1)S(1)} %shard_map.191.refs_0_), custom_call_target="tpu_custom_call" | custom-call | flops 1610612736 | bytes 3432448 | tf_op jit(solution)/shard_map/pallas_call | solution.py:25
  75.9 0.5 shard_map.193
  76.4 1.5 %collective-permute-start.27 = (bf16[512,256]{1,0:T(8,128)(2,1)S(1)}, bf16[512,256]{1,0:T(8,128)(2,1)S(1)}, u32[]{:S(2)}, u32[]{:S(2)}) collective-permute-start(bf16[512,256]{1,0:T(8,128)(2,1)S(1)} %get-tuple-element.61), channel_id=1, source_target_pairs={{0,4},{4,0},{8,12},{12,8},{16,20},{20,16},{24,28},{28,24},{1,5},{5... | collective-permute-start | bytes 786440 | tf_op jit(solution)/shard_map/ppermute | solution.py:218
  77.9 1.5 %collective-permute-start.28 = (bf16[512,256]{1,0:T(8,128)(2,1)S(1)}, bf16[512,256]{1,0:T(8,128)(2,1)S(1)}, u32[]{:S(2)}, u32[]{:S(2)}) collective-permute-start(bf16[512,256]{1,0:T(8,128)(2,1)S(1)} %get-tuple-element.62), channel_id=1, source_target_pairs={{0,16},{4,8},{8,4},{12,28},{16,0},{20,24},{24,20},{28,12},{1,17},{... | collective-permute-start | bytes 786440 | tf_op jit(solution)/shard_map/ppermute | solution.py:218
  79.5 2.6 %shard_map.194.local_ref = bf16[5120,256]{1,0:T(8,128)(2,1)S(1)} custom-call(s32[48,128]{1,0:T(8,128)S(1)} %bitcast.26, f32[48,128]{1,0:T(8,128)S(1)} %bitcast.28, bf16[256,256]{1,0:T(8,128)(2,1)S(1)} %shard_map.181.refs_1_, bf16[256,256]{1,0:T(8,128)(2,1)S(1)} %shard_map.185.refs_2_, bf16[5120,256]{1,0:T(8,128)(2,1)S(1)} %get-tuple-element.63.refs_3_), custom_call_target="tpu_custom_call" | custom-call | flops 1342177280 | bytes 5554176 | tf_op jit(solution)/shard_map/pallas_call | solution.py:25
  82.1 5.8 %shard_map.195.total_ref = f32[2048,256]{1,0:T(8,128)S(1)} custom-call(s32[48,128]{1,0:T(8,128)S(1)} %bitcast.29, bf16[5120,256]{1,0:T(8,128)(2,1)S(1)} %shard_map.194.local_ref), custom_call_target="tpu_custom_call" | custom-call | flops 5368709120 | bytes 4743168 | tf_op jit(solution)/shard_map/pallas_call | solution.py:25
  87.9 3.0 %grid.1 = (bf16[1024,256]{1,0:T(8,128)(2,1)}, bf16[2048,256]{1,0:T(8,128)(2,1)}) custom-call(s32[1,1]{1,0:T(1,128)} %bitcast.10.count_ref, s32[48,128]{1,0:T(8,128)S(1)} %bitcast.30, bf16[512,256]{1,0:T(8,128)(2,1)S(1)} %collective-permute-done.27.first_ref, bf16[512,256]{1,0:T(8,128)(2,1)S(1)} %collective-permute-done.28.second_ref, ...), custom_call_target="tpu_custom_call" | custom-call | flops 1073741824 | bytes 4194304 | tf_op jit(solution)/shard_map/grid/pallas_call | solution.py:247
  (57 shorter events, 0.2 us)
Async XLA Ops:
  0.6 8.2 %copy-start.13 = (s32[1,32,128]{2,1,0:T(8,128)S(1)}, s32[1,32,128]{2,1,0:T(8,128)}, u32[]{:S(2)}) copy-start(s32[1,32,128]{2,1,0:T(8,128)} %param.19) | copy-start | bytes 49156
  0.6 8.1 %copy-start.14 = (f32[1,32,128]{2,1,0:T(8,128)S(1)}, f32[1,32,128]{2,1,0:T(8,128)}, u32[]{:S(2)}) copy-start(f32[1,32,128]{2,1,0:T(8,128)} %param.21) | copy-start | bytes 49156
  0.6 8.1 %copy-start.5 = (bf16[2048,256]{1,0:T(8,128)(2,1)S(1)}, bf16[2048,256]{1,0:T(8,128)(2,1)}, u32[]{:S(2)}) copy-start(bf16[2048,256]{1,0:T(8,128)(2,1)} %grid_ref.1) | copy-start | bytes 3145732
  4.1 10.4 %collective-permute-start = (bf16[512,256]{1,0:T(8,128)(2,1)}, bf16[512,256]{1,0:T(8,128)(2,1)S(1)}, u32[]{:S(2)}, u32[]{:S(2)}) collective-permute-start(bf16[512,256]{1,0:T(8,128)(2,1)} %get-tuple-element.33), channel_id=1, source_target_pairs={{0,4},{4,0},{8,12},{12,8},{16,20},{20,16},{24,28},{28,24},{1,5},{5... | collective-permute-start | bytes 786440 | tf_op jit(solution)/shard_map/ppermute | solution.py:218
  7.3 5.5 %copy-start.6 = (s32[1,32,128]{2,1,0:T(8,128)S(1)}, s32[1,32,128]{2,1,0:T(8,128)}, u32[]{:S(2)}) copy-start(s32[1,32,128]{2,1,0:T(8,128)} %param.20) | copy-start | bytes 49156
  7.3 8.0 %collective-permute-start.1 = (bf16[512,256]{1,0:T(8,128)(2,1)}, bf16[512,256]{1,0:T(8,128)(2,1)S(1)}, u32[]{:S(2)}, u32[]{:S(2)}) collective-permute-start(bf16[512,256]{1,0:T(8,128)(2,1)} %get-tuple-element.34), channel_id=1, source_target_pairs={{0,16},{4,8},{8,4},{12,28},{16,0},{20,24},{24,20},{28,12},{1,17},{... | collective-permute-start | bytes 786440 | tf_op jit(solution)/shard_map/ppermute | solution.py:218
  12.8 2.5 %copy-start.2 = (bf16[1024,256]{1,0:T(8,128)(2,1)S(1)}, bf16[1024,256]{1,0:T(8,128)(2,1)}, u32[]{:S(2)}) copy-start(bf16[1024,256]{1,0:T(8,128)(2,1)} %embed_ref.7) | copy-start | bytes 1572868
  15.6 5.3 %collective-permute-start.2 = (bf16[256,256]{1,0:T(8,128)(2,1)S(1)}, bf16[256,256]{1,0:T(8,128)(2,1)S(1)}, u32[]{:S(2)}, u32[]{:S(2)}) collective-permute-start(bf16[256,256]{1,0:T(8,128)(2,1)S(1)} %shard_map.170.refs_0_), channel_id=1, source_target_pairs={{0,1},{1,0},{2,3},{3,2},{4,5},{5,4},{6,7},{7,6},{8,9},{9,8},{10,11... | collective-permute-start | bytes 393224 | tf_op jit(solution)/shard_map/ppermute | solution.py:424
  15.9 15.0 %copy-start.1 = (bf16[1024,768]{1,0:T(8,128)(2,1)S(1)}, bf16[1024,768]{1,0:T(8,128)(2,1)}, u32[]{:S(2)}) copy-start(bf16[1024,768]{1,0:T(8,128)(2,1)} %refs_5_.8) | copy-start | bytes 4718596
  16.0 15.0 %copy-start.7 = (f32[1024]{0:T(1024)S(1)}, f32[1024]{0:T(1024)}, u32[]{:S(2)}) copy-start(f32[1024]{0:T(1024)} %param.25) | copy-start | bytes 12292
  16.0 6.4 %collective-permute-start.12 = (bf16[256,256]{1,0:T(8,128)(2,1)S(1)}, bf16[256,256]{1,0:T(8,128)(2,1)S(1)}, u32[]{:S(2)}, u32[]{:S(2)}) collective-permute-start(bf16[256,256]{1,0:T(8,128)(2,1)S(1)} %shard_map.176.refs_0_), channel_id=1, source_target_pairs={{0,2},{2,0},{1,3},{3,1},{4,6},{6,4},{5,7},{7,5},{8,10},{10,8},{9,1... | collective-permute-start | bytes 393224 | tf_op jit(solution)/shard_map/ppermute | solution.py:423
  17.5 7.7 %collective-permute-start.3 = (bf16[256,256]{1,0:T(8,128)(2,1)S(1)}, bf16[256,256]{1,0:T(8,128)(2,1)S(1)}, u32[]{:S(2)}, u32[]{:S(2)}) collective-permute-start(bf16[256,256]{1,0:T(8,128)(2,1)S(1)} %shard_map.170.refs_0_), channel_id=1, source_target_pairs={{0,2},{2,0},{1,3},{3,1},{4,6},{6,4},{5,7},{7,5},{8,10},{10,8},{9,1... | collective-permute-start | bytes 393224 | tf_op jit(solution)/shard_map/ppermute | solution.py:423
  18.4 9.6 %collective-permute-start.6 = (bf16[256,256]{1,0:T(8,128)(2,1)S(1)}, bf16[256,256]{1,0:T(8,128)(2,1)S(1)}, u32[]{:S(2)}, u32[]{:S(2)}) collective-permute-start(bf16[256,256]{1,0:T(8,128)(2,1)S(1)} %shard_map.172.refs_0_.refs_1_), channel_id=1, source_target_pairs={{0,2},{2,0},{1,3},{3,1},{4,6},{6,4},{5,7},{7,5},{8,10},{10,8},{9,1... | collective-permute-start | bytes 393224 | tf_op jit(solution)/shard_map/ppermute | solution.py:423
  20.2 10.1 %collective-permute-start.9 = (bf16[256,256]{1,0:T(8,128)(2,1)S(1)}, bf16[256,256]{1,0:T(8,128)(2,1)S(1)}, u32[]{:S(2)}, u32[]{:S(2)}) collective-permute-start(bf16[256,256]{1,0:T(8,128)(2,1)S(1)} %shard_map.174.refs_0_), channel_id=1, source_target_pairs={{0,2},{2,0},{1,3},{3,1},{4,6},{6,4},{5,7},{7,5},{8,10},{10,8},{9,1... | collective-permute-start | bytes 393224 | tf_op jit(solution)/shard_map/ppermute | solution.py:423
  20.8 9.5 %collective-permute-start.11 = (bf16[256,256]{1,0:T(8,128)(2,1)S(1)}, bf16[256,256]{1,0:T(8,128)(2,1)S(1)}, u32[]{:S(2)}, u32[]{:S(2)}) collective-permute-start(bf16[256,256]{1,0:T(8,128)(2,1)S(1)} %shard_map.176.refs_0_), channel_id=1, source_target_pairs={{0,1},{1,0},{2,3},{3,2},{4,5},{5,4},{6,7},{7,6},{8,9},{9,8},{10,11... | collective-permute-start | bytes 393224 | tf_op jit(solution)/shard_map/ppermute | solution.py:424
  22.4 8.5 %collective-permute-start.13 = (bf16[256,256]{1,0:T(8,128)(2,1)S(1)}, bf16[256,256]{1,0:T(8,128)(2,1)S(1)}, u32[]{:S(2)}, u32[]{:S(2)}) collective-permute-start(bf16[256,256]{1,0:T(8,128)(2,1)S(1)} %collective-permute-done.12.refs_2_), channel_id=1, source_target_pairs={{0,1},{1,0},{2,3},{3,2},{4,5},{5,4},{6,7},{7,6},{8,9},{9,8},{10,11... | collective-permute-start | bytes 393224 | tf_op jit(solution)/shard_map/ppermute | solution.py:425
  25.2 6.7 %collective-permute-start.4 = (bf16[256,256]{1,0:T(8,128)(2,1)S(1)}, bf16[256,256]{1,0:T(8,128)(2,1)S(1)}, u32[]{:S(2)}, u32[]{:S(2)}) collective-permute-start(bf16[256,256]{1,0:T(8,128)(2,1)S(1)} %collective-permute-done.3.refs_2_), channel_id=1, source_target_pairs={{0,1},{1,0},{2,3},{3,2},{4,5},{5,4},{6,7},{7,6},{8,9},{9,8},{10,11... | collective-permute-start | bytes 393224 | tf_op jit(solution)/shard_map/ppermute | solution.py:425
  28.0 6.5 %collective-permute-start.5 = (bf16[256,256]{1,0:T(8,128)(2,1)S(1)}, bf16[256,256]{1,0:T(8,128)(2,1)S(1)}, u32[]{:S(2)}, u32[]{:S(2)}) collective-permute-start(bf16[256,256]{1,0:T(8,128)(2,1)S(1)} %shard_map.172.refs_0_.refs_1_), channel_id=1, source_target_pairs={{0,1},{1,0},{2,3},{3,2},{4,5},{5,4},{6,7},{7,6},{8,9},{9,8},{10,11... | collective-permute-start | bytes 393224 | tf_op jit(solution)/shard_map/ppermute | solution.py:424
  30.4 4.7 %collective-permute-start.7 = (bf16[256,256]{1,0:T(8,128)(2,1)S(1)}, bf16[256,256]{1,0:T(8,128)(2,1)S(1)}, u32[]{:S(2)}, u32[]{:S(2)}) collective-permute-start(bf16[256,256]{1,0:T(8,128)(2,1)S(1)} %collective-permute-done.6.refs_2_), channel_id=1, source_target_pairs={{0,1},{1,0},{2,3},{3,2},{4,5},{5,4},{6,7},{7,6},{8,9},{9,8},{10,11... | collective-permute-start | bytes 393224 | tf_op jit(solution)/shard_map/ppermute | solution.py:425
  30.4 7.2 %collective-permute-start.8 = (bf16[256,256]{1,0:T(8,128)(2,1)S(1)}, bf16[256,256]{1,0:T(8,128)(2,1)S(1)}, u32[]{:S(2)}, u32[]{:S(2)}) collective-permute-start(bf16[256,256]{1,0:T(8,128)(2,1)S(1)} %shard_map.174.refs_0_), channel_id=1, source_target_pairs={{0,1},{1,0},{2,3},{3,2},{4,5},{5,4},{6,7},{7,6},{8,9},{9,8},{10,11... | collective-permute-start | bytes 393224 | tf_op jit(solution)/shard_map/ppermute | solution.py:424
  30.9 6.7 %collective-permute-start.10 = (bf16[256,256]{1,0:T(8,128)(2,1)S(1)}, bf16[256,256]{1,0:T(8,128)(2,1)S(1)}, u32[]{:S(2)}, u32[]{:S(2)}) collective-permute-start(bf16[256,256]{1,0:T(8,128)(2,1)S(1)} %collective-permute-done.9.refs_2_), channel_id=1, source_target_pairs={{0,1},{1,0},{2,3},{3,2},{4,5},{5,4},{6,7},{7,6},{8,9},{9,8},{10,11... | collective-permute-start | bytes 393224 | tf_op jit(solution)/shard_map/ppermute | solution.py:425
  31.9 10.7 %collective-permute-start.14 = (bf16[256,512]{1,0:T(8,128)(2,1)S(1)}, bf16[256,512]{1,0:T(8,128)(2,1)S(1)}, u32[]{:S(2)}, u32[]{:S(2)}) collective-permute-start(bf16[256,512]{1,0:T(8,128)(2,1)S(1)} %get-tuple-element.39.refs_3_.refs_2_.refs_0_), channel_id=1, source_target_pairs={{0,16},{4,8},{8,4},{12,28},{16,0},{20,24},{24,20},{28,12},{1,17},{... | collective-permute-start | bytes 786440 | tf_op jit(solution)/shard_map/ppermute | solution.py:558
  34.5 4.7 %copy-start = (bf16[1024,1024]{1,0:T(8,128)(2,1)S(1)}, bf16[1024,1024]{1,0:T(8,128)(2,1)}, u32[]{:S(2)}) copy-start(bf16[1024,1024]{1,0:T(8,128)(2,1)} %w_ref.7) | copy-start | bytes 6291460
  34.5 4.7 %copy-start.8 = (s32[1024]{0:T(1024)S(1)}, s32[1024]{0:T(1024)}, u32[]{:S(2)}) copy-start(s32[1024]{0:T(1024)} %param.29) | copy-start | bytes 12292
  34.5 19.6 %collective-permute-start.18 = (bf16[256,512]{1,0:T(8,128)(2,1)S(1)}, bf16[256,512]{1,0:T(8,128)(2,1)S(1)}, u32[]{:S(2)}, u32[]{:S(2)}) collective-permute-start(bf16[256,512]{1,0:T(8,128)(2,1)S(1)} %get-tuple-element.38.refs_2_.refs_1_.refs_0_), channel_id=1, source_target_pairs={{0,16},{4,8},{8,4},{12,28},{16,0},{20,24},{24,20},{28,12},{1,17},{... | collective-permute-start | bytes 786440 | tf_op jit(solution)/shard_map/ppermute | solution.py:558
  36.1 10.6 %collective-permute-start.22 = (bf16[256,512]{1,0:T(8,128)(2,1)S(1)}, bf16[256,512]{1,0:T(8,128)(2,1)S(1)}, u32[]{:S(2)}, u32[]{:S(2)}) collective-permute-start(bf16[256,512]{1,0:T(8,128)(2,1)S(1)} %get-tuple-element.36.refs_0_.refs_3_.refs_2_), channel_id=1, source_target_pairs={{0,4},{4,0},{8,12},{12,8},{16,20},{20,16},{24,28},{28,24},{1,5},{5... | collective-permute-start | bytes 786440 | tf_op jit(solution)/shard_map/ppermute | solution.py:558
  38.5 11.4 %collective-permute-start.23 = (bf16[256,512]{1,0:T(8,128)(2,1)S(1)}, bf16[256,512]{1,0:T(8,128)(2,1)S(1)}, u32[]{:S(2)}, u32[]{:S(2)}) collective-permute-start(bf16[256,512]{1,0:T(8,128)(2,1)S(1)} %get-tuple-element.37.refs_1_.refs_0_.refs_2_), channel_id=1, source_target_pairs={{0,4},{4,0},{8,12},{12,8},{16,20},{20,16},{24,28},{28,24},{1,5},{5... | collective-permute-start | bytes 786440 | tf_op jit(solution)/shard_map/ppermute | solution.py:558
  41.7 3.4 %copy-start.3 = (bf16[1024,1024]{1,0:T(8,128)(2,1)S(1)}, bf16[1024,1024]{1,0:T(8,128)(2,1)}, u32[]{:S(2)}) copy-start(bf16[1024,1024]{1,0:T(8,128)(2,1)} %refs_5_.9) | copy-start | bytes 6291460
  41.7 3.4 %copy-start.4 = (bf16[256,1024]{1,0:T(8,128)(2,1)S(1)}, bf16[256,1024]{1,0:T(8,128)(2,1)}, u32[]{:S(2)}) copy-start(bf16[256,1024]{1,0:T(8,128)(2,1)} %refs_4_.1) | copy-start | bytes 1572868
  41.7 3.4 %copy-start.12 = (s32[1024]{0:T(1024)S(1)}, s32[1024]{0:T(1024)}, u32[]{:S(2)}) copy-start(s32[1024]{0:T(1024)} %param.31) | copy-start | bytes 12292
  46.1 14.8 %collective-permute-start.15 = (bf16[256,256]{1,0:T(8,128)(2,1)S(1)}, bf16[256,256]{1,0:T(8,128)(2,1)S(1)}, u32[]{:S(2)}, u32[]{:S(2)}) collective-permute-start(bf16[256,256]{1,0:T(8,128)(2,1)S(1)} %get-tuple-element.42), channel_id=1, source_target_pairs={{0,1},{1,0},{2,3},{3,2},{4,5},{5,4},{6,7},{7,6},{8,9},{9,8},{10,11... | collective-permute-start | bytes 393224 | tf_op jit(solution)/shard_map/ppermute | solution.py:434
  46.1 12.0 %collective-permute-start.16 = (bf16[256,256]{1,0:T(8,128)(2,1)S(1)}, bf16[256,256]{1,0:T(8,128)(2,1)S(1)}, u32[]{:S(2)}, u32[]{:S(2)}) collective-permute-start(bf16[256,256]{1,0:T(8,128)(2,1)S(1)} %get-tuple-element.44), channel_id=1, source_target_pairs={{0,1},{1,0},{2,3},{3,2},{4,5},{5,4},{6,7},{7,6},{8,9},{9,8},{10,11... | collective-permute-start | bytes 393224 | tf_op jit(solution)/shard_map/ppermute | solution.py:433
  54.0 4.6 %collective-permute-start.25 = (bf16[512,256]{1,0:T(8,128)(2,1)S(1)}, bf16[512,256]{1,0:T(8,128)(2,1)S(1)}, u32[]{:S(2)}, u32[]{:S(2)}) collective-permute-start(bf16[512,256]{1,0:T(8,128)(2,1)S(1)} %get-tuple-element.58), channel_id=1, source_target_pairs={{0,1},{1,0},{2,3},{3,2},{4,5},{5,4},{6,7},{7,6},{8,9},{9,8},{10,11... | collective-permute-start | bytes 786440 | tf_op jit(solution)/shard_map/ppermute | solution.py:433
  57.5 7.6 %collective-permute-start.19 = (bf16[256,256]{1,0:T(8,128)(2,1)S(1)}, bf16[256,256]{1,0:T(8,128)(2,1)S(1)}, u32[]{:S(2)}, u32[]{:S(2)}) collective-permute-start(bf16[256,256]{1,0:T(8,128)(2,1)S(1)} %get-tuple-element.48), channel_id=1, source_target_pairs={{0,1},{1,0},{2,3},{3,2},{4,5},{5,4},{6,7},{7,6},{8,9},{9,8},{10,11... | collective-permute-start | bytes 393224 | tf_op jit(solution)/shard_map/ppermute | solution.py:434
  58.0 2.2 %collective-permute-start.20 = (bf16[256,256]{1,0:T(8,128)(2,1)S(1)}, bf16[256,256]{1,0:T(8,128)(2,1)S(1)}, u32[]{:S(2)}, u32[]{:S(2)}) collective-permute-start(bf16[256,256]{1,0:T(8,128)(2,1)S(1)} %get-tuple-element.50), channel_id=1, source_target_pairs={{0,1},{1,0},{2,3},{3,2},{4,5},{5,4},{6,7},{7,6},{8,9},{9,8},{10,11... | collective-permute-start | bytes 393224 | tf_op jit(solution)/shard_map/ppermute | solution.py:433
  58.1 14.5 %collective-permute-start.24 = (bf16[512,256]{1,0:T(8,128)(2,1)S(1)}, bf16[512,256]{1,0:T(8,128)(2,1)S(1)}, u32[]{:S(2)}, u32[]{:S(2)}) collective-permute-start(bf16[512,256]{1,0:T(8,128)(2,1)S(1)} %get-tuple-element.56), channel_id=1, source_target_pairs={{0,1},{1,0},{2,3},{3,2},{4,5},{5,4},{6,7},{7,6},{8,9},{9,8},{10,11... | collective-permute-start | bytes 786440 | tf_op jit(solution)/shard_map/ppermute | solution.py:434
  58.5 14.3 %copy-start.9 = (s32[1,48,128]{2,1,0:T(8,128)S(1)}, s32[1,48,128]{2,1,0:T(8,128)}, u32[]{:S(2)}) copy-start(s32[1,48,128]{2,1,0:T(8,128)} %param.22) | copy-start | bytes 73732
  58.6 6.4 %collective-permute-start.17 = (bf16[256,256]{1,0:T(8,128)(2,1)S(1)}, bf16[256,256]{1,0:T(8,128)(2,1)S(1)}, u32[]{:S(2)}, u32[]{:S(2)}) collective-permute-start(bf16[256,256]{1,0:T(8,128)(2,1)S(1)} %add_convert_fusion.2), channel_id=1, source_target_pairs={{0,2},{2,0},{1,3},{3,1},{4,6},{6,4},{5,7},{7,5},{8,10},{10,8},{9,1... | collective-permute-start | bytes 393224 | tf_op jit(solution)/shard_map/ppermute | solution.py:436
  60.2 12.4 %collective-permute-start.26 = (bf16[512,256]{1,0:T(8,128)(2,1)S(1)}, bf16[512,256]{1,0:T(8,128)(2,1)S(1)}, u32[]{:S(2)}, u32[]{:S(2)}) collective-permute-start(bf16[512,256]{1,0:T(8,128)(2,1)S(1)} %add_convert_fusion), channel_id=1, source_target_pairs={{0,2},{2,0},{1,3},{3,1},{4,6},{6,4},{5,7},{7,5},{8,10},{10,8},{9,1... | collective-permute-start | bytes 786440 | tf_op jit(solution)/shard_map/ppermute | solution.py:436
  60.9 11.6 %collective-permute-start.21 = (bf16[256,256]{1,0:T(8,128)(2,1)S(1)}, bf16[256,256]{1,0:T(8,128)(2,1)S(1)}, u32[]{:S(2)}, u32[]{:S(2)}) collective-permute-start(bf16[256,256]{1,0:T(8,128)(2,1)S(1)} %add_convert_fusion.1), channel_id=1, source_target_pairs={{0,2},{2,0},{1,3},{3,1},{4,6},{6,4},{5,7},{7,5},{8,10},{10,8},{9,1... | collective-permute-start | bytes 393224 | tf_op jit(solution)/shard_map/ppermute | solution.py:436
  72.8 3.1 %copy-start.10 = (f32[1,48,128]{2,1,0:T(8,128)S(1)}, f32[1,48,128]{2,1,0:T(8,128)}, u32[]{:S(2)}) copy-start(f32[1,48,128]{2,1,0:T(8,128)} %param.24) | copy-start | bytes 73732
  76.4 11.5 %collective-permute-start.27 = (bf16[512,256]{1,0:T(8,128)(2,1)S(1)}, bf16[512,256]{1,0:T(8,128)(2,1)S(1)}, u32[]{:S(2)}, u32[]{:S(2)}) collective-permute-start(bf16[512,256]{1,0:T(8,128)(2,1)S(1)} %get-tuple-element.61), channel_id=1, source_target_pairs={{0,4},{4,0},{8,12},{12,8},{16,20},{20,16},{24,28},{28,24},{1,5},{5... | collective-permute-start | bytes 786440 | tf_op jit(solution)/shard_map/ppermute | solution.py:218
  77.9 10.0 %collective-permute-start.28 = (bf16[512,256]{1,0:T(8,128)(2,1)S(1)}, bf16[512,256]{1,0:T(8,128)(2,1)S(1)}, u32[]{:S(2)}, u32[]{:S(2)}) collective-permute-start(bf16[512,256]{1,0:T(8,128)(2,1)S(1)} %get-tuple-element.62), channel_id=1, source_target_pairs={{0,16},{4,8},{8,4},{12,28},{16,0},{20,24},{24,20},{28,12},{1,17},{... | collective-permute-start | bytes 786440 | tf_op jit(solution)/shard_map/ppermute | solution.py:218
  79.5 2.6 %copy-start.11 = (s32[1,48,128]{2,1,0:T(8,128)S(1)}, s32[1,48,128]{2,1,0:T(8,128)}, u32[]{:S(2)}) copy-start(s32[1,48,128]{2,1,0:T(8,128)} %param.23) | copy-start | bytes 73732

commit v5 on v4

--- a/solution.py
+++ b/solution.py
@@ -15,18 +15,19 @@
 STEP = 4
 BLOCK = 256
 NEG = -1e30
+LOG2E = 1.4426950408889634
 BF = jnp.bfloat16
 F32 = jnp.float32
 
 
-def call(body, outs, args, flops, scratch=(), spare=8, space=pltpu.VMEM, limit=None):
+def call(body, outs, args, flops, scratch=(), spare=8, space=pltpu.VMEM, out_space=pltpu.VMEM, limit=None):
     moved = sum(a.size * a.dtype.itemsize for a in args)
     moved += sum(o.size * o.dtype.itemsize for o in outs)
     return pl.pallas_call(
         body,
         out_shape=tuple(outs),
         in_specs=[pl.BlockSpec(memory_space=space)] * len(args),
-        out_specs=tuple(pl.BlockSpec(memory_space=pltpu.VMEM) for _ in outs),
+        out_specs=tuple(pl.BlockSpec(memory_space=out_space) for _ in outs),
         scratch_shapes=list(scratch),
         cost_estimate=pl.CostEstimate(flops=flops, bytes_accessed=moved, transcendentals=0),
         compiler_params=pltpu.CompilerParams(vmem_limit_bytes=limit or moved + spare * 1024 * 1024),
@@ -37,10 +38,13 @@
     return jnp.transpose(jnp.broadcast_to(row, (TILE, TILE)))
 
 
-def picks(rows_ref, first, base, source_rows):
-    tiles = [column(rows_ref[pl.ds(first + i, 1), :] - base) for i in range(STEP)]
-    cols = jnp.concatenate(tiles, axis=0)
-    cols = cols.astype(jnp.int16)
+def columns(rows_ref, first):
+    tiles = [column(rows_ref[pl.ds(first + i, 1), :]) for i in range(STEP)]
+    return jnp.concatenate(tiles, axis=0).astype(jnp.int16)
+
+
+def picks(cols, base, source_rows):
+    cols = cols - jnp.asarray(base, jnp.int32).astype(jnp.int16)
     lane = lax.broadcasted_iota(jnp.int32, cols.shape, 1).astype(jnp.int16)
     tiles = []
     for j in range(source_rows // TILE):
@@ -49,13 +53,11 @@
     return jnp.concatenate(tiles, axis=1)
 
 
-def picked(src_ref, first, sources, bases):
+def picked(cols, sources, bases):
     total = None
     for source_ref, base in zip(sources, bases):
         part = jnp.dot(
-            picks(src_ref, first, base, source_ref.shape[0]),
-            source_ref[...],
-            preferred_element_type=F32,
+            picks(cols, base, source_ref.shape[0]), source_ref[...], preferred_element_type=F32
         )
         total = part if total is None else total + part
     return total
@@ -104,32 +106,64 @@
         for k in range(out.shape[0] // edges):
             at = slice(k * edges, (k + 1) * edges)
             first = outward(which, side) + k * STEP
-            rows = picked(src_ref, first, sources, bases)
+            rows = picked(columns(src_ref, first), sources, bases)
             if before is not None:
                 rows = rows + before[which][at, :].astype(F32)
             out[at, :] = rows.astype(BF) if weight_ref is None else scaled(rows, weight_ref, first)
 
 
 def fetch_side_body(side, *refs):
-    sources, outs, held, sems = refs[:3], refs[3:5], refs[5:8], refs[8]
-    copies = [pltpu.make_async_copy(a, b, sems.at[i]) for i, (a, b) in enumerate(zip(sources, held))]
-    for copy in copies:
-        copy.start()
-    for copy in copies:
-        copy.wait()
-    sides(side, held[0], held[1], held[2:], (0,), outs)
-
-
-def locals_(start, src_ref, weight_ref, sources, bases, out_ref, before_ref=None):
+    (src_ref, weight_ref, source_ref), outs, refs = refs[:3], refs[3:5], refs[5:]
+    src, weight, source, *made, sems = refs
+    half = source_ref.shape[0] // 2
+    loads = [
+        pltpu.make_async_copy(src_ref, src, sems.at[0]),
+        pltpu.make_async_copy(weight_ref, weight, sems.at[1]),
+    ]
+    for i in range(2):
+        at = slice(i * half, (i + 1) * half)
+        loads.append(pltpu.make_async_copy(source_ref.at[at, :], source.at[at, :], sems.at[2 + i]))
+    for load in loads:
+        load.start()
+    loads[0].wait()
     edges = STEP * TILE
-    pair = 2
+    firsts = [
+        (which, k, outward(which, side) + k * STEP)
+        for which, value_ref in enumerate(made)
+        for k in range(value_ref.shape[0] // edges)
+    ]
+    cols = [columns(src, first) for _, _, first in firsts]
+    loads[1].wait()
+    totals = [None] * len(firsts)
+    for i in range(2):
+        loads[2 + i].wait()
+        at = slice(i * half, (i + 1) * half)
+        for n, col in enumerate(cols):
+            part = picked(col, (source.at[at, :],), (i * half,))
+            totals[n] = part if totals[n] is None else totals[n] + part
+    stores = []
+    for (which, k, first), total in zip(firsts, totals):
+        made[which][k * edges : (k + 1) * edges, :] = scaled(total, weight, first)
+        if (k + 1) * edges == made[which].shape[0]:
+            stores.append(pltpu.make_async_copy(made[which], outs[which], sems.at[4 + which]))
+            stores[-1].start()
+    for store in stores:
+        store.wait()
+
+
+def locals_(start, src_ref, weight_ref, sources, bases, out_ref, before_ref, keep_ref, kept_ref):
+    edges = STEP * TILE
+    pair = 5 if out_ref.shape[0] % (5 * edges) == 0 else 2
 
     def step(k, carry):
         for i in range(pair):
             n = k * pair + i
             at = pl.ds(pl.multiple_of(n * edges, edges), edges)
             first = start + n * STEP
-            rows = picked(src_ref, first, sources, bases)
+            cols = columns(src_ref, first) if kept_ref is None else kept_ref[at, :]
+            if keep_ref is not None:
+                keep_ref[at, :] = cols
+            rows = picked(cols, sources, bases)
             if before_ref is not None:
                 rows = rows + before_ref[at, :].astype(F32)
             out_ref[at, :] = rows.astype(BF) if weight_ref is None else scaled(rows, weight_ref, first)
@@ -139,7 +173,7 @@
 
 
 def gather_body(start, src_ref, weight_ref, source_ref, out_ref):
-    locals_(start, src_ref, weight_ref, (source_ref,), (0,), out_ref)
+    locals_(start, src_ref, weight_ref, (source_ref,), (0,), out_ref, None, None, None)
 
 
 def lands(rows_ref, tiles, base, target_rows, there=None):
@@ -204,12 +238,12 @@
         row = at + lax.broadcasted_iota(jnp.int32, got.shape, 0)
         value = grid_ref[from_, :].astype(F32) + got
         out_ref[here, :] = jnp.where(row < count_ref[0, 0], value, 0.0).astype(BF)
-    for unit, unit_ref in zip(UNITS, hiddens):
-        for k, start in enumerate(unit_starts(unit, count)):
-
-            @pl.when(start == step * BLOCK)
-            def _():
-                hidden_ref[...] = unit_ref[k * BLOCK : (k + 1) * BLOCK, :]
+    for c, chunk_ref in enumerate(hiddens):
+        n = WIN // BLOCK
+
+        @pl.when(step // n == block_of(c, count))
+        def _():
+            hidden_ref[...] = chunk_ref[pl.ds(pl.multiple_of(step % n * BLOCK, BLOCK), BLOCK), :]
 
 
 def swapped(first, second):
@@ -301,7 +335,7 @@
         out = jnp.dot(normed_ref[at, :], w_ref[...], preferred_element_type=F32)
         for pair in range(q_ref.shape[1] // TILE):
             a, b, c = [out[:, (3 * pair + i) * TILE : (3 * pair + i + 1) * TILE] for i in range(3)]
-            q = pltpu.roll(jnp.where(lane < HD, a, b), HD, 1)
+            q = pltpu.roll(jnp.where(lane < HD, a, b), HD, 1) * (HD**-0.5 * LOG2E)
             q_ref[at, pair * TILE : (pair + 1) * TILE] = q.astype(BF)
             kv_ref[at, 2 * pair * TILE : (2 * pair + 1) * TILE] = jnp.where(lane < HD, b, a).astype(BF)
             kv_ref[at, (2 * pair + 1) * TILE : (2 * pair + 2) * TILE] = c.astype(BF)
@@ -343,7 +377,7 @@
 
 
 def query_of(q_ref, pair, half):
-    q = q_ref[:, pair * TILE : (pair + 1) * TILE] * BF(HD**-0.5)
+    q = q_ref[:, pair * TILE : (pair + 1) * TILE]
     keep = (lane_ids() >= HD) if half == 0 else (lane_ids() < HD)
     return jnp.where(keep, q, jnp.zeros_like(q))
 
@@ -357,19 +391,6 @@
     for s in scores[1:]:
         peak = jnp.maximum(peak, s)
     return jnp.max(peak, axis=1, keepdims=True)
-
-
-def weighed(scores, peak, keys):
-    probs = [jnp.exp(s - peak) for s in scores]
-    total = probs[0]
-    for p in probs[1:]:
-        total = total + p
-    mixed = jnp.dot(
-        jnp.concatenate([p.astype(BF) for p in probs], axis=1),
-        jnp.concatenate(keys, axis=0),
-        preferred_element_type=F32,
-    )
-    return jnp.sum(total, axis=1, keepdims=True), mixed
 
 
 def attend_body(which, b, q_ref, *refs):
@@ -379,20 +400,35 @@
     inner_mask = jnp.where(ahead <= 0, 0.0, NEG).astype(F32)
     outer_mask = jnp.where(ahead >= 0, bias, NEG).astype(F32)
     left = lane_ids() < HD
-    for pair in range(q_ref.shape[1] // TILE):
-        outs = []
-        for half in range(2):
-            cols = slice((2 * pair + half) * TILE, (2 * pair + half + 1) * TILE)
-            q = query_of(q_ref, pair, half)
-            keys = [ref[:, cols] for ref in refs]
-            scores = [scored(q, key) for key in keys]
-            scores[0] = scores[0] + inner_mask
-            scores[4] = scores[4] + outer_mask
-            if b == 1:
-                scores[3] = scores[3] + bias
-            total, mixed = weighed(scores, peak_of(scores), keys)
-            outs.append(mixed / total)
-        out_ref[:, pair * TILE : (pair + 1) * TILE] = jnp.where(left, outs[0], outs[1]).astype(BF)
+    jobs = [(pair, half) for pair in range(q_ref.shape[1] // TILE) for half in range(2)]
+
+    def scores_of(pair, half):
+        cols = slice((2 * pair + half) * TILE, (2 * pair + half + 1) * TILE)
+        q = query_of(q_ref, pair, half)
+        keys = [ref[:, cols] for ref in refs]
+        scores = [scored(q, key) for key in keys]
+        scores[0] = scores[0] + inner_mask
+        scores[4] = scores[4] + outer_mask
+        if b == 1:
+            scores[3] = scores[3] + bias
+        return keys, scores
+
+    outs = []
+    ready = scores_of(*jobs[0])
+    for n, (pair, half) in enumerate(jobs):
+        keys, scores = ready
+        if n + 1 < len(jobs):
+            ready = scores_of(*jobs[n + 1])
+        peak = peak_of(scores)
+        probs = jnp.concatenate([jnp.exp2(s - peak).astype(BF) for s in scores], axis=1)
+        keep = left if half == 0 else jnp.logical_not(left)
+        values = [jnp.where(keep, key, jnp.ones_like(key)) for key in keys]
+        outs.append(jnp.dot(probs, jnp.concatenate(values, axis=0), preferred_element_type=F32))
+        if half:
+            sums = pltpu.roll(jnp.where(left, outs[1], outs[0]), HD, 1)
+            mixed = jnp.where(left, outs[0], outs[1])
+            out_ref[:, pair * TILE : (pair + 1) * TILE] = (mixed / sums).astype(BF)
+            outs = []
 
 
 def down_body(parts, n, *refs):
@@ -436,52 +472,62 @@
     return [own, near_got, lax.ppermute(far_sum, "mp", SWAP)]
 
 
-def settle_body(n, *refs):
-    latents, adds, out = refs[:n], refs[n:-1], refs[-1]
-    for k in range(n):
+def settle_body(unit, *refs):
+    n = len(unit)
+    latents, (*adds, out) = refs[:n], refs[n:]
+    if out.shape[0] > n * BLOCK:
+        earlier_ref, *adds = adds
+        other = spot(PIECES[unit[0]][0], 1 - PIECES[unit[0]][1])
+        out[pl.ds(pl.multiple_of(other, BLOCK), BLOCK), :] = earlier_ref[...]
+    for k, g in enumerate(unit):
         at = slice(k * BLOCK, (k + 1) * BLOCK)
         total = adds[0][at, :].astype(F32)
         for term in adds[1:]:
             total = total + term[at, :].astype(F32)
-        out[at, :] = (latents[k][...].astype(F32) + total).astype(BF)
-
-
-def unit_starts(unit, count):
-    return [start_of(*PIECES[g], count) for g in unit]
-
-
-def unit_sources(unit, hidden_ref):
-    return [hidden_ref.at[k * BLOCK : (k + 1) * BLOCK, :] for k in range(len(unit))]
-
-
-def collect_body(side, units, count, part, weighted, earlier, src_ref, *refs):
-    weight_ref, refs = (refs[0], refs[1:]) if weighted else (None, refs)
-    hiddens, refs = refs[: len(units)], refs[len(units) :]
-    n = {"sides": 2, "local": 1, "all": 3}[part]
-    before, outs = refs[: n * earlier], refs[n * earlier :]
-    before = list(before) or [None] * n
-    sources, bases = [], []
-    for unit, hidden_ref in zip(units, hiddens):
-        sources += unit_sources(unit, hidden_ref)
-        bases += unit_starts(unit, count)
-    if part != "local":
-        sides(side, src_ref, weight_ref, sources, bases, outs[:2], before[:2] if earlier else None)
-    if part != "sides":
-        locals_(2 * side, src_ref, weight_ref, sources, bases, outs[-1], before[-1])
-
-
-def collect(side, units, count, part, edges, hiddens, before):
-    features = hiddens[0].shape[1]
-    out = jax.ShapeDtypeStruct((side * TILE, features), BF)
-    local = jax.ShapeDtypeStruct(((edges[0].shape[0] - 2 * side) * TILE, features), BF)
-    outs = {"sides": [out, out], "local": [local], "all": [out, out, local]}[part]
+        start = 0 if out.shape[0] == BLOCK else spot(*PIECES[g])
+        spots = pl.ds(pl.multiple_of(start, BLOCK), BLOCK) if out.shape[0] > BLOCK else slice(None)
+        out[spots, :] = (latents[k][...].astype(F32) + total).astype(BF)
+
+
+def leave_body(side, c, count, src_ref, *refs):
+    last = c == count - 1
+    weight_ref, refs = (refs[0], refs[1:]) if last else (None, refs)
+    hidden_ref, before, outs = refs[:1], refs[1:-2], refs[-2:]
+    sides(side, src_ref, weight_ref, hidden_ref, (block_of(c, count) * WIN,), outs, before or None)
+
+
+def stay_body(side, c, count, src_ref, *refs):
+    base = (block_of(c, count) * WIN,)
+    if c == count - 1:
+        weight_ref, hidden_ref, before_ref, kept_ref, out_ref = refs
+        locals_(
+            2 * side, src_ref, weight_ref, (hidden_ref,), base, out_ref, before_ref, None, kept_ref
+        )
+    else:
+        hidden_ref, out_ref, keep_ref = refs
+        locals_(2 * side, src_ref, None, (hidden_ref,), base, out_ref, None, keep_ref, None)
+
+
+def leaving(side, c, count, args, hidden, before):
+    out = jax.ShapeDtypeStruct((side * TILE, hidden.shape[1]), BF)
     return call(
-        functools.partial(
-            collect_body, side, units, count, part, len(edges) > 1, 1 if before else 0
-        ),
+        functools.partial(leave_body, side, c, count),
+        (out, out),
+        (*args, hidden, *before),
+        4 * side * TILE * hidden.size,
+    )
+
+
+def staying(side, c, count, args, hidden, before):
+    edges = (args[0].shape[0] - 2 * side) * TILE
+    outs = [jax.ShapeDtypeStruct((edges, hidden.shape[1]), BF)]
+    if not before:
+        outs.append(jax.ShapeDtypeStruct((edges, TILE), jnp.int16))
+    return call(
+        functools.partial(stay_body, side, c, count),
         outs,
-        (*edges, *hiddens, *before),
-        2 * sum(h.size for h in hiddens) * sum(o.shape[0] for o in outs),
+        (*args, hidden, *before),
+        2 * edges * hidden.size,
     )
 
 
@@ -515,19 +561,20 @@
     src, dst, wts = enc_src_rows[0], enc_dst_rows[0], enc_weight[0]
     out = jax.ShapeDtypeStruct((ESIDE * TILE, features), BF)
     args = (src, wts, grid_latent)
-    leaving = call(
+    out = call(
         functools.partial(fetch_side_body, ESIDE),
         (out, out),
         args,
         4 * ESIDE * TILE * grid_latent.size,
         scratch=[
-            *(pltpu.VMEM(a.shape, a.dtype) for a in args),
-            pltpu.SemaphoreType.DMA((len(args),)),
+            *(pltpu.VMEM(a.shape, a.dtype) for a in (*args, out, out)),
+            pltpu.SemaphoreType.DMA((6,)),
         ],
         space=pltpu.HBM,
+        out_space=pltpu.HBM,
         limit=60 * 1024 * 1024,
     )
-    arrived = swapped(*leaving)
+    arrived = swapped(*out)
     moved = gathered(src, wts, grid_latent, ESIDE)
     total = spread(dst, moved, hid_rows, ESIDE)
     latents, gathers = [], []
@@ -577,7 +624,7 @@
         attended.append(att)
     src, dst, wts = dec_src_rows[0], dec_dst_rows[0], dec_weight[0]
     hiddens = []
-    for unit in UNITS:
+    for u, unit in enumerate(UNITS):
         size = len(unit) * BLOCK
         outs = call(
             functools.partial(down_body, parts, len(unit)),
@@ -592,18 +639,20 @@
             2 * size * (w_out.size + w_down.size),
         )
         sums = reduce_parts(outs, split)
+        earlier = hiddens[-1:] if u == len(UNITS) - 1 else []
         (hidden,) = call(
-            functools.partial(settle_body, len(unit)),
-            (jax.ShapeDtypeStruct((size, features), BF),),
-            (*(latents[g] for g in unit), *sums),
+            functools.partial(settle_body, unit),
+            (jax.ShapeDtypeStruct((size + len(earlier) * BLOCK, features), BF),),
+            (*(latents[g] for g in unit), *earlier, *sums),
             4 * size * features,
         )
         hiddens.append(hidden)
-    before = collect(DSIDE, UNITS[:1], count, "all", (src,), hiddens[:1], ())
+    hiddens = [hiddens[0], hiddens[-1]]
+    before = leaving(DSIDE, 0, count, (src,), hiddens[0], ())
+    kept = staying(DSIDE, 0, count, (src,), hiddens[0], ())
     args = (src, wts)
-    leaving = collect(DSIDE, UNITS[1:], count, "sides", args, hiddens[1:], before[:2])
-    arrived = swapped(*leaving)
-    (moved,) = collect(DSIDE, UNITS[1:], count, "local", args, hiddens[1:], before[2:])
+    arrived = swapped(*leaving(DSIDE, 1, count, args, hiddens[1], before))
+    (moved,) = staying(DSIDE, 1, count, args, hiddens[1], kept)
     total = spread(dst, moved, grid_latent.shape[0], DSIDE)
     return settled(DSIDE, count, grid_count[None, :], dst, *arrived, total, grid_latent, hiddens)
 

time: 91.1 us -> 86.5 us (0.950)
  Pallas kernels: 46.5 us -> 43.2 us
  waiting for transfers between devices: 20.1 us -> 17.8 us
  starting transfers between devices: 22.3 us -> 23.3 us
    pallas_call x29 -> x30, Pallas kernels: 43.5 us -> 40.3 us  [call(): pl.pallas_call(body, out_shape=tuple(outs), in_specs=[pl.BlockSpec(memory...]
    ppermute x4, waiting for transfers between devices: 9.5 us -> 7.69 us  [gather(): far = lax.ppermute(rows, 'mp', SWAP)]
    ppermute x4, starting transfers between devices: 4.31 us -> 5.38 us  [shards(): outer.append(lax.ppermute(part, ('ens', 'seq'), links[c]))]
  transfers between devices with their start and end apart: 29 -> 29, of which waited for: 8 -> 6; matrix products, arithmetic and copies ran while one was open for 0% -> 0% of each run, Pallas kernels for 40% -> 39%
where the time goes in v5:
time: 86.5 us; the launch traced here: 86.3 us
  Pallas kernels  43.2 us (50%)
  starting transfers between devices  23.3 us (27%)
  waiting for transfers between devices  17.8 us (21%)
  between operations  1.79 us (2%)
    pallas_call x30, Pallas kernels, call(): pl.pallas_call(body, out_shape=tuple(outs), in_specs=[pl.BlockSpec(memory...  40.3 us
    ppermute x3, waiting for transfers between devices, reduce_parts(): return [own, near_got, lax.ppermute(far_sum, 'mp', SWAP)]  9.41 us
    ppermute x4, waiting for transfers between devices, gather(): far = lax.ppermute(rows, 'mp', SWAP)  7.69 us
    ppermute x4, starting transfers between devices, swapped(): return (lax.ppermute(first, axes, one), lax.ppermute(second, axes, two))  7.07 us
    ppermute x4, starting transfers between devices, shards(): outer.append(lax.ppermute(part, ('ens', 'seq'), links[c]))  5.38 us
    ppermute x4, starting transfers between devices, gather(): far = lax.ppermute(rows, 'mp', SWAP)  4.31 us
    ppermute x3, starting transfers between devices, reduce_parts(): return [own, near_got, lax.ppermute(far_sum, 'mp', SWAP)]  3.71 us
    pallas_call x1, Pallas kernels, settled(): pl.pallas_call(functools.partial(grid_body, side, count), grid=(steps,),...  2.98 us
  transfers between devices with their start and end apart: 29, of which 6 were waited for; matrix products, arithmetic and copies ran while one was open for 0% of the time, Pallas kernels for 39%

profile of v5, /device:TPU:0, one launch (start us, length us, event | category | flops | bytes accessed | tf_op | source)
XLA Modules:
  0.0 86.3 jit_solution(17019429717324460775)
XLA Ops:
  0.7 3.4 %shard_map.167 = (bf16[512,256]{1,0:T(8,128)(2,1)}, bf16[512,256]{1,0:T(8,128)(2,1)}) custom-call(s32[32,128]{1,0:T(8,128)} %bitcast.35, f32[32,128]{1,0:T(8,128)} %bitcast.37, bf16[2048,256]{1,0:T(8,128)(2,1)} %grid_ref.1), custom_call_target="tpu_custom_call" | custom-call | flops 1073741824 | bytes 1605632 | tf_op jit(solution)/shard_map/pallas_call | solution.py:26
  4.1 3.1 %collective-permute-start = (bf16[512,256]{1,0:T(8,128)(2,1)}, bf16[512,256]{1,0:T(8,128)(2,1)S(1)}, u32[]{:S(2)}, u32[]{:S(2)}) collective-permute-start(bf16[512,256]{1,0:T(8,128)(2,1)} %get-tuple-element.34), channel_id=1, source_target_pairs={{0,4},{4,0},{8,12},{12,8},{16,20},{20,16},{24,28},{28,24},{1,5},{5... | collective-permute-start | bytes 786440 | tf_op jit(solution)/shard_map/ppermute | solution.py:252
  7.2 1.5 %collective-permute-start.1 = (bf16[512,256]{1,0:T(8,128)(2,1)}, bf16[512,256]{1,0:T(8,128)(2,1)S(1)}, u32[]{:S(2)}, u32[]{:S(2)}) collective-permute-start(bf16[512,256]{1,0:T(8,128)(2,1)} %get-tuple-element.35), channel_id=1, source_target_pairs={{0,16},{4,8},{8,4},{12,28},{16,0},{20,24},{24,20},{28,12},{1,17},{... | collective-permute-start | bytes 786440 | tf_op jit(solution)/shard_map/ppermute | solution.py:252
  8.7 4.0 %shard_map.168.local_ref = bf16[3072,256]{1,0:T(8,128)(2,1)S(1)} custom-call(s32[32,128]{1,0:T(8,128)S(1)} %bitcast.36, f32[32,128]{1,0:T(8,128)S(1)} %bitcast.38, bf16[2048,256]{1,0:T(8,128)(2,1)S(1)} %copy-done.5), custom_call_target="tpu_custom_call" | custom-call | flops 3221225472 | bytes 2654208 | tf_op jit(solution)/shard_map/pallas_call | solution.py:26
  12.7 0.0 copy-start.2
  12.7 1.8 %shard_map.169.total_ref = f32[1024,256]{1,0:T(8,128)S(1)} custom-call(s32[32,128]{1,0:T(8,128)S(1)} %bitcast.11, bf16[3072,256]{1,0:T(8,128)(2,1)S(1)} %shard_map.168.local_ref), custom_call_target="tpu_custom_call" | custom-call | flops 1610612736 | bytes 2637824 | tf_op jit(solution)/shard_map/pallas_call | solution.py:26
  14.5 0.7 collective-permute-done.1.second_ref
  15.2 0.3 shard_map.175.refs_0_
  15.5 1.6 %collective-permute-start.9 = (bf16[256,256]{1,0:T(8,128)(2,1)S(1)}, bf16[256,256]{1,0:T(8,128)(2,1)S(1)}, u32[]{:S(2)}, u32[]{:S(2)}) collective-permute-start(bf16[256,256]{1,0:T(8,128)(2,1)S(1)} %shard_map.175.refs_0_), channel_id=1, source_target_pairs={{0,2},{2,0},{1,3},{3,1},{4,6},{6,4},{5,7},{7,5},{8,10},{10,8},{9,1... | collective-permute-start | bytes 393224 | tf_op jit(solution)/shard_map/ppermute | solution.py:459
  17.1 0.3 shard_map.170.refs_0_
  17.4 0.0 copy-start.1
  17.4 0.6 collective-permute-start.12
  18.0 0.3 shard_map.173.refs_0_.refs_1_
  18.3 1.6 %collective-permute-start.6 = (bf16[256,256]{1,0:T(8,128)(2,1)S(1)}, bf16[256,256]{1,0:T(8,128)(2,1)S(1)}, u32[]{:S(2)}, u32[]{:S(2)}) collective-permute-start(bf16[256,256]{1,0:T(8,128)(2,1)S(1)} %shard_map.173.refs_0_.refs_1_), channel_id=1, source_target_pairs={{0,2},{2,0},{1,3},{3,1},{4,6},{6,4},{5,7},{7,5},{8,10},{10,8},{9,1... | collective-permute-start | bytes 393224 | tf_op jit(solution)/shard_map/ppermute | solution.py:459
  19.9 0.3 shard_map.171.refs_0_
  20.2 0.6 collective-permute-start.3
  20.8 0.5 collective-permute-start.10
  21.3 2.5 %collective-permute-done.12.refs_2_ = bf16[256,256]{1,0:T(8,128)(2,1)S(1)} collective-permute-done((bf16[256,256]{1,0:T(8,128)(2,1)S(1)}, bf16[256,256]{1,0:T(8,128)(2,1)S(1)}, u32[]{:S(2)}, u32[]{:S(2)}) %collective-permute-start.12) | collective-permute-done | bytes 131104 | tf_op jit(solution)/shard_map/ppermute | solution.py:459
  23.8 2.8 %collective-permute-done.6.refs_2_ = bf16[256,256]{1,0:T(8,128)(2,1)S(1)} collective-permute-done((bf16[256,256]{1,0:T(8,128)(2,1)S(1)}, bf16[256,256]{1,0:T(8,128)(2,1)S(1)}, u32[]{:S(2)}, u32[]{:S(2)}) %collective-permute-start.6) | collective-permute-done | bytes 131104 | tf_op jit(solution)/shard_map/ppermute | solution.py:459
  26.6 2.3 %collective-permute-done.3.refs_2_ = bf16[256,256]{1,0:T(8,128)(2,1)S(1)} collective-permute-done((bf16[256,256]{1,0:T(8,128)(2,1)S(1)}, bf16[256,256]{1,0:T(8,128)(2,1)S(1)}, u32[]{:S(2)}, u32[]{:S(2)}) %collective-permute-start.3) | collective-permute-done | bytes 131104 | tf_op jit(solution)/shard_map/ppermute | solution.py:459
  29.0 0.5 collective-permute-start.2
  29.5 0.1 collective-permute-start.4
  29.6 1.0 %shard_map.176 = (bf16[256,1024]{1,0:T(8,128)(2,1)S(1)}, bf16[256,256]{1,0:T(8,128)(2,1)S(1)}, bf16[256,512]{1,0:T(8,128)(2,1)S(1)}) custom-call(bf16[256,256]{1,0:T(8,128)(2,1)S(1)} %shard_map.175.refs_0_, bf16[256,256]{1,0:T(8,128)(2,1)S(1)} %collective-permute-done.8.refs_1_, bf16[256,256]{1,0:T(8,128)(2,1)S(1)} %collective-permute-done.9.refs_2_, ...), custom_call_target="tpu_custom_call" | custom-call | flops 402653184 | bytes 3018752 | tf_op jit(solution)/shard_map/pallas_call | solution.py:26
  30.6 1.5 %collective-permute-start.23 = (bf16[256,512]{1,0:T(8,128)(2,1)S(1)}, bf16[256,512]{1,0:T(8,128)(2,1)S(1)}, u32[]{:S(2)}, u32[]{:S(2)}) collective-permute-start(bf16[256,512]{1,0:T(8,128)(2,1)S(1)} %get-tuple-element.38.refs_1_.refs_0_.refs_2_), channel_id=1, source_target_pairs={{0,4},{4,0},{8,12},{12,8},{16,20},{20,16},{24,28},{28,24},{1,5},{5... | collective-permute-start | bytes 786440 | tf_op jit(solution)/shard_map/ppermute | solution.py:605
  32.0 1.0 %shard_map.177 = (bf16[256,1024]{1,0:T(8,128)(2,1)S(1)}, bf16[256,256]{1,0:T(8,128)(2,1)S(1)}, bf16[256,512]{1,0:T(8,128)(2,1)S(1)}) custom-call(bf16[256,256]{1,0:T(8,128)(2,1)S(1)} %shard_map.170.refs_0_, bf16[256,256]{1,0:T(8,128)(2,1)S(1)} %collective-permute-done.11.refs_1_, bf16[256,256]{1,0:T(8,128)(2,1)S(1)} %collective-permute-done.12.refs_2_, ...), custom_call_target="tpu_custom_call" | custom-call | flops 402653184 | bytes 3018752 | tf_op jit(solution)/shard_map/pallas_call | solution.py:26
  33.1 1.6 %collective-permute-start.14 = (bf16[256,512]{1,0:T(8,128)(2,1)S(1)}, bf16[256,512]{1,0:T(8,128)(2,1)S(1)}, u32[]{:S(2)}, u32[]{:S(2)}) collective-permute-start(bf16[256,512]{1,0:T(8,128)(2,1)S(1)} %get-tuple-element.40.refs_3_.refs_2_.refs_0_), channel_id=1, source_target_pairs={{0,16},{4,8},{8,4},{12,28},{16,0},{20,24},{24,20},{28,12},{1,17},{... | collective-permute-start | bytes 786440 | tf_op jit(solution)/shard_map/ppermute | solution.py:605
  34.6 1.0 %shard_map.174 = (bf16[256,1024]{1,0:T(8,128)(2,1)S(1)}, bf16[256,256]{1,0:T(8,128)(2,1)S(1)}, bf16[256,512]{1,0:T(8,128)(2,1)S(1)}) custom-call(bf16[256,256]{1,0:T(8,128)(2,1)S(1)} %shard_map.173.refs_0_.refs_1_, bf16[256,256]{1,0:T(8,128)(2,1)S(1)} %collective-permute-done.5.refs_1_, bf16[256,256]{1,0:T(8,128)(2,1)S(1)} %collective-permute-done.6.refs_2_, ...), custom_call_target="tpu_custom_call" | custom-call | flops 402653184 | bytes 3018752 | tf_op jit(solution)/shard_map/pallas_call | solution.py:26
  35.6 0.7 collective-permute-start.22
  36.4 1.0 %shard_map.172 = (bf16[256,1024]{1,0:T(8,128)(2,1)S(1)}, bf16[256,256]{1,0:T(8,128)(2,1)S(1)}, bf16[256,512]{1,0:T(8,128)(2,1)S(1)}) custom-call(bf16[256,256]{1,0:T(8,128)(2,1)S(1)} %shard_map.171.refs_0_, bf16[256,256]{1,0:T(8,128)(2,1)S(1)} %collective-permute-done.2.refs_1_, bf16[256,256]{1,0:T(8,128)(2,1)S(1)} %collective-permute-done.3.refs_2_, ...), custom_call_target="tpu_custom_call" | custom-call | flops 402653184 | bytes 3018752 | tf_op jit(solution)/shard_map/pallas_call | solution.py:26
  37.4 1.6 %collective-permute-start.18 = (bf16[256,512]{1,0:T(8,128)(2,1)S(1)}, bf16[256,512]{1,0:T(8,128)(2,1)S(1)}, u32[]{:S(2)}, u32[]{:S(2)}) collective-permute-start(bf16[256,512]{1,0:T(8,128)(2,1)S(1)} %get-tuple-element.39.refs_2_.refs_1_.refs_0_), channel_id=1, source_target_pairs={{0,16},{4,8},{8,4},{12,28},{16,0},{20,24},{24,20},{28,12},{1,17},{... | collective-permute-start | bytes 786440 | tf_op jit(solution)/shard_map/ppermute | solution.py:605
  39.0 0.8 shard_map.188.refs_2_
  39.8 0.8 shard_map.189.refs_3_
  40.6 0.8 shard_map.183.refs_1_
  41.5 0.8 shard_map.179.refs_1_
  42.3 2.0 %shard_map.178.refs_0_ = bf16[256,256]{1,0:T(8,128)(2,1)S(1)} custom-call(bf16[256,256]{1,0:T(8,128)(2,1)S(1)} %get-tuple-element.36.q_ref, bf16[256,512]{1,0:T(8,128)(2,1)S(1)} %get-tuple-element.37.refs_0_.refs_3_.refs_2_, bf16[256,512]{1,0:T(8,128)(2,1)S(1)} %get-tuple-element.38.refs_1_.refs_0_.refs_2_, ...), custom_call_target="tpu_custom_call" | custom-call | flops 335544320 | bytes 1572864 | tf_op jit(solution)/shard_map/pallas_call | solution.py:26
  44.4 0.9 %shard_map.180 = (bf16[256,256]{1,0:T(8,128)(2,1)S(1)}, bf16[256,256]{1,0:T(8,128)(2,1)S(1)}, bf16[256,256]{1,0:T(8,128)(2,1)S(1)}, bf16[256,256]{1,0:T(8,128)(2,1)S(1)}) custom-call(bf16[256,256]{1,0:T(8,128)(2,1)S(1)} %shard_map.178.refs_0_, bf16[256,1024]{1,0:T(8,128)(2,1)S(1)} %shard_map.179.refs_1_, bf16[256,1024]{1,0:T(8,128)(2,1)S(1)} %copy-done.4, ...), custom_call_target="tpu_custom_call" | custom-call | flops 671088640 | bytes 3805184 | tf_op jit(solution)/shard_map/pallas_call | solution.py:26
  45.3 0.1 collective-permute-start.16
  45.4 2.2 %shard_map.186.refs_0_ = bf16[256,256]{1,0:T(8,128)(2,1)S(1)} custom-call(bf16[256,256]{1,0:T(8,128)(2,1)S(1)} %get-tuple-element.52.q_ref, bf16[256,512]{1,0:T(8,128)(2,1)S(1)} %get-tuple-element.40.refs_3_.refs_2_.refs_0_, bf16[256,512]{1,0:T(8,128)(2,1)S(1)} %get-tuple-element.39.refs_2_.refs_1_.refs_0_, ...), custom_call_target="tpu_custom_call" | custom-call | flops 335544320 | bytes 1572864 | tf_op jit(solution)/shard_map/pallas_call | solution.py:26
  47.7 2.0 %shard_map.187.refs_1_ = bf16[256,256]{1,0:T(8,128)(2,1)S(1)} custom-call(bf16[256,256]{1,0:T(8,128)(2,1)S(1)} %get-tuple-element.53.q_ref, bf16[256,512]{1,0:T(8,128)(2,1)S(1)} %get-tuple-element.39.refs_2_.refs_1_.refs_0_, bf16[256,512]{1,0:T(8,128)(2,1)S(1)} %get-tuple-element.38.refs_1_.refs_0_.refs_2_, ...), custom_call_target="tpu_custom_call" | custom-call | flops 335544320 | bytes 1572864 | tf_op jit(solution)/shard_map/pallas_call | solution.py:26
  49.7 1.6 %shard_map.190 = (bf16[512,256]{1,0:T(8,128)(2,1)S(1)}, bf16[512,256]{1,0:T(8,128)(2,1)S(1)}, bf16[512,256]{1,0:T(8,128)(2,1)S(1)}, bf16[512,256]{1,0:T(8,128)(2,1)S(1)}) custom-call(bf16[256,256]{1,0:T(8,128)(2,1)S(1)} %shard_map.186.refs_0_, bf16[256,256]{1,0:T(8,128)(2,1)S(1)} %shard_map.187.refs_1_, bf16[256,1024]{1,0:T(8,128)(2,1)S(1)} %shard_map.188.refs_2_, ...), custom_call_target="tpu_custom_call" | custom-call | flops 1342177280 | bytes 4984832 | tf_op jit(solution)/shard_map/pallas_call | solution.py:26
  51.3 0.6 collective-permute-start.25
  51.8 0.1 collective-permute-start.24
  51.9 2.0 %shard_map.182.refs_0_ = bf16[256,256]{1,0:T(8,128)(2,1)S(1)} custom-call(bf16[256,256]{1,0:T(8,128)(2,1)S(1)} %get-tuple-element.46.q_ref, bf16[256,512]{1,0:T(8,128)(2,1)S(1)} %get-tuple-element.38.refs_1_.refs_0_.refs_2_, bf16[256,512]{1,0:T(8,128)(2,1)S(1)} %get-tuple-element.39.refs_2_.refs_1_.refs_0_, ...), custom_call_target="tpu_custom_call" | custom-call | flops 335544320 | bytes 1572864 | tf_op jit(solution)/shard_map/pallas_call | solution.py:26
  53.9 0.9 %shard_map.184 = (bf16[256,256]{1,0:T(8,128)(2,1)S(1)}, bf16[256,256]{1,0:T(8,128)(2,1)S(1)}, bf16[256,256]{1,0:T(8,128)(2,1)S(1)}, bf16[256,256]{1,0:T(8,128)(2,1)S(1)}) custom-call(bf16[256,256]{1,0:T(8,128)(2,1)S(1)} %shard_map.182.refs_0_, bf16[256,1024]{1,0:T(8,128)(2,1)S(1)} %shard_map.183.refs_1_, bf16[256,1024]{1,0:T(8,128)(2,1)S(1)} %copy-done.4, ...), custom_call_target="tpu_custom_call" | custom-call | flops 671088640 | bytes 3805184 | tf_op jit(solution)/shard_map/pallas_call | solution.py:26
  54.8 0.5 collective-permute-start.20
  55.3 0.1 collective-permute-start.19
  55.4 0.4 collective-permute-start.15
  55.9 1.6 %collective-permute-start.17 = (bf16[256,256]{1,0:T(8,128)(2,1)S(1)}, bf16[256,256]{1,0:T(8,128)(2,1)S(1)}, u32[]{:S(2)}, u32[]{:S(2)}) collective-permute-start(bf16[256,256]{1,0:T(8,128)(2,1)S(1)} %add_convert_fusion.2), channel_id=1, source_target_pairs={{0,2},{2,0},{1,3},{3,1},{4,6},{6,4},{5,7},{7,5},{8,10},{10,8},{9,1... | collective-permute-start | bytes 393224 | tf_op jit(solution)/shard_map/ppermute | solution.py:472
  57.5 0.1 add_convert_fusion
  57.5 0.6 collective-permute-start.26
  58.2 1.6 %collective-permute-start.21 = (bf16[256,256]{1,0:T(8,128)(2,1)S(1)}, bf16[256,256]{1,0:T(8,128)(2,1)S(1)}, u32[]{:S(2)}, u32[]{:S(2)}) collective-permute-start(bf16[256,256]{1,0:T(8,128)(2,1)S(1)} %add_convert_fusion.1), channel_id=1, source_target_pairs={{0,2},{2,0},{1,3},{3,1},{4,6},{6,4},{5,7},{7,5},{8,10},{10,8},{9,1... | collective-permute-start | bytes 393224 | tf_op jit(solution)/shard_map/ppermute | solution.py:472
  60.4 1.9 %collective-permute-done.17.refs_3_ = bf16[256,256]{1,0:T(8,128)(2,1)S(1)} collective-permute-done((bf16[256,256]{1,0:T(8,128)(2,1)S(1)}, bf16[256,256]{1,0:T(8,128)(2,1)S(1)}, u32[]{:S(2)}, u32[]{:S(2)}) %collective-permute-start.17) | collective-permute-done | bytes 131104 | tf_op jit(solution)/shard_map/ppermute | solution.py:472
  62.3 0.1 shard_map.181.refs_1_
  62.4 7.5 %collective-permute-done.21.refs_4_ = bf16[256,256]{1,0:T(8,128)(2,1)S(1)} collective-permute-done((bf16[256,256]{1,0:T(8,128)(2,1)S(1)}, bf16[256,256]{1,0:T(8,128)(2,1)S(1)}, u32[]{:S(2)}, u32[]{:S(2)}) %collective-permute-start.21) | collective-permute-done | bytes 131104 | tf_op jit(solution)/shard_map/ppermute | solution.py:472
  69.9 0.1 shard_map.185.refs_1_
  70.0 0.1 shard_map.191.refs_0_
  70.1 1.9 %shard_map.194 = (bf16[5120,256]{1,0:T(8,128)(2,1)S(1)}, s16[5120,128]{1,0:T(8,128)(2,1)S(1)}) custom-call(s32[48,128]{1,0:T(8,128)S(1)} %bitcast.24, bf16[512,256]{1,0:T(8,128)(2,1)S(1)} %shard_map.191.refs_0_), custom_call_target="tpu_custom_call" | custom-call | flops 1342177280 | bytes 4218880 | tf_op jit(solution)/shard_map/pallas_call | solution.py:26
  72.0 0.5 shard_map.192
  72.6 0.5 shard_map.193
  73.1 1.7 %collective-permute-start.27 = (bf16[512,256]{1,0:T(8,128)(2,1)S(1)}, bf16[512,256]{1,0:T(8,128)(2,1)S(1)}, u32[]{:S(2)}, u32[]{:S(2)}) collective-permute-start(bf16[512,256]{1,0:T(8,128)(2,1)S(1)} %get-tuple-element.62), channel_id=1, source_target_pairs={{0,4},{4,0},{8,12},{12,8},{16,20},{20,16},{24,28},{28,24},{1,5},{5... | collective-permute-start | bytes 786440 | tf_op jit(solution)/shard_map/ppermute | solution.py:252
  74.7 0.8 collective-permute-start.28
  75.5 2.0 %shard_map.195.local_ref = bf16[5120,256]{1,0:T(8,128)(2,1)S(1)} custom-call(s32[48,128]{1,0:T(8,128)S(1)} %bitcast.27, f32[48,128]{1,0:T(8,128)S(1)} %bitcast.29, bf16[512,256]{1,0:T(8,128)(2,1)S(1)} %shard_map.185.refs_1_, bf16[5120,256]{1,0:T(8,128)(2,1)S(1)} %get-tuple-element.64.refs_2_, s16[5120,128]{1,0:T(8,128)(2,1)S(1)} %get-tuple-element.65.refs_3_), custom_call_target="tpu_custom_call" | custom-call | flops 1342177280 | bytes 6864896 | tf_op jit(solution)/shard_map/pallas_call | solution.py:26
  77.5 5.8 %shard_map.196.total_ref = f32[2048,256]{1,0:T(8,128)S(1)} custom-call(s32[48,128]{1,0:T(8,128)S(1)} %bitcast.30, bf16[5120,256]{1,0:T(8,128)(2,1)S(1)} %shard_map.195.local_ref), custom_call_target="tpu_custom_call" | custom-call | flops 5368709120 | bytes 4743168 | tf_op jit(solution)/shard_map/pallas_call | solution.py:26
  83.4 3.0 %grid.1 = (bf16[1024,256]{1,0:T(8,128)(2,1)}, bf16[2048,256]{1,0:T(8,128)(2,1)}) custom-call(s32[1,1]{1,0:T(1,128)} %bitcast.10.count_ref, s32[48,128]{1,0:T(8,128)S(1)} %bitcast.31, bf16[512,256]{1,0:T(8,128)(2,1)S(1)} %collective-permute-done.27.first_ref, bf16[512,256]{1,0:T(8,128)(2,1)S(1)} %collective-permute-done.28.second_ref, ...), custom_call_target="tpu_custom_call" | custom-call | flops 1073741824 | bytes 4194304 | tf_op jit(solution)/shard_map/grid/pallas_call | solution.py:281
  (58 shorter events, 0.2 us)
Async XLA Ops:
  0.6 8.1 %copy-start.13 = (s32[1,32,128]{2,1,0:T(8,128)S(1)}, s32[1,32,128]{2,1,0:T(8,128)}, u32[]{:S(2)}) copy-start(s32[1,32,128]{2,1,0:T(8,128)} %param.19) | copy-start | bytes 49156
  0.6 8.1 %copy-start.14 = (f32[1,32,128]{2,1,0:T(8,128)S(1)}, f32[1,32,128]{2,1,0:T(8,128)}, u32[]{:S(2)}) copy-start(f32[1,32,128]{2,1,0:T(8,128)} %param.21) | copy-start | bytes 49156
  0.6 8.1 %copy-start.5 = (bf16[2048,256]{1,0:T(8,128)(2,1)S(1)}, bf16[2048,256]{1,0:T(8,128)(2,1)}, u32[]{:S(2)}) copy-start(bf16[2048,256]{1,0:T(8,128)(2,1)} %grid_ref.1) | copy-start | bytes 3145732
  4.1 10.4 %collective-permute-start = (bf16[512,256]{1,0:T(8,128)(2,1)}, bf16[512,256]{1,0:T(8,128)(2,1)S(1)}, u32[]{:S(2)}, u32[]{:S(2)}) collective-permute-start(bf16[512,256]{1,0:T(8,128)(2,1)} %get-tuple-element.34), channel_id=1, source_target_pairs={{0,4},{4,0},{8,12},{12,8},{16,20},{20,16},{24,28},{28,24},{1,5},{5... | collective-permute-start | bytes 786440 | tf_op jit(solution)/shard_map/ppermute | solution.py:252
  7.2 5.5 %copy-start.6 = (s32[1,32,128]{2,1,0:T(8,128)S(1)}, s32[1,32,128]{2,1,0:T(8,128)}, u32[]{:S(2)}) copy-start(s32[1,32,128]{2,1,0:T(8,128)} %param.20) | copy-start | bytes 49156
  7.2 8.0 %collective-permute-start.1 = (bf16[512,256]{1,0:T(8,128)(2,1)}, bf16[512,256]{1,0:T(8,128)(2,1)S(1)}, u32[]{:S(2)}, u32[]{:S(2)}) collective-permute-start(bf16[512,256]{1,0:T(8,128)(2,1)} %get-tuple-element.35), channel_id=1, source_target_pairs={{0,16},{4,8},{8,4},{12,28},{16,0},{20,24},{24,20},{28,12},{1,17},{... | collective-permute-start | bytes 786440 | tf_op jit(solution)/shard_map/ppermute | solution.py:252
  12.7 2.5 %copy-start.2 = (bf16[1024,256]{1,0:T(8,128)(2,1)S(1)}, bf16[1024,256]{1,0:T(8,128)(2,1)}, u32[]{:S(2)}) copy-start(bf16[1024,256]{1,0:T(8,128)(2,1)} %embed_ref.7) | copy-start | bytes 1572868
  15.5 5.3 %collective-permute-start.9 = (bf16[256,256]{1,0:T(8,128)(2,1)S(1)}, bf16[256,256]{1,0:T(8,128)(2,1)S(1)}, u32[]{:S(2)}, u32[]{:S(2)}) collective-permute-start(bf16[256,256]{1,0:T(8,128)(2,1)S(1)} %shard_map.175.refs_0_), channel_id=1, source_target_pairs={{0,2},{2,0},{1,3},{3,1},{4,6},{6,4},{5,7},{7,5},{8,10},{10,8},{9,1... | collective-permute-start | bytes 393224 | tf_op jit(solution)/shard_map/ppermute | solution.py:459
  17.0 3.7 %collective-permute-start.8 = (bf16[256,256]{1,0:T(8,128)(2,1)S(1)}, bf16[256,256]{1,0:T(8,128)(2,1)S(1)}, u32[]{:S(2)}, u32[]{:S(2)}) collective-permute-start(bf16[256,256]{1,0:T(8,128)(2,1)S(1)} %shard_map.175.refs_0_), channel_id=1, source_target_pairs={{0,1},{1,0},{2,3},{3,2},{4,5},{5,4},{6,7},{7,6},{8,9},{9,8},{10,11... | collective-permute-start | bytes 393224 | tf_op jit(solution)/shard_map/ppermute | solution.py:460
  17.4 12.2 %copy-start.1 = (bf16[1024,768]{1,0:T(8,128)(2,1)S(1)}, bf16[1024,768]{1,0:T(8,128)(2,1)}, u32[]{:S(2)}) copy-start(bf16[1024,768]{1,0:T(8,128)(2,1)} %refs_5_.8) | copy-start | bytes 4718596
  17.4 12.2 %copy-start.7 = (f32[1024]{0:T(1024)S(1)}, f32[1024]{0:T(1024)}, u32[]{:S(2)}) copy-start(f32[1024]{0:T(1024)} %param.25) | copy-start | bytes 12292
  17.4 6.4 %collective-permute-start.12 = (bf16[256,256]{1,0:T(8,128)(2,1)S(1)}, bf16[256,256]{1,0:T(8,128)(2,1)S(1)}, u32[]{:S(2)}, u32[]{:S(2)}) collective-permute-start(bf16[256,256]{1,0:T(8,128)(2,1)S(1)} %shard_map.170.refs_0_), channel_id=1, source_target_pairs={{0,2},{2,0},{1,3},{3,1},{4,6},{6,4},{5,7},{7,5},{8,10},{10,8},{9,1... | collective-permute-start | bytes 393224 | tf_op jit(solution)/shard_map/ppermute | solution.py:459
  18.3 8.3 %collective-permute-start.6 = (bf16[256,256]{1,0:T(8,128)(2,1)S(1)}, bf16[256,256]{1,0:T(8,128)(2,1)S(1)}, u32[]{:S(2)}, u32[]{:S(2)}) collective-permute-start(bf16[256,256]{1,0:T(8,128)(2,1)S(1)} %shard_map.173.refs_0_.refs_1_), channel_id=1, source_target_pairs={{0,2},{2,0},{1,3},{3,1},{4,6},{6,4},{5,7},{7,5},{8,10},{10,8},{9,1... | collective-permute-start | bytes 393224 | tf_op jit(solution)/shard_map/ppermute | solution.py:459
  20.2 8.8 %collective-permute-start.3 = (bf16[256,256]{1,0:T(8,128)(2,1)S(1)}, bf16[256,256]{1,0:T(8,128)(2,1)S(1)}, u32[]{:S(2)}, u32[]{:S(2)}) collective-permute-start(bf16[256,256]{1,0:T(8,128)(2,1)S(1)} %shard_map.171.refs_0_), channel_id=1, source_target_pairs={{0,2},{2,0},{1,3},{3,1},{4,6},{6,4},{5,7},{7,5},{8,10},{10,8},{9,1... | collective-permute-start | bytes 393224 | tf_op jit(solution)/shard_map/ppermute | solution.py:459
  20.8 8.2 %collective-permute-start.11 = (bf16[256,256]{1,0:T(8,128)(2,1)S(1)}, bf16[256,256]{1,0:T(8,128)(2,1)S(1)}, u32[]{:S(2)}, u32[]{:S(2)}) collective-permute-start(bf16[256,256]{1,0:T(8,128)(2,1)S(1)} %shard_map.170.refs_0_), channel_id=1, source_target_pairs={{0,1},{1,0},{2,3},{3,2},{4,5},{5,4},{6,7},{7,6},{8,9},{9,8},{10,11... | collective-permute-start | bytes 393224 | tf_op jit(solution)/shard_map/ppermute | solution.py:460
  20.8 8.7 %collective-permute-start.10 = (bf16[256,256]{1,0:T(8,128)(2,1)S(1)}, bf16[256,256]{1,0:T(8,128)(2,1)S(1)}, u32[]{:S(2)}, u32[]{:S(2)}) collective-permute-start(bf16[256,256]{1,0:T(8,128)(2,1)S(1)} %collective-permute-done.9.refs_2_), channel_id=1, source_target_pairs={{0,1},{1,0},{2,3},{3,2},{4,5},{5,4},{6,7},{7,6},{8,9},{9,8},{10,11... | collective-permute-start | bytes 393224 | tf_op jit(solution)/shard_map/ppermute | solution.py:461
  23.8 6.7 %collective-permute-start.13 = (bf16[256,256]{1,0:T(8,128)(2,1)S(1)}, bf16[256,256]{1,0:T(8,128)(2,1)S(1)}, u32[]{:S(2)}, u32[]{:S(2)}) collective-permute-start(bf16[256,256]{1,0:T(8,128)(2,1)S(1)} %collective-permute-done.12.refs_2_), channel_id=1, source_target_pairs={{0,1},{1,0},{2,3},{3,2},{4,5},{5,4},{6,7},{7,6},{8,9},{9,8},{10,11... | collective-permute-start | bytes 393224 | tf_op jit(solution)/shard_map/ppermute | solution.py:461
  26.6 6.4 %collective-permute-start.5 = (bf16[256,256]{1,0:T(8,128)(2,1)S(1)}, bf16[256,256]{1,0:T(8,128)(2,1)S(1)}, u32[]{:S(2)}, u32[]{:S(2)}) collective-permute-start(bf16[256,256]{1,0:T(8,128)(2,1)S(1)} %shard_map.173.refs_0_.refs_1_), channel_id=1, source_target_pairs={{0,1},{1,0},{2,3},{3,2},{4,5},{5,4},{6,7},{7,6},{8,9},{9,8},{10,11... | collective-permute-start | bytes 393224 | tf_op jit(solution)/shard_map/ppermute | solution.py:460
  29.0 5.7 %collective-permute-start.7 = (bf16[256,256]{1,0:T(8,128)(2,1)S(1)}, bf16[256,256]{1,0:T(8,128)(2,1)S(1)}, u32[]{:S(2)}, u32[]{:S(2)}) collective-permute-start(bf16[256,256]{1,0:T(8,128)(2,1)S(1)} %collective-permute-done.6.refs_2_), channel_id=1, source_target_pairs={{0,1},{1,0},{2,3},{3,2},{4,5},{5,4},{6,7},{7,6},{8,9},{9,8},{10,11... | collective-permute-start | bytes 393224 | tf_op jit(solution)/shard_map/ppermute | solution.py:461
  29.0 7.4 %collective-permute-start.2 = (bf16[256,256]{1,0:T(8,128)(2,1)S(1)}, bf16[256,256]{1,0:T(8,128)(2,1)S(1)}, u32[]{:S(2)}, u32[]{:S(2)}) collective-permute-start(bf16[256,256]{1,0:T(8,128)(2,1)S(1)} %shard_map.171.refs_0_), channel_id=1, source_target_pairs={{0,1},{1,0},{2,3},{3,2},{4,5},{5,4},{6,7},{7,6},{8,9},{9,8},{10,11... | collective-permute-start | bytes 393224 | tf_op jit(solution)/shard_map/ppermute | solution.py:460
  29.5 6.9 %collective-permute-start.4 = (bf16[256,256]{1,0:T(8,128)(2,1)S(1)}, bf16[256,256]{1,0:T(8,128)(2,1)S(1)}, u32[]{:S(2)}, u32[]{:S(2)}) collective-permute-start(bf16[256,256]{1,0:T(8,128)(2,1)S(1)} %collective-permute-done.3.refs_2_), channel_id=1, source_target_pairs={{0,1},{1,0},{2,3},{3,2},{4,5},{5,4},{6,7},{7,6},{8,9},{9,8},{10,11... | collective-permute-start | bytes 393224 | tf_op jit(solution)/shard_map/ppermute | solution.py:461
  30.6 17.1 %collective-permute-start.23 = (bf16[256,512]{1,0:T(8,128)(2,1)S(1)}, bf16[256,512]{1,0:T(8,128)(2,1)S(1)}, u32[]{:S(2)}, u32[]{:S(2)}) collective-permute-start(bf16[256,512]{1,0:T(8,128)(2,1)S(1)} %get-tuple-element.38.refs_1_.refs_0_.refs_2_), channel_id=1, source_target_pairs={{0,4},{4,0},{8,12},{12,8},{16,20},{20,16},{24,28},{28,24},{1,5},{5... | collective-permute-start | bytes 786440 | tf_op jit(solution)/shard_map/ppermute | solution.py:605
  33.0 5.9 %copy-start = (bf16[1024,1024]{1,0:T(8,128)(2,1)S(1)}, bf16[1024,1024]{1,0:T(8,128)(2,1)}, u32[]{:S(2)}) copy-start(bf16[1024,1024]{1,0:T(8,128)(2,1)} %w_ref.7) | copy-start | bytes 6291460
  33.0 5.9 %copy-start.8 = (s32[1024]{0:T(1024)S(1)}, s32[1024]{0:T(1024)}, u32[]{:S(2)}) copy-start(s32[1024]{0:T(1024)} %param.29) | copy-start | bytes 12292
  33.1 9.3 %collective-permute-start.14 = (bf16[256,512]{1,0:T(8,128)(2,1)S(1)}, bf16[256,512]{1,0:T(8,128)(2,1)S(1)}, u32[]{:S(2)}, u32[]{:S(2)}) collective-permute-start(bf16[256,512]{1,0:T(8,128)(2,1)S(1)} %get-tuple-element.40.refs_3_.refs_2_.refs_0_), channel_id=1, source_target_pairs={{0,16},{4,8},{8,4},{12,28},{16,0},{20,24},{24,20},{28,12},{1,17},{... | collective-permute-start | bytes 786440 | tf_op jit(solution)/shard_map/ppermute | solution.py:605
  35.6 9.8 %collective-permute-start.22 = (bf16[256,512]{1,0:T(8,128)(2,1)S(1)}, bf16[256,512]{1,0:T(8,128)(2,1)S(1)}, u32[]{:S(2)}, u32[]{:S(2)}) collective-permute-start(bf16[256,512]{1,0:T(8,128)(2,1)S(1)} %get-tuple-element.37.refs_0_.refs_3_.refs_2_), channel_id=1, source_target_pairs={{0,4},{4,0},{8,12},{12,8},{16,20},{20,16},{24,28},{28,24},{1,5},{5... | collective-permute-start | bytes 786440 | tf_op jit(solution)/shard_map/ppermute | solution.py:605
  37.4 14.6 %collective-permute-start.18 = (bf16[256,512]{1,0:T(8,128)(2,1)S(1)}, bf16[256,512]{1,0:T(8,128)(2,1)S(1)}, u32[]{:S(2)}, u32[]{:S(2)}) collective-permute-start(bf16[256,512]{1,0:T(8,128)(2,1)S(1)} %get-tuple-element.39.refs_2_.refs_1_.refs_0_), channel_id=1, source_target_pairs={{0,16},{4,8},{8,4},{12,28},{16,0},{20,24},{24,20},{28,12},{1,17},{... | collective-permute-start | bytes 786440 | tf_op jit(solution)/shard_map/ppermute | solution.py:605
  41.5 2.9 %copy-start.3 = (bf16[1024,1024]{1,0:T(8,128)(2,1)S(1)}, bf16[1024,1024]{1,0:T(8,128)(2,1)}, u32[]{:S(2)}) copy-start(bf16[1024,1024]{1,0:T(8,128)(2,1)} %refs_5_.9) | copy-start | bytes 6291460
  41.5 2.9 %copy-start.4 = (bf16[256,1024]{1,0:T(8,128)(2,1)S(1)}, bf16[256,1024]{1,0:T(8,128)(2,1)}, u32[]{:S(2)}) copy-start(bf16[256,1024]{1,0:T(8,128)(2,1)} %refs_4_.1) | copy-start | bytes 1572868
  41.5 2.9 %copy-start.12 = (s32[1024]{0:T(1024)S(1)}, s32[1024]{0:T(1024)}, u32[]{:S(2)}) copy-start(s32[1024]{0:T(1024)} %param.31) | copy-start | bytes 12292
  45.3 10.1 %collective-permute-start.16 = (bf16[256,256]{1,0:T(8,128)(2,1)S(1)}, bf16[256,256]{1,0:T(8,128)(2,1)S(1)}, u32[]{:S(2)}, u32[]{:S(2)}) collective-permute-start(bf16[256,256]{1,0:T(8,128)(2,1)S(1)} %get-tuple-element.45), channel_id=1, source_target_pairs={{0,1},{1,0},{2,3},{3,2},{4,5},{5,4},{6,7},{7,6},{8,9},{9,8},{10,11... | collective-permute-start | bytes 393224 | tf_op jit(solution)/shard_map/ppermute | solution.py:469
  51.3 4.6 %collective-permute-start.25 = (bf16[512,256]{1,0:T(8,128)(2,1)S(1)}, bf16[512,256]{1,0:T(8,128)(2,1)S(1)}, u32[]{:S(2)}, u32[]{:S(2)}) collective-permute-start(bf16[512,256]{1,0:T(8,128)(2,1)S(1)} %get-tuple-element.59), channel_id=1, source_target_pairs={{0,1},{1,0},{2,3},{3,2},{4,5},{5,4},{6,7},{7,6},{8,9},{9,8},{10,11... | collective-permute-start | bytes 786440 | tf_op jit(solution)/shard_map/ppermute | solution.py:469
  51.8 18.1 %collective-permute-start.24 = (bf16[512,256]{1,0:T(8,128)(2,1)S(1)}, bf16[512,256]{1,0:T(8,128)(2,1)S(1)}, u32[]{:S(2)}, u32[]{:S(2)}) collective-permute-start(bf16[512,256]{1,0:T(8,128)(2,1)S(1)} %get-tuple-element.57), channel_id=1, source_target_pairs={{0,1},{1,0},{2,3},{3,2},{4,5},{5,4},{6,7},{7,6},{8,9},{9,8},{10,11... | collective-permute-start | bytes 786440 | tf_op jit(solution)/shard_map/ppermute | solution.py:470
  54.8 2.7 %collective-permute-start.20 = (bf16[256,256]{1,0:T(8,128)(2,1)S(1)}, bf16[256,256]{1,0:T(8,128)(2,1)S(1)}, u32[]{:S(2)}, u32[]{:S(2)}) collective-permute-start(bf16[256,256]{1,0:T(8,128)(2,1)S(1)} %get-tuple-element.51), channel_id=1, source_target_pairs={{0,1},{1,0},{2,3},{3,2},{4,5},{5,4},{6,7},{7,6},{8,9},{9,8},{10,11... | collective-permute-start | bytes 393224 | tf_op jit(solution)/shard_map/ppermute | solution.py:469
  55.3 7.1 %collective-permute-start.19 = (bf16[256,256]{1,0:T(8,128)(2,1)S(1)}, bf16[256,256]{1,0:T(8,128)(2,1)S(1)}, u32[]{:S(2)}, u32[]{:S(2)}) collective-permute-start(bf16[256,256]{1,0:T(8,128)(2,1)S(1)} %get-tuple-element.49), channel_id=1, source_target_pairs={{0,1},{1,0},{2,3},{3,2},{4,5},{5,4},{6,7},{7,6},{8,9},{9,8},{10,11... | collective-permute-start | bytes 393224 | tf_op jit(solution)/shard_map/ppermute | solution.py:470
  55.4 2.8 %collective-permute-start.15 = (bf16[256,256]{1,0:T(8,128)(2,1)S(1)}, bf16[256,256]{1,0:T(8,128)(2,1)S(1)}, u32[]{:S(2)}, u32[]{:S(2)}) collective-permute-start(bf16[256,256]{1,0:T(8,128)(2,1)S(1)} %get-tuple-element.43), channel_id=1, source_target_pairs={{0,1},{1,0},{2,3},{3,2},{4,5},{5,4},{6,7},{7,6},{8,9},{9,8},{10,11... | collective-permute-start | bytes 393224 | tf_op jit(solution)/shard_map/ppermute | solution.py:470
  55.9 14.2 %copy-start.9 = (s32[1,48,128]{2,1,0:T(8,128)S(1)}, s32[1,48,128]{2,1,0:T(8,128)}, u32[]{:S(2)}) copy-start(s32[1,48,128]{2,1,0:T(8,128)} %param.22) | copy-start | bytes 73732
  55.9 6.4 %collective-permute-start.17 = (bf16[256,256]{1,0:T(8,128)(2,1)S(1)}, bf16[256,256]{1,0:T(8,128)(2,1)S(1)}, u32[]{:S(2)}, u32[]{:S(2)}) collective-permute-start(bf16[256,256]{1,0:T(8,128)(2,1)S(1)} %add_convert_fusion.2), channel_id=1, source_target_pairs={{0,2},{2,0},{1,3},{3,1},{4,6},{6,4},{5,7},{7,5},{8,10},{10,8},{9,1... | collective-permute-start | bytes 393224 | tf_op jit(solution)/shard_map/ppermute | solution.py:472
  57.5 12.4 %collective-permute-start.26 = (bf16[512,256]{1,0:T(8,128)(2,1)S(1)}, bf16[512,256]{1,0:T(8,128)(2,1)S(1)}, u32[]{:S(2)}, u32[]{:S(2)}) collective-permute-start(bf16[512,256]{1,0:T(8,128)(2,1)S(1)} %add_convert_fusion), channel_id=1, source_target_pairs={{0,2},{2,0},{1,3},{3,1},{4,6},{6,4},{5,7},{7,5},{8,10},{10,8},{9,1... | collective-permute-start | bytes 786440 | tf_op jit(solution)/shard_map/ppermute | solution.py:472
  58.2 11.7 %collective-permute-start.21 = (bf16[256,256]{1,0:T(8,128)(2,1)S(1)}, bf16[256,256]{1,0:T(8,128)(2,1)S(1)}, u32[]{:S(2)}, u32[]{:S(2)}) collective-permute-start(bf16[256,256]{1,0:T(8,128)(2,1)S(1)} %add_convert_fusion.1), channel_id=1, source_target_pairs={{0,2},{2,0},{1,3},{3,1},{4,6},{6,4},{5,7},{7,5},{8,10},{10,8},{9,1... | collective-permute-start | bytes 393224 | tf_op jit(solution)/shard_map/ppermute | solution.py:472
  70.1 2.4 %copy-start.10 = (f32[1,48,128]{2,1,0:T(8,128)S(1)}, f32[1,48,128]{2,1,0:T(8,128)}, u32[]{:S(2)}) copy-start(f32[1,48,128]{2,1,0:T(8,128)} %param.24) | copy-start | bytes 73732
  73.1 10.3 %collective-permute-start.27 = (bf16[512,256]{1,0:T(8,128)(2,1)S(1)}, bf16[512,256]{1,0:T(8,128)(2,1)S(1)}, u32[]{:S(2)}, u32[]{:S(2)}) collective-permute-start(bf16[512,256]{1,0:T(8,128)(2,1)S(1)} %get-tuple-element.62), channel_id=1, source_target_pairs={{0,4},{4,0},{8,12},{12,8},{16,20},{20,16},{24,28},{28,24},{1,5},{5... | collective-permute-start | bytes 786440 | tf_op jit(solution)/shard_map/ppermute | solution.py:252
  74.7 8.6 %collective-permute-start.28 = (bf16[512,256]{1,0:T(8,128)(2,1)S(1)}, bf16[512,256]{1,0:T(8,128)(2,1)S(1)}, u32[]{:S(2)}, u32[]{:S(2)}) collective-permute-start(bf16[512,256]{1,0:T(8,128)(2,1)S(1)} %get-tuple-element.63), channel_id=1, source_target_pairs={{0,16},{4,8},{8,4},{12,28},{16,0},{20,24},{24,20},{28,12},{1,17},{... | collective-permute-start | bytes 786440 | tf_op jit(solution)/shard_map/ppermute | solution.py:252
  75.5 2.0 %copy-start.11 = (s32[1,48,128]{2,1,0:T(8,128)S(1)}, s32[1,48,128]{2,1,0:T(8,128)}, u32[]{:S(2)}) copy-start(s32[1,48,128]{2,1,0:T(8,128)} %param.23) | copy-start | bytes 73732

commit v6 on v5

--- a/solution.py
+++ b/solution.py
@@ -20,14 +20,17 @@
 F32 = jnp.float32
 
 
-def call(body, outs, args, flops, scratch=(), spare=8, space=pltpu.VMEM, out_space=pltpu.VMEM, limit=None):
+def call(body, outs, args, flops, scratch=(), spare=8, space=pltpu.VMEM, out_space=pltpu.VMEM, last_space=None, limit=None):
     moved = sum(a.size * a.dtype.itemsize for a in args)
     moved += sum(o.size * o.dtype.itemsize for o in outs)
     return pl.pallas_call(
         body,
         out_shape=tuple(outs),
         in_specs=[pl.BlockSpec(memory_space=space)] * len(args),
-        out_specs=tuple(pl.BlockSpec(memory_space=out_space) for _ in outs),
+        out_specs=tuple(
+            pl.BlockSpec(memory_space=(out_space if i == 0 else last_space or out_space))
+            for i in range(len(outs))
+        ),
         scratch_shapes=list(scratch),
         cost_estimate=pl.CostEstimate(flops=flops, bytes_accessed=moved, transcendentals=0),
         compiler_params=pltpu.CompilerParams(vmem_limit_bytes=limit or moved + spare * 1024 * 1024),
@@ -153,7 +156,8 @@
 
 def locals_(start, src_ref, weight_ref, sources, bases, out_ref, before_ref, keep_ref, kept_ref):
     edges = STEP * TILE
-    pair = 5 if out_ref.shape[0] % (5 * edges) == 0 else 2
+    count = out_ref.shape[0] // edges
+    pair = max(n for n in range(1, 7) if count % n == 0)
 
     def step(k, carry):
         for i in range(pair):
@@ -169,7 +173,7 @@
             out_ref[at, :] = rows.astype(BF) if weight_ref is None else scaled(rows, weight_ref, first)
         return carry
 
-    lax.fori_loop(0, out_ref.shape[0] // (pair * edges), step, 0)
+    lax.fori_loop(0, count // pair, step, 0)
 
 
 def gather_body(start, src_ref, weight_ref, source_ref, out_ref):
@@ -188,16 +192,15 @@
 
 
 def landed(side, dst_ref, first_ref, second_ref, base, target_rows):
-    total = None
+    hits, got = [], []
     for which, got_ref in enumerate((first_ref, second_ref)):
         first = outward(which, side)
-        got = jnp.dot(
-            lands(dst_ref, [first + i for i in range(side)], base, target_rows, has_partner(which)),
-            got_ref[...],
-            preferred_element_type=F32,
-        )
-        total = got if total is None else total + got
-    return total
+        tiles = [first + i for i in range(side)]
+        hits.append(lands(dst_ref, tiles, base, target_rows, has_partner(which)))
+        got.append(got_ref[...])
+    return jnp.dot(
+        jnp.concatenate(hits, axis=1), jnp.concatenate(got, axis=0), preferred_element_type=F32
+    )
 
 
 def spread_body(side, dst_ref, local_ref, out_ref):
@@ -219,6 +222,18 @@
     return block_of(c, count) * WIN + spot(c, b)
 
 
+def spread_last_body(side, count, dst_ref, local_ref, *refs):
+    hiddens, (out_ref, hidden_ref, sems) = refs[:count], refs[count:]
+    copies = []
+    for c, chunk_ref in enumerate(hiddens):
+        at = pl.ds(pl.multiple_of(block_of(c, count) * WIN, WIN), WIN)
+        copies.append(pltpu.make_async_copy(chunk_ref, hidden_ref.at[at, :], sems.at[c]))
+        copies[-1].start()
+    spread_body(side, dst_ref, local_ref, out_ref)
+    for copy in copies:
+        copy.wait()
+
+
 def latent_body(side, c, b, count, dst_ref, first_ref, second_ref, total_ref, embed_ref, out_ref):
     at = pl.multiple_of(start_of(c, b, count), BLOCK)
     got = landed(side, dst_ref, first_ref, second_ref, at, BLOCK)
@@ -226,24 +241,15 @@
     out_ref[...] = (embed_ref[pl.ds(at, BLOCK), :].astype(F32) + got).astype(BF)
 
 
-def grid_body(side, count, count_ref, dst_ref, first_ref, second_ref, total_ref, grid_ref, *refs):
-    *hiddens, hidden_ref, out_ref = refs
+def grid_body(side, count_ref, dst_ref, first_ref, second_ref, total_ref, grid_ref, out_ref):
     rows = out_ref.shape[0]
     step = pl.program_id(0)
-    for h in range(rows // BLOCK):
-        at = pl.multiple_of(step * rows + h * BLOCK, BLOCK)
-        here = slice(h * BLOCK, (h + 1) * BLOCK)
-        from_ = pl.ds(at, BLOCK)
-        got = landed(side, dst_ref, first_ref, second_ref, at, BLOCK) + total_ref[from_, :]
-        row = at + lax.broadcasted_iota(jnp.int32, got.shape, 0)
-        value = grid_ref[from_, :].astype(F32) + got
-        out_ref[here, :] = jnp.where(row < count_ref[0, 0], value, 0.0).astype(BF)
-    for c, chunk_ref in enumerate(hiddens):
-        n = WIN // BLOCK
-
-        @pl.when(step // n == block_of(c, count))
-        def _():
-            hidden_ref[...] = chunk_ref[pl.ds(pl.multiple_of(step % n * BLOCK, BLOCK), BLOCK), :]
+    at = pl.multiple_of(step * rows, rows)
+    here = pl.ds(at, rows)
+    got = landed(side, dst_ref, first_ref, second_ref, at, rows) + total_ref[here, :]
+    row = at + lax.broadcasted_iota(jnp.int32, got.shape, 0)
+    value = grid_ref[here, :].astype(F32) + got
+    out_ref[...] = jnp.where(row < count_ref[:1, :1], value, 0.0).astype(BF)
 
 
 def swapped(first, second):
@@ -273,23 +279,16 @@
     return total
 
 
-def settled(side, count, grid_count, edge_dst, first, second, total, grid_latent, hiddens):
+def settled(side, grid_count, edge_dst, first, second, total, grid_latent):
     rows, features = grid_latent.shape
-    steps = sum(h.shape[0] for h in hiddens) // BLOCK
-    block = rows // steps
-    args = (grid_count, edge_dst, first, second, total, grid_latent, *hiddens)
+    block = 512
+    args = (grid_count, edge_dst, first, second, total, grid_latent)
     return pl.pallas_call(
-        functools.partial(grid_body, side, count),
-        grid=(steps,),
-        out_shape=(
-            jax.ShapeDtypeStruct((steps * BLOCK, features), BF),
-            jax.ShapeDtypeStruct((rows, features), BF),
-        ),
+        functools.partial(grid_body, side),
+        grid=(rows // block,),
+        out_shape=jax.ShapeDtypeStruct((rows, features), BF),
         in_specs=[pl.BlockSpec(memory_space=pltpu.VMEM)] * len(args),
-        out_specs=(
-            pl.BlockSpec((BLOCK, features), lambda i: (i, 0)),
-            pl.BlockSpec((block, features), lambda i: (i, 0)),
-        ),
+        out_specs=pl.BlockSpec((block, features), lambda i: (i, 0)),
         cost_estimate=pl.CostEstimate(
             flops=4 * side * TILE * grid_latent.size,
             bytes_accessed=8 * grid_latent.size,
@@ -325,9 +324,10 @@
     def step(k, carry):
         at = pl.ds(pl.multiple_of(k * block, block), block)
         values = [p[at, :].astype(F32) for p in pieces]
-        mean = sum(jnp.sum(v, axis=1, keepdims=True) for v in values) / total
+        mean = jnp.sum(sum(values[1:], values[0]), axis=1, keepdims=True) / total
         values = [v - mean for v in values]
-        var = sum(jnp.sum(v * v, axis=1, keepdims=True) for v in values) / total
+        squares = [v * v for v in values]
+        var = jnp.sum(sum(squares[1:], squares[0]), axis=1, keepdims=True) / total
         scale = lax.rsqrt(var + 1e-05)
         for i, v in enumerate(values):
             cols = pl.ds(pl.multiple_of(place(i, parts) * width, width), width)
@@ -653,8 +653,19 @@
     args = (src, wts)
     arrived = swapped(*leaving(DSIDE, 1, count, args, hiddens[1], before))
     (moved,) = staying(DSIDE, 1, count, args, hiddens[1], kept)
-    total = spread(dst, moved, grid_latent.shape[0], DSIDE)
-    return settled(DSIDE, count, grid_count[None, :], dst, *arrived, total, grid_latent, hiddens)
+    total, hidden_out = call(
+        functools.partial(spread_last_body, DSIDE, count),
+        (
+            jax.ShapeDtypeStruct(grid_latent.shape, F32),
+            jax.ShapeDtypeStruct(hidden_embed.shape, BF),
+        ),
+        (dst, moved, *hiddens),
+        2 * moved.size * grid_latent.shape[0],
+        scratch=[pltpu.SemaphoreType.DMA((count,))],
+        last_space=pltpu.HBM,
+    )
+    live = jnp.broadcast_to(grid_count[None, :], (8, TILE))
+    return hidden_out, settled(DSIDE, live, dst, *arrived, total, grid_latent)
 
 
 def solution(mesh):

time: 86.5 us -> 88.9 us (1.028)
  waiting for transfers between devices: 17.8 us -> 21.6 us
  starting transfers between devices: 23.3 us -> 22.3 us
    ppermute x4, waiting for transfers between devices: 7.69 us -> 9.5 us  [gather(): far = lax.ppermute(rows, 'mp', SWAP)]
    ppermute x4, waiting for transfers between devices: 0.01 us -> 1.48 us  [shards(): outer.append(lax.ppermute(part, ('ens', 'seq'), links[c]))]
    ppermute x4, starting transfers between devices: 5.38 us -> 4.31 us  [shards(): outer.append(lax.ppermute(part, ('ens', 'seq'), links[c]))]
  transfers between devices with their start and end apart: 29 -> 29, of which waited for: 6 -> 8; matrix products, arithmetic and copies ran while one was open for 0% -> 0% of each run, Pallas kernels for 39% -> 37%
where the time goes in v6:
time: 88.9 us; the launch traced here: 88.7 us
  Pallas kernels  42.8 us (48%)
  starting transfers between devices  22.3 us (25%)
  waiting for transfers between devices  21.6 us (24%)
  between operations  1.8 us (2%)
    pallas_call x30, Pallas kernels, call(): pl.pallas_call(body, out_shape=tuple(outs), in_specs=[pl.BlockSpec(memory...  40 us
    ppermute x4, waiting for transfers between devices, gather(): far = lax.ppermute(rows, 'mp', SWAP)  9.5 us
    ppermute x3, waiting for transfers between devices, reduce_parts(): return [own, near_got, lax.ppermute(far_sum, 'mp', SWAP)]  9.38 us
    ppermute x4, starting transfers between devices, swapped(): return (lax.ppermute(first, axes, one), lax.ppermute(second, axes, two))  7.66 us
    ppermute x4, starting transfers between devices, shards(): outer.append(lax.ppermute(part, ('ens', 'seq'), links[c]))  4.31 us
    ppermute x4, starting transfers between devices, gather(): far = lax.ppermute(rows, 'mp', SWAP)  4.25 us
    ppermute x3, starting transfers between devices, reduce_parts(): return [own, near_got, lax.ppermute(far_sum, 'mp', SWAP)]  3.73 us
    pallas_call x1, Pallas kernels, settled(): pl.pallas_call(functools.partial(grid_body, side), grid=(rows // block,),...  2.79 us
  transfers between devices with their start and end apart: 29, of which 8 were waited for; matrix products, arithmetic and copies ran while one was open for 0% of the time, Pallas kernels for 37%

profile of v6, /device:TPU:0, one launch (start us, length us, event | category | flops | bytes accessed | tf_op | source)
XLA Modules:
  0.0 88.7 jit_solution(9083897974496794557)
XLA Ops:
  0.7 3.4 %shard_map.167 = (bf16[512,256]{1,0:T(8,128)(2,1)}, bf16[512,256]{1,0:T(8,128)(2,1)}) custom-call(s32[32,128]{1,0:T(8,128)} %bitcast.35, f32[32,128]{1,0:T(8,128)} %bitcast.37, bf16[2048,256]{1,0:T(8,128)(2,1)} %grid_ref.1), custom_call_target="tpu_custom_call" | custom-call | flops 1073741824 | bytes 1605632 | tf_op jit(solution)/shard_map/pallas_call | solution.py:26
  4.1 3.1 %collective-permute-start = (bf16[512,256]{1,0:T(8,128)(2,1)}, bf16[512,256]{1,0:T(8,128)(2,1)S(1)}, u32[]{:S(2)}, u32[]{:S(2)}) collective-permute-start(bf16[512,256]{1,0:T(8,128)(2,1)} %get-tuple-element.36), channel_id=1, source_target_pairs={{0,4},{4,0},{8,12},{12,8},{16,20},{20,16},{24,28},{28,24},{1,5},{5... | collective-permute-start | bytes 786440 | tf_op jit(solution)/shard_map/ppermute | solution.py:258
  7.2 1.5 %collective-permute-start.1 = (bf16[512,256]{1,0:T(8,128)(2,1)}, bf16[512,256]{1,0:T(8,128)(2,1)S(1)}, u32[]{:S(2)}, u32[]{:S(2)}) collective-permute-start(bf16[512,256]{1,0:T(8,128)(2,1)} %get-tuple-element.37), channel_id=1, source_target_pairs={{0,16},{4,8},{8,4},{12,28},{16,0},{20,24},{24,20},{28,12},{1,17},{... | collective-permute-start | bytes 786440 | tf_op jit(solution)/shard_map/ppermute | solution.py:258
  8.7 3.5 %shard_map.168.local_ref = bf16[3072,256]{1,0:T(8,128)(2,1)S(1)} custom-call(s32[32,128]{1,0:T(8,128)S(1)} %bitcast.36, f32[32,128]{1,0:T(8,128)S(1)} %bitcast.38, bf16[2048,256]{1,0:T(8,128)(2,1)S(1)} %copy-done.5), custom_call_target="tpu_custom_call" | custom-call | flops 3221225472 | bytes 2654208 | tf_op jit(solution)/shard_map/pallas_call | solution.py:26
  12.2 1.8 %shard_map.169.total_ref = f32[1024,256]{1,0:T(8,128)S(1)} custom-call(s32[32,128]{1,0:T(8,128)S(1)} %bitcast.11, bf16[3072,256]{1,0:T(8,128)(2,1)S(1)} %shard_map.168.local_ref), custom_call_target="tpu_custom_call" | custom-call | flops 1610612736 | bytes 2637824 | tf_op jit(solution)/shard_map/pallas_call | solution.py:26
  14.0 1.2 %collective-permute-done.1.second_ref = bf16[512,256]{1,0:T(8,128)(2,1)S(1)} collective-permute-done((bf16[512,256]{1,0:T(8,128)(2,1)}, bf16[512,256]{1,0:T(8,128)(2,1)S(1)}, u32[]{:S(2)}, u32[]{:S(2)}) %collective-permute-start.1) | collective-permute-done | bytes 262176 | tf_op jit(solution)/shard_map/ppermute | solution.py:258
  15.2 0.3 shard_map.171.refs_0_
  15.5 0.1 collective-permute-start.2
  15.6 0.3 shard_map.170.refs_0_
  15.9 1.6 %collective-permute-start.12 = (bf16[256,256]{1,0:T(8,128)(2,1)S(1)}, bf16[256,256]{1,0:T(8,128)(2,1)S(1)}, u32[]{:S(2)}, u32[]{:S(2)}) collective-permute-start(bf16[256,256]{1,0:T(8,128)(2,1)S(1)} %shard_map.170.refs_0_), channel_id=1, source_target_pairs={{0,2},{2,0},{1,3},{3,1},{4,6},{6,4},{5,7},{7,5},{8,10},{10,8},{9,1... | collective-permute-start | bytes 393224 | tf_op jit(solution)/shard_map/ppermute | solution.py:459
  17.5 0.5 collective-permute-start.3
  18.0 0.3 shard_map.173.refs_0_.refs_1_
  18.3 1.6 %collective-permute-start.6 = (bf16[256,256]{1,0:T(8,128)(2,1)S(1)}, bf16[256,256]{1,0:T(8,128)(2,1)S(1)}, u32[]{:S(2)}, u32[]{:S(2)}) collective-permute-start(bf16[256,256]{1,0:T(8,128)(2,1)S(1)} %shard_map.173.refs_0_.refs_1_), channel_id=1, source_target_pairs={{0,2},{2,0},{1,3},{3,1},{4,6},{6,4},{5,7},{7,5},{8,10},{10,8},{9,1... | collective-permute-start | bytes 393224 | tf_op jit(solution)/shard_map/ppermute | solution.py:459
  19.9 0.3 shard_map.175.refs_0_
  20.2 0.6 collective-permute-start.9
  20.8 1.6 %collective-permute-done.12.refs_2_ = bf16[256,256]{1,0:T(8,128)(2,1)S(1)} collective-permute-done((bf16[256,256]{1,0:T(8,128)(2,1)S(1)}, bf16[256,256]{1,0:T(8,128)(2,1)S(1)}, u32[]{:S(2)}, u32[]{:S(2)}) %collective-permute-start.12) | collective-permute-done | bytes 131104 | tf_op jit(solution)/shard_map/ppermute | solution.py:459
  22.3 2.8 %collective-permute-done.3.refs_2_ = bf16[256,256]{1,0:T(8,128)(2,1)S(1)} collective-permute-done((bf16[256,256]{1,0:T(8,128)(2,1)S(1)}, bf16[256,256]{1,0:T(8,128)(2,1)S(1)}, u32[]{:S(2)}, u32[]{:S(2)}) %collective-permute-start.3) | collective-permute-done | bytes 131104 | tf_op jit(solution)/shard_map/ppermute | solution.py:459
  25.2 2.8 %collective-permute-done.6.refs_2_ = bf16[256,256]{1,0:T(8,128)(2,1)S(1)} collective-permute-done((bf16[256,256]{1,0:T(8,128)(2,1)S(1)}, bf16[256,256]{1,0:T(8,128)(2,1)S(1)}, u32[]{:S(2)}, u32[]{:S(2)}) %collective-permute-start.6) | collective-permute-done | bytes 131104 | tf_op jit(solution)/shard_map/ppermute | solution.py:459
  28.0 2.3 %collective-permute-done.9.refs_2_ = bf16[256,256]{1,0:T(8,128)(2,1)S(1)} collective-permute-done((bf16[256,256]{1,0:T(8,128)(2,1)S(1)}, bf16[256,256]{1,0:T(8,128)(2,1)S(1)}, u32[]{:S(2)}, u32[]{:S(2)}) %collective-permute-start.9) | collective-permute-done | bytes 131104 | tf_op jit(solution)/shard_map/ppermute | solution.py:459
  30.3 0.5 collective-permute-start.8
  30.8 0.1 collective-permute-start.10
  30.9 0.9 %shard_map.177 = (bf16[256,1024]{1,0:T(8,128)(2,1)S(1)}, bf16[256,256]{1,0:T(8,128)(2,1)S(1)}, bf16[256,512]{1,0:T(8,128)(2,1)S(1)}) custom-call(bf16[256,256]{1,0:T(8,128)(2,1)S(1)} %shard_map.170.refs_0_, bf16[256,256]{1,0:T(8,128)(2,1)S(1)} %collective-permute-done.11.refs_1_, bf16[256,256]{1,0:T(8,128)(2,1)S(1)} %collective-permute-done.12.refs_2_, ...), custom_call_target="tpu_custom_call" | custom-call | flops 402653184 | bytes 3018752 | tf_op jit(solution)/shard_map/pallas_call | solution.py:26
  31.9 1.6 %collective-permute-start.14 = (bf16[256,512]{1,0:T(8,128)(2,1)S(1)}, bf16[256,512]{1,0:T(8,128)(2,1)S(1)}, u32[]{:S(2)}, u32[]{:S(2)}) collective-permute-start(bf16[256,512]{1,0:T(8,128)(2,1)S(1)} %get-tuple-element.42.refs_3_.refs_2_.refs_0_), channel_id=1, source_target_pairs={{0,16},{4,8},{8,4},{12,28},{16,0},{20,24},{24,20},{28,12},{1,17},{... | collective-permute-start | bytes 786440 | tf_op jit(solution)/shard_map/ppermute | solution.py:605
  33.4 0.9 %shard_map.172 = (bf16[256,1024]{1,0:T(8,128)(2,1)S(1)}, bf16[256,256]{1,0:T(8,128)(2,1)S(1)}, bf16[256,512]{1,0:T(8,128)(2,1)S(1)}) custom-call(bf16[256,256]{1,0:T(8,128)(2,1)S(1)} %shard_map.171.refs_0_, bf16[256,256]{1,0:T(8,128)(2,1)S(1)} %collective-permute-done.2.refs_1_, bf16[256,256]{1,0:T(8,128)(2,1)S(1)} %collective-permute-done.3.refs_2_, ...), custom_call_target="tpu_custom_call" | custom-call | flops 402653184 | bytes 3018752 | tf_op jit(solution)/shard_map/pallas_call | solution.py:26
  34.4 0.6 collective-permute-start.18
  35.0 1.0 %shard_map.174 = (bf16[256,1024]{1,0:T(8,128)(2,1)S(1)}, bf16[256,256]{1,0:T(8,128)(2,1)S(1)}, bf16[256,512]{1,0:T(8,128)(2,1)S(1)}) custom-call(bf16[256,256]{1,0:T(8,128)(2,1)S(1)} %shard_map.173.refs_0_.refs_1_, bf16[256,256]{1,0:T(8,128)(2,1)S(1)} %collective-permute-done.5.refs_1_, bf16[256,256]{1,0:T(8,128)(2,1)S(1)} %collective-permute-done.6.refs_2_, ...), custom_call_target="tpu_custom_call" | custom-call | flops 402653184 | bytes 3018752 | tf_op jit(solution)/shard_map/pallas_call | solution.py:26
  36.0 1.5 %collective-permute-start.22 = (bf16[256,512]{1,0:T(8,128)(2,1)S(1)}, bf16[256,512]{1,0:T(8,128)(2,1)S(1)}, u32[]{:S(2)}, u32[]{:S(2)}) collective-permute-start(bf16[256,512]{1,0:T(8,128)(2,1)S(1)} %get-tuple-element.39.refs_0_.refs_3_.refs_2_), channel_id=1, source_target_pairs={{0,4},{4,0},{8,12},{12,8},{16,20},{20,16},{24,28},{28,24},{1,5},{5... | collective-permute-start | bytes 786440 | tf_op jit(solution)/shard_map/ppermute | solution.py:605
  37.4 1.0 %shard_map.176 = (bf16[256,1024]{1,0:T(8,128)(2,1)S(1)}, bf16[256,256]{1,0:T(8,128)(2,1)S(1)}, bf16[256,512]{1,0:T(8,128)(2,1)S(1)}) custom-call(bf16[256,256]{1,0:T(8,128)(2,1)S(1)} %shard_map.175.refs_0_, bf16[256,256]{1,0:T(8,128)(2,1)S(1)} %collective-permute-done.8.refs_1_, bf16[256,256]{1,0:T(8,128)(2,1)S(1)} %collective-permute-done.9.refs_2_, ...), custom_call_target="tpu_custom_call" | custom-call | flops 402653184 | bytes 3018752 | tf_op jit(solution)/shard_map/pallas_call | solution.py:26
  38.4 0.7 collective-permute-start.23
  39.1 0.8 shard_map.179.refs_1_
  39.9 0.8 shard_map.183.refs_1_
  40.8 0.8 shard_map.188.refs_2_
  41.6 0.8 shard_map.189.refs_3_
  42.5 2.2 %shard_map.178.refs_0_ = bf16[256,256]{1,0:T(8,128)(2,1)S(1)} custom-call(bf16[256,256]{1,0:T(8,128)(2,1)S(1)} %get-tuple-element.38.q_ref, bf16[256,512]{1,0:T(8,128)(2,1)S(1)} %get-tuple-element.39.refs_0_.refs_3_.refs_2_, bf16[256,512]{1,0:T(8,128)(2,1)S(1)} %get-tuple-element.40.refs_1_.refs_0_.refs_2_, ...), custom_call_target="tpu_custom_call" | custom-call | flops 335544320 | bytes 1572864 | tf_op jit(solution)/shard_map/pallas_call | solution.py:26
  44.8 0.9 %shard_map.180 = (bf16[256,256]{1,0:T(8,128)(2,1)S(1)}, bf16[256,256]{1,0:T(8,128)(2,1)S(1)}, bf16[256,256]{1,0:T(8,128)(2,1)S(1)}, bf16[256,256]{1,0:T(8,128)(2,1)S(1)}) custom-call(bf16[256,256]{1,0:T(8,128)(2,1)S(1)} %shard_map.178.refs_0_, bf16[256,1024]{1,0:T(8,128)(2,1)S(1)} %shard_map.179.refs_1_, bf16[256,1024]{1,0:T(8,128)(2,1)S(1)} %copy-done.4, ...), custom_call_target="tpu_custom_call" | custom-call | flops 671088640 | bytes 3805184 | tf_op jit(solution)/shard_map/pallas_call | solution.py:26
  45.7 0.1 collective-permute-start.15
  45.8 0.5 collective-permute-start.16
  46.3 2.0 %shard_map.186.refs_0_ = bf16[256,256]{1,0:T(8,128)(2,1)S(1)} custom-call(bf16[256,256]{1,0:T(8,128)(2,1)S(1)} %get-tuple-element.54.q_ref, bf16[256,512]{1,0:T(8,128)(2,1)S(1)} %get-tuple-element.42.refs_3_.refs_2_.refs_0_, bf16[256,512]{1,0:T(8,128)(2,1)S(1)} %get-tuple-element.41.refs_2_.refs_1_.refs_0_, ...), custom_call_target="tpu_custom_call" | custom-call | flops 335544320 | bytes 1572864 | tf_op jit(solution)/shard_map/pallas_call | solution.py:26
  48.3 1.5 %collective-permute-done.23.refs_4_ = bf16[256,512]{1,0:T(8,128)(2,1)S(1)} collective-permute-done((bf16[256,512]{1,0:T(8,128)(2,1)S(1)}, bf16[256,512]{1,0:T(8,128)(2,1)S(1)}, u32[]{:S(2)}, u32[]{:S(2)}) %collective-permute-start.23) | collective-permute-done | bytes 262176 | tf_op jit(solution)/shard_map/ppermute | solution.py:605
  49.8 2.0 %shard_map.187.refs_1_ = bf16[256,256]{1,0:T(8,128)(2,1)S(1)} custom-call(bf16[256,256]{1,0:T(8,128)(2,1)S(1)} %get-tuple-element.55.q_ref, bf16[256,512]{1,0:T(8,128)(2,1)S(1)} %get-tuple-element.41.refs_2_.refs_1_.refs_0_, bf16[256,512]{1,0:T(8,128)(2,1)S(1)} %get-tuple-element.40.refs_1_.refs_0_.refs_2_, ...), custom_call_target="tpu_custom_call" | custom-call | flops 335544320 | bytes 1572864 | tf_op jit(solution)/shard_map/pallas_call | solution.py:26
  51.8 1.6 %shard_map.190 = (bf16[512,256]{1,0:T(8,128)(2,1)S(1)}, bf16[512,256]{1,0:T(8,128)(2,1)S(1)}, bf16[512,256]{1,0:T(8,128)(2,1)S(1)}, bf16[512,256]{1,0:T(8,128)(2,1)S(1)}) custom-call(bf16[256,256]{1,0:T(8,128)(2,1)S(1)} %shard_map.186.refs_0_, bf16[256,256]{1,0:T(8,128)(2,1)S(1)} %shard_map.187.refs_1_, bf16[256,1024]{1,0:T(8,128)(2,1)S(1)} %shard_map.188.refs_2_, ...), custom_call_target="tpu_custom_call" | custom-call | flops 1342177280 | bytes 4984832 | tf_op jit(solution)/shard_map/pallas_call | solution.py:26
  53.4 0.1 collective-permute-start.25
  53.5 2.0 %shard_map.182.refs_0_ = bf16[256,256]{1,0:T(8,128)(2,1)S(1)} custom-call(bf16[256,256]{1,0:T(8,128)(2,1)S(1)} %get-tuple-element.48.q_ref, bf16[256,512]{1,0:T(8,128)(2,1)S(1)} %get-tuple-element.40.refs_1_.refs_0_.refs_2_, bf16[256,512]{1,0:T(8,128)(2,1)S(1)} %get-tuple-element.41.refs_2_.refs_1_.refs_0_, ...), custom_call_target="tpu_custom_call" | custom-call | flops 335544320 | bytes 1572864 | tf_op jit(solution)/shard_map/pallas_call | solution.py:26
  55.5 0.9 %shard_map.184 = (bf16[256,256]{1,0:T(8,128)(2,1)S(1)}, bf16[256,256]{1,0:T(8,128)(2,1)S(1)}, bf16[256,256]{1,0:T(8,128)(2,1)S(1)}, bf16[256,256]{1,0:T(8,128)(2,1)S(1)}) custom-call(bf16[256,256]{1,0:T(8,128)(2,1)S(1)} %shard_map.182.refs_0_, bf16[256,1024]{1,0:T(8,128)(2,1)S(1)} %shard_map.183.refs_1_, bf16[256,1024]{1,0:T(8,128)(2,1)S(1)} %copy-done.4, ...), custom_call_target="tpu_custom_call" | custom-call | flops 671088640 | bytes 3805184 | tf_op jit(solution)/shard_map/pallas_call | solution.py:26
  56.4 0.5 collective-permute-start.19
  56.9 0.1 collective-permute-start.20
  57.0 0.4 collective-permute-start.24
  57.5 1.6 %collective-permute-start.17 = (bf16[256,256]{1,0:T(8,128)(2,1)S(1)}, bf16[256,256]{1,0:T(8,128)(2,1)S(1)}, u32[]{:S(2)}, u32[]{:S(2)}) collective-permute-start(bf16[256,256]{1,0:T(8,128)(2,1)S(1)} %add_convert_fusion.2), channel_id=1, source_target_pairs={{0,2},{2,0},{1,3},{3,1},{4,6},{6,4},{5,7},{7,5},{8,10},{10,8},{9,1... | collective-permute-start | bytes 393224 | tf_op jit(solution)/shard_map/ppermute | solution.py:472
  59.1 0.1 add_convert_fusion
  59.2 0.6 collective-permute-start.26
  59.8 1.5 %collective-permute-start.21 = (bf16[256,256]{1,0:T(8,128)(2,1)S(1)}, bf16[256,256]{1,0:T(8,128)(2,1)S(1)}, u32[]{:S(2)}, u32[]{:S(2)}) collective-permute-start(bf16[256,256]{1,0:T(8,128)(2,1)S(1)} %add_convert_fusion.1), channel_id=1, source_target_pairs={{0,2},{2,0},{1,3},{3,1},{4,6},{6,4},{5,7},{7,5},{8,10},{10,8},{9,1... | collective-permute-start | bytes 393224 | tf_op jit(solution)/shard_map/ppermute | solution.py:472
  62.0 1.9 %collective-permute-done.17.refs_3_ = bf16[256,256]{1,0:T(8,128)(2,1)S(1)} collective-permute-done((bf16[256,256]{1,0:T(8,128)(2,1)S(1)}, bf16[256,256]{1,0:T(8,128)(2,1)S(1)}, u32[]{:S(2)}, u32[]{:S(2)}) %collective-permute-start.17) | collective-permute-done | bytes 131104 | tf_op jit(solution)/shard_map/ppermute | solution.py:472
  64.0 0.1 shard_map.181.refs_1_
  64.0 7.5 %collective-permute-done.21.refs_4_ = bf16[256,256]{1,0:T(8,128)(2,1)S(1)} collective-permute-done((bf16[256,256]{1,0:T(8,128)(2,1)S(1)}, bf16[256,256]{1,0:T(8,128)(2,1)S(1)}, u32[]{:S(2)}, u32[]{:S(2)}) %collective-permute-start.21) | collective-permute-done | bytes 131104 | tf_op jit(solution)/shard_map/ppermute | solution.py:472
  71.5 0.1 shard_map.185.refs_1_
  71.6 0.1 shard_map.191.refs_0_
  71.8 2.1 %shard_map.192 = (bf16[5120,256]{1,0:T(8,128)(2,1)S(1)}, s16[5120,128]{1,0:T(8,128)(2,1)S(1)}) custom-call(s32[48,128]{1,0:T(8,128)S(1)} %bitcast.24, bf16[512,256]{1,0:T(8,128)(2,1)S(1)} %shard_map.191.refs_0_), custom_call_target="tpu_custom_call" | custom-call | flops 1342177280 | bytes 4218880 | tf_op jit(solution)/shard_map/pallas_call | solution.py:26
  73.9 0.5 shard_map.195
  74.4 0.5 shard_map.196
  74.9 1.5 %collective-permute-start.27 = (bf16[512,256]{1,0:T(8,128)(2,1)S(1)}, bf16[512,256]{1,0:T(8,128)(2,1)S(1)}, u32[]{:S(2)}, u32[]{:S(2)}) collective-permute-start(bf16[512,256]{1,0:T(8,128)(2,1)S(1)} %get-tuple-element.67), channel_id=1, source_target_pairs={{0,4},{4,0},{8,12},{12,8},{16,20},{20,16},{24,28},{28,24},{1,5},{5... | collective-permute-start | bytes 786440 | tf_op jit(solution)/shard_map/ppermute | solution.py:258
  76.4 1.5 %collective-permute-start.28 = (bf16[512,256]{1,0:T(8,128)(2,1)S(1)}, bf16[512,256]{1,0:T(8,128)(2,1)S(1)}, u32[]{:S(2)}, u32[]{:S(2)}) collective-permute-start(bf16[512,256]{1,0:T(8,128)(2,1)S(1)} %get-tuple-element.68), channel_id=1, source_target_pairs={{0,16},{4,8},{8,4},{12,28},{16,0},{20,24},{24,20},{28,12},{1,17},{... | collective-permute-start | bytes 786440 | tf_op jit(solution)/shard_map/ppermute | solution.py:258
  77.9 2.1 %shard_map.193.local_ref = bf16[5120,256]{1,0:T(8,128)(2,1)S(1)} custom-call(s32[48,128]{1,0:T(8,128)S(1)} %bitcast.27, f32[48,128]{1,0:T(8,128)S(1)} %bitcast.29, bf16[512,256]{1,0:T(8,128)(2,1)S(1)} %shard_map.185.refs_1_, bf16[5120,256]{1,0:T(8,128)(2,1)S(1)} %get-tuple-element.62.refs_2_, s16[5120,128]{1,0:T(8,128)(2,1)S(1)} %get-tuple-element.63.refs_3_), custom_call_target="tpu_custom_call" | custom-call | flops 1342177280 | bytes 6864896 | tf_op jit(solution)/shard_map/pallas_call | solution.py:26
  80.0 5.8 %shard_map.194 = (f32[2048,256]{1,0:T(8,128)S(1)}, bf16[1024,256]{1,0:T(8,128)(2,1)}) custom-call(s32[48,128]{1,0:T(8,128)S(1)} %bitcast.30, bf16[5120,256]{1,0:T(8,128)(2,1)S(1)} %shard_map.193.local_ref, bf16[512,256]{1,0:T(8,128)(2,1)S(1)} %shard_map.191.refs_0_, bf16[512,256]{1,0:T(8,128)(2,1)S(1)} %shard_map.185.refs_1_), custom_call_target="tpu_custom_call" | custom-call | flops 5368709120 | bytes 5791744 | tf_op jit(solution)/shard_map/pallas_call | solution.py:26
  85.9 2.8 %grid.1 = bf16[2048,256]{1,0:T(8,128)(2,1)} custom-call(s32[8,128]{1,0:T(8,128)S(1)} %broadcast_in_dim.14.count_ref, s32[48,128]{1,0:T(8,128)S(1)} %bitcast.31, bf16[512,256]{1,0:T(8,128)(2,1)S(1)} %collective-permute-done.27.first_ref, bf16[512,256]{1,0:T(8,128)(2,1)S(1)} %collective-permute-done.28.second_ref, ...), custom_call_target="tpu_custom_call" | custom-call | flops 1073741824 | bytes 4194304 | tf_op jit(solution)/shard_map/grid/pallas_call | solution.py:286
  (59 shorter events, 0.2 us)
Async XLA Ops:
  0.6 8.1 %copy-start.13 = (s32[1,32,128]{2,1,0:T(8,128)S(1)}, s32[1,32,128]{2,1,0:T(8,128)}, u32[]{:S(2)}) copy-start(s32[1,32,128]{2,1,0:T(8,128)} %param.19) | copy-start | bytes 49156
  0.6 8.1 %copy-start.14 = (f32[1,32,128]{2,1,0:T(8,128)S(1)}, f32[1,32,128]{2,1,0:T(8,128)}, u32[]{:S(2)}) copy-start(f32[1,32,128]{2,1,0:T(8,128)} %param.21) | copy-start | bytes 49156
  0.6 8.1 %copy-start.5 = (bf16[2048,256]{1,0:T(8,128)(2,1)S(1)}, bf16[2048,256]{1,0:T(8,128)(2,1)}, u32[]{:S(2)}) copy-start(bf16[2048,256]{1,0:T(8,128)(2,1)} %grid_ref.1) | copy-start | bytes 3145732
  4.1 9.9 %collective-permute-start = (bf16[512,256]{1,0:T(8,128)(2,1)}, bf16[512,256]{1,0:T(8,128)(2,1)S(1)}, u32[]{:S(2)}, u32[]{:S(2)}) collective-permute-start(bf16[512,256]{1,0:T(8,128)(2,1)} %get-tuple-element.36), channel_id=1, source_target_pairs={{0,4},{4,0},{8,12},{12,8},{16,20},{20,16},{24,28},{28,24},{1,5},{5... | collective-permute-start | bytes 786440 | tf_op jit(solution)/shard_map/ppermute | solution.py:258
  7.2 5.0 %copy-start.6 = (s32[1,32,128]{2,1,0:T(8,128)S(1)}, s32[1,32,128]{2,1,0:T(8,128)}, u32[]{:S(2)}) copy-start(s32[1,32,128]{2,1,0:T(8,128)} %param.20) | copy-start | bytes 49156
  7.2 8.0 %collective-permute-start.1 = (bf16[512,256]{1,0:T(8,128)(2,1)}, bf16[512,256]{1,0:T(8,128)(2,1)S(1)}, u32[]{:S(2)}, u32[]{:S(2)}) collective-permute-start(bf16[512,256]{1,0:T(8,128)(2,1)} %get-tuple-element.37), channel_id=1, source_target_pairs={{0,16},{4,8},{8,4},{12,28},{16,0},{20,24},{24,20},{28,12},{1,17},{... | collective-permute-start | bytes 786440 | tf_op jit(solution)/shard_map/ppermute | solution.py:258
  12.2 3.0 %copy-start.2 = (bf16[1024,256]{1,0:T(8,128)(2,1)S(1)}, bf16[1024,256]{1,0:T(8,128)(2,1)}, u32[]{:S(2)}) copy-start(bf16[1024,256]{1,0:T(8,128)(2,1)} %embed_ref.7) | copy-start | bytes 1572868
  15.5 5.3 %collective-permute-start.2 = (bf16[256,256]{1,0:T(8,128)(2,1)S(1)}, bf16[256,256]{1,0:T(8,128)(2,1)S(1)}, u32[]{:S(2)}, u32[]{:S(2)}) collective-permute-start(bf16[256,256]{1,0:T(8,128)(2,1)S(1)} %shard_map.171.refs_0_), channel_id=1, source_target_pairs={{0,1},{1,0},{2,3},{3,2},{4,5},{5,4},{6,7},{7,6},{8,9},{9,8},{10,11... | collective-permute-start | bytes 393224 | tf_op jit(solution)/shard_map/ppermute | solution.py:460
  15.9 15.0 %copy-start.1 = (bf16[1024,768]{1,0:T(8,128)(2,1)S(1)}, bf16[1024,768]{1,0:T(8,128)(2,1)}, u32[]{:S(2)}) copy-start(bf16[1024,768]{1,0:T(8,128)(2,1)} %refs_5_.8) | copy-start | bytes 4718596
  15.9 15.0 %copy-start.7 = (f32[1024]{0:T(1024)S(1)}, f32[1024]{0:T(1024)}, u32[]{:S(2)}) copy-start(f32[1024]{0:T(1024)} %param.25) | copy-start | bytes 12292
  15.9 6.4 %collective-permute-start.12 = (bf16[256,256]{1,0:T(8,128)(2,1)S(1)}, bf16[256,256]{1,0:T(8,128)(2,1)S(1)}, u32[]{:S(2)}, u32[]{:S(2)}) collective-permute-start(bf16[256,256]{1,0:T(8,128)(2,1)S(1)} %shard_map.170.refs_0_), channel_id=1, source_target_pairs={{0,2},{2,0},{1,3},{3,1},{4,6},{6,4},{5,7},{7,5},{8,10},{10,8},{9,1... | collective-permute-start | bytes 393224 | tf_op jit(solution)/shard_map/ppermute | solution.py:459
  17.5 7.7 %collective-permute-start.3 = (bf16[256,256]{1,0:T(8,128)(2,1)S(1)}, bf16[256,256]{1,0:T(8,128)(2,1)S(1)}, u32[]{:S(2)}, u32[]{:S(2)}) collective-permute-start(bf16[256,256]{1,0:T(8,128)(2,1)S(1)} %shard_map.171.refs_0_), channel_id=1, source_target_pairs={{0,2},{2,0},{1,3},{3,1},{4,6},{6,4},{5,7},{7,5},{8,10},{10,8},{9,1... | collective-permute-start | bytes 393224 | tf_op jit(solution)/shard_map/ppermute | solution.py:459
  18.3 9.6 %collective-permute-start.6 = (bf16[256,256]{1,0:T(8,128)(2,1)S(1)}, bf16[256,256]{1,0:T(8,128)(2,1)S(1)}, u32[]{:S(2)}, u32[]{:S(2)}) collective-permute-start(bf16[256,256]{1,0:T(8,128)(2,1)S(1)} %shard_map.173.refs_0_.refs_1_), channel_id=1, source_target_pairs={{0,2},{2,0},{1,3},{3,1},{4,6},{6,4},{5,7},{7,5},{8,10},{10,8},{9,1... | collective-permute-start | bytes 393224 | tf_op jit(solution)/shard_map/ppermute | solution.py:459
  20.2 10.1 %collective-permute-start.9 = (bf16[256,256]{1,0:T(8,128)(2,1)S(1)}, bf16[256,256]{1,0:T(8,128)(2,1)S(1)}, u32[]{:S(2)}, u32[]{:S(2)}) collective-permute-start(bf16[256,256]{1,0:T(8,128)(2,1)S(1)} %shard_map.175.refs_0_), channel_id=1, source_target_pairs={{0,2},{2,0},{1,3},{3,1},{4,6},{6,4},{5,7},{7,5},{8,10},{10,8},{9,1... | collective-permute-start | bytes 393224 | tf_op jit(solution)/shard_map/ppermute | solution.py:459
  20.8 9.5 %collective-permute-start.11 = (bf16[256,256]{1,0:T(8,128)(2,1)S(1)}, bf16[256,256]{1,0:T(8,128)(2,1)S(1)}, u32[]{:S(2)}, u32[]{:S(2)}) collective-permute-start(bf16[256,256]{1,0:T(8,128)(2,1)S(1)} %shard_map.170.refs_0_), channel_id=1, source_target_pairs={{0,1},{1,0},{2,3},{3,2},{4,5},{5,4},{6,7},{7,6},{8,9},{9,8},{10,11... | collective-permute-start | bytes 393224 | tf_op jit(solution)/shard_map/ppermute | solution.py:460
  22.3 8.5 %collective-permute-start.13 = (bf16[256,256]{1,0:T(8,128)(2,1)S(1)}, bf16[256,256]{1,0:T(8,128)(2,1)S(1)}, u32[]{:S(2)}, u32[]{:S(2)}) collective-permute-start(bf16[256,256]{1,0:T(8,128)(2,1)S(1)} %collective-permute-done.12.refs_2_), channel_id=1, source_target_pairs={{0,1},{1,0},{2,3},{3,2},{4,5},{5,4},{6,7},{7,6},{8,9},{9,8},{10,11... | collective-permute-start | bytes 393224 | tf_op jit(solution)/shard_map/ppermute | solution.py:461
  25.2 6.7 %collective-permute-start.4 = (bf16[256,256]{1,0:T(8,128)(2,1)S(1)}, bf16[256,256]{1,0:T(8,128)(2,1)S(1)}, u32[]{:S(2)}, u32[]{:S(2)}) collective-permute-start(bf16[256,256]{1,0:T(8,128)(2,1)S(1)} %collective-permute-done.3.refs_2_), channel_id=1, source_target_pairs={{0,1},{1,0},{2,3},{3,2},{4,5},{5,4},{6,7},{7,6},{8,9},{9,8},{10,11... | collective-permute-start | bytes 393224 | tf_op jit(solution)/shard_map/ppermute | solution.py:461
  28.0 6.4 %collective-permute-start.5 = (bf16[256,256]{1,0:T(8,128)(2,1)S(1)}, bf16[256,256]{1,0:T(8,128)(2,1)S(1)}, u32[]{:S(2)}, u32[]{:S(2)}) collective-permute-start(bf16[256,256]{1,0:T(8,128)(2,1)S(1)} %shard_map.173.refs_0_.refs_1_), channel_id=1, source_target_pairs={{0,1},{1,0},{2,3},{3,2},{4,5},{5,4},{6,7},{7,6},{8,9},{9,8},{10,11... | collective-permute-start | bytes 393224 | tf_op jit(solution)/shard_map/ppermute | solution.py:460
  30.3 4.7 %collective-permute-start.7 = (bf16[256,256]{1,0:T(8,128)(2,1)S(1)}, bf16[256,256]{1,0:T(8,128)(2,1)S(1)}, u32[]{:S(2)}, u32[]{:S(2)}) collective-permute-start(bf16[256,256]{1,0:T(8,128)(2,1)S(1)} %collective-permute-done.6.refs_2_), channel_id=1, source_target_pairs={{0,1},{1,0},{2,3},{3,2},{4,5},{5,4},{6,7},{7,6},{8,9},{9,8},{10,11... | collective-permute-start | bytes 393224 | tf_op jit(solution)/shard_map/ppermute | solution.py:461
  30.3 7.1 %collective-permute-start.8 = (bf16[256,256]{1,0:T(8,128)(2,1)S(1)}, bf16[256,256]{1,0:T(8,128)(2,1)S(1)}, u32[]{:S(2)}, u32[]{:S(2)}) collective-permute-start(bf16[256,256]{1,0:T(8,128)(2,1)S(1)} %shard_map.175.refs_0_), channel_id=1, source_target_pairs={{0,1},{1,0},{2,3},{3,2},{4,5},{5,4},{6,7},{7,6},{8,9},{9,8},{10,11... | collective-permute-start | bytes 393224 | tf_op jit(solution)/shard_map/ppermute | solution.py:460
  30.8 6.6 %collective-permute-start.10 = (bf16[256,256]{1,0:T(8,128)(2,1)S(1)}, bf16[256,256]{1,0:T(8,128)(2,1)S(1)}, u32[]{:S(2)}, u32[]{:S(2)}) collective-permute-start(bf16[256,256]{1,0:T(8,128)(2,1)S(1)} %collective-permute-done.9.refs_2_), channel_id=1, source_target_pairs={{0,1},{1,0},{2,3},{3,2},{4,5},{5,4},{6,7},{7,6},{8,9},{9,8},{10,11... | collective-permute-start | bytes 393224 | tf_op jit(solution)/shard_map/ppermute | solution.py:461
  31.9 10.6 %collective-permute-start.14 = (bf16[256,512]{1,0:T(8,128)(2,1)S(1)}, bf16[256,512]{1,0:T(8,128)(2,1)S(1)}, u32[]{:S(2)}, u32[]{:S(2)}) collective-permute-start(bf16[256,512]{1,0:T(8,128)(2,1)S(1)} %get-tuple-element.42.refs_3_.refs_2_.refs_0_), channel_id=1, source_target_pairs={{0,16},{4,8},{8,4},{12,28},{16,0},{20,24},{24,20},{28,12},{1,17},{... | collective-permute-start | bytes 786440 | tf_op jit(solution)/shard_map/ppermute | solution.py:605
  34.4 4.7 %copy-start = (bf16[1024,1024]{1,0:T(8,128)(2,1)S(1)}, bf16[1024,1024]{1,0:T(8,128)(2,1)}, u32[]{:S(2)}) copy-start(bf16[1024,1024]{1,0:T(8,128)(2,1)} %w_ref.7) | copy-start | bytes 6291460
  34.4 4.7 %copy-start.8 = (s32[1024]{0:T(1024)S(1)}, s32[1024]{0:T(1024)}, u32[]{:S(2)}) copy-start(s32[1024]{0:T(1024)} %param.29) | copy-start | bytes 12292
  34.4 19.1 %collective-permute-start.18 = (bf16[256,512]{1,0:T(8,128)(2,1)S(1)}, bf16[256,512]{1,0:T(8,128)(2,1)S(1)}, u32[]{:S(2)}, u32[]{:S(2)}) collective-permute-start(bf16[256,512]{1,0:T(8,128)(2,1)S(1)} %get-tuple-element.41.refs_2_.refs_1_.refs_0_), channel_id=1, source_target_pairs={{0,16},{4,8},{8,4},{12,28},{16,0},{20,24},{24,20},{28,12},{1,17},{... | collective-permute-start | bytes 786440 | tf_op jit(solution)/shard_map/ppermute | solution.py:605
  36.0 10.3 %collective-permute-start.22 = (bf16[256,512]{1,0:T(8,128)(2,1)S(1)}, bf16[256,512]{1,0:T(8,128)(2,1)S(1)}, u32[]{:S(2)}, u32[]{:S(2)}) collective-permute-start(bf16[256,512]{1,0:T(8,128)(2,1)S(1)} %get-tuple-element.39.refs_0_.refs_3_.refs_2_), channel_id=1, source_target_pairs={{0,4},{4,0},{8,12},{12,8},{16,20},{20,16},{24,28},{28,24},{1,5},{5... | collective-permute-start | bytes 786440 | tf_op jit(solution)/shard_map/ppermute | solution.py:605
  38.4 11.4 %collective-permute-start.23 = (bf16[256,512]{1,0:T(8,128)(2,1)S(1)}, bf16[256,512]{1,0:T(8,128)(2,1)S(1)}, u32[]{:S(2)}, u32[]{:S(2)}) collective-permute-start(bf16[256,512]{1,0:T(8,128)(2,1)S(1)} %get-tuple-element.40.refs_1_.refs_0_.refs_2_), channel_id=1, source_target_pairs={{0,4},{4,0},{8,12},{12,8},{16,20},{20,16},{24,28},{28,24},{1,5},{5... | collective-permute-start | bytes 786440 | tf_op jit(solution)/shard_map/ppermute | solution.py:605
  41.6 3.1 %copy-start.3 = (bf16[1024,1024]{1,0:T(8,128)(2,1)S(1)}, bf16[1024,1024]{1,0:T(8,128)(2,1)}, u32[]{:S(2)}) copy-start(bf16[1024,1024]{1,0:T(8,128)(2,1)} %refs_5_.9) | copy-start | bytes 6291460
  41.6 3.1 %copy-start.4 = (bf16[256,1024]{1,0:T(8,128)(2,1)S(1)}, bf16[256,1024]{1,0:T(8,128)(2,1)}, u32[]{:S(2)}) copy-start(bf16[256,1024]{1,0:T(8,128)(2,1)} %refs_4_.1) | copy-start | bytes 1572868
  41.6 3.1 %copy-start.12 = (s32[1024]{0:T(1024)S(1)}, s32[1024]{0:T(1024)}, u32[]{:S(2)}) copy-start(s32[1024]{0:T(1024)} %param.31) | copy-start | bytes 12292
  45.7 14.2 %collective-permute-start.15 = (bf16[256,256]{1,0:T(8,128)(2,1)S(1)}, bf16[256,256]{1,0:T(8,128)(2,1)S(1)}, u32[]{:S(2)}, u32[]{:S(2)}) collective-permute-start(bf16[256,256]{1,0:T(8,128)(2,1)S(1)} %get-tuple-element.45), channel_id=1, source_target_pairs={{0,1},{1,0},{2,3},{3,2},{4,5},{5,4},{6,7},{7,6},{8,9},{9,8},{10,11... | collective-permute-start | bytes 393224 | tf_op jit(solution)/shard_map/ppermute | solution.py:470
  45.8 11.3 %collective-permute-start.16 = (bf16[256,256]{1,0:T(8,128)(2,1)S(1)}, bf16[256,256]{1,0:T(8,128)(2,1)S(1)}, u32[]{:S(2)}, u32[]{:S(2)}) collective-permute-start(bf16[256,256]{1,0:T(8,128)(2,1)S(1)} %get-tuple-element.47), channel_id=1, source_target_pairs={{0,1},{1,0},{2,3},{3,2},{4,5},{5,4},{6,7},{7,6},{8,9},{9,8},{10,11... | collective-permute-start | bytes 393224 | tf_op jit(solution)/shard_map/ppermute | solution.py:469
  53.4 4.1 %collective-permute-start.25 = (bf16[512,256]{1,0:T(8,128)(2,1)S(1)}, bf16[512,256]{1,0:T(8,128)(2,1)S(1)}, u32[]{:S(2)}, u32[]{:S(2)}) collective-permute-start(bf16[512,256]{1,0:T(8,128)(2,1)S(1)} %get-tuple-element.61), channel_id=1, source_target_pairs={{0,1},{1,0},{2,3},{3,2},{4,5},{5,4},{6,7},{7,6},{8,9},{9,8},{10,11... | collective-permute-start | bytes 786440 | tf_op jit(solution)/shard_map/ppermute | solution.py:469
  56.4 7.6 %collective-permute-start.19 = (bf16[256,256]{1,0:T(8,128)(2,1)S(1)}, bf16[256,256]{1,0:T(8,128)(2,1)S(1)}, u32[]{:S(2)}, u32[]{:S(2)}) collective-permute-start(bf16[256,256]{1,0:T(8,128)(2,1)S(1)} %get-tuple-element.51), channel_id=1, source_target_pairs={{0,1},{1,0},{2,3},{3,2},{4,5},{5,4},{6,7},{7,6},{8,9},{9,8},{10,11... | collective-permute-start | bytes 393224 | tf_op jit(solution)/shard_map/ppermute | solution.py:470
  56.9 2.2 %collective-permute-start.20 = (bf16[256,256]{1,0:T(8,128)(2,1)S(1)}, bf16[256,256]{1,0:T(8,128)(2,1)S(1)}, u32[]{:S(2)}, u32[]{:S(2)}) collective-permute-start(bf16[256,256]{1,0:T(8,128)(2,1)S(1)} %get-tuple-element.53), channel_id=1, source_target_pairs={{0,1},{1,0},{2,3},{3,2},{4,5},{5,4},{6,7},{7,6},{8,9},{9,8},{10,11... | collective-permute-start | bytes 393224 | tf_op jit(solution)/shard_map/ppermute | solution.py:469
  57.0 14.5 %collective-permute-start.24 = (bf16[512,256]{1,0:T(8,128)(2,1)S(1)}, bf16[512,256]{1,0:T(8,128)(2,1)S(1)}, u32[]{:S(2)}, u32[]{:S(2)}) collective-permute-start(bf16[512,256]{1,0:T(8,128)(2,1)S(1)} %get-tuple-element.59), channel_id=1, source_target_pairs={{0,1},{1,0},{2,3},{3,2},{4,5},{5,4},{6,7},{7,6},{8,9},{9,8},{10,11... | collective-permute-start | bytes 786440 | tf_op jit(solution)/shard_map/ppermute | solution.py:470
  57.5 14.2 %copy-start.9 = (s32[1,48,128]{2,1,0:T(8,128)S(1)}, s32[1,48,128]{2,1,0:T(8,128)}, u32[]{:S(2)}) copy-start(s32[1,48,128]{2,1,0:T(8,128)} %param.22) | copy-start | bytes 73732
  57.5 6.4 %collective-permute-start.17 = (bf16[256,256]{1,0:T(8,128)(2,1)S(1)}, bf16[256,256]{1,0:T(8,128)(2,1)S(1)}, u32[]{:S(2)}, u32[]{:S(2)}) collective-permute-start(bf16[256,256]{1,0:T(8,128)(2,1)S(1)} %add_convert_fusion.2), channel_id=1, source_target_pairs={{0,2},{2,0},{1,3},{3,1},{4,6},{6,4},{5,7},{7,5},{8,10},{10,8},{9,1... | collective-permute-start | bytes 393224 | tf_op jit(solution)/shard_map/ppermute | solution.py:472
  59.2 12.4 %collective-permute-start.26 = (bf16[512,256]{1,0:T(8,128)(2,1)S(1)}, bf16[512,256]{1,0:T(8,128)(2,1)S(1)}, u32[]{:S(2)}, u32[]{:S(2)}) collective-permute-start(bf16[512,256]{1,0:T(8,128)(2,1)S(1)} %add_convert_fusion), channel_id=1, source_target_pairs={{0,2},{2,0},{1,3},{3,1},{4,6},{6,4},{5,7},{7,5},{8,10},{10,8},{9,1... | collective-permute-start | bytes 786440 | tf_op jit(solution)/shard_map/ppermute | solution.py:472
  59.8 11.6 %collective-permute-start.21 = (bf16[256,256]{1,0:T(8,128)(2,1)S(1)}, bf16[256,256]{1,0:T(8,128)(2,1)S(1)}, u32[]{:S(2)}, u32[]{:S(2)}) collective-permute-start(bf16[256,256]{1,0:T(8,128)(2,1)S(1)} %add_convert_fusion.1), channel_id=1, source_target_pairs={{0,2},{2,0},{1,3},{3,1},{4,6},{6,4},{5,7},{7,5},{8,10},{10,8},{9,1... | collective-permute-start | bytes 393224 | tf_op jit(solution)/shard_map/ppermute | solution.py:472
  71.7 2.6 %copy-start.10 = (f32[1,48,128]{2,1,0:T(8,128)S(1)}, f32[1,48,128]{2,1,0:T(8,128)}, u32[]{:S(2)}) copy-start(f32[1,48,128]{2,1,0:T(8,128)} %param.24) | copy-start | bytes 73732
  74.9 11.0 %collective-permute-start.27 = (bf16[512,256]{1,0:T(8,128)(2,1)S(1)}, bf16[512,256]{1,0:T(8,128)(2,1)S(1)}, u32[]{:S(2)}, u32[]{:S(2)}) collective-permute-start(bf16[512,256]{1,0:T(8,128)(2,1)S(1)} %get-tuple-element.67), channel_id=1, source_target_pairs={{0,4},{4,0},{8,12},{12,8},{16,20},{20,16},{24,28},{28,24},{1,5},{5... | collective-permute-start | bytes 786440 | tf_op jit(solution)/shard_map/ppermute | solution.py:258
  76.4 9.5 %collective-permute-start.28 = (bf16[512,256]{1,0:T(8,128)(2,1)S(1)}, bf16[512,256]{1,0:T(8,128)(2,1)S(1)}, u32[]{:S(2)}, u32[]{:S(2)}) collective-permute-start(bf16[512,256]{1,0:T(8,128)(2,1)S(1)} %get-tuple-element.68), channel_id=1, source_target_pairs={{0,16},{4,8},{8,4},{12,28},{16,0},{20,24},{24,20},{28,12},{1,17},{... | collective-permute-start | bytes 786440 | tf_op jit(solution)/shard_map/ppermute | solution.py:258
  77.9 2.1 %copy-start.11 = (s32[1,48,128]{2,1,0:T(8,128)S(1)}, s32[1,48,128]{2,1,0:T(8,128)}, u32[]{:S(2)}) copy-start(s32[1,48,128]{2,1,0:T(8,128)} %param.23) | copy-start | bytes 73732
